TPU v7x, 32 devices: a whole 2x2x4 slice. The times are simulated.
32 devices in a mesh: wide: 8 (over z, y), narrow: 4 (over x, core).
Axes of the slice: x: 2, y: 2, z: 4, core: 2. Of those that a mesh axis runs over, the one named last changes fastest.
Arguments:
- tokens: bfloat16 [8192, 2048], P(('wide', 'narrow')), may hold values from -6 to 6
- out_grad: bfloat16 [8192, 2048], P(('wide', 'narrow')), may hold values from -6 to 6
- attn_norm: bfloat16 [2048], P(('wide', 'narrow')), may hold values from 0.099609375 to 1.8984375
- w_query: bfloat16 [2048, 2048], P(('wide', 'narrow')), may hold values from -0.125 to 0.125
- key_weight: bfloat16 [2048, 1024], P(('wide', 'narrow')), may hold values from -0.125 to 0.125
- value_weight: bfloat16 [2048, 1024], P(('wide', 'narrow')), may hold values from -0.125 to 0.125
- query_norm: bfloat16 [128], P(('wide', 'narrow')), may hold values from 0.099609375 to 1.8984375
- key_norm_gain: bfloat16 [128], P(('wide', 'narrow')), may hold values from 0.099609375 to 1.8984375
- w_out: bfloat16 [2048, 2048], P(('wide', 'narrow')), may hold values from -0.75 to 0.75
- mlp_norm: bfloat16 [2048], P(('wide', 'narrow')), may hold values from 0.099609375 to 1.8984375
- w_gate: bfloat16 [2048, 6144], P(('wide', 'narrow')), may hold values from -0.125 to 0.125
- w_up: bfloat16 [2048, 6144], P(('wide', 'narrow')), may hold values from -0.125 to 0.125
- w_down: bfloat16 [6144, 2048], P(('wide', 'narrow')), may hold values from -0.078125 to 0.078125
- doc_blocks: int32 [4, 8], replicated, may hold values from 1 to 4, 16 in all within a row
- doc_tail: int32 [4, 8], replicated, may hold values from 1 to 128
- doc_order: int32 [4, 8], replicated, may hold values from 0 to 7, each once within a row
- block_home: int32 [4, 8], replicated, may hold values from 0 to 7, each once within a row
Outputs:
- output: bfloat16 [8192, 2048], P(('wide', 'narrow'))
- tokens_grad: bfloat16 [8192, 2048], P(('wide', 'narrow'))
- attn_norm_grad: float32 [2048], P(('wide', 'narrow'))
- w_query_grad: float32 [2048, 2048], P(('wide', 'narrow'))
- w_key_grad: float32 [2048, 1024], P(('wide', 'narrow'))
- w_value_grad: float32 [2048, 1024], P(('wide', 'narrow'))
- query_norm_grad: float32 [128], P(('wide', 'narrow'))
- key_norm_grad: float32 [128], P(('wide', 'narrow'))
- w_out_grad: float32 [2048, 2048], P(('wide', 'narrow'))
- mlp_norm_grad: float32 [2048], P(('wide', 'narrow'))
- w_gate_grad: float32 [2048, 6144], P(('wide', 'narrow'))
- w_up_grad: float32 [2048, 6144], P(('wide', 'narrow'))
- w_down_grad: float32 [6144, 2048], P(('wide', 'narrow'))
Inputs may be any that keep to these rules, and one draw needn't show every extreme that they name: Owner o of narrow group n gets one document of doc_blocks[n, o] blocks; each row sums to 16, and in each row some owner gets 4. `doc_order`: each row is a permutation of the owners. `block_home`: each row is a permutation of the wide indices.
All inputs are finite; a program needn't handle non-finite values.
Results may differ from a plain program's by a relative error of at most 0.019.
Values may be sent and summed in bfloat16 or wider, within the bound.
No kernel may reach another device: no remote copies, remote signals or barrier semaphores. Data moves between devices by JAX's collectives and lax.ppermute only.
A program may use at most 448 MiB of HBM per device.

v0:
```python
import jax
import jax.numpy as jnp
from jax import lax
from jax.sharding import PartitionSpec as P

BLK = 128
OWN_BLK = 4


EPSILON = 1e-06
THETA = 1000000.0
CONTRACT_ROWS = (((0,), (0,)), ((), ()))
CONTRACT_COLS = (((1,), (1,)), ((), ()))


def row_normalize(values, gain_row):
    return (
        values * lax.rsqrt(jnp.mean(values * values, axis=-1, keepdims=True) + EPSILON) * gain_row
    )


def apply_rotary(values, token_position):
    half_size = values.shape[-1] // 2
    frequency = THETA ** (-2.0 * jnp.arange(half_size, dtype=jnp.float32) / values.shape[-1])
    angles = token_position.astype(jnp.float32)[:, None] * frequency[None, :]
    angles = jnp.concatenate([angles, angles], axis=-1)[:, None, :]
    turned = jnp.concatenate([-values[..., half_size:], values[..., :half_size]], axis=-1)
    return values * jnp.cos(angles) + turned * jnp.sin(angles)


def finish_heads(query_raw, key_unscaled, query_scale, key_scale, token_position):
    row_count = query_raw.shape[0]
    head_size = query_scale.shape[0]
    query_rows = apply_rotary(
        row_normalize(query_raw.reshape(row_count, -1, head_size), query_scale), token_position
    )
    key_row_block = apply_rotary(
        row_normalize(key_unscaled.reshape(row_count, -1, head_size), key_scale), token_position
    )
    return (query_rows.reshape(row_count, -1), key_row_block.reshape(row_count, -1))


def gated(gate_sum, up_sum):
    return jax.nn.silu(gate_sum) * up_sum


def outer_sum(left_rows, right_rows):
    return lax.dot_general(left_rows, right_rows, CONTRACT_ROWS, preferred_element_type=jnp.float32)


def times_transpose(left_rows, matrix):
    return lax.dot_general(left_rows, matrix, CONTRACT_COLS, preferred_element_type=jnp.float32)


def regroup(values, wide_count, narrow_count):
    row_count, width = values.shape
    return (
        values.reshape(row_count, wide_count, narrow_count, width // (wide_count * narrow_count))
        .transpose(0, 2, 1, 3)
        .reshape(row_count, width)
    )


def regroup_rows(values, wide_count, narrow_count):
    width, cols = values.shape
    return (
        values.reshape(wide_count, narrow_count, width // (wide_count * narrow_count), cols)
        .transpose(1, 0, 2, 3)
        .reshape(width, cols)
    )


def spread_gain(gain_grad, spacing):
    count = gain_grad.shape[0]
    return jnp.concatenate(
        [gain_grad[:, None], jnp.zeros((count, spacing - 1), jnp.float32)], axis=1
    ).reshape(count * spacing)


def term_maker(left_perm, right_rows, extra_rows):
    product = outer_sum(left_perm, right_rows)
    if extra_rows is None:
        return product
    return jnp.concatenate([product, extra_rows], axis=1)


def routing(doc_blocks, doc_tail, doc_order, block_home, owners, my_owner, my_group, block_count):
    blocks_row = lax.dynamic_index_in_dim(doc_blocks, my_group, 0, keepdims=False)
    tails_row = lax.dynamic_index_in_dim(doc_tail, my_group, 0, keepdims=False)
    order_row = lax.dynamic_index_in_dim(doc_order, my_group, 0, keepdims=False)
    homes_row = lax.dynamic_index_in_dim(block_home, my_group, 0, keepdims=False)
    owner_ids = jnp.arange(owners, dtype=jnp.int32)
    order_hits = (order_row[:, None] == owner_ids[None, :]).astype(jnp.int32)
    in_stream = jnp.sum(order_hits * blocks_row[None, :], axis=1)
    stream_start = jnp.cumsum(in_stream) - in_stream
    owner_start = jnp.sum(order_hits * stream_start[:, None], axis=0)
    my_column = jnp.sum(jnp.where(homes_row == my_owner, owner_ids, 0))
    stream_ids = jnp.arange(block_count, dtype=jnp.int32) * owners + my_column
    member = (owner_start[None, :] <= stream_ids[:, None]) & (
        stream_ids[:, None] < (owner_start + blocks_row)[None, :]
    )
    offsets = stream_ids - jnp.sum(jnp.where(member, owner_start[None, :], 0), axis=1)
    is_mine = owner_ids == my_owner
    my_start = jnp.sum(jnp.where(is_mine, owner_start, 0))
    my_blocks = jnp.sum(jnp.where(is_mine, blocks_row, 0))
    my_tail = jnp.sum(jnp.where(is_mine, tails_row, 0))
    slot_ids = jnp.arange(OWN_BLK, dtype=jnp.int32)
    columns = (my_start + slot_ids) % owners
    sources = jnp.sum(
        jnp.where(columns[:, None] == owner_ids[None, :], homes_row[None, :], 0), axis=1
    )
    picker = (slot_ids[:, None] < my_blocks) & (sources[:, None] == owner_ids[None, :])
    doc_length = (my_blocks - 1) * BLK + my_tail
    return (member.astype(jnp.bfloat16), offsets, picker.astype(jnp.bfloat16), doc_length)


def split_heads(packed_rows, query_heads, value_heads, head_size):
    document_extent = packed_rows.shape[0]
    query_rows = packed_rows[:, : query_heads * head_size].reshape(
        document_extent, value_heads, query_heads // value_heads, head_size
    )
    key_row_block = packed_rows[
        :, query_heads * head_size : (query_heads + value_heads) * head_size
    ].reshape(document_extent, value_heads, head_size)
    value_row_block = packed_rows[:, (query_heads + value_heads) * head_size :].reshape(
        document_extent, value_heads, head_size
    )
    return (query_rows, key_row_block, value_row_block)


def doc_scores(query_rows, key_row_block, doc_length):
    document_extent = query_rows.shape[0]
    places = jnp.arange(document_extent, dtype=jnp.int32)
    allowed = (places[None, :] <= places[:, None]) & (places[None, :] < doc_length)
    scores = jnp.einsum(
        "qgec,kgc->geqk", query_rows, key_row_block, preferred_element_type=jnp.float32
    ) * query_rows.shape[-1] ** (-0.5)
    return (jnp.where(allowed, scores, -1e30), allowed)


def attend_forward(packed_rows, doc_length, query_heads, value_heads, head_size):
    query_rows, key_row_block, value_row_block = split_heads(
        packed_rows, query_heads, value_heads, head_size
    )
    scores, allowed = doc_scores(query_rows, key_row_block, doc_length)
    highest = jnp.max(scores, axis=-1, keepdims=True)
    exponent = jnp.exp(scores - highest)
    totals = jnp.sum(exponent, axis=-1, keepdims=True)
    weights_low = (exponent / totals).astype(jnp.bfloat16)
    mixed_rows = jnp.einsum(
        "geqk,kgc->qgec", weights_low, value_row_block, preferred_element_type=jnp.float32
    )
    return (
        mixed_rows.reshape(packed_rows.shape[0], -1).astype(jnp.bfloat16),
        highest + jnp.log(totals),
    )


def attend_backward(
    packed_rows, log_total, grad_mixed, doc_length, query_heads, value_heads, head_size
):
    document_extent = packed_rows.shape[0]
    query_rows, key_row_block, value_row_block = split_heads(
        packed_rows, query_heads, value_heads, head_size
    )
    scores, allowed = doc_scores(query_rows, key_row_block, doc_length)
    weights = jnp.where(allowed, jnp.exp(scores - log_total), 0.0)
    grad_rows = grad_mixed.reshape(
        document_extent, value_heads, query_heads // value_heads, head_size
    )
    grad_weights = jnp.einsum(
        "qgec,kgc->geqk", grad_rows, value_row_block, preferred_element_type=jnp.float32
    )
    grad_scores = (
        weights * (grad_weights - jnp.sum(weights * grad_weights, axis=-1, keepdims=True))
    ).astype(jnp.bfloat16)
    scale_factor = head_size ** (-0.5)
    grad_queries = (
        jnp.einsum("geqk,kgc->qgec", grad_scores, key_row_block, preferred_element_type=jnp.float32)
        * scale_factor
    )
    grad_keys = (
        jnp.einsum("geqk,qgec->kgc", grad_scores, query_rows, preferred_element_type=jnp.float32)
        * scale_factor
    )
    grad_values = jnp.einsum(
        "geqk,qgec->kgc",
        weights.astype(jnp.bfloat16),
        grad_rows,
        preferred_element_type=jnp.float32,
    )
    return jnp.concatenate(
        [
            grad_queries.reshape(document_extent, -1),
            grad_keys.reshape(document_extent, -1),
            grad_values.reshape(document_extent, -1),
        ],
        axis=1,
    ).astype(jnp.bfloat16)


def body(
    tokens,
    out_grad,
    attn_norm,
    w_query,
    key_weight,
    value_weight,
    query_norm,
    key_norm_gain,
    w_out,
    mlp_norm,
    w_gate,
    w_up,
    w_down,
    doc_blocks,
    doc_tail,
    doc_order,
    block_home,
):
    owners = lax.axis_size("wide")
    my_owner = lax.axis_index("wide")
    my_group = lax.axis_index("narrow")
    local_rows = tokens.shape[0]
    block_count = local_rows // BLK
    member, offsets, picker, doc_length = routing(
        doc_blocks, doc_tail, doc_order, block_home, owners, my_owner, my_group, block_count
    )
    token_position = (offsets[:, None] * BLK + jnp.arange(BLK, dtype=jnp.int32)[None, :]).reshape(
        local_rows
    )
    attention_gain, query_full, key_full, value_full, query_gain, key_gain, out_full = (
        lax.all_gather(attn_norm, ("wide", "narrow"), axis=0, tiled=True),
        lax.all_gather(w_query, ("wide", "narrow"), axis=0, tiled=True),
        lax.all_gather(key_weight, ("wide", "narrow"), axis=0, tiled=True),
        lax.all_gather(value_weight, ("wide", "narrow"), axis=0, tiled=True),
        lax.all_gather(query_norm, ("wide", "narrow"), axis=0, tiled=True),
        lax.all_gather(key_norm_gain, ("wide", "narrow"), axis=0, tiled=True),
        lax.all_gather(w_out, ("wide", "narrow"), axis=0, tiled=True),
    )
    head_size = query_gain.shape[0]
    query_heads = query_full.shape[1] // head_size
    value_heads = key_full.shape[1] // head_size
    model_width = attention_gain.shape[0]
    hidden_width = w_gate.shape[1]
    inputs = tokens.astype(jnp.float32)
    normalized_rows = row_normalize(inputs, attention_gain.astype(jnp.float32)).astype(jnp.bfloat16)
    query_raw = jnp.dot(normalized_rows, query_full, preferred_element_type=jnp.float32)
    key_unscaled = jnp.dot(normalized_rows, key_full, preferred_element_type=jnp.float32)
    value_row_block = jnp.dot(
        normalized_rows, value_full, preferred_element_type=jnp.float32
    ).astype(jnp.bfloat16)
    query_rows, key_row_block = finish_heads(
        query_raw,
        key_unscaled,
        query_gain.astype(jnp.float32),
        key_gain.astype(jnp.float32),
        token_position,
    )
    packed_rows = jnp.concatenate(
        [query_rows.astype(jnp.bfloat16), key_row_block.astype(jnp.bfloat16), value_row_block],
        axis=1,
    )
    outgoing = jnp.einsum(
        "jo,jrc->orc",
        member,
        packed_rows.reshape(block_count, BLK, -1),
        preferred_element_type=jnp.float32,
    ).astype(jnp.bfloat16)
    arrived = lax.all_to_all(outgoing, "wide", split_axis=0, concat_axis=0, tiled=True)
    assembled = (
        jnp.einsum("is,src->irc", picker, arrived, preferred_element_type=jnp.float32)
        .astype(jnp.bfloat16)
        .reshape(OWN_BLK * BLK, -1)
    )
    attended, log_total = attend_forward(assembled, doc_length, query_heads, value_heads, head_size)
    homeward = jnp.einsum(
        "is,irc->src",
        picker,
        attended.reshape(OWN_BLK, BLK, -1),
        preferred_element_type=jnp.float32,
    ).astype(jnp.bfloat16)
    returned = lax.all_to_all(homeward, "wide", split_axis=0, concat_axis=0, tiled=True)
    mixed_rows = (
        jnp.einsum("jo,orc->jrc", member, returned, preferred_element_type=jnp.float32)
        .astype(jnp.bfloat16)
        .reshape(local_rows, -1)
    )
    middle = inputs + jnp.dot(mixed_rows, out_full, preferred_element_type=jnp.float32)
    mlp_gain, gate_full, up_full, down_full = (
        lax.all_gather(mlp_norm, ("wide", "narrow"), axis=0, tiled=True),
        lax.all_gather(w_gate, ("wide", "narrow"), axis=0, tiled=True),
        lax.all_gather(w_up, ("wide", "narrow"), axis=0, tiled=True),
        lax.all_gather(w_down, ("wide", "narrow"), axis=0, tiled=True),
    )
    normed_two = row_normalize(middle, mlp_gain.astype(jnp.float32)).astype(jnp.bfloat16)
    gate_sum = jnp.dot(normed_two, gate_full, preferred_element_type=jnp.float32)
    up_sum = jnp.dot(normed_two, up_full, preferred_element_type=jnp.float32)
    hidden = gated(gate_sum, up_sum).astype(jnp.bfloat16)
    output = (middle + jnp.dot(hidden, down_full, preferred_element_type=jnp.float32)).astype(
        jnp.bfloat16
    )
    mlp_gain_again, gate_again, up_again, down_again = (mlp_gain, gate_full, up_full, down_full)
    wide_count = lax.axis_size("wide")
    narrow_count = lax.axis_size("narrow")
    grad_hidden = times_transpose(out_grad, down_again)
    unused_gated, gated_pull = jax.vjp(gated, gate_sum, up_sum)
    grad_gate, grad_up = gated_pull(grad_hidden)
    gate_up_grad = jnp.concatenate(
        [grad_gate.astype(jnp.bfloat16), grad_up.astype(jnp.bfloat16)], axis=1
    )
    grad_normed_two = times_transpose(gate_up_grad[:, :hidden_width], gate_again) + times_transpose(
        gate_up_grad[:, hidden_width:], up_again
    )
    unused_norm, second_pull = jax.vjp(row_normalize, middle, mlp_gain_again.astype(jnp.float32))
    grad_middle_part, grad_mlp_gain = second_pull(grad_normed_two)
    grad_middle = out_grad.astype(jnp.float32) + grad_middle_part
    ffn_share = lax.psum_scatter(
        term_maker(regroup(normed_two, wide_count, narrow_count), gate_up_grad, None).astype(
            jnp.bfloat16
        ),
        "narrow",
        scatter_dimension=0,
        tiled=True,
    )
    down_share = lax.psum_scatter(
        term_maker(regroup(hidden, wide_count, narrow_count), out_grad, None).astype(jnp.bfloat16),
        "narrow",
        scatter_dimension=0,
        tiled=True,
    )
    ffn_sums = (
        lax.psum_scatter(ffn_share, "wide", scatter_dimension=0, tiled=True).astype(jnp.float32),
        lax.psum_scatter(down_share, "wide", scatter_dimension=0, tiled=True).astype(jnp.float32),
    )
    gain_again, query_again, key_again, value_again, query_gain_again, key_gain_again, out_again = (
        attention_gain,
        query_full,
        key_full,
        value_full,
        query_gain,
        key_gain,
        out_full,
    )
    grad_branch = grad_middle.astype(jnp.bfloat16)
    grad_mixed = times_transpose(grad_branch, out_again).astype(jnp.bfloat16)
    outgoing_grad = jnp.einsum(
        "jo,jrc->orc",
        member,
        grad_mixed.reshape(block_count, BLK, -1),
        preferred_element_type=jnp.float32,
    ).astype(jnp.bfloat16)
    arrived_grad = lax.all_to_all(outgoing_grad, "wide", split_axis=0, concat_axis=0, tiled=True)
    assembled_grad = (
        jnp.einsum("is,src->irc", picker, arrived_grad, preferred_element_type=jnp.float32)
        .astype(jnp.bfloat16)
        .reshape(OWN_BLK * BLK, -1)
    )
    grad_packed = attend_backward(
        assembled, log_total, assembled_grad, doc_length, query_heads, value_heads, head_size
    )
    homeward_grad = jnp.einsum(
        "is,irc->src",
        picker,
        grad_packed.reshape(OWN_BLK, BLK, -1),
        preferred_element_type=jnp.float32,
    ).astype(jnp.bfloat16)
    returned_grad = lax.all_to_all(homeward_grad, "wide", split_axis=0, concat_axis=0, tiled=True)
    grad_local = (
        jnp.einsum("jo,orc->jrc", member, returned_grad, preferred_element_type=jnp.float32)
        .astype(jnp.bfloat16)
        .reshape(local_rows, -1)
    )
    query_width = query_heads * head_size
    key_width = value_heads * head_size
    grad_queries = grad_local[:, :query_width]
    grad_keys = grad_local[:, query_width : query_width + key_width]
    grad_values = grad_local[:, query_width + key_width :]

    def heads_only(query_input, key_input, query_scale, key_scale):
        return finish_heads(query_input, key_input, query_scale, key_scale, token_position)

    unused_heads, heads_pull = jax.vjp(
        heads_only,
        query_raw,
        key_unscaled,
        query_gain_again.astype(jnp.float32),
        key_gain_again.astype(jnp.float32),
    )
    grad_query_raw, grad_key_raw, grad_query_gain, grad_key_gain = heads_pull(
        (grad_queries.astype(jnp.float32), grad_keys.astype(jnp.float32))
    )
    projection_grad = jnp.concatenate(
        [grad_query_raw.astype(jnp.bfloat16), grad_key_raw.astype(jnp.bfloat16), grad_values],
        axis=1,
    )
    grad_normed = (
        times_transpose(projection_grad[:, :query_width], query_again)
        + times_transpose(projection_grad[:, query_width : query_width + key_width], key_again)
        + times_transpose(grad_values, value_again)
    )
    unused_first, first_pull = jax.vjp(row_normalize, inputs, gain_again.astype(jnp.float32))
    grad_inputs_part, grad_attention_gain = first_pull(grad_normed)
    tokens_grad = (grad_middle + grad_inputs_part).astype(jnp.bfloat16)
    spacing = model_width // head_size
    gain_block = jnp.concatenate(
        [
            grad_attention_gain[:, None],
            grad_mlp_gain[:, None],
            spread_gain(grad_query_gain, spacing)[:, None],
            spread_gain(grad_key_gain, spacing)[:, None],
            jnp.zeros((model_width, 124), jnp.float32),
        ],
        axis=1,
    )
    proj_share = lax.psum_scatter(
        term_maker(
            regroup(normalized_rows, wide_count, narrow_count),
            projection_grad,
            regroup_rows(gain_block, wide_count, narrow_count),
        ),
        "narrow",
        scatter_dimension=0,
        tiled=True,
    )
    mixer_share = lax.psum_scatter(
        term_maker(regroup(mixed_rows, wide_count, narrow_count), grad_branch, None).astype(
            jnp.bfloat16
        ),
        "narrow",
        scatter_dimension=0,
        tiled=True,
    ).astype(jnp.float32)
    attn_sums = (
        lax.psum_scatter(proj_share, "wide", scatter_dimension=0, tiled=True),
        lax.psum_scatter(mixer_share, "wide", scatter_dimension=0, tiled=True),
    )
    projection_total = query_width + 2 * key_width
    proj_rows = attn_sums[0]
    gains_part = proj_rows[:, projection_total:]
    attn_norm_grad = gains_part[:, 0]
    mlp_norm_grad = gains_part[:, 1]
    query_norm_grad = gains_part[::spacing, 2]
    key_norm_grad = gains_part[::spacing, 3]
    w_query_grad = proj_rows[:, :query_width]
    w_key_grad = proj_rows[:, query_width : query_width + key_width]
    w_value_grad = proj_rows[:, query_width + key_width : projection_total]
    w_out_grad = attn_sums[1]
    w_gate_grad = ffn_sums[0][:, :hidden_width]
    w_up_grad = ffn_sums[0][:, hidden_width:]
    w_down_grad = ffn_sums[1]
    return (
        output,
        tokens_grad,
        attn_norm_grad,
        w_query_grad,
        w_key_grad,
        w_value_grad,
        query_norm_grad,
        key_norm_grad,
        w_out_grad,
        mlp_norm_grad,
        w_gate_grad,
        w_up_grad,
        w_down_grad,
    )


def solution(mesh):
    in_specs = (
        P(("wide", "narrow"), None),
        P(("wide", "narrow"), None),
        P(("wide", "narrow")),
        P(("wide", "narrow"), None),
        P(("wide", "narrow"), None),
        P(("wide", "narrow"), None),
        P(("wide", "narrow")),
        P(("wide", "narrow")),
        P(("wide", "narrow"), None),
        P(("wide", "narrow")),
        P(("wide", "narrow"), None),
        P(("wide", "narrow"), None),
        P(("wide", "narrow"), None),
        P(),
        P(),
        P(),
        P(),
    )
    out_specs = (
        P(("wide", "narrow"), None),
        P(("wide", "narrow"), None),
        P(("wide", "narrow")),
        P(("wide", "narrow"), None),
        P(("wide", "narrow"), None),
        P(("wide", "narrow"), None),
        P(("wide", "narrow")),
        P(("wide", "narrow")),
        P(("wide", "narrow"), None),
        P(("wide", "narrow")),
        P(("wide", "narrow"), None),
        P(("wide", "narrow"), None),
        P(("wide", "narrow"), None),
    )
    return jax.shard_map(body, mesh=mesh, in_specs=in_specs, out_specs=out_specs, check_vma=False)
```

profile of v0, /device:TPU:9, one launch (start us, length us, event | category | flops | bytes accessed | tf_op | source)
XLA Modules:
  0.0 2780.5 jit_solution(12800595395763115021)
XLA Ops:
  14.0 40.3 %all-reduce.10 = (bf16[2048]{0:T(1024)(128)(2,1)S(1)}, bf16[128]{0:T(256)(128)(2,1)S(1)}, bf16[128]{0:T(256)(128)(2,1)S(1)}, bf16[2048]{0:T(1024)(128)(2,1)}) all-reduce(bf16[2048]{0:T(1024)(128)(2,1)S(1)} %dynamic-update-slice, bf16[128]{0:T(256)(128)(2,1)S(1)} %dynamic-update-slice.2, ...), channel_id=1, replica_groups=mesh['wide'=8,'narrow'=4] {'wide','narrow'}, use_global_device_ids=true, to_apply=%add.6 | all-reduce | flops 4352 | bytes 17408
  60.4 13.8 all-gather.10.cloned.1.call-done
  74.2 3.5 fusion.119
  83.3 54.3 %all-gather.12.cloned.1.call-done = bf16[2048,1024]{1,0:T(8,128)(2,1)} async-done(((bf16[64,1024]{1,0:T(8,128)(2,1)}), bf16[2048,1024]{1,0:T(8,128)(2,1)}) %all-gather.12.cloned.1.call-update) | async-done | bytes 4194320 | tf_op jit(solution)/shard_map/all_gather | solution.py:236
  137.6 3.5 convolution_convert_fusion.8
  141.1 75.3 %all-gather.8.cloned.1.call-done = bf16[2048,2048]{1,0:T(8,128)(2,1)} async-done(((bf16[64,2048]{1,0:T(8,128)(2,1)}), bf16[2048,2048]{1,0:T(8,128)(2,1)}) %all-gather.8.cloned.1.call-update) | async-done | bytes 8388624 | tf_op jit(solution)/shard_map/all_gather | solution.py:234
  216.4 5.8 fusion.118
  232.3 5.4 convolution_convert_fusion.3
  237.6 11.3 copy.209
  248.9 5.6 all-to-all-start
  258.2 268.5 %all-to-all-done = bf16[8,128,4096]{2,1,0:T(8,128)(2,1)} async-done(((bf16[8,128,4096]{2,1,0:T(8,128)(2,1)}), bf16[8,128,4096]{2,1,0:T(8,128)(2,1)}, u32[]{:S(2)}, u32[]{:S(2)}) %all-to-all-start) | async-done | bytes 8388640 | tf_op jit(solution)/shard_map/all_to_all | solution.py:270
  526.7 13.1 fusion.22
  549.1 7.7 fusion.117
  556.8 8.8 fusion.3
  565.7 9.5 convert_bitcast_fusion.1
  577.2 4.7 copy.218
  583.9 4.3 copy.219
  588.2 5.6 all-to-all-start.1
  593.8 141.0 %all-to-all-done.1 = bf16[8,128,2048]{2,1,0:T(8,128)(2,1)} async-done(((bf16[8,128,2048]{2,1,0:T(8,128)(2,1)}), bf16[8,128,2048]{2,1,0:T(8,128)(2,1)}, u32[]{:S(2)}, u32[]{:S(2)}) %all-to-all-start.1) | async-done | bytes 4194336 | tf_op jit(solution)/shard_map/all_to_all | solution.py:283
  734.9 5.5 fusion.41
  741.8 6.1 multiply_reduce_fusion.4
  749.4 14.9 fusion.120
  764.4 46.6 %all-gather.18.cloned.1.call-done = bf16[2048,6144]{1,0:T(8,128)(2,1)} async-done(((bf16[64,6144]{1,0:T(8,128)(2,1)}), bf16[2048,6144]{1,0:T(8,128)(2,1)}) %all-gather.18.cloned.1.call-update) | async-done | bytes 25165840 | tf_op jit(solution)/shard_map/all_gather | solution.py:293
  811.0 14.2 fusion.121
  825.2 140.8 %all-gather.20.cloned.1.call-done = bf16[6144,2048]{1,0:T(8,128)(2,1)} async-done(((bf16[192,2048]{1,0:T(8,128)(2,1)}), bf16[6144,2048]{1,0:T(8,128)(2,1)}) %all-gather.20.cloned.1.call-update) | async-done | bytes 25165840 | tf_op jit(solution)/shard_map/all_gather | solution.py:294
  966.1 19.5 multiply_convert_fusion
  985.6 4.7 copy.254
  992.4 13.1 convolution_convert_fusion.1
  1005.5 16.6 fusion.122
  1022.1 21.3 multiply_reduce_fusion.1
  1045.6 7.2 convolution_convert_fusion.7
  1054.6 4.3 copy.223
  1058.9 7.3 all-to-all-start.2
  1066.2 91.4 %all-to-all-done.2 = bf16[8,128,2048]{2,1,0:T(8,128)(2,1)} async-done(((bf16[8,128,2048]{2,1,0:T(8,128)(2,1)}), bf16[8,128,2048]{2,1,0:T(8,128)(2,1)}, u32[]{:S(2)}, u32[]{:S(2)}) %all-to-all-start.2) | async-done | bytes 4194336 | tf_op jit(solution)/shard_map/all_to_all | solution.py:353
  1157.7 5.3 fusion.37
  1163.0 3.5 copy.273
  1169.3 10.0 fusion.70
  1181.5 3.4 copy.234
  1184.9 11.9 fusion
  1196.9 12.3 fusion.2
  1218.3 6.0 fusion.66
  1227.0 4.0 copy.232
  1231.0 7.0 convolution_convert_fusion.4
  1238.0 11.3 copy.235
  1249.3 6.5 all-to-all-start.3
  1259.0 178.2 %all-to-all-done.3 = bf16[8,128,4096]{2,1,0:T(8,128)(2,1)} async-done(((bf16[8,128,4096]{2,1,0:T(8,128)(2,1)}), bf16[8,128,4096]{2,1,0:T(8,128)(2,1)}, u32[]{:S(2)}, u32[]{:S(2)}) %all-to-all-start.3) | async-done | bytes 8388640 | tf_op jit(solution)/shard_map/all_to_all | solution.py:368
  1437.1 13.1 fusion.25
  1474.1 5.9 fusion.108
  1482.6 4.2 fusion.47
  1492.5 4.2 concatenate.76
  1496.7 14.7 fusion.58
  1511.4 22.7 pad_maximum_fusion
  1536.0 36.7 %convolution_convert_fusion = bf16[2048,12288]{1,0:T(8,128)(2,1)} fusion(bf16[256,2048]{0,1:T(8,128)(2,1)S(1)} %bitcast.272, bf16[256,6144]{1,0:T(8,128)(2,1)} %get-tuple-element.33, bf16[256,6144]{1,0:T(8,128)(2,1)} %get-tuple-element.34), kind=kOutput, calls=%fused_computation | convolution fusion | flops 12922650624 | bytes 57671680 | tf_op jit(solution)/shard_map/dot_general | solution.py:48
  1572.8 5.4 copy.250
  1582.0 5.8 convolution_convert_fusion.2
  1588.5 185.1 %reduce-scatter.9.cloned.1.call-done = f32[512,4224]{1,0:T(8,128)} async-done(((f32[2048,4224]{1,0:T(8,128)}), f32[512,4224]{1,0:T(8,128)}) %reduce-scatter.9.cloned.1.call-update) | async-done | bytes 8650768 | tf_op jit(solution)/shard_map/reduce_scatter | solution.py:416
  1773.7 348.9 %reduce-scatter.17.cloned.1.call-done = bf16[512,12288]{1,0:T(8,128)(2,1)} async-done(((bf16[2048,12288]{1,0:T(8,128)(2,1)}), bf16[512,12288]{1,0:T(8,128)(2,1)}) %reduce-scatter.17.cloned.1.call-update) | async-done | bytes 12582928 | tf_op jit(solution)/shard_map/reduce_scatter | solution.py:318
  2122.7 73.9 %reduce-scatter.13.cloned.1.call-done = bf16[512,2048]{1,0:T(8,128)(2,1)} async-done(((bf16[2048,2048]{1,0:T(8,128)(2,1)}), bf16[512,2048]{1,0:T(8,128)(2,1)}) %reduce-scatter.13.cloned.1.call-update) | async-done | bytes 2097168 | tf_op jit(solution)/shard_map/reduce_scatter | solution.py:426
  2196.7 4.1 convert_element_type.190
  2200.8 14.7 fusion.40
  2217.2 100.3 %reduce-scatter.23.cloned.1.call-done = bf16[192,2048]{1,0:T(8,128)(2,1)} async-done(((bf16[1536,2048]{1,0:T(8,128)(2,1)}), bf16[192,2048]{1,0:T(8,128)(2,1)}) %reduce-scatter.23.cloned.1.call-update) | async-done | bytes 786448 | tf_op jit(solution)/shard_map/reduce_scatter | solution.py:334
  2319.9 151.1 %reduce-scatter.11.cloned.1.call-done = f32[64,4224]{1,0:T(8,128)} async-done(((f32[512,4224]{1,0:T(8,128)}), f32[64,4224]{1,0:T(8,128)}) %reduce-scatter.11.cloned.1.call-update) | async-done | bytes 1081360 | tf_op jit(solution)/shard_map/reduce_scatter | solution.py:435
  2478.4 202.1 %reduce-scatter.19.cloned.1.call-done = bf16[64,12288]{1,0:T(8,128)(2,1)} async-done(((bf16[512,12288]{1,0:T(8,128)(2,1)}), bf16[64,12288]{1,0:T(8,128)(2,1)}) %reduce-scatter.19.cloned.1.call-update) | async-done | bytes 1572880 | tf_op jit(solution)/shard_map/reduce_scatter | solution.py:333
  2683.9 89.9 %reduce-scatter.15.cloned.1.call-done = f32[64,2048]{1,0:T(8,128)} async-done(((f32[512,2048]{1,0:T(8,128)}), f32[64,2048]{1,0:T(8,128)}) %reduce-scatter.15.cloned.1.call-update) | async-done | bytes 524304 | tf_op jit(solution)/shard_map/reduce_scatter | solution.py:436
  (326 shorter events, 125.9 us)
Async XLA Ops:
  7.2 4.8 copy-start
  7.2 4.8 copy-start.71
  7.2 5.8 copy-start.73
  7.2 6.0 copy-start.74
  7.2 6.3 copy-start.75
  7.2 6.5 copy-start.76
  7.2 51.3 %copy-start.16 = (bf16[256,2048]{1,0:T(8,128)(2,1)S(1)}, bf16[256,2048]{1,0:T(8,128)(2,1)}, u32[]{:S(2)}) copy-start(bf16[256,2048]{1,0:T(8,128)(2,1)} %param.17) | copy-start | bytes 3145732
  7.3 66.9 %all-gather.10.cloned.1.call-start = ((), (), s32[]{:S(2)}) async-start(), calls=%async_computation.13 | async-start | bytes 4325376 | tf_op jit(solution)/shard_map/all_gather | solution.py:235
  8.0 129.6 %all-gather.12.cloned.1.call-start = ((), (), s32[]{:S(2)}) async-start(), calls=%async_computation.14 | async-start | bytes 4325376 | tf_op jit(solution)/shard_map/all_gather | solution.py:236
  8.7 207.7 %all-gather.8.cloned.1.call-start = ((), (), s32[]{:S(2)}) async-start(), calls=%async_computation.12 | async-start | bytes 8650752 | tf_op jit(solution)/shard_map/all_gather | solution.py:234
  9.5 732.3 %all-gather.14.cloned.1.call-start = ((), (), s32[]{:S(2)}) async-start(), calls=%async_computation.15 | async-start | bytes 8650752 | tf_op jit(solution)/shard_map/all_gather | solution.py:239
  10.1 739.4 %all-gather.16.cloned.1.call-start = ((), (), s32[]{:S(2)}) async-start(), calls=%async_computation.16 | async-start | bytes 25952256 | tf_op jit(solution)/shard_map/all_gather | solution.py:292
  10.6 800.3 %all-gather.18.cloned.1.call-start = ((), (), s32[]{:S(2)}) async-start(), calls=%async_computation.17 | async-start | bytes 25952256 | tf_op jit(solution)/shard_map/all_gather | solution.py:293
  11.2 954.9 %all-gather.20.cloned.1.call-start = ((), (), s32[]{:S(2)}) async-start(), calls=%async_computation.18 | async-start | bytes 25952256 | tf_op jit(solution)/shard_map/all_gather | solution.py:294
  54.3 6.1 copy-start.51
  54.3 6.1 copy-start.63
  54.3 23.4 copy-start.60
  58.5 168.0 %copy-start.41 = (f32[256,128]{1,0:T(8,128)}, f32[256,128]{1,0:T(8,128)S(1)}, u32[]{:S(2)}) copy-start(f32[256,128]{1,0:T(8,128)S(1)} %get-tuple-element.53) | copy-start | bytes 393220
  58.5 168.7 %copy-start.37 = (f32[256,128]{1,0:T(8,128)}, f32[256,128]{1,0:T(8,128)S(1)}, u32[]{:S(2)}) copy-start(f32[256,128]{1,0:T(8,128)S(1)} %get-tuple-element.52) | copy-start | bytes 393220
  59.4 18.3 copy-start.56
  60.4 156.0 %copy-start.35 = (bf16[256,2048]{1,0:T(8,128)(2,1)}, bf16[256,2048]{1,0:T(8,128)(2,1)S(1)}, u32[]{:S(2)}) copy-start(bf16[256,2048]{1,0:T(8,128)(2,1)S(1)} %fusion.46) | copy-start | bytes 3145732
  77.9 3.2 copy-start.5
  228.8 3.3 copy-start.46
  248.9 7.5 copy-start.69
  248.9 8.9 copy-start.70
  248.9 277.8 %all-to-all-start = ((bf16[8,128,4096]{2,1,0:T(8,128)(2,1)}), bf16[8,128,4096]{2,1,0:T(8,128)(2,1)}, u32[]{:S(2)}, u32[]{:S(2)}) async-start(bf16[8,128,4096]{2,1,0:T(8,128)(2,1)} %copy.209), calls=%async_computation | async-start | bytes 16777216 | tf_op jit(solution)/shard_map/all_to_all | solution.py:270
  258.2 290.9 %copy-start.25 = (pred[512,512]{0,1:T(8,128)(4,1)}, pred[512,512]{0,1:T(8,128)(4,1)S(1)}, u32[]{:S(2)}) copy-start(pred[512,512]{0,1:T(8,128)(4,1)S(1)} %fusion.79) | copy-start | bytes 786436
  545.8 11.0 copy-start.13
  549.1 7.8 copy-start.7
  556.8 8.8 copy-start.30
  588.2 5.6 copy-start.65
  588.2 146.7 %all-to-all-start.1 = ((bf16[8,128,2048]{2,1,0:T(8,128)(2,1)}), bf16[8,128,2048]{2,1,0:T(8,128)(2,1)}, u32[]{:S(2)}, u32[]{:S(2)}) async-start(bf16[8,128,2048]{2,1,0:T(8,128)(2,1)} %copy.219), calls=%async_computation.1 | async-start | bytes 8388608 | tf_op jit(solution)/shard_map/all_to_all | solution.py:283
  593.8 994.2 %reduce-scatter.21.cloned.1.call-start = ((), (), s32[]{:S(2)}) async-start(), calls=%async_computation.25 | async-start | bytes 31457280 | tf_op jit(solution)/shard_map/reduce_scatter | solution.py:326
  593.8 147.9 %copy-start.17 = (bf16[256,2048]{1,0:T(8,128)(2,1)S(1)}, bf16[256,2048]{1,0:T(8,128)(2,1)}, u32[]{:S(2)}) copy-start(bf16[256,2048]{1,0:T(8,128)(2,1)} %param.17) | copy-start | bytes 3145732
  749.4 61.6 %copy-start.33 = (bf16[256,2048]{1,0:T(8,128)(2,1)}, bf16[256,2048]{1,0:T(8,128)(2,1)S(1)}, u32[]{:S(2)}) copy-start(bf16[256,2048]{1,0:T(8,128)(2,1)S(1)} %multiply_convert_fusion.3) | copy-start | bytes 3145732
  764.4 201.7 %copy-start.28 = (bf16[256,2048]{1,0:T(8,128)(2,1)S(1)}, bf16[256,2048]{1,0:T(8,128)(2,1)}, u32[]{:S(2)}) copy-start(bf16[256,2048]{1,0:T(8,128)(2,1)} %param.18) | copy-start | bytes 3145732
  1005.5 16.6 copy-start.21
  1022.1 21.3 copy-start.29
  1045.6 7.2 copy-start.9
  1058.9 98.7 %all-to-all-start.2 = ((bf16[8,128,2048]{2,1,0:T(8,128)(2,1)}), bf16[8,128,2048]{2,1,0:T(8,128)(2,1)}, u32[]{:S(2)}, u32[]{:S(2)}) async-start(bf16[8,128,2048]{2,1,0:T(8,128)(2,1)} %copy.223), calls=%async_computation.2 | async-start | bytes 8388608 | tf_op jit(solution)/shard_map/all_to_all | solution.py:353
  1179.3 5.7 copy-start.31
  1196.9 15.6 copy-start.8
  1209.2 3.3 copy-start.2
  1215.3 3.1 copy-start.14
  1226.9 4.0 copy-start.47
  1249.3 6.5 copy-start.36
  1249.3 187.9 %all-to-all-start.3 = ((bf16[8,128,4096]{2,1,0:T(8,128)(2,1)}), bf16[8,128,4096]{2,1,0:T(8,128)(2,1)}, u32[]{:S(2)}, u32[]{:S(2)}) async-start(bf16[8,128,4096]{2,1,0:T(8,128)(2,1)} %copy.235), calls=%async_computation.3 | async-start | bytes 16777216 | tf_op jit(solution)/shard_map/all_to_all | solution.py:368
  1255.8 517.9 %reduce-scatter.9.cloned.1.call-start = ((), (), s32[]{:S(2)}) async-start(), calls=%async_computation.19 | async-start | bytes 43253760 | tf_op jit(solution)/shard_map/reduce_scatter | solution.py:416
  1461.3 4.3 copy-start.54
  1462.7 8.6 copy-start.48
  1474.1 5.9 copy-start.32
  1482.6 5.6 copy-start.66
  1482.6 7.2 copy-start.67
  1492.5 4.2 copy-start.27
  1534.2 588.5 %reduce-scatter.17.cloned.1.call-start = ((), (), s32[]{:S(2)}) async-start(), calls=%async_computation.23 | async-start | bytes 62914560 | tf_op jit(solution)/shard_map/reduce_scatter | solution.py:318
  1572.7 9.3 copy-start.10
  1572.7 623.9 %reduce-scatter.13.cloned.1.call-start = ((), (), s32[]{:S(2)}) async-start(), calls=%async_computation.21 | async-start | bytes 10485760 | tf_op jit(solution)/shard_map/reduce_scatter | solution.py:426
  1587.9 729.6 %reduce-scatter.23.cloned.1.call-start = ((), (), s32[]{:S(2)}) async-start(), calls=%async_computation.26 | async-start | bytes 7077888 | tf_op jit(solution)/shard_map/reduce_scatter | solution.py:334
  1588.5 882.5 %reduce-scatter.11.cloned.1.call-start = ((), (), s32[]{:S(2)}) async-start(), calls=%async_computation.20 | async-start | bytes 9732096 | tf_op jit(solution)/shard_map/reduce_scatter | solution.py:435
  1773.7 906.8 %reduce-scatter.19.cloned.1.call-start = ((), (), s32[]{:S(2)}) async-start(), calls=%async_computation.24 | async-start | bytes 14155776 | tf_op jit(solution)/shard_map/reduce_scatter | solution.py:333
  2122.7 651.1 %reduce-scatter.15.cloned.1.call-start = ((), (), s32[]{:S(2)}) async-start(), calls=%async_computation.22 | async-start | bytes 4718592 | tf_op jit(solution)/shard_map/reduce_scatter | solution.py:436
  2200.8 14.7 copy-start.59
  2200.8 14.7 copy-start.45
  2476.6 297.2 %copy-start.1 = (s32[4,8]{1,0:T(4,128)S(1)}, s32[4,8]{1,0:T(4,128)}, u32[]{:S(2)}) copy-start(s32[4,8]{1,0:T(4,128)} %param.32) | copy-start | bytes 388
  (32 other events, 51.8 us)
Sparse Core Ops, SparseCore 0:
  10.9 63.2 all-gather.9
  77.0 60.4 all-gather.11
  140.5 75.8 all-gather.7
  219.1 159.9 all-gather.13
  381.8 199.4 all-gather.15
  584.0 226.9 all-gather.17
  813.8 152.1 all-gather.19
  1005.6 181.2 reduce-scatter.20
  1534.3 239.3 reduce-scatter.8
  1776.1 346.5 reduce-scatter.16
  2125.2 71.3 reduce-scatter.12
  2200.1 117.2 reduce-scatter.22
  2321.0 149.8 reduce-scatter.10
  2474.4 206.0 reduce-scatter.18
  2684.6 89.1 reduce-scatter.14
where the time goes:
time: 2790 us; the launch traced here: 2780 us
  waiting for transfers between devices  2170 us (78%)
  matrix products  310 us (11%)
  local copies, waits for them, and re-layouts  134 us (5%)
  other arithmetic  87.5 us (3%)
  blocking collectives  40.3 us (1%)
    reduce_scatter x1, waiting for transfers between devices, body(): lax.psum_scatter(term_maker(regroup(normed_two, wide_count, narrow_count)...  349 us
    all_to_all x1, waiting for transfers between devices, body(): lax.all_to_all(outgoing, 'wide', split_axis=0, concat_axis=0, tiled=True)  268 us
    reduce_scatter x1, waiting for transfers between devices, body(): lax.psum_scatter(ffn_share, 'wide', scatter_dimension=0, tiled=True)  202 us
    reduce_scatter x1, waiting for transfers between devices, body(): lax.psum_scatter(term_maker(regroup(normalized_rows, wide_count, narrow_c...  185 us
    all_to_all x1, waiting for transfers between devices, body(): lax.all_to_all(homeward_grad, 'wide', split_axis=0, concat_axis=0, tiled=...  178 us
    reduce_scatter x1, waiting for transfers between devices, body(): lax.psum_scatter(proj_share, 'wide', scatter_dimension=0, tiled=True)  151 us
    all_to_all x1, waiting for transfers between devices, body(): lax.all_to_all(homeward, 'wide', split_axis=0, concat_axis=0, tiled=True)  141 us
    all_gather x1, waiting for transfers between devices, body(): lax.all_gather(w_down, ('wide', 'narrow'), axis=0, tiled=True)  141 us
  transfers between devices with their start and end apart: 19, of which 16 were waited for; matrix products, arithmetic and copies ran while one was open for 17% of the time, Pallas kernels for 0%

commit v1 on v0

v1 whole, which is shorter than its diff:
```python
import functools

import jax
import jax.numpy as jnp
import numpy as np
from jax import lax
from jax.experimental import pallas as pl
from jax.experimental.pallas import tpu as pltpu
from jax.sharding import PartitionSpec as P

BLK = 128
OWN_BLK = 4
EPSILON = 1e-06
THETA = 1000000.0
LANES = 128
NARROW = 4
CONTRACT_ROWS = (((0,), (0,)), ((), ()))
CONTRACT_COLS = (((1,), (1,)), ((), ()))
NEGATIVE = -1e30
F32 = jnp.float32
BF16 = jnp.bfloat16
DEVICES = ("wide", "narrow")


def row_normalize(values, gain_row):
    return (
        values * lax.rsqrt(jnp.mean(values * values, axis=-1, keepdims=True) + EPSILON) * gain_row
    )


def apply_rotary(values, cosines, sines):
    half_size = values.shape[-1] // 2
    turned = jnp.concatenate([-values[..., half_size:], values[..., :half_size]], axis=-1)
    return values * cosines[:, None, :] + turned * sines[:, None, :]


def finish_heads(raw, scale, cosines, sines):
    rows = raw.shape[0]
    heads = raw.reshape(rows, -1, scale.shape[0])
    return apply_rotary(row_normalize(heads, scale), cosines, sines).reshape(rows, -1)


def gated(gate_sum, up_sum):
    return jax.nn.silu(gate_sum) * up_sum


def dot(left, right):
    return jnp.dot(left, right, preferred_element_type=F32)


def outer_sum(left_rows, right_rows):
    return lax.dot_general(left_rows, right_rows, CONTRACT_ROWS, preferred_element_type=F32)


def times_transpose(left_rows, matrix):
    return lax.dot_general(left_rows, matrix, CONTRACT_COLS, preferred_element_type=F32)


def ring_order(count):
    rows = count // 2
    return [2 * i for i in range(rows)] + [2 * i + 1 for i in reversed(range(rows))]


class Ring:
    def __init__(self, count):
        self.count = count
        order = ring_order(count)
        place = np.zeros(count, np.int32)
        for i, device in enumerate(order):
            place[device] = i
        self.onward = [(order[i], order[(i + 1) % count]) for i in range(count)]
        self.back = [(b, a) for a, b in self.onward]
        self.order = jnp.asarray(np.array(order + order + order, np.int32))
        self.place = jnp.asarray(place)[lax.axis_index("wide")]

    def device(self, shift):
        return self.order[self.place + self.count + shift]

    def send(self, value, forward):
        return lax.ppermute(value, "wide", self.onward if forward else self.back)


def no_op(out_ref):
    pass


def blank(shape, dtype):
    return pl.pallas_call(
        no_op,
        out_shape=jax.ShapeDtypeStruct(shape, dtype),
        out_specs=pl.BlockSpec(memory_space=pl.ANY),
    )()


def ring_gather(ring, part):
    if ring.count > 8:
        return lax.all_gather(part, "wide", axis=0, tiled=True)
    rows, cols = part.shape
    half = rows // 2
    whole = blank((ring.count * rows, cols), part.dtype)

    def put(whole, value, shift, extra):
        return lax.dynamic_update_slice(whole, value, (ring.device(shift) * rows + extra, 0))

    whole = put(whole, part, 0, 0)
    ahead, behind = part, part
    for step in range(1, ring.count // 2):
        ahead, behind = ring.send(ahead, True), ring.send(behind, False)
        whole = put(put(whole, ahead, -step, 0), behind, step, 0)
    last = ring.count // 2
    whole = put(whole, ring.send(ahead[:half], True), -last, 0)
    return put(whole, ring.send(behind[half:], False), last, half)


def ring_reduce(ring, terms):
    if ring.count > 8:
        return lax.psum_scatter(terms, "wide", scatter_dimension=0, tiled=True).astype(F32)
    rows = terms.shape[0] // ring.count
    cols = terms.shape[1]
    half = rows // 2

    def term(shift):
        return lax.dynamic_slice(terms, (ring.device(shift) * rows, 0), (rows, cols))

    last = ring.count // 2
    far = term(last)
    ahead, behind = ring.send(far[:half], True), ring.send(far[half:], False)
    for step in range(last - 1, 0, -1):
        mine, other = term(step), term(-step)
        if step == last - 1:
            ahead = jnp.concatenate([join(mine[:half], ahead), mine[half:]], axis=0)
            behind = jnp.concatenate([other[:half], join(other[half:], behind)], axis=0)
        else:
            ahead, behind = join(mine, ahead), join(other, behind)
        ahead, behind = ring.send(ahead, True), ring.send(behind, False)
    return term(0).astype(F32) + ahead.astype(F32) + behind.astype(F32)


def join(left, right):
    return (left.astype(F32) + right.astype(F32)).astype(BF16)


def swap(value, bit):
    return lax.ppermute(value, "narrow", [(i, i ^ bit) for i in range(NARROW)])


def narrow_gather(value):
    across = swap(value, 2)
    return jnp.concatenate([value, swap(value, 1), across, swap(across, 1)], axis=0)


def narrow_reduce(terms):
    rows = terms.shape[0] // NARROW
    low = terms.astype(BF16)
    parts = [low[i * rows : (i + 1) * rows] for i in range(NARROW)]
    near, far = swap(parts[1], 1), swap(parts[3], 1)
    across = swap(join(parts[2], far), 2)
    return parts[0].astype(F32) + near.astype(F32) + across.astype(F32)


def everyone_sum(vector, wide_count):
    for bit in (1, 2):
        vector = vector + swap(vector, bit)
    bit = 1
    while bit < wide_count:
        vector = vector + lax.ppermute(
            vector, "wide", [(i, i ^ bit) for i in range(wide_count)]
        )
        bit *= 2
    return vector


def layout(doc_blocks, doc_order, block_home, my_wide, block_count):
    owners = doc_blocks.shape[1]
    owner_ids = jnp.arange(owners, dtype=jnp.int32)
    hits = (doc_order[:, :, None] == owner_ids[None, None, :]).astype(jnp.int32)
    in_stream = jnp.sum(hits * doc_blocks[:, None, :], axis=2)
    before = (owner_ids[:, None] < owner_ids[None, :]).astype(jnp.int32)
    stream_start = jnp.sum(in_stream[:, :, None] * before[None], axis=1)
    owner_start = jnp.sum(hits * stream_start[:, :, None], axis=1)
    column = jnp.sum(jnp.where(block_home == my_wide, owner_ids[None, :], 0), axis=1)
    stream_ids = jnp.arange(block_count, dtype=jnp.int32)[None, :] * owners + column[:, None]
    member = (owner_start[:, None, :] <= stream_ids[:, :, None]) & (
        stream_ids[:, :, None] < (owner_start + doc_blocks)[:, None, :]
    )
    offsets = stream_ids - jnp.sum(jnp.where(member, owner_start[:, None, :], 0), axis=2)
    return owner_start, offsets


def stream_table(group, owner_start, doc_blocks, doc_tail, block_home, block_count):
    def pick(table):
        return lax.dynamic_index_in_dim(table, group, 0, keepdims=False)

    starts, blocks, tails, homes = pick(owner_start), pick(doc_blocks), pick(doc_tail), pick(block_home)
    owners = starts.shape[0]
    ids = jnp.arange(owners * block_count, dtype=jnp.int32)
    member = (starts[None, :] <= ids[:, None]) & (ids[:, None] < (starts + blocks)[None, :])

    def chosen(values):
        return jnp.sum(jnp.where(member, values[None, :], 0), axis=1)

    home = jnp.sum(
        jnp.where(
            (ids % owners)[:, None] == jnp.arange(owners, dtype=jnp.int32)[None, :],
            homes[None, :],
            0,
        ),
        axis=1,
    )
    place = home * block_count + ids // owners
    return jnp.stack([place, chosen(starts), chosen((blocks - 1) * BLK + tails)])


def window(table, rows_ref, b, heads, size):
    first, length = table[1, b], table[2, b]
    width = heads * size
    mine = rows_ref[pl.ds(pl.multiple_of(table[0, b] * BLK, BLK), BLK), :width]
    queries = jnp.concatenate([mine[:, i * size : (i + 1) * size] for i in range(heads)], axis=0)
    spot = (b - first) * BLK
    row = lax.broadcasted_iota(jnp.int32, (heads, BLK, BLK), 1).reshape(heads * BLK, BLK) + spot
    col = lax.broadcasted_iota(jnp.int32, (heads * BLK, BLK), 1) + spot
    starts, keys, values, scores = [], [], [], []
    for i in range(OWN_BLK):
        start = pl.multiple_of(table[0, jnp.maximum(b - i, 0)] * BLK, BLK)
        key = rows_ref[pl.ds(start, BLK), width : width + size]
        col_i = col - i * BLK
        allowed = (col_i <= row) & (col_i < length) & (col_i >= 0)
        score = times_transpose(queries, key) * size ** (-0.5)
        starts.append(start)
        keys.append(key)
        values.append(rows_ref[pl.ds(start, BLK), width + size : width + 2 * size])
        scores.append(jnp.where(allowed, score, NEGATIVE))
    highest = scores[0]
    for score in scores[1:]:
        highest = jnp.maximum(highest, score)
    highest = jnp.max(highest, axis=-1, keepdims=True)
    powers = [jnp.exp(score - highest) for score in scores]
    total = powers[0]
    for power in powers[1:]:
        total = total + power
    total = jnp.sum(total, axis=-1, keepdims=True)
    weights = [power / total for power in powers]
    return mine, queries, starts, keys, values, weights


def forward_kernel(heads, size, table, rows_ref, out_ref):
    def step(b, carry):
        _, _, starts, _, values, weights = window(table, rows_ref, b, heads, size)
        mixed = dot(weights[0].astype(BF16), values[0])
        for weight, value in zip(weights[1:], values[1:]):
            mixed = mixed + dot(weight.astype(BF16), value)
        for i in range(heads):
            out_ref[pl.ds(starts[0], BLK), i * size : (i + 1) * size] = mixed[
                i * BLK : (i + 1) * BLK
            ].astype(BF16)
        return carry

    lax.fori_loop(0, table.shape[1], step, 0)


def backward_kernel(heads, size, table, rows_ref, grad_ref, out_ref, sums):
    sums[...] = jnp.zeros_like(sums)
    scale = size ** (-0.5)

    def step(b, carry):
        _, queries, starts, keys, values, weights = window(table, rows_ref, b, heads, size)
        grads = grad_ref[pl.ds(starts[0], BLK), :]
        grads = jnp.concatenate([grads[:, i * size : (i + 1) * size] for i in range(heads)], axis=0)
        pulls = [times_transpose(grads, value) for value in values]
        total = weights[0] * pulls[0]
        for weight, pull in zip(weights[1:], pulls[1:]):
            total = total + weight * pull
        total = jnp.sum(total, axis=-1, keepdims=True)
        grad_query = None
        for i in range(OWN_BLK):
            grad_score = (weights[i] * (pulls[i] - total)).astype(BF16)
            part = dot(grad_score, keys[i])
            grad_query = part if grad_query is None else grad_query + part
            spot = pl.ds(starts[i], BLK)
            sums[spot, :size] += outer_sum(grad_score, queries) * scale
            sums[spot, size:] += outer_sum(weights[i].astype(BF16), grads)
        for i in range(heads):
            out_ref[pl.ds(starts[0], BLK), i * size : (i + 1) * size] = (
                grad_query[i * BLK : (i + 1) * BLK] * scale
            ).astype(BF16)
        return carry

    lax.fori_loop(0, table.shape[1], step, 0)
    out_ref[:, heads * size :] = sums[...].astype(BF16)


def attend(table, rows, heads, size):
    return pl.pallas_call(
        functools.partial(forward_kernel, heads, size),
        out_shape=jax.ShapeDtypeStruct((rows.shape[0], heads * size), BF16),
        in_specs=[
            pl.BlockSpec(memory_space=pltpu.SMEM),
            pl.BlockSpec(memory_space=pltpu.VMEM),
        ],
        out_specs=pl.BlockSpec(memory_space=pltpu.VMEM),
        name="attend",
    )(table, rows)


def attend_back(table, rows, grads, heads, size):
    return pl.pallas_call(
        functools.partial(backward_kernel, heads, size),
        out_shape=jax.ShapeDtypeStruct(rows.shape, BF16),
        in_specs=[
            pl.BlockSpec(memory_space=pltpu.SMEM),
            pl.BlockSpec(memory_space=pltpu.VMEM),
            pl.BlockSpec(memory_space=pltpu.VMEM),
        ],
        out_specs=pl.BlockSpec(memory_space=pltpu.VMEM),
        scratch_shapes=[pltpu.VMEM((rows.shape[0], 2 * size), F32)],
        name="attend_back",
    )(table, rows, grads)


def body(
    tokens,
    out_grad,
    attn_norm,
    w_query,
    key_weight,
    value_weight,
    query_norm,
    key_norm_gain,
    w_out,
    mlp_norm,
    w_gate,
    w_up,
    w_down,
    doc_blocks,
    doc_tail,
    doc_order,
    block_home,
):
    wide_count = lax.axis_size("wide")
    my_wide = lax.axis_index("wide")
    me = lax.axis_index("narrow")
    device_count = wide_count * NARROW
    ring = Ring(wide_count)
    rows = tokens.shape[0]
    block_count = rows // BLK
    head_size = query_norm.shape[0] * device_count
    query_width = w_query.shape[1] // NARROW
    key_width = key_weight.shape[1] // NARROW
    value_heads = key_width // head_size
    group_heads = query_width // key_width
    hidden = w_gate.shape[1] // NARROW
    shard = w_query.shape[0]
    model_width = w_query.shape[1]
    parts = wide_count // (NARROW * value_heads)
    head_width = (group_heads + 2) * head_size

    def narrow_columns(weight):
        return weight.reshape(shard, NARROW, -1).transpose(1, 0, 2)

    def hidden_columns(weight):
        return (
            weight.reshape(shard, wide_count, NARROW, -1)
            .transpose(2, 0, 1, 3)
            .reshape(NARROW, shard, hidden)
        )

    def pad_rows(values):
        return jnp.concatenate([values, jnp.zeros((shard - values.shape[0],), BF16)])

    gains = jnp.stack(
        [attn_norm, mlp_norm, pad_rows(query_norm), pad_rows(key_norm_gain)], axis=1
    )
    gains = jnp.concatenate([gains, jnp.zeros((shard, LANES - 4), BF16)], axis=1)
    first_pieces = jnp.concatenate(
        [
            narrow_columns(w_query),
            narrow_columns(key_weight),
            narrow_columns(value_weight),
            jnp.broadcast_to(gains[None], (NARROW, shard, LANES)),
        ],
        axis=2,
    )
    first_slice = lax.all_to_all(
        first_pieces, "narrow", split_axis=0, concat_axis=0, tiled=True
    ).reshape(NARROW * shard, -1)
    first_full = ring_gather(ring, first_slice)
    projection_width = query_width + 2 * key_width
    projection = first_full[:, :projection_width]
    gain_columns = first_full[:, projection_width : projection_width + 4].astype(F32)
    attention_gain = gain_columns[:, 0]
    mlp_gain = gain_columns[:, 1]
    norm_gains = gain_columns.reshape(device_count, shard, 4)[:, : query_norm.shape[0]]
    query_gain = norm_gains[:, :, 2].reshape(head_size)
    key_gain = norm_gains[:, :, 3].reshape(head_size)

    out_moves = [
        (g, (g % wide_count) * NARROW + g // wide_count) for g in range(device_count)
    ]
    out_weight = ring_gather(ring, lax.ppermute(w_out, DEVICES, out_moves))
    gate_up_pieces = jnp.concatenate([hidden_columns(w_gate), hidden_columns(w_up)], axis=2)
    gate_up = ring_gather(
        ring,
        lax.all_to_all(
            gate_up_pieces, "narrow", split_axis=0, concat_axis=0, tiled=True
        ).reshape(NARROW * shard, -1),
    )
    down = ring_gather(ring, w_down)

    inputs = tokens.astype(F32)
    all_inputs = narrow_gather(tokens).astype(F32)
    normed = row_normalize(all_inputs, attention_gain).astype(BF16)
    raw = dot(normed, projection)
    query_raw = raw[:, :query_width]
    key_raw = raw[:, query_width : query_width + key_width]
    value_rows = raw[:, query_width + key_width :].astype(BF16)
    owner_start, offsets = layout(doc_blocks, doc_order, block_home, my_wide, block_count)
    block_order = me ^ jnp.arange(NARROW, dtype=jnp.int32)
    my_offsets = jnp.take(offsets, block_order, axis=0)
    position = (
        my_offsets.reshape(-1, 1) * BLK + jnp.arange(BLK, dtype=jnp.int32)[None, :]
    ).reshape(-1)
    half_size = head_size // 2
    frequency = THETA ** (-2.0 * jnp.arange(half_size, dtype=F32) / head_size)
    angles = position.astype(F32)[:, None] * frequency[None, :]
    cosines, sines = jnp.cos(angles), jnp.sin(angles)
    cosines = jnp.concatenate([cosines, cosines], axis=-1)
    sines = jnp.concatenate([sines, sines], axis=-1)
    query_rows, query_pull = jax.vjp(
        lambda value, gain: finish_heads(value, gain, cosines, sines), query_raw, query_gain
    )
    key_rows, key_pull = jax.vjp(
        lambda value, gain: finish_heads(value, gain, cosines, sines), key_raw, key_gain
    )

    def by_group(values):
        return jnp.take(values.reshape(NARROW, rows, -1), block_order, axis=0)

    def to_heads(values, per_head):
        values = by_group(values).reshape(NARROW, rows, value_heads, per_head)
        return values.transpose(0, 2, 1, 3)

    def exchange(pieces):
        pieces = jnp.broadcast_to(
            pieces[:, :, None], pieces.shape[:2] + (parts,) + pieces.shape[2:]
        ).reshape(wide_count, rows, -1)
        return lax.all_to_all(pieces, "wide", split_axis=0, concat_axis=0, tiled=True).reshape(
            wide_count * rows, -1
        )

    def exchange_back(values):
        pieces = lax.all_to_all(
            values.reshape(wide_count, rows, -1), "wide", split_axis=0, concat_axis=0, tiled=True
        )
        return pieces.reshape(NARROW, value_heads, parts, rows, -1)[:, :, 0]

    def from_heads(pieces):
        values = pieces.transpose(0, 2, 1, 3).reshape(NARROW, rows, -1)
        return jnp.take(values, block_order, axis=0).reshape(NARROW * rows, -1)

    per_group = group_heads * head_size
    arrived = exchange(
        jnp.concatenate(
            [
                to_heads(query_rows.astype(BF16), per_group),
                to_heads(key_rows.astype(BF16), head_size),
                to_heads(value_rows, head_size),
            ],
            axis=3,
        )
    )
    table = stream_table(
        my_wide // (wide_count // NARROW), owner_start, doc_blocks, doc_tail, block_home, block_count
    )
    attended = attend(table, arrived, group_heads, head_size)
    mixed = from_heads(exchange_back(attended))

    middle = inputs + narrow_reduce(dot(mixed, out_weight))
    normed_two = narrow_gather(row_normalize(middle, mlp_gain).astype(BF16))
    gate_sum = dot(normed_two, gate_up[:, :hidden])
    up_sum = dot(normed_two, gate_up[:, hidden:])
    hidden_rows = gated(gate_sum, up_sum).astype(BF16)
    output = (middle + narrow_reduce(dot(hidden_rows, down))).astype(BF16)

    all_out_grad = narrow_gather(out_grad)
    down_share = ring_reduce(ring, outer_sum(hidden_rows, all_out_grad).astype(BF16))
    grad_hidden = times_transpose(all_out_grad, down)
    unused_gated, gated_pull = jax.vjp(gated, gate_sum, up_sum)
    grad_gate, grad_up = gated_pull(grad_hidden)
    gate_up_grad = jnp.concatenate([grad_gate.astype(BF16), grad_up.astype(BF16)], axis=1)
    grad_normed_two = narrow_reduce(times_transpose(gate_up_grad, gate_up))
    gate_up_share = ring_reduce(ring, outer_sum(normed_two, gate_up_grad).astype(BF16))
    unused_norm, second_pull = jax.vjp(lambda value: row_normalize(value, mlp_gain), middle)
    grad_middle = out_grad.astype(F32) + second_pull(grad_normed_two)[0]

    grad_branch = narrow_gather(grad_middle.astype(BF16))
    grad_mixed = times_transpose(grad_branch, out_weight).astype(BF16)
    arrived_grad = exchange(to_heads(grad_mixed, per_group))
    out_share = ring_reduce(ring, outer_sum(mixed, grad_branch).astype(BF16))
    grad_pieces = exchange_back(
        attend_back(table, arrived, arrived_grad, group_heads, head_size)
    )
    grad_queries = from_heads(grad_pieces[..., :per_group])
    grad_keys = from_heads(grad_pieces[..., per_group : per_group + head_size])
    grad_values = from_heads(grad_pieces[..., per_group + head_size :])
    grad_query_raw, grad_query_gain = query_pull(grad_queries.astype(F32))
    grad_key_raw, grad_key_gain = key_pull(grad_keys.astype(F32))
    projection_grad = jnp.concatenate(
        [grad_query_raw.astype(BF16), grad_key_raw.astype(BF16), grad_values], axis=1
    )
    first_share = ring_reduce(ring, outer_sum(normed, projection_grad).astype(BF16))
    grad_normed = narrow_reduce(times_transpose(projection_grad, projection))
    unused_first, first_pull = jax.vjp(lambda value: row_normalize(value, attention_gain), inputs)
    tokens_grad = (grad_middle + first_pull(grad_normed)[0]).astype(BF16)

    def narrow_rows(share):
        pieces = share.astype(BF16).reshape(NARROW, shard, -1)
        return lax.all_to_all(pieces, "narrow", split_axis=0, concat_axis=0, tiled=True).astype(F32)

    def all_columns(pieces):
        return pieces.transpose(1, 0, 2).reshape(shard, -1)

    def all_hidden(pieces):
        return (
            pieces.reshape(NARROW, shard, wide_count, -1)
            .transpose(1, 2, 0, 3)
            .reshape(shard, NARROW * hidden)
        )

    first_rows = narrow_rows(first_share)
    w_query_grad = all_columns(first_rows[:, :, :query_width])
    w_key_grad = all_columns(first_rows[:, :, query_width : query_width + key_width])
    w_value_grad = all_columns(first_rows[:, :, query_width + key_width :])
    gate_up_rows = narrow_rows(gate_up_share)
    w_gate_grad = all_hidden(gate_up_rows[:, :, :hidden])
    w_up_grad = all_hidden(gate_up_rows[:, :, hidden:])
    w_out_grad = lax.ppermute(
        out_share.astype(BF16), DEVICES, [(b, a) for a, b in out_moves]
    ).astype(F32)

    def row_sums(pairs):
        total = 0.0
        for weight, grad in pairs:
            total = total + jnp.sum(weight.astype(F32) * grad, axis=1)
        return total

    attn_norm_grad = row_sums(
        [(w_query, w_query_grad), (key_weight, w_key_grad), (value_weight, w_value_grad)]
    ) / attn_norm.astype(F32)
    mlp_norm_grad = row_sums([(w_gate, w_gate_grad), (w_up, w_up_grad)]) / mlp_norm.astype(F32)
    norm_grads = everyone_sum(jnp.stack([grad_query_gain, grad_key_gain]), wide_count)
    few = query_norm.shape[0]
    mine = lax.dynamic_slice(norm_grads, (0, (my_wide * NARROW + me) * few), (2, few))
    return (
        output,
        tokens_grad,
        attn_norm_grad,
        w_query_grad,
        w_key_grad,
        w_value_grad,
        mine[0],
        mine[1],
        w_out_grad,
        mlp_norm_grad,
        w_gate_grad,
        w_up_grad,
        down_share,
    )


def solution(mesh):
    rows = P(DEVICES, None)
    vector = P(DEVICES)
    in_specs = (
        (rows, rows, vector, rows, rows, rows, vector, vector, rows, vector, rows, rows, rows)
        + (P(),) * 4
    )
    out_specs = (
        (rows, rows, vector, rows, rows, rows, vector, vector, rows, vector, rows, rows, rows)
    )
    return jax.shard_map(body, mesh=mesh, in_specs=in_specs, out_specs=out_specs, check_vma=False)
```

time: 2790 us -> 1090 us (0.39)
  waiting for transfers between devices: 2170 us -> 384 us
  matrix products: 310 us -> 134 us
  starting transfers between devices: 25.5 us -> 193 us
  other arithmetic: 87.5 us -> 149 us
  blocking collectives: 40.3 us -> 0 us
  Pallas kernels: 0 us -> 33.2 us
    reduce_scatter x8 -> x0, waiting for transfers between devices: 1150 us -> none  [the longest x1 349 us: body(): lax.psum_scatter(term_maker(regroup(normed_two, wide_count, narrow_count)...]
    all_to_all x4 -> x8, waiting for transfers between devices: 679 us -> 26.3 us  [the longest x2 13.2 us: exchange(): lax.all_to_all(pieces, 'wide', split_axis=0, concat_axis=0, tiled=True)]
    ppermute x0 -> x95, waiting for transfers between devices: none -> 357 us  [the longest x64 304 us: send(): return lax.ppermute(value, 'wide', self.onward if forward else self.back)]
    all_gather x7 -> x0, waiting for transfers between devices: 331 us -> none  [the longest x1 141 us: body(): lax.all_gather(w_down, ('wide', 'narrow'), axis=0, tiled=True)]
    ppermute x0 -> x95, starting transfers between devices: none -> 140 us  [the longest x64 78.4 us: send(): return lax.ppermute(value, 'wide', self.onward if forward else self.back)]
    dot_general x21 -> x5, matrix products: 164 us -> 50.4 us  [dot(): return jnp.dot(left, right, preferred_element_type=F32)]
    convert_element_type x13 -> x4, local copies, waits for them, and re-layouts: 53.3 us -> 5.7 us  [the longest x2 3.89 us: body(): grad_query_raw, grad_query_gain = query_pull(grad_queries.astype(F32))]
    convert_element_type x15 -> x37, other arithmetic: 29.3 us -> 71.1 us  [the longest x20 37.1 us: join(): return (left.astype(F32) + right.astype(F32)).astype(BF16)]
  transfers between devices with their start and end apart: 19 -> 103, of which waited for: 16 -> 41; matrix products, arithmetic and copies ran while one was open for 17% -> 22% of each run, Pallas kernels for 0% -> 3%
where the time goes in v1:
time: 1090 us; the launch traced here: 1070 us
  waiting for transfers between devices  384 us (35%)
  starting transfers between devices  193 us (18%)
  other arithmetic  149 us (14%)
  local copies, waits for them, and re-layouts  148 us (14%)
  matrix products  134 us (12%)
  Pallas kernels  33.2 us (3%)
  between operations  31.9 us (3%)
    ppermute x64, waiting for transfers between devices, send(): return lax.ppermute(value, 'wide', self.onward if forward else self.back)  304 us
    ppermute x64, starting transfers between devices, send(): return lax.ppermute(value, 'wide', self.onward if forward else self.back)  78.4 us
    dot_general x5, matrix products, dot(): return jnp.dot(left, right, preferred_element_type=F32)  50.4 us
    ppermute x26, starting transfers between devices, swap(): return lax.ppermute(value, 'narrow', [(i, i ^ bit) for i in range(NARROW)])  49.9 us
    dot_general x4, matrix products, outer_sum(): lax.dot_general(left_rows, right_rows, CONTRACT_ROWS, preferred_element_t...  42.7 us
    dot_general x4, matrix products, times_transpose(): lax.dot_general(left_rows, matrix, CONTRACT_COLS, preferred_element_type=...  41.4 us
    convert_element_type x20, other arithmetic, join(): return (left.astype(F32) + right.astype(F32)).astype(BF16)  37.1 us
    dynamic_update_slice x36, local copies, waits for them, and re-layouts, put(): lax.dynamic_update_slice(whole, value, (ring.device(shift) * rows + extra...  34.9 us
  transfers between devices with their start and end apart: 103, of which 41 were waited for; matrix products, arithmetic and copies ran while one was open for 22% of the time, Pallas kernels for 3%

profile of v1, /device:TPU:9, one launch (start us, length us, event | category | flops | bytes accessed | tf_op | source)
XLA Modules:
  0.0 1073.3 jit_solution(14903872206980676410)
XLA Ops:
  38.7 9.5 collective-permute-done.3
  53.7 8.5 collective-permute-done.5
  67.9 7.5 collective-permute-done.7
  77.1 4.3 collective-permute-done.9
  85.2 5.8 fusion.14
  131.8 4.7 all-to-all-start.1
  165.7 26.1 %collective-permute-done.11 = bf16[64,2048]{1,0:T(8,128)(2,1)S(1)} collective-permute-done((bf16[64,2048]{1,0:T(8,128)(2,1)}, bf16[64,2048]{1,0:T(8,128)(2,1)S(1)}, u32[]{:S(2)}, u32[]{:S(2)}) %collective-permute-start.11) | collective-permute-done | bytes 262176 | tf_op jit(solution)/shard_map/ppermute | solution.py:399
  191.8 21.3 %collective-permute-start.12 = (bf16[64,2048]{1,0:T(8,128)(2,1)S(1)}, bf16[64,2048]{1,0:T(8,128)(2,1)}, u32[]{:S(2)}, u32[]{:S(2)}) collective-permute-start(bf16[64,2048]{1,0:T(8,128)(2,1)S(1)} %collective-permute-done.11), channel_id=1, source_target_pairs={{0,8},{8,16},{16,24},{24,28},{28,20},{20,12},{12,4},{4,0},{1,9},{9... | collective-permute-start | bytes 786440 | tf_op jit(solution)/shard_map/ppermute | solution.py:80
  230.8 4.3 collective-permute-done.13
  237.8 4.9 all-to-all-start.3
  260.2 14.3 %attend.1 = bf16[2048,256]{1,0:T(8,128)(2,1)} custom-call(s32[3,16]{1,0:T(4,128)} %pad_add_fusion.2.table, bf16[2048,512]{1,0:T(8,128)(2,1)} %bitcast.226), custom_call_target="tpu_custom_call" | custom-call | tf_op jit(solution)/shard_map/attend/pallas_call | solution.py:293
  293.3 9.0 all-to-all-done.2
  304.3 4.3 convolution_convert_fusion.3
  311.7 41.2 %collective-permute-done.38 = bf16[192,2048]{1,0:T(8,128)(2,1)} collective-permute-done((bf16[192,2048]{1,0:T(8,128)(2,1)}, bf16[192,2048]{1,0:T(8,128)(2,1)}, u32[]{:S(2)}, u32[]{:S(2)}) %collective-permute-start.38) | collective-permute-done | bytes 786464 | tf_op jit(solution)/shard_map/ppermute | solution.py:80
  371.9 11.1 %fusion.61 = f32[1024,1536]{1,0:T(8,128)} fusion(bf16[1024,2048]{1,0:T(8,128)(2,1)} %constant_dynamic-update-slice_fusion.36, bf16[1536,2048]{1,0:T(8,128)(2,1)S(1)} %constant_dynamic-update-slice_fusion), kind=kOutput, calls=%fused_computation.313 | convolution fusion | flops 6442450944 | bytes 16777216 | tf_op jit(solution)/shard_map/dot_general | solution.py:56
  384.7 13.3 %collective-permute-done.28 = bf16[256,3072]{1,0:T(8,128)(2,1)} collective-permute-done((bf16[256,3072]{1,0:T(8,128)(2,1)}, bf16[256,3072]{1,0:T(8,128)(2,1)}, u32[]{:S(2)}, u32[]{:S(2)}) %collective-permute-start.28) | collective-permute-done | bytes 1572896 | tf_op jit(solution)/shard_map/ppermute | solution.py:80
  407.4 25.6 %collective-permute-done.30 = bf16[256,3072]{1,0:T(8,128)(2,1)S(1)} collective-permute-done((bf16[256,3072]{1,0:T(8,128)(2,1)}, bf16[256,3072]{1,0:T(8,128)(2,1)S(1)}, u32[]{:S(2)}, u32[]{:S(2)}) %collective-permute-start.30) | collective-permute-done | bytes 1572896 | tf_op jit(solution)/shard_map/ppermute | solution.py:80
  440.0 10.0 collective-permute-done.32
  453.5 4.5 copy-done.20
  459.5 11.4 %fusion.6 = f32[1024,1536]{1,0:T(8,128)} fusion(bf16[2048,3072]{1,0:T(8,128)(2,1)S(1)} %constant_dynamic-update-slice_fusion.9, bf16[256,2048]{1,0:T(8,128)(2,1)S(1)} %collective-permute-done.25, bf16[256,2048]{1,0:T(8,128)(2,1)S(1)} %collective-permute-done.24, bf16[256,2048]{1,0:T(8,128)(2,1)S(1)} %collective-permute-done.23, ...), kind=kOutput, calls=%fused_computation.20 | convolution fusion | flops 6459228160 | bytes 16777216 | tf_op jit(solution)/shard_map/dot_general | solution.py:48
  470.9 17.4 %fusion.5 = (bf16[1024,1536]{1,0:T(8,128)(2,1)}, bf16[1024,1536]{1,0:T(8,128)(2,1)}, bf16[1024,1536]{1,0:T(8,128)(2,1)}) fusion(f32[1024,1536]{1,0:T(8,128)} %fusion.61, f32[1024,1536]{1,0:T(8,128)} %fusion.6, bf16[2048,3072]{1,0:T(8,128)(2,1)} %copy-done.20, bf16[256,2048]{1,0:T(8,128)(2,1)} %copy-done.89, bf16[256,2048]{1,0:T(8,128)(2,1)} %copy-done.87, ...), kind=kOutput, calls=%fused_computation.19 | convolution fusion | flops 6484393984 | bytes 32505856 | tf_op jit(solution)/shard_map/dot_general | solution.py:48
  488.3 11.4 %convolution_convert_fusion.1 = bf16[1536,2048]{1,0:T(8,128)(2,1)} fusion(bf16[1024,1536]{1,0:T(8,128)(2,1)} %get-tuple-element.43, bf16[1024,2048]{1,0:T(8,128)(2,1)} %constant_dynamic-update-slice_fusion.36), kind=kOutput, calls=%fused_computation.16 | convolution fusion | flops 6445596672 | bytes 13631488 | tf_op jit(solution)/shard_map/dot_general | solution.py:52
  499.7 11.5 %convolution_convert_fusion.2 = bf16[1024,2048]{1,0:T(8,128)(2,1)} fusion(bf16[1024,1536]{1,0:T(8,128)(2,1)S(1)} %copy-done.91, bf16[1536,2048]{1,0:T(8,128)(2,1)} %copy-done.29), kind=kOutput, calls=%fused_computation.33 | convolution fusion | flops 6444548096 | bytes 13631488 | tf_op jit(solution)/shard_map/dot_general | solution.py:48
  511.2 18.5 %fusion.12 = bf16[1024,2048]{1,0:T(8,128)(2,1)} fusion(bf16[2048,3072]{1,0:T(8,128)(2,1)} %copy-done.20, bf16[1024,1536]{1,0:T(8,128)(2,1)} %get-tuple-element.42, bf16[1024,1536]{1,0:T(8,128)(2,1)S(1)} %copy-done.92), kind=kOutput, calls=%fused_computation.34 | convolution fusion | flops 12899581952 | bytes 23068672 | tf_op jit(solution)/shard_map/dot_general | solution.py:56
  529.7 19.8 %convolution_convert_fusion = bf16[2048,3072]{1,0:T(8,128)(2,1)} fusion(bf16[1024,1536]{1,0:T(8,128)(2,1)} %get-tuple-element.42, bf16[1024,1536]{1,0:T(8,128)(2,1)} %get-tuple-element.41, bf16[256,2048]{1,0:T(8,128)(2,1)} %copy-done.89, bf16[256,2048]{1,0:T(8,128)(2,1)} %copy-done.87, bf16[256,2048]{1,0:T(8,128)(2,1)} %copy-done.88, ...), kind=kOutput, calls=%fused_computation.9 | convolution fusion | flops 12920553472 | bytes 23068672 | tf_op jit(solution)/shard_map/dot_general | solution.py:52
  553.5 3.9 collective-permute-start.43
  558.3 9.3 collective-permute-done.79
  578.6 5.1 collective-permute-start.42
  583.7 8.8 collective-permute-done.50
  594.5 7.9 collective-permute-done.80
  607.4 6.8 collective-permute-done.44
  614.1 4.4 fusion.49
  623.1 6.1 collective-permute-start.51
  629.2 8.7 collective-permute-done.52
  637.8 6.6 collective-permute-start.53
  644.6 5.7 add_convert_fusion.3
  652.3 9.1 collective-permute-done.88
  665.1 4.5 convolution_convert_fusion.7
  670.3 6.6 collective-permute-done.85
  681.8 5.0 all-to-all-start.4
  686.7 4.5 convolution_convert_fusion.6
  692.6 19.4 %collective-permute-done.82 = bf16[256,3072]{1,0:T(8,128)(2,1)} collective-permute-done((bf16[256,3072]{1,0:T(8,128)(2,1)}, bf16[256,3072]{1,0:T(8,128)(2,1)}, u32[]{:S(2)}, u32[]{:S(2)}) %collective-permute-start.82) | collective-permute-done | bytes 1572896 | tf_op jit(solution)/shard_map/ppermute | solution.py:80
  712.0 15.4 %collective-permute-done.86 = bf16[256,3072]{1,0:T(8,128)(2,1)} collective-permute-done((bf16[256,3072]{1,0:T(8,128)(2,1)}, bf16[256,3072]{1,0:T(8,128)(2,1)}, u32[]{:S(2)}, u32[]{:S(2)}) %collective-permute-start.86) | collective-permute-done | bytes 1572896 | tf_op jit(solution)/shard_map/ppermute | solution.py:80
  727.4 4.3 add_convert_fusion
  731.7 13.2 %all-to-all-done.4 = bf16[8,256,256]{2,1,0:T(8,128)(2,1)S(1)} async-done(((bf16[8,256,256]{2,1,0:T(8,128)(2,1)}), bf16[8,256,256]{2,1,0:T(8,128)(2,1)S(1)}, u32[]{:S(2)}, u32[]{:S(2)}) %all-to-all-start.4) | async-done | bytes 1048608 | tf_op jit(solution)/shard_map/all_to_all | solution.py:446
  744.9 17.5 %all-to-all-start.7 = ((bf16[4,64,3072]{2,1,0:T(8,128)(2,1)}), bf16[4,64,3072]{2,1,0:T(8,128)(2,1)S(1)}, u32[]{:S(2)}, u32[]{:S(2)}) async-start(bf16[4,64,3072]{2,1,0:T(8,128)(2,1)} %bitcast.101), calls=%async_computation.7 | async-start | bytes 3145728 | tf_op jit(solution)/shard_map/all_to_all | solution.py:517
  773.2 18.9 %attend_back.1 = bf16[2048,512]{1,0:T(8,128)(2,1)} custom-call(s32[3,16]{1,0:T(4,128)} %pad_add_fusion.2.table, bf16[2048,512]{1,0:T(8,128)(2,1)} %bitcast.227, bf16[2048,256]{1,0:T(8,128)(2,1)} %bitcast.244), custom_call_target="tpu_custom_call" | custom-call | tf_op jit(solution)/shard_map/attend_back/pallas_call | solution.py:306
  792.1 4.3 all-to-all-start.5
  799.9 48.6 %collective-permute-done.72 = bf16[64,2048]{1,0:T(8,128)(2,1)S(1)} collective-permute-done((bf16[64,2048]{1,0:T(8,128)(2,1)S(1)}, bf16[64,2048]{1,0:T(8,128)(2,1)S(1)}, u32[]{:S(2)}, u32[]{:S(2)}) %collective-permute-start.72) | collective-permute-done | bytes 262176 | tf_op jit(solution)/shard_map/ppermute | solution.py:80
  859.8 11.2 %collective-permute-done.73 = bf16[64,2048]{1,0:T(8,128)(2,1)} collective-permute-done((bf16[64,2048]{1,0:T(8,128)(2,1)S(1)}, bf16[64,2048]{1,0:T(8,128)(2,1)}, u32[]{:S(2)}, u32[]{:S(2)}) %collective-permute-start.73) | collective-permute-done | bytes 262176 | tf_op jit(solution)/shard_map/ppermute | solution.py:80
  870.9 9.7 collective-permute-done.77
  881.8 4.3 collective-permute-start.78
  923.7 7.8 multiply_reduce_fusion
  931.5 17.6 %multiply_reduce_fusion.7 = (f32[128]{0:T(128)S(1)}, f32[1024,2]{1,0:T(8,128)}, f32[1024,2,128]{2,1,0:T(2,128)}) fusion(f32[1024,2,128]{2,1,0:T(2,128)S(1)} %copy-done.3, f32[1024,2]{1,0:T(8,128)S(1)} %copy-done.18, f32[128]{0:T(128)S(1)} %copy-done.81, f32[1024,2,64]{2,1,0:T(2,128)S(1)} %get-tuple-element.88, f32[1024,2,64]{2,1,0:T(2,128)S(1)} %get-tuple-element.87, ...), kind=kLoop, calls=%fused_computation.117 | loop fusion | flops 2357120 | bytes 4736000 | tf_op jit(solution)/shard_map/transpose(jvp())/reduce_sum | solution.py:27
  953.6 5.0 fusion.17
  962.1 5.6 fusion.26
  968.1 7.2 convolution_convert_fusion.5
  975.3 7.0 convolution_convert_fusion.4
  983.3 6.7 collective-permute-start.57
  1020.6 5.4 collective-permute-done.62
  1033.1 7.8 collective-permute-done.63
  1044.0 7.7 collective-permute-done.64
  1053.8 8.9 all-to-all-start.6
  1066.6 4.0 all-to-all-done.6
  (616 shorter events, 361.1 us)
Async XLA Ops:
  0.6 49.0 %collective-permute-start.1 = (bf16[256,2048]{1,0:T(8,128)(2,1)}, bf16[256,2048]{1,0:T(8,128)(2,1)S(1)}, u32[]{:S(2)}, u32[]{:S(2)}) collective-permute-start(bf16[256,2048]{1,0:T(8,128)(2,1)} %param.23), channel_id=1, source_target_pairs={{0,2},{1,3},{2,0},{3,1},{4,6},{5,7},{6,4},{7,5},{8,10},{9,11},{10,... | collective-permute-start | bytes 3145736 | tf_op jit(solution)/shard_map/ppermute | solution.py:144
  1.9 63.4 %collective-permute-start = (bf16[256,2048]{1,0:T(8,128)(2,1)}, bf16[256,2048]{1,0:T(8,128)(2,1)}, u32[]{:S(2)}, u32[]{:S(2)}) collective-permute-start(bf16[256,2048]{1,0:T(8,128)(2,1)} %param.23), channel_id=1, source_target_pairs={{0,1},{1,0},{2,3},{3,2},{4,5},{5,4},{6,7},{7,6},{8,9},{9,8},{10,11... | collective-permute-start | bytes 3145736 | tf_op jit(solution)/shard_map/ppermute | solution.py:144
  9.0 24.3 %all-to-all-start = ((bf16[4,64,1152]{2,1,0:T(8,128)(2,1)}), bf16[4,64,1152]{2,1,0:T(8,128)(2,1)S(1)}, u32[]{:S(2)}, u32[]{:S(2)}) async-start(bf16[4,64,1152]{2,1,0:T(8,128)(2,1)} %pad_maximum_fusion.20), calls=%async_computation | async-start | bytes 1179648 | tf_op jit(solution)/shard_map/all_to_all | solution.py:383
  131.8 106.0 %all-to-all-start.1 = ((bf16[8,256,512]{2,1,0:T(8,128)(2,1)}), bf16[8,256,512]{2,1,0:T(8,128)(2,1)S(1)}, u32[]{:S(2)}, u32[]{:S(2)}) async-start(bf16[8,256,512]{2,1,0:T(8,128)(2,1)} %bitcast.237), calls=%async_computation.1 | async-start | bytes 4194304 | tf_op jit(solution)/shard_map/all_to_all | solution.py:446
  136.5 110.4 %collective-permute-start.34 = (bf16[192,2048]{1,0:T(8,128)(2,1)}, bf16[192,2048]{1,0:T(8,128)(2,1)}, u32[]{:S(2)}, u32[]{:S(2)}) collective-permute-start(bf16[192,2048]{1,0:T(8,128)(2,1)} %param.35), channel_id=1, source_target_pairs={{0,8},{8,16},{16,24},{24,28},{28,20},{20,12},{12,4},{4,0},{1,9},{9... | collective-permute-start | bytes 2359304 | tf_op jit(solution)/shard_map/ppermute | solution.py:80
  137.7 111.3 %collective-permute-start.35 = (bf16[192,2048]{1,0:T(8,128)(2,1)}, bf16[192,2048]{1,0:T(8,128)(2,1)}, u32[]{:S(2)}, u32[]{:S(2)}) collective-permute-start(bf16[192,2048]{1,0:T(8,128)(2,1)} %param.35), channel_id=1, source_target_pairs={{8,0},{16,8},{24,16},{28,24},{20,28},{12,20},{4,12},{0,4},{9,1},{1... | collective-permute-start | bytes 2359304 | tf_op jit(solution)/shard_map/ppermute | solution.py:80
  137.9 53.8 %collective-permute-start.11 = (bf16[64,2048]{1,0:T(8,128)(2,1)}, bf16[64,2048]{1,0:T(8,128)(2,1)S(1)}, u32[]{:S(2)}, u32[]{:S(2)}) collective-permute-start(bf16[64,2048]{1,0:T(8,128)(2,1)} %param.31), channel_id=1, source_target_pairs={{0,0},{1,4},{2,8},{3,12},{4,16},{5,20},{6,24},{7,28},{8,1},{9,5},{... | collective-permute-start | bytes 786440 | tf_op jit(solution)/shard_map/ppermute | solution.py:399
  141.0 114.8 %collective-permute-start.46 = (bf16[256,2048]{1,0:T(8,128)(2,1)}, bf16[256,2048]{1,0:T(8,128)(2,1)}, u32[]{:S(2)}, u32[]{:S(2)}) collective-permute-start(bf16[256,2048]{1,0:T(8,128)(2,1)} %param.24), channel_id=1, source_target_pairs={{0,2},{1,3},{2,0},{3,1},{4,6},{5,7},{6,4},{7,5},{8,10},{9,11},{10,... | collective-permute-start | bytes 3145736 | tf_op jit(solution)/shard_map/ppermute | solution.py:144
  191.8 35.2 %collective-permute-start.12 = (bf16[64,2048]{1,0:T(8,128)(2,1)S(1)}, bf16[64,2048]{1,0:T(8,128)(2,1)}, u32[]{:S(2)}, u32[]{:S(2)}) collective-permute-start(bf16[64,2048]{1,0:T(8,128)(2,1)S(1)} %collective-permute-done.11), channel_id=1, source_target_pairs={{0,8},{8,16},{16,24},{24,28},{28,20},{20,12},{12,4},{4,0},{1,9},{9... | collective-permute-start | bytes 786440 | tf_op jit(solution)/shard_map/ppermute | solution.py:80
  235.1 20.8 %collective-permute-start.45 = (bf16[256,2048]{1,0:T(8,128)(2,1)}, bf16[256,2048]{1,0:T(8,128)(2,1)}, u32[]{:S(2)}, u32[]{:S(2)}) collective-permute-start(bf16[256,2048]{1,0:T(8,128)(2,1)} %param.24), channel_id=1, source_target_pairs={{0,1},{1,0},{2,3},{3,2},{4,5},{5,4},{6,7},{7,6},{8,9},{9,8},{10,11... | collective-permute-start | bytes 3145736 | tf_op jit(solution)/shard_map/ppermute | solution.py:144
  237.8 36.7 %all-to-all-start.3 = ((bf16[4,64,3072]{2,1,0:T(8,128)(2,1)}), bf16[4,64,3072]{2,1,0:T(8,128)(2,1)}, u32[]{:S(2)}, u32[]{:S(2)}) async-start(bf16[4,64,3072]{2,1,0:T(8,128)(2,1)} %pad_maximum_fusion.10), calls=%async_computation.3 | async-start | bytes 3145728 | tf_op jit(solution)/shard_map/all_to_all | solution.py:403
  249.0 38.7 %collective-permute-start.36 = (bf16[192,2048]{1,0:T(8,128)(2,1)}, bf16[192,2048]{1,0:T(8,128)(2,1)}, u32[]{:S(2)}, u32[]{:S(2)}) collective-permute-start(bf16[192,2048]{1,0:T(8,128)(2,1)} %collective-permute-done.34), channel_id=1, source_target_pairs={{0,8},{8,16},{16,24},{24,28},{28,20},{20,12},{12,4},{4,0},{1,9},{9... | collective-permute-start | bytes 2359304 | tf_op jit(solution)/shard_map/ppermute | solution.py:80
  252.5 36.3 %collective-permute-start.37 = (bf16[192,2048]{1,0:T(8,128)(2,1)}, bf16[192,2048]{1,0:T(8,128)(2,1)}, u32[]{:S(2)}, u32[]{:S(2)}) collective-permute-start(bf16[192,2048]{1,0:T(8,128)(2,1)} %collective-permute-done.35), channel_id=1, source_target_pairs={{8,0},{16,8},{24,16},{28,24},{20,28},{12,20},{4,12},{0,4},{9,1},{1... | collective-permute-start | bytes 2359304 | tf_op jit(solution)/shard_map/ppermute | solution.py:80
  254.1 28.0 %collective-permute-start.18 = (bf16[32,2048]{1,0:T(8,128)(2,1)S(1)}, bf16[32,2048]{1,0:T(8,128)(2,1)S(1)}, u32[]{:S(2)}, u32[]{:S(2)}) collective-permute-start(bf16[32,2048]{1,0:T(8,128)(2,1)S(1)} %slice.336), channel_id=1, source_target_pairs={{0,8},{8,16},{16,24},{24,28},{28,20},{20,12},{12,4},{4,0},{1,9},{9... | collective-permute-start | bytes 393224 | tf_op jit(solution)/shard_map/ppermute | solution.py:80
  255.8 27.0 %collective-permute-start.19 = (bf16[32,2048]{1,0:T(8,128)(2,1)S(1)}, bf16[32,2048]{1,0:T(8,128)(2,1)S(1)}, u32[]{:S(2)}, u32[]{:S(2)}) collective-permute-start(bf16[32,2048]{1,0:T(8,128)(2,1)S(1)} %slice.337), channel_id=1, source_target_pairs={{8,0},{16,8},{24,16},{28,24},{20,28},{12,20},{4,12},{0,4},{9,1},{1... | collective-permute-start | bytes 393224 | tf_op jit(solution)/shard_map/ppermute | solution.py:80
  255.9 52.9 %collective-permute-start.47 = (bf16[256,2048]{1,0:T(8,128)(2,1)}, bf16[256,2048]{1,0:T(8,128)(2,1)}, u32[]{:S(2)}, u32[]{:S(2)}) collective-permute-start(bf16[256,2048]{1,0:T(8,128)(2,1)} %collective-permute-done.46), channel_id=1, source_target_pairs={{0,1},{1,0},{2,3},{3,2},{4,5},{5,4},{6,7},{7,6},{8,9},{9,8},{10,11... | collective-permute-start | bytes 3145736 | tf_op jit(solution)/shard_map/ppermute | solution.py:144
  274.6 27.8 %all-to-all-start.2 = ((bf16[8,256,256]{2,1,0:T(8,128)(2,1)}), bf16[8,256,256]{2,1,0:T(8,128)(2,1)S(1)}, u32[]{:S(2)}, u32[]{:S(2)}) async-start(bf16[8,256,256]{2,1,0:T(8,128)(2,1)} %bitcast.253), calls=%async_computation.2 | async-start | bytes 2097152 | tf_op jit(solution)/shard_map/all_to_all | solution.py:451
  283.4 76.3 %collective-permute-start.26 = (bf16[256,3072]{1,0:T(8,128)(2,1)}, bf16[256,3072]{1,0:T(8,128)(2,1)}, u32[]{:S(2)}, u32[]{:S(2)}) collective-permute-start(bf16[256,3072]{1,0:T(8,128)(2,1)} %bitcast.71), channel_id=1, source_target_pairs={{0,8},{8,16},{16,24},{24,28},{28,20},{20,12},{12,4},{4,0},{1,9},{9... | collective-permute-start | bytes 4718600 | tf_op jit(solution)/shard_map/ppermute | solution.py:80
  284.6 76.6 %collective-permute-start.27 = (bf16[256,3072]{1,0:T(8,128)(2,1)}, bf16[256,3072]{1,0:T(8,128)(2,1)}, u32[]{:S(2)}, u32[]{:S(2)}) collective-permute-start(bf16[256,3072]{1,0:T(8,128)(2,1)} %bitcast.71), channel_id=1, source_target_pairs={{8,0},{16,8},{24,16},{28,24},{20,28},{12,20},{4,12},{0,4},{9,1},{1... | collective-permute-start | bytes 4718600 | tf_op jit(solution)/shard_map/ppermute | solution.py:80
  287.6 65.3 %collective-permute-start.38 = (bf16[192,2048]{1,0:T(8,128)(2,1)}, bf16[192,2048]{1,0:T(8,128)(2,1)}, u32[]{:S(2)}, u32[]{:S(2)}) collective-permute-start(bf16[192,2048]{1,0:T(8,128)(2,1)} %collective-permute-done.36), channel_id=1, source_target_pairs={{0,8},{8,16},{16,24},{24,28},{28,20},{20,12},{12,4},{4,0},{1,9},{9... | collective-permute-start | bytes 2359304 | tf_op jit(solution)/shard_map/ppermute | solution.py:80
  288.8 67.4 %collective-permute-start.39 = (bf16[192,2048]{1,0:T(8,128)(2,1)}, bf16[192,2048]{1,0:T(8,128)(2,1)}, u32[]{:S(2)}, u32[]{:S(2)}) collective-permute-start(bf16[192,2048]{1,0:T(8,128)(2,1)} %collective-permute-done.37), channel_id=1, source_target_pairs={{8,0},{16,8},{24,16},{28,24},{20,28},{12,20},{4,12},{0,4},{9,1},{1... | collective-permute-start | bytes 2359304 | tf_op jit(solution)/shard_map/ppermute | solution.py:80
  308.8 61.3 %collective-permute-start.21 = (bf16[256,2048]{1,0:T(8,128)(2,1)S(1)}, bf16[256,2048]{1,0:T(8,128)(2,1)S(1)}, u32[]{:S(2)}, u32[]{:S(2)}) collective-permute-start(bf16[256,2048]{1,0:T(8,128)(2,1)S(1)} %get-tuple-element.67), channel_id=1, source_target_pairs={{0,1},{1,0},{2,3},{3,2},{4,5},{5,4},{6,7},{7,6},{8,9},{9,8},{10,11... | collective-permute-start | bytes 3145736 | tf_op jit(solution)/shard_map/ppermute | solution.py:144
  359.7 38.2 %collective-permute-start.28 = (bf16[256,3072]{1,0:T(8,128)(2,1)}, bf16[256,3072]{1,0:T(8,128)(2,1)}, u32[]{:S(2)}, u32[]{:S(2)}) collective-permute-start(bf16[256,3072]{1,0:T(8,128)(2,1)} %collective-permute-done.26), channel_id=1, source_target_pairs={{0,8},{8,16},{16,24},{24,28},{28,20},{20,12},{12,4},{4,0},{1,9},{9... | collective-permute-start | bytes 4718600 | tf_op jit(solution)/shard_map/ppermute | solution.py:80
  361.2 40.6 %collective-permute-start.29 = (bf16[256,3072]{1,0:T(8,128)(2,1)}, bf16[256,3072]{1,0:T(8,128)(2,1)S(1)}, u32[]{:S(2)}, u32[]{:S(2)}) collective-permute-start(bf16[256,3072]{1,0:T(8,128)(2,1)} %collective-permute-done.27), channel_id=1, source_target_pairs={{8,0},{16,8},{24,16},{28,24},{20,28},{12,20},{4,12},{0,4},{9,1},{1... | collective-permute-start | bytes 4718600 | tf_op jit(solution)/shard_map/ppermute | solution.py:80
  367.3 34.5 %collective-permute-start.20 = (bf16[256,2048]{1,0:T(8,128)(2,1)S(1)}, bf16[256,2048]{1,0:T(8,128)(2,1)}, u32[]{:S(2)}, u32[]{:S(2)}) collective-permute-start(bf16[256,2048]{1,0:T(8,128)(2,1)S(1)} %get-tuple-element.66), channel_id=1, source_target_pairs={{0,1},{1,0},{2,3},{3,2},{4,5},{5,4},{6,7},{7,6},{8,9},{9,8},{10,11... | collective-permute-start | bytes 3145736 | tf_op jit(solution)/shard_map/ppermute | solution.py:144
  370.5 31.3 %collective-permute-start.22 = (bf16[256,2048]{1,0:T(8,128)(2,1)S(1)}, bf16[256,2048]{1,0:T(8,128)(2,1)}, u32[]{:S(2)}, u32[]{:S(2)}) collective-permute-start(bf16[256,2048]{1,0:T(8,128)(2,1)S(1)} %add_convert_fusion.9), channel_id=1, source_target_pairs={{0,2},{1,3},{2,0},{3,1},{4,6},{5,7},{6,4},{7,5},{8,10},{9,11},{10,... | collective-permute-start | bytes 3145736 | tf_op jit(solution)/shard_map/ppermute | solution.py:144
  398.0 34.9 %collective-permute-start.30 = (bf16[256,3072]{1,0:T(8,128)(2,1)}, bf16[256,3072]{1,0:T(8,128)(2,1)S(1)}, u32[]{:S(2)}, u32[]{:S(2)}) collective-permute-start(bf16[256,3072]{1,0:T(8,128)(2,1)} %collective-permute-done.28), channel_id=1, source_target_pairs={{0,8},{8,16},{16,24},{24,28},{28,20},{20,12},{12,4},{4,0},{1,9},{9... | collective-permute-start | bytes 4718600 | tf_op jit(solution)/shard_map/ppermute | solution.py:80
  401.8 34.4 %collective-permute-start.31 = (bf16[256,3072]{1,0:T(8,128)(2,1)S(1)}, bf16[256,3072]{1,0:T(8,128)(2,1)S(1)}, u32[]{:S(2)}, u32[]{:S(2)}) collective-permute-start(bf16[256,3072]{1,0:T(8,128)(2,1)S(1)} %collective-permute-done.29), channel_id=1, source_target_pairs={{8,0},{16,8},{24,16},{28,24},{20,28},{12,20},{4,12},{0,4},{9,1},{1... | collective-permute-start | bytes 4718600 | tf_op jit(solution)/shard_map/ppermute | solution.py:80
  404.4 35.3 %collective-permute-start.24 = (bf16[256,2048]{1,0:T(8,128)(2,1)S(1)}, bf16[256,2048]{1,0:T(8,128)(2,1)S(1)}, u32[]{:S(2)}, u32[]{:S(2)}) collective-permute-start(bf16[256,2048]{1,0:T(8,128)(2,1)S(1)} %multiply_convert_fusion.2), channel_id=1, source_target_pairs={{0,2},{1,3},{2,0},{3,1},{4,6},{5,7},{6,4},{7,5},{8,10},{9,11},{10,... | collective-permute-start | bytes 3145736 | tf_op jit(solution)/shard_map/ppermute | solution.py:144
  553.5 23.6 %collective-permute-start.43 = (bf16[256,2048]{1,0:T(8,128)(2,1)S(1)}, bf16[256,2048]{1,0:T(8,128)(2,1)S(1)}, u32[]{:S(2)}, u32[]{:S(2)}) collective-permute-start(bf16[256,2048]{1,0:T(8,128)(2,1)S(1)} %get-tuple-element.65), channel_id=1, source_target_pairs={{0,1},{1,0},{2,3},{3,2},{4,5},{5,4},{6,7},{7,6},{8,9},{9,8},{10,11... | collective-permute-start | bytes 3145736 | tf_op jit(solution)/shard_map/ppermute | solution.py:144
  557.8 20.8 %collective-permute-start.48 = (bf16[256,2048]{1,0:T(8,128)(2,1)S(1)}, bf16[256,2048]{1,0:T(8,128)(2,1)S(1)}, u32[]{:S(2)}, u32[]{:S(2)}) collective-permute-start(bf16[256,2048]{1,0:T(8,128)(2,1)S(1)} %get-tuple-element.62), channel_id=1, source_target_pairs={{0,1},{1,0},{2,3},{3,2},{4,5},{5,4},{6,7},{7,6},{8,9},{9,8},{10,11... | collective-permute-start | bytes 3145736 | tf_op jit(solution)/shard_map/ppermute | solution.py:144
  570.5 31.8 %collective-permute-start.80 = (bf16[256,3072]{1,0:T(8,128)(2,1)S(1)}, bf16[256,3072]{1,0:T(8,128)(2,1)S(1)}, u32[]{:S(2)}, u32[]{:S(2)}) collective-permute-start(bf16[256,3072]{1,0:T(8,128)(2,1)S(1)} %pad_maximum_fusion.11), channel_id=1, source_target_pairs={{0,8},{8,16},{16,24},{24,28},{28,20},{20,12},{12,4},{4,0},{1,9},{9... | collective-permute-start | bytes 4718600 | tf_op jit(solution)/shard_map/ppermute | solution.py:80
  571.8 20.6 %collective-permute-start.50 = (bf16[256,2048]{1,0:T(8,128)(2,1)S(1)}, bf16[256,2048]{1,0:T(8,128)(2,1)S(1)}, u32[]{:S(2)}, u32[]{:S(2)}) collective-permute-start(bf16[256,2048]{1,0:T(8,128)(2,1)S(1)} %add_convert_fusion.6), channel_id=1, source_target_pairs={{0,2},{1,3},{2,0},{3,1},{4,6},{5,7},{6,4},{7,5},{8,10},{9,11},{10,... | collective-permute-start | bytes 3145736 | tf_op jit(solution)/shard_map/ppermute | solution.py:144
  575.5 44.5 %collective-permute-start.87 = (bf16[96,2048]{1,0:T(8,128)(2,1)}, bf16[96,2048]{1,0:T(8,128)(2,1)}, u32[]{:S(2)}, u32[]{:S(2)}) collective-permute-start(bf16[96,2048]{1,0:T(8,128)(2,1)} %get-tuple-element.48), channel_id=1, source_target_pairs={{0,8},{8,16},{16,24},{24,28},{28,20},{20,12},{12,4},{4,0},{1,9},{9... | collective-permute-start | bytes 1179656 | tf_op jit(solution)/shard_map/ppermute | solution.py:80
  577.0 42.9 %collective-permute-start.91 = (bf16[96,2048]{1,0:T(8,128)(2,1)S(1)}, bf16[96,2048]{1,0:T(8,128)(2,1)}, u32[]{:S(2)}, u32[]{:S(2)}) collective-permute-start(bf16[96,2048]{1,0:T(8,128)(2,1)S(1)} %get-tuple-element.50), channel_id=1, source_target_pairs={{8,0},{16,8},{24,16},{28,24},{20,28},{12,20},{4,12},{0,4},{9,1},{1... | collective-permute-start | bytes 1179656 | tf_op jit(solution)/shard_map/ppermute | solution.py:80
  578.6 27.0 %collective-permute-start.42 = (bf16[256,2048]{1,0:T(8,128)(2,1)S(1)}, bf16[256,2048]{1,0:T(8,128)(2,1)S(1)}, u32[]{:S(2)}, u32[]{:S(2)}) collective-permute-start(bf16[256,2048]{1,0:T(8,128)(2,1)S(1)} %get-tuple-element.64), channel_id=1, source_target_pairs={{0,1},{1,0},{2,3},{3,2},{4,5},{5,4},{6,7},{7,6},{8,9},{9,8},{10,11... | collective-permute-start | bytes 3145736 | tf_op jit(solution)/shard_map/ppermute | solution.py:144
  592.4 21.7 %collective-permute-start.44 = (bf16[256,2048]{1,0:T(8,128)(2,1)S(1)}, bf16[256,2048]{1,0:T(8,128)(2,1)S(1)}, u32[]{:S(2)}, u32[]{:S(2)}) collective-permute-start(bf16[256,2048]{1,0:T(8,128)(2,1)S(1)} %add_convert_fusion.8), channel_id=1, source_target_pairs={{0,2},{1,3},{2,0},{3,1},{4,6},{5,7},{6,4},{7,5},{8,10},{9,11},{10,... | collective-permute-start | bytes 3145736 | tf_op jit(solution)/shard_map/ppermute | solution.py:144
  602.3 42.1 %collective-permute-start.84 = (bf16[256,3072]{1,0:T(8,128)(2,1)}, bf16[256,3072]{1,0:T(8,128)(2,1)}, u32[]{:S(2)}, u32[]{:S(2)}) collective-permute-start(bf16[256,3072]{1,0:T(8,128)(2,1)} %pad_maximum_fusion.12), channel_id=1, source_target_pairs={{8,0},{16,8},{24,16},{28,24},{20,28},{12,20},{4,12},{0,4},{9,1},{1... | collective-permute-start | bytes 4718600 | tf_op jit(solution)/shard_map/ppermute | solution.py:80
  605.5 39.0 %collective-permute-start.81 = (bf16[256,3072]{1,0:T(8,128)(2,1)}, bf16[256,3072]{1,0:T(8,128)(2,1)}, u32[]{:S(2)}, u32[]{:S(2)}) collective-permute-start(bf16[256,3072]{1,0:T(8,128)(2,1)} %add_convert_fusion.4), channel_id=1, source_target_pairs={{0,8},{8,16},{16,24},{24,28},{28,20},{20,12},{12,4},{4,0},{1,9},{9... | collective-permute-start | bytes 4718600 | tf_op jit(solution)/shard_map/ppermute | solution.py:80
  618.6 19.3 %collective-permute-start.52 = (bf16[256,2048]{1,0:T(8,128)(2,1)}, bf16[256,2048]{1,0:T(8,128)(2,1)}, u32[]{:S(2)}, u32[]{:S(2)}) collective-permute-start(bf16[256,2048]{1,0:T(8,128)(2,1)} %get-tuple-element.29), channel_id=1, source_target_pairs={{0,2},{1,3},{2,0},{3,1},{4,6},{5,7},{6,4},{7,5},{8,10},{9,11},{10,... | collective-permute-start | bytes 3145736 | tf_op jit(solution)/shard_map/ppermute | solution.py:144
  622.5 38.9 %collective-permute-start.88 = (bf16[192,2048]{1,0:T(8,128)(2,1)}, bf16[192,2048]{1,0:T(8,128)(2,1)}, u32[]{:S(2)}, u32[]{:S(2)}) collective-permute-start(bf16[192,2048]{1,0:T(8,128)(2,1)} %pad_maximum_fusion.16), channel_id=1, source_target_pairs={{0,8},{8,16},{16,24},{24,28},{28,20},{20,12},{12,4},{4,0},{1,9},{9... | collective-permute-start | bytes 2359304 | tf_op jit(solution)/shard_map/ppermute | solution.py:80
  623.1 41.8 %collective-permute-start.51 = (bf16[256,2048]{1,0:T(8,128)(2,1)}, bf16[256,2048]{1,0:T(8,128)(2,1)}, u32[]{:S(2)}, u32[]{:S(2)}) collective-permute-start(bf16[256,2048]{1,0:T(8,128)(2,1)} %get-tuple-element.29), channel_id=1, source_target_pairs={{0,1},{1,0},{2,3},{3,2},{4,5},{5,4},{6,7},{7,6},{8,9},{9,8},{10,11... | collective-permute-start | bytes 3145736 | tf_op jit(solution)/shard_map/ppermute | solution.py:144
  637.8 27.3 %collective-permute-start.53 = (bf16[256,2048]{1,0:T(8,128)(2,1)}, bf16[256,2048]{1,0:T(8,128)(2,1)}, u32[]{:S(2)}, u32[]{:S(2)}) collective-permute-start(bf16[256,2048]{1,0:T(8,128)(2,1)} %collective-permute-done.52), channel_id=1, source_target_pairs={{0,1},{1,0},{2,3},{3,2},{4,5},{5,4},{6,7},{7,6},{8,9},{9,8},{10,11... | collective-permute-start | bytes 3145736 | tf_op jit(solution)/shard_map/ppermute | solution.py:144
  650.2 26.6 %collective-permute-start.85 = (bf16[256,3072]{1,0:T(8,128)(2,1)}, bf16[256,3072]{1,0:T(8,128)(2,1)}, u32[]{:S(2)}, u32[]{:S(2)}) collective-permute-start(bf16[256,3072]{1,0:T(8,128)(2,1)} %get-tuple-element.34), channel_id=1, source_target_pairs={{8,0},{16,8},{24,16},{28,24},{20,28},{12,20},{4,12},{0,4},{9,1},{1... | collective-permute-start | bytes 4718600 | tf_op jit(solution)/shard_map/ppermute | solution.py:80
  651.4 114.9 %collective-permute-start.92 = (bf16[192,2048]{1,0:T(8,128)(2,1)}, bf16[192,2048]{1,0:T(8,128)(2,1)}, u32[]{:S(2)}, u32[]{:S(2)}) collective-permute-start(bf16[192,2048]{1,0:T(8,128)(2,1)} %pad_maximum_fusion.17), channel_id=1, source_target_pairs={{8,0},{16,8},{24,16},{28,24},{20,28},{12,20},{4,12},{0,4},{9,1},{1... | collective-permute-start | bytes 2359304 | tf_op jit(solution)/shard_map/ppermute | solution.py:80
  663.9 102.4 %collective-permute-start.89 = (bf16[192,2048]{1,0:T(8,128)(2,1)}, bf16[192,2048]{1,0:T(8,128)(2,1)}, u32[]{:S(2)}, u32[]{:S(2)}) collective-permute-start(bf16[192,2048]{1,0:T(8,128)(2,1)} %add_convert_fusion.13), channel_id=1, source_target_pairs={{0,8},{8,16},{16,24},{24,28},{28,20},{20,12},{12,4},{4,0},{1,9},{9... | collective-permute-start | bytes 2359304 | tf_op jit(solution)/shard_map/ppermute | solution.py:80
  665.0 47.1 %collective-permute-start.82 = (bf16[256,3072]{1,0:T(8,128)(2,1)}, bf16[256,3072]{1,0:T(8,128)(2,1)}, u32[]{:S(2)}, u32[]{:S(2)}) collective-permute-start(bf16[256,3072]{1,0:T(8,128)(2,1)} %get-tuple-element.33), channel_id=1, source_target_pairs={{0,8},{8,16},{16,24},{24,28},{28,20},{20,12},{12,4},{4,0},{1,9},{9... | collective-permute-start | bytes 4718600 | tf_op jit(solution)/shard_map/ppermute | solution.py:80
  680.5 46.9 %collective-permute-start.86 = (bf16[256,3072]{1,0:T(8,128)(2,1)}, bf16[256,3072]{1,0:T(8,128)(2,1)}, u32[]{:S(2)}, u32[]{:S(2)}) collective-permute-start(bf16[256,3072]{1,0:T(8,128)(2,1)} %add_convert_fusion.1), channel_id=1, source_target_pairs={{8,0},{16,8},{24,16},{28,24},{20,28},{12,20},{4,12},{0,4},{9,1},{1... | collective-permute-start | bytes 4718600 | tf_op jit(solution)/shard_map/ppermute | solution.py:80
  681.8 63.2 %all-to-all-start.4 = ((bf16[8,256,256]{2,1,0:T(8,128)(2,1)}), bf16[8,256,256]{2,1,0:T(8,128)(2,1)S(1)}, u32[]{:S(2)}, u32[]{:S(2)}) async-start(bf16[8,256,256]{2,1,0:T(8,128)(2,1)} %bitcast.82), calls=%async_computation.4 | async-start | bytes 2097152 | tf_op jit(solution)/shard_map/all_to_all | solution.py:446
  691.4 71.0 %collective-permute-start.70 = (bf16[32,2048]{1,0:T(8,128)(2,1)S(1)}, bf16[32,2048]{1,0:T(8,128)(2,1)S(1)}, u32[]{:S(2)}, u32[]{:S(2)}) collective-permute-start(bf16[32,2048]{1,0:T(8,128)(2,1)S(1)} %get-tuple-element.72), channel_id=1, source_target_pairs={{0,8},{8,16},{16,24},{24,28},{28,20},{20,12},{12,4},{4,0},{1,9},{9... | collective-permute-start | bytes 393224 | tf_op jit(solution)/shard_map/ppermute | solution.py:80
  712.0 50.4 %collective-permute-start.74 = (bf16[32,2048]{1,0:T(8,128)(2,1)S(1)}, bf16[32,2048]{1,0:T(8,128)(2,1)S(1)}, u32[]{:S(2)}, u32[]{:S(2)}) collective-permute-start(bf16[32,2048]{1,0:T(8,128)(2,1)S(1)} %get-tuple-element.74), channel_id=1, source_target_pairs={{8,0},{16,8},{24,16},{28,24},{20,28},{12,20},{4,12},{0,4},{9,1},{1... | collective-permute-start | bytes 393224 | tf_op jit(solution)/shard_map/ppermute | solution.py:80
  744.9 47.2 %all-to-all-start.7 = ((bf16[4,64,3072]{2,1,0:T(8,128)(2,1)}), bf16[4,64,3072]{2,1,0:T(8,128)(2,1)S(1)}, u32[]{:S(2)}, u32[]{:S(2)}) async-start(bf16[4,64,3072]{2,1,0:T(8,128)(2,1)} %bitcast.101), calls=%async_computation.7 | async-start | bytes 3145728 | tf_op jit(solution)/shard_map/all_to_all | solution.py:517
  764.2 32.3 %collective-permute-start.71 = (bf16[64,2048]{1,0:T(8,128)(2,1)}, bf16[64,2048]{1,0:T(8,128)(2,1)}, u32[]{:S(2)}, u32[]{:S(2)}) collective-permute-start(bf16[64,2048]{1,0:T(8,128)(2,1)} %pad_maximum_fusion.25), channel_id=1, source_target_pairs={{0,8},{8,16},{16,24},{24,28},{28,20},{20,12},{12,4},{4,0},{1,9},{9... | collective-permute-start | bytes 786440 | tf_op jit(solution)/shard_map/ppermute | solution.py:80
  769.7 80.1 %collective-permute-start.93 = (bf16[192,2048]{1,0:T(8,128)(2,1)}, bf16[192,2048]{1,0:T(8,128)(2,1)S(1)}, u32[]{:S(2)}, u32[]{:S(2)}) collective-permute-start(bf16[192,2048]{1,0:T(8,128)(2,1)} %get-tuple-element.45), channel_id=1, source_target_pairs={{8,0},{16,8},{24,16},{28,24},{20,28},{12,20},{4,12},{0,4},{9,1},{1... | collective-permute-start | bytes 2359304 | tf_op jit(solution)/shard_map/ppermute | solution.py:80
  771.6 28.3 %collective-permute-start.75 = (bf16[64,2048]{1,0:T(8,128)(2,1)S(1)}, bf16[64,2048]{1,0:T(8,128)(2,1)}, u32[]{:S(2)}, u32[]{:S(2)}) collective-permute-start(bf16[64,2048]{1,0:T(8,128)(2,1)S(1)} %pad_maximum_fusion.26), channel_id=1, source_target_pairs={{8,0},{16,8},{24,16},{28,24},{20,28},{12,20},{4,12},{0,4},{9,1},{1... | collective-permute-start | bytes 786440 | tf_op jit(solution)/shard_map/ppermute | solution.py:80
  792.1 108.9 %all-to-all-start.5 = ((bf16[8,256,512]{2,1,0:T(8,128)(2,1)}), bf16[8,256,512]{2,1,0:T(8,128)(2,1)}, u32[]{:S(2)}, u32[]{:S(2)}) async-start(bf16[8,256,512]{2,1,0:T(8,128)(2,1)} %bitcast.233), calls=%async_computation.5 | async-start | bytes 4194304 | tf_op jit(solution)/shard_map/all_to_all | solution.py:451
  797.5 50.9 %collective-permute-start.72 = (bf16[64,2048]{1,0:T(8,128)(2,1)S(1)}, bf16[64,2048]{1,0:T(8,128)(2,1)S(1)}, u32[]{:S(2)}, u32[]{:S(2)}) collective-permute-start(bf16[64,2048]{1,0:T(8,128)(2,1)S(1)} %add_convert_fusion.27), channel_id=1, source_target_pairs={{0,8},{8,16},{16,24},{24,28},{28,20},{20,12},{12,4},{4,0},{1,9},{9... | collective-permute-start | bytes 786440 | tf_op jit(solution)/shard_map/ppermute | solution.py:80
  798.7 87.5 %collective-permute-start.90 = (bf16[192,2048]{1,0:T(8,128)(2,1)S(1)}, bf16[192,2048]{1,0:T(8,128)(2,1)}, u32[]{:S(2)}, u32[]{:S(2)}) collective-permute-start(bf16[192,2048]{1,0:T(8,128)(2,1)S(1)} %get-tuple-element.44), channel_id=1, source_target_pairs={{0,8},{8,16},{16,24},{24,28},{28,20},{20,12},{12,4},{4,0},{1,9},{9... | collective-permute-start | bytes 2359304 | tf_op jit(solution)/shard_map/ppermute | solution.py:80
  852.1 34.1 %collective-permute-start.94 = (bf16[192,2048]{1,0:T(8,128)(2,1)}, bf16[192,2048]{1,0:T(8,128)(2,1)S(1)}, u32[]{:S(2)}, u32[]{:S(2)}) collective-permute-start(bf16[192,2048]{1,0:T(8,128)(2,1)} %add_convert_fusion.10), channel_id=1, source_target_pairs={{8,0},{16,8},{24,16},{28,24},{20,28},{12,20},{4,12},{0,4},{9,1},{1... | collective-permute-start | bytes 2359304 | tf_op jit(solution)/shard_map/ppermute | solution.py:80
  859.8 20.9 %collective-permute-start.77 = (bf16[64,2048]{1,0:T(8,128)(2,1)}, bf16[64,2048]{1,0:T(8,128)(2,1)}, u32[]{:S(2)}, u32[]{:S(2)}) collective-permute-start(bf16[64,2048]{1,0:T(8,128)(2,1)} %add_convert_fusion.24), channel_id=1, source_target_pairs={{8,0},{16,8},{24,16},{28,24},{20,28},{12,20},{4,12},{0,4},{9,1},{1... | collective-permute-start | bytes 786440 | tf_op jit(solution)/shard_map/ppermute | solution.py:80
  949.2 40.8 %collective-permute-start.65 = (f32[2,128]{1,0:T(2,128)S(1)}, f32[2,128]{1,0:T(2,128)S(1)}, u32[]{:S(2)}, u32[]{:S(2)}) collective-permute-start(f32[2,128]{1,0:T(2,128)S(1)} %pad_maximum_fusion.27), channel_id=1, source_target_pairs={{0,1},{1,0},{2,3},{3,2},{4,5},{5,4},{6,7},{7,6},{8,9},{9,8},{10,11... | collective-permute-start | bytes 3080 | tf_op jit(solution)/shard_map/ppermute | solution.py:144
  993.8 23.8 %collective-permute-start.55 = (bf16[256,2048]{1,0:T(8,128)(2,1)}, bf16[256,2048]{1,0:T(8,128)(2,1)}, u32[]{:S(2)}, u32[]{:S(2)}) collective-permute-start(bf16[256,2048]{1,0:T(8,128)(2,1)} %get-tuple-element.61), channel_id=1, source_target_pairs={{0,1},{1,0},{2,3},{3,2},{4,5},{5,4},{6,7},{7,6},{8,9},{9,8},{10,11... | collective-permute-start | bytes 3145736 | tf_op jit(solution)/shard_map/ppermute | solution.py:144
  1009.8 33.3 %collective-permute-start.54 = (bf16[256,2048]{1,0:T(8,128)(2,1)}, bf16[256,2048]{1,0:T(8,128)(2,1)S(1)}, u32[]{:S(2)}, u32[]{:S(2)}) collective-permute-start(bf16[256,2048]{1,0:T(8,128)(2,1)} %get-tuple-element.60), channel_id=1, source_target_pairs={{0,1},{1,0},{2,3},{3,2},{4,5},{5,4},{6,7},{7,6},{8,9},{9,8},{10,11... | collective-permute-start | bytes 3145736 | tf_op jit(solution)/shard_map/ppermute | solution.py:144
  1019.3 23.8 %collective-permute-start.56 = (bf16[256,2048]{1,0:T(8,128)(2,1)S(1)}, bf16[256,2048]{1,0:T(8,128)(2,1)S(1)}, u32[]{:S(2)}, u32[]{:S(2)}) collective-permute-start(bf16[256,2048]{1,0:T(8,128)(2,1)S(1)} %add_convert_fusion.5), channel_id=1, source_target_pairs={{0,2},{1,3},{2,0},{3,1},{4,6},{5,7},{6,4},{7,5},{8,10},{9,11},{10,... | collective-permute-start | bytes 3145736 | tf_op jit(solution)/shard_map/ppermute | solution.py:144
  (137 other events, 1937.1 us)

commit v2 on v1

v2 whole, which is shorter than its diff:
```python
import functools

import jax
import jax.numpy as jnp
import numpy as np
from jax import lax
from jax.experimental import pallas as pl
from jax.experimental.pallas import tpu as pltpu
from jax.sharding import PartitionSpec as P

BLK = 128
OWN_BLK = 4
EPSILON = 1e-06
THETA = 1000000.0
LANES = 128
NARROW = 4
CONTRACT_ROWS = (((0,), (0,)), ((), ()))
CONTRACT_COLS = (((1,), (1,)), ((), ()))
NEGATIVE = -1e30
F32 = jnp.float32
BF16 = jnp.bfloat16
DEVICES = ("wide", "narrow")


def row_normalize(values, gain_row):
    return (
        values * lax.rsqrt(jnp.mean(values * values, axis=-1, keepdims=True) + EPSILON) * gain_row
    )


def gated(gate_sum, up_sum):
    return jax.nn.silu(gate_sum) * up_sum


def dot(left, right):
    return jnp.dot(left, right, preferred_element_type=F32)


def outer_sum(left_rows, right_rows):
    return lax.dot_general(left_rows, right_rows, CONTRACT_ROWS, preferred_element_type=F32)


def times_transpose(left_rows, matrix):
    return lax.dot_general(left_rows, matrix, CONTRACT_COLS, preferred_element_type=F32)


def ring_order(count):
    rows = count // 2
    return [2 * i for i in range(rows)] + [2 * i + 1 for i in reversed(range(rows))]


class Ring:
    def __init__(self, count):
        self.count = count
        order = ring_order(count)
        place = np.zeros(count, np.int32)
        for i, device in enumerate(order):
            place[device] = i
        self.onward = [(order[i], order[(i + 1) % count]) for i in range(count)]
        self.back = [(b, a) for a, b in self.onward]
        self.order = jnp.asarray(np.array(order + order + order, np.int32))
        self.place = jnp.asarray(place)[lax.axis_index("wide")]

    def device(self, shift):
        return self.order[self.place + self.count + shift]

    def send(self, value, forward):
        return lax.ppermute(value, "wide", self.onward if forward else self.back)


def no_op(out_ref):
    pass


def blank(shape, dtype):
    return pl.pallas_call(
        no_op,
        out_shape=jax.ShapeDtypeStruct(shape, dtype),
        out_specs=pl.BlockSpec(memory_space=pl.ANY),
    )()


def tie(value, *after):
    after = [leaf for leaf in jax.tree.leaves(after)]
    return lax.optimization_barrier((value, after))[0] if after else value


class Gather:
    def __init__(self, ring, part, later=False):
        self.ring, self.rows, self.step, self.later = ring, part.shape[0], 0, later
        self.ahead, self.behind, self.kept = part, part, []
        if ring.count > 8:
            self.whole = lax.all_gather(part, "wide", axis=0, tiled=True)
        else:
            self.whole = blank((ring.count * self.rows, part.shape[1]), part.dtype)
            self.put(part, 0, 0)

    def put(self, value, shift, extra):
        if self.later:
            self.kept.append((value, shift, extra))
        else:
            start = self.ring.device(shift) * self.rows + extra
            self.whole = lax.dynamic_update_slice(self.whole, value, (start, 0))

    def assemble(self, *after):
        if self.ring.count <= 8:
            self.later, kept = False, self.kept
            values = tie([value for value, shift, extra in kept], after)
            for value, (unused_value, shift, extra) in zip(values, kept):
                self.put(value, shift, extra)
        return self.whole

    def advance(self, *after):
        ring, half = self.ring, self.rows // 2
        if ring.count > 8:
            return []
        self.step += 1
        last = self.step == ring.count // 2
        ahead, behind = tie((self.ahead, self.behind), after)
        if last:
            ahead, behind = ahead[:half], behind[half:]
        self.ahead, self.behind = ring.send(ahead, True), ring.send(behind, False)
        self.put(self.ahead, -self.step, 0)
        self.put(self.behind, self.step, half if last else 0)
        return [self.ahead, self.behind]


class Reduce:
    def __init__(self, ring, *terms):
        self.ring, self.terms, self.step = ring, terms, 0
        self.rows = sum(term.shape[0] for term in terms) // ring.count
        if ring.count > 8:
            parts = [term.reshape(ring.count, -1, term.shape[1]) for term in terms]
            whole = jnp.concatenate(parts, axis=1).reshape(-1, terms[0].shape[1])
            self.total = lax.psum_scatter(whole, "wide", scatter_dimension=0, tiled=True)

    def term(self, shift):
        parts = []
        for term in self.terms:
            rows = term.shape[0] // self.ring.count
            start = self.ring.device(shift) * rows
            parts.append(lax.dynamic_slice(term, (start, 0), (rows, term.shape[1])))
        return parts[0] if len(parts) == 1 else jnp.concatenate(parts, axis=0)

    def advance(self, *after):
        ring, half = self.ring, self.rows // 2
        if ring.count > 8:
            return []
        shift = ring.count // 2 - self.step
        if self.step:
            ahead, behind = tie((self.ahead, self.behind), after)
            mine, other = self.term(shift), self.term(-shift)
            if self.step == 1:
                ahead = jnp.concatenate([join(mine[:half], ahead), mine[half:]], axis=0)
                behind = jnp.concatenate([other[:half], join(other[half:], behind)], axis=0)
            else:
                ahead, behind = join(mine, ahead), join(other, behind)
        else:
            far = tie(self.term(shift), after)
            ahead, behind = far[:half], far[half:]
        self.step += 1
        self.ahead, self.behind = ring.send(ahead, True), ring.send(behind, False)
        return [self.ahead, self.behind]

    def result(self):
        if self.ring.count > 8:
            return self.total.astype(F32)
        return self.term(0).astype(F32) + self.ahead.astype(F32) + self.behind.astype(F32)


def join(left, right):
    return (left.astype(F32) + right.astype(F32)).astype(BF16)


def swap(value, bit):
    return lax.ppermute(value, "narrow", [(i, i ^ bit) for i in range(NARROW)])


def narrow_gather(value, across=None):
    across = swap(value, 2) if across is None else across
    chips = jnp.concatenate([value, across], axis=0)
    return jnp.concatenate([chips, swap(chips, 1)], axis=0), across


def narrow_reduce(terms):
    rows = terms.shape[0] // NARROW
    low = terms.astype(BF16)
    other = swap(low[2 * rows :], 1)
    across = swap(join(low[rows : 2 * rows], other[rows:]), 2)
    total = low[:rows].astype(F32) + other[:rows].astype(F32) + across.astype(F32)
    return total, other, across


def layout(doc_blocks, doc_order, block_home, my_wide, block_count):
    owners = doc_blocks.shape[1]
    owner_ids = jnp.arange(owners, dtype=jnp.int32)
    hits = (doc_order[:, :, None] == owner_ids[None, None, :]).astype(jnp.int32)
    in_stream = jnp.sum(hits * doc_blocks[:, None, :], axis=2)
    before = (owner_ids[:, None] < owner_ids[None, :]).astype(jnp.int32)
    stream_start = jnp.sum(in_stream[:, :, None] * before[None], axis=1)
    owner_start = jnp.sum(hits * stream_start[:, :, None], axis=1)
    column = jnp.sum(jnp.where(block_home == my_wide, owner_ids[None, :], 0), axis=1)
    stream_ids = jnp.arange(block_count, dtype=jnp.int32)[None, :] * owners + column[:, None]
    member = (owner_start[:, None, :] <= stream_ids[:, :, None]) & (
        stream_ids[:, :, None] < (owner_start + doc_blocks)[:, None, :]
    )
    offsets = stream_ids - jnp.sum(jnp.where(member, owner_start[:, None, :], 0), axis=2)
    return owner_start, offsets


def stream_table(group, owner_start, doc_blocks, doc_tail, block_home, block_count):
    def pick(table):
        return lax.dynamic_index_in_dim(table, group, 0, keepdims=False)

    starts, blocks, tails, homes = pick(owner_start), pick(doc_blocks), pick(doc_tail), pick(block_home)
    owners = starts.shape[0]
    ids = jnp.arange(owners * block_count, dtype=jnp.int32)
    member = (starts[None, :] <= ids[:, None]) & (ids[:, None] < (starts + blocks)[None, :])

    def chosen(values):
        return jnp.sum(jnp.where(member, values[None, :], 0), axis=1)

    home = jnp.sum(
        jnp.where(
            (ids % owners)[:, None] == jnp.arange(owners, dtype=jnp.int32)[None, :],
            homes[None, :],
            0,
        ),
        axis=1,
    )
    place = home * block_count + ids // owners
    return jnp.stack([place, chosen(starts), chosen((blocks - 1) * BLK + tails)])


def window(table, rows_ref, b, heads, size):
    first, length = table[1, b], table[2, b]
    width = heads * size
    mine = rows_ref[pl.ds(pl.multiple_of(table[0, b] * BLK, BLK), BLK), :width]
    queries = jnp.concatenate([mine[:, i * size : (i + 1) * size] for i in range(heads)], axis=0)
    spot = (b - first) * BLK
    row = lax.broadcasted_iota(jnp.int32, (heads, BLK, BLK), 1).reshape(heads * BLK, BLK) + spot
    col = lax.broadcasted_iota(jnp.int32, (heads * BLK, BLK), 1) + spot
    starts, keys, values, scores = [], [], [], []
    for i in range(OWN_BLK):
        start = pl.multiple_of(table[0, jnp.maximum(b - i, 0)] * BLK, BLK)
        key = rows_ref[pl.ds(start, BLK), width : width + size]
        col_i = col - i * BLK
        allowed = (col_i <= row) & (col_i < length) & (col_i >= 0)
        score = times_transpose(queries, key) * size ** (-0.5)
        starts.append(start)
        keys.append(key)
        values.append(rows_ref[pl.ds(start, BLK), width + size : width + 2 * size])
        scores.append(jnp.where(allowed, score, NEGATIVE))
    highest = scores[0]
    for score in scores[1:]:
        highest = jnp.maximum(highest, score)
    highest = jnp.max(highest, axis=-1, keepdims=True)
    powers = [jnp.exp(score - highest) for score in scores]
    total = powers[0]
    for power in powers[1:]:
        total = total + power
    total = jnp.sum(total, axis=-1, keepdims=True)
    weights = [power / total for power in powers]
    return mine, queries, starts, keys, values, weights


def forward_kernel(heads, size, table, rows_ref, out_ref):
    def step(b, carry):
        _, _, starts, _, values, weights = window(table, rows_ref, b, heads, size)
        mixed = dot(weights[0].astype(BF16), values[0])
        for weight, value in zip(weights[1:], values[1:]):
            mixed = mixed + dot(weight.astype(BF16), value)
        for i in range(heads):
            out_ref[pl.ds(starts[0], BLK), i * size : (i + 1) * size] = mixed[
                i * BLK : (i + 1) * BLK
            ].astype(BF16)
        return carry

    lax.fori_loop(0, table.shape[1], step, 0)


def backward_kernel(heads, size, table, rows_ref, grad_ref, out_ref, sums):
    sums[...] = jnp.zeros_like(sums)
    scale = size ** (-0.5)

    def step(b, carry):
        _, queries, starts, keys, values, weights = window(table, rows_ref, b, heads, size)
        grads = grad_ref[pl.ds(starts[0], BLK), :]
        grads = jnp.concatenate([grads[:, i * size : (i + 1) * size] for i in range(heads)], axis=0)
        pulls = [times_transpose(grads, value) for value in values]
        total = weights[0] * pulls[0]
        for weight, pull in zip(weights[1:], pulls[1:]):
            total = total + weight * pull
        total = jnp.sum(total, axis=-1, keepdims=True)
        grad_query = None
        for i in range(OWN_BLK):
            grad_score = (weights[i] * (pulls[i] - total)).astype(BF16)
            part = dot(grad_score, keys[i])
            grad_query = part if grad_query is None else grad_query + part
            spot = pl.ds(starts[i], BLK)
            sums[spot, :size] += outer_sum(grad_score, queries) * scale
            sums[spot, size:] += outer_sum(weights[i].astype(BF16), grads)
        for i in range(heads):
            out_ref[pl.ds(starts[0], BLK), i * size : (i + 1) * size] = (
                grad_query[i * BLK : (i + 1) * BLK] * scale
            ).astype(BF16)
        return carry

    lax.fori_loop(0, table.shape[1], step, 0)
    out_ref[:, heads * size :] = sums[...].astype(BF16)


def attend(table, rows, heads, size):
    return pl.pallas_call(
        functools.partial(forward_kernel, heads, size),
        out_shape=jax.ShapeDtypeStruct((rows.shape[0], heads * size), BF16),
        in_specs=[
            pl.BlockSpec(memory_space=pltpu.SMEM),
            pl.BlockSpec(memory_space=pltpu.VMEM),
        ],
        out_specs=pl.BlockSpec(memory_space=pltpu.VMEM),
        name="attend",
    )(table, rows)


def attend_back(table, rows, grads, heads, size):
    return pl.pallas_call(
        functools.partial(backward_kernel, heads, size),
        out_shape=jax.ShapeDtypeStruct(rows.shape, BF16),
        in_specs=[
            pl.BlockSpec(memory_space=pltpu.SMEM),
            pl.BlockSpec(memory_space=pltpu.VMEM),
            pl.BlockSpec(memory_space=pltpu.VMEM),
        ],
        out_specs=pl.BlockSpec(memory_space=pltpu.VMEM),
        scratch_shapes=[pltpu.VMEM((rows.shape[0], 2 * size), F32)],
        name="attend_back",
    )(table, rows, grads)


def unit_rows(values):
    return lax.rsqrt(jnp.mean(values * values, axis=-1, keepdims=True) + EPSILON)


def finish_kernel(sizes, order, raw_ref, cos_ref, sin_ref, gains_ref, out_ref):
    value_heads, group_heads, size = sizes
    per_group = group_heads * size
    query_width = value_heads * per_group
    key_width = value_heads * size

    def turned(start, gain):
        values = raw_ref[:, start : start + size]
        values = values * unit_rows(values) * gain
        return (
            values * cos_ref[...] + pltpu.roll(values, size // 2, 1) * sin_ref[...]
        ).astype(BF16)

    for head in range(value_heads):
        for i in range(group_heads):
            start = head * per_group + i * size
            out_ref[0, head, :, i * size : (i + 1) * size] = turned(start, gains_ref[0:1, :])
        start = query_width + head * size
        out_ref[0, head, :, per_group : per_group + size] = turned(start, gains_ref[1:2, :])
        start = query_width + key_width + head * size
        out_ref[0, head, :, per_group + size :] = raw_ref[:, start : start + size].astype(BF16)


def unfinish_kernel(
    sizes, order, raw_ref, grad_ref, cos_ref, sin_ref, gains_ref, out_ref, sums_ref
):
    value_heads, group_heads, size = sizes
    per_group = group_heads * size
    query_width = value_heads * per_group
    key_width = value_heads * size

    @pl.when(pl.program_id(0) == 0)
    def _():
        sums_ref[...] = jnp.zeros_like(sums_ref)

    def pull(grad, start, which):
        grad = grad.astype(F32)
        values = raw_ref[:, start : start + size]
        unit = unit_rows(values)
        values = values * unit
        grad = grad * cos_ref[...] + pltpu.roll(grad * sin_ref[...], size // 2, 1)
        sums_ref[which * 8 : which * 8 + 8, :] += jnp.sum(
            (grad * values).reshape(-1, 8, size), axis=0
        )
        grad = grad * gains_ref[which : which + 1, :]
        grad = unit * (grad - values * jnp.mean(grad * values, axis=-1, keepdims=True))
        out_ref[:, start : start + size] = grad.astype(BF16)

    for head in range(value_heads):
        for i in range(group_heads):
            pull(
                grad_ref[0, head, :, i * size : (i + 1) * size], head * per_group + i * size, 0
            )
        pull(grad_ref[0, head, :, per_group : per_group + size], query_width + head * size, 1)
        start = query_width + key_width + head * size
        out_ref[:, start : start + size] = grad_ref[0, head, :, per_group + size :]


def pack_kernel(heads, order, rows_ref, out_ref):
    width = out_ref.shape[3]
    for head in range(heads):
        out_ref[0, head] = rows_ref[:, head * width : (head + 1) * width]


def unpack_kernel(heads, order, pieces_ref, out_ref):
    width = pieces_ref.shape[3]
    for head in range(heads):
        out_ref[:, head * width : (head + 1) * width] = pieces_ref[0, head]


def row_spec(rows, cols):
    return pl.BlockSpec((rows, cols), lambda i, order: (i, 0))


def whole_spec(shape):
    return pl.BlockSpec(shape, lambda i, order: (0,) * len(shape))


def piece_spec(heads, rows, cols):
    return pl.BlockSpec((1, heads, rows, cols), lambda i, order: (order[i], 0, 0, 0))


def by_rows(kernel, name, order, args, in_specs, out_shape, out_specs, cost):
    return pl.pallas_call(
        kernel,
        grid_spec=pltpu.PrefetchScalarGridSpec(
            num_scalar_prefetch=1, grid=(NARROW,), in_specs=in_specs, out_specs=out_specs
        ),
        out_shape=out_shape,
        cost_estimate=pl.CostEstimate(flops=cost, bytes_accessed=cost, transcendentals=0),
        name=name,
    )(order, *args)


def finish(sizes, order, raw, cosines, sines, gains):
    value_heads, group_heads, size = sizes
    rows = raw.shape[0] // NARROW
    width = (group_heads + 2) * size
    return by_rows(
        functools.partial(finish_kernel, sizes),
        "finish",
        order,
        (raw, cosines, sines, gains),
        [
            row_spec(rows, raw.shape[1]),
            row_spec(rows, size),
            row_spec(rows, size),
            whole_spec(gains.shape),
        ],
        jax.ShapeDtypeStruct((NARROW, value_heads, rows, width), BF16),
        piece_spec(value_heads, rows, width),
        8 << 20,
    )


def unfinish(sizes, order, raw, pieces, cosines, sines, gains):
    value_heads, group_heads, size = sizes
    rows = raw.shape[0] // NARROW
    return by_rows(
        functools.partial(unfinish_kernel, sizes),
        "unfinish",
        order,
        (raw, pieces, cosines, sines, gains),
        [
            row_spec(rows, raw.shape[1]),
            piece_spec(value_heads, rows, pieces.shape[3]),
            row_spec(rows, size),
            row_spec(rows, size),
            whole_spec(gains.shape),
        ],
        (
            jax.ShapeDtypeStruct(raw.shape, BF16),
            jax.ShapeDtypeStruct((16, size), F32),
        ),
        (row_spec(rows, raw.shape[1]), whole_spec((16, size))),
        8 << 20,
    )


def pack(heads, order, values):
    rows = values.shape[0] // NARROW
    width = values.shape[1] // heads
    return by_rows(
        functools.partial(pack_kernel, heads),
        "pack",
        order,
        (values,),
        [row_spec(rows, values.shape[1])],
        jax.ShapeDtypeStruct((NARROW, heads, rows, width), BF16),
        piece_spec(heads, rows, width),
        2 << 20,
    )


def unpack(order, pieces):
    heads, rows, width = pieces.shape[1:]
    return by_rows(
        functools.partial(unpack_kernel, heads),
        "unpack",
        order,
        (pieces,),
        [piece_spec(heads, rows, width)],
        jax.ShapeDtypeStruct((NARROW * rows, heads * width), BF16),
        row_spec(rows, heads * width),
        2 << 20,
    )


def split_kernel(block, gate_ref, up_ref, out_ref):
    places = gate_ref.shape[1] // (block * NARROW)
    half = out_ref.shape[2] // 2
    for i, ref in enumerate((gate_ref, up_ref)):
        for n in range(NARROW):
            for place in range(places):
                chunk, spot = divmod(place, places // 2)
                start = chunk * half + i * (half // 2) + spot * block
                source = (place * NARROW + n) * block
                out_ref[n, :, start : start + block] = ref[:, source : source + block]


def merge_kernel(block, first_ref, second_ref, gate_ref, up_ref):
    places = gate_ref.shape[1] // (block * NARROW)
    half = first_ref.shape[2]
    for i, ref in enumerate((gate_ref, up_ref)):
        for n in range(NARROW):
            for place in range(places):
                chunk, spot = divmod(place, places // 2)
                source = (first_ref, second_ref)[chunk]
                start = i * (half // 2) + spot * block
                target = (place * NARROW + n) * block
                ref[:, target : target + block] = source[n, :, start : start + block].astype(F32)


def split_columns(block, gate, up):
    rows, cols = gate.shape
    if block % 64:
        def by_chunk(values):
            values = values.reshape(rows, 2, -1, NARROW, block).transpose(3, 0, 1, 2, 4)
            return values.reshape(NARROW, rows, 2, -1)

        both = jnp.concatenate([by_chunk(gate), by_chunk(up)], axis=3)
        return both.reshape(NARROW, rows, -1)
    return pl.pallas_call(
        functools.partial(split_kernel, block),
        out_shape=jax.ShapeDtypeStruct((NARROW, rows, 2 * cols // NARROW), BF16),
        name="split_columns",
    )(gate, up)


def merge_columns(block, first, second):
    rows, half = first.shape[1:]
    cols = half * NARROW
    if block % 64:
        both = jnp.stack([first, second], axis=2).reshape(NARROW, rows, 2, 2, -1, block)
        both = both.transpose(3, 1, 2, 4, 0, 5).reshape(2, rows, cols).astype(F32)
        return both[0], both[1]
    return pl.pallas_call(
        functools.partial(merge_kernel, block),
        out_shape=(jax.ShapeDtypeStruct((rows, cols), F32),) * 2,
        name="merge_columns",
    )(first, second)


def body(
    tokens,
    out_grad,
    attn_norm,
    w_query,
    key_weight,
    value_weight,
    query_norm,
    key_norm_gain,
    w_out,
    mlp_norm,
    w_gate,
    w_up,
    w_down,
    doc_blocks,
    doc_tail,
    doc_order,
    block_home,
):
    wide_count = lax.axis_size("wide")
    my_wide = lax.axis_index("wide")
    me = lax.axis_index("narrow")
    device_count = wide_count * NARROW
    ring = Ring(wide_count)
    rows = tokens.shape[0]
    block_count = rows // BLK
    head_size = query_norm.shape[0] * device_count
    query_width = w_query.shape[1] // NARROW
    key_width = key_weight.shape[1] // NARROW
    value_heads = key_width // head_size
    group_heads = query_width // key_width
    hidden = w_gate.shape[1] // NARROW
    shard = w_query.shape[0]
    parts = wide_count // (NARROW * value_heads)

    order = me ^ jnp.array([0, 2, 1, 3], dtype=jnp.int32)
    partner = me ^ jnp.arange(NARROW, dtype=jnp.int32)
    sizes = (value_heads, group_heads, head_size)

    def narrow_exchange(pieces):
        pieces = jnp.take(pieces, partner, axis=0)
        moved = [pieces[0]] + [swap(pieces[i], i) for i in range(1, NARROW)]
        return jnp.take(jnp.stack(moved), partner, axis=0)

    def narrow_columns(weight):
        return weight.reshape(shard, NARROW, -1).transpose(1, 0, 2)

    def pad_lanes(values, size):
        return jnp.concatenate([values, jnp.zeros((size - values.shape[0],), BF16)])

    projection_width = query_width + 2 * key_width
    gains = [pad_lanes(gain, shard) for gain in (attn_norm, mlp_norm, query_norm, key_norm_gain)]
    gains = pad_lanes(jnp.concatenate(gains), projection_width)[None, :]
    extra = 32
    at_row = lax.broadcasted_iota(jnp.int32, (extra, projection_width), 0) == me
    gain_rows = jnp.broadcast_to(jnp.where(at_row, gains, 0)[None], (NARROW, extra, projection_width))
    first_pieces = jnp.concatenate(
        [narrow_columns(w_query), narrow_columns(key_weight), narrow_columns(value_weight)], axis=2
    )
    first_pieces = narrow_exchange(jnp.concatenate([first_pieces, gain_rows], axis=1))
    tokens_across = swap(tokens, 2)
    moves = [(g, (g % wide_count) * NARROW + g // wide_count) for g in range(device_count)]
    moves_back = [(b, a) for a, b in moves]
    out_part = lax.ppermute(w_out, DEVICES, moves)
    folds = w_out.shape[1] // projection_width
    out_part = out_part.reshape(shard, folds, -1).transpose(1, 0, 2).reshape(folds * shard, -1)
    gain_rows = jnp.sum(first_pieces[:, shard:].astype(F32), axis=0).astype(BF16)
    first_part = jnp.concatenate(
        [first_pieces[:, :shard].reshape(NARROW * shard, -1), out_part, gain_rows], axis=0
    )
    block = w_down.shape[0]
    first_ring = Gather(ring, first_part)
    down_ring = Gather(ring, w_down, later=True)
    begun = first_ring.advance(down_ring.advance())
    first_ring.advance()
    gate_part, up_part = tie((w_gate, w_up), begun)
    gate_up_pieces = split_columns(block, gate_part, up_part)
    gate_up_part = narrow_exchange(gate_up_pieces).reshape(NARROW * shard, -1)
    first_ring.advance(tokens_across)
    first_done = first_ring.advance()
    gathered = first_ring.whole.reshape(wide_count, -1, projection_width)
    projection = gathered[:, : NARROW * shard].reshape(-1, projection_width)
    out_rows = gathered[:, NARROW * shard : (NARROW + folds) * shard]
    out_rows = out_rows.reshape(wide_count, folds, shard, -1).transpose(0, 2, 1, 3)
    out_weight = out_rows.reshape(wide_count * shard, -1)
    gain_rows = gathered[:, (NARROW + folds) * shard :][:, :NARROW, : 4 * shard]
    gain_rows = gain_rows.reshape(device_count, 4, shard).astype(F32)
    attention_gain, mlp_gain = gain_rows[:, 0].reshape(-1), gain_rows[:, 1].reshape(-1)
    few = query_norm.shape[0]
    norm_gains = jnp.stack(
        [gain_rows[:, 2, :few].reshape(head_size), gain_rows[:, 3, :few].reshape(head_size)]
    )
    norm_gains = jnp.concatenate([norm_gains, jnp.zeros((6, head_size), F32)])
    rings = [
        Gather(ring, gate_up_part[:, :hidden], later=True),
        Gather(ring, gate_up_part[:, hidden:]),
    ]

    inputs = tokens.astype(F32)
    all_inputs = narrow_gather(tokens, tokens_across)[0].astype(F32)
    normed = row_normalize(all_inputs, attention_gain).astype(BF16)
    raw = dot(normed, projection)
    owner_start, offsets = layout(
        doc_blocks, doc_order, tie(block_home, begun), my_wide, block_count
    )
    my_offsets = jnp.take(offsets, order, axis=0)
    position = (
        my_offsets.reshape(-1, 1) * BLK + jnp.arange(BLK, dtype=jnp.int32)[None, :]
    ).reshape(-1)
    half_size = head_size // 2
    frequency = THETA ** (-2.0 * jnp.arange(half_size, dtype=F32) / head_size)
    angles = position.astype(F32)[:, None] * frequency[None, :]
    cosines, sines = jnp.cos(angles), jnp.sin(angles)
    cosines = jnp.concatenate([cosines, cosines], axis=-1)
    sines = jnp.concatenate([-sines, sines], axis=-1)

    def exchange(pieces):
        pieces = jnp.broadcast_to(
            pieces[:, :, None], pieces.shape[:2] + (parts,) + pieces.shape[2:]
        ).reshape(wide_count, rows, -1)
        return lax.all_to_all(pieces, "wide", split_axis=0, concat_axis=0, tiled=True).reshape(
            wide_count * rows, -1
        )

    def exchange_back(values):
        pieces = lax.all_to_all(
            values.reshape(wide_count, rows, -1), "wide", split_axis=0, concat_axis=0, tiled=True
        )
        return pieces.reshape(NARROW, value_heads, parts, rows, -1)[:, :, 0]

    finished = finish(sizes, order, raw, cosines, sines, norm_gains)
    arrived = exchange(tie(finished, down_ring.advance(first_done, gate_up_part)))
    table = stream_table(
        my_wide // (wide_count // NARROW), owner_start, doc_blocks, doc_tail, block_home, block_count
    )
    all_out_grad, unused_across = narrow_gather(tie(out_grad, finished))
    arrived = tie(arrived, rings[0].advance(finished), all_out_grad)
    attended = tie(attend(table, arrived, group_heads, head_size), rings[0].advance(arrived))
    mixed = tie(exchange_back(attended), down_ring.advance(attended))
    early = rings[0].advance(mixed)
    mixed = unpack(order, mixed)

    reduced, unused_other, across = narrow_reduce(dot(mixed, out_weight))
    middle = inputs + tie(reduced, early)
    normed_rows = row_normalize(middle, mlp_gain).astype(BF16)
    early = [rings[0].advance(normed_rows), rings[1].advance(normed_rows)]
    across = tie(swap(normed_rows, 2), early)
    late = down_ring.advance(normed_rows)
    normed_two, across = narrow_gather(normed_rows, across)
    normed_two = tie(normed_two, late)
    gate_up_first, down = rings[0].assemble(middle), down_ring.assemble(middle)
    part = hidden // 2

    def half_forward(rows, weights):
        gate_sum, up_sum = dot(rows, weights[:, :part]), dot(rows, weights[:, part:])
        return gate_sum, up_sum, gated(gate_sum, up_sum).astype(BF16)

    def half_back(gate_sum, up_sum, grad_hidden):
        unused_gated, pull = jax.vjp(gated, gate_sum, up_sum)
        return jnp.concatenate([grad.astype(BF16) for grad in pull(grad_hidden)], axis=1)

    early = rings[1].advance(normed_two)
    gate_sum, up_sum, hidden_first = half_forward(normed_two, gate_up_first)
    wait_first = tie(all_out_grad, hidden_first, early)
    early = rings[1].advance(hidden_first)
    grad_first = half_back(gate_sum, up_sum, times_transpose(wait_first, down[:part]))
    grad_first = tie(grad_first, early)
    early = rings[1].advance(grad_first)
    first_half_terms = outer_sum(normed_two, grad_first).astype(BF16)
    first_half = Reduce(ring, first_half_terms)
    grad_terms = times_transpose(tie(grad_first, first_half_terms, early), gate_up_first)
    grad_terms = tie(grad_terms, first_half.advance())
    early = first_half.advance(grad_terms)
    gate_sum, up_sum, hidden_second = half_forward(tie(normed_two, grad_terms), rings[1].whole)
    wait_second = tie(all_out_grad, hidden_second, early)
    early = first_half.advance(hidden_second)
    grad_second = half_back(gate_sum, up_sum, times_transpose(wait_second, down[part:]))
    grad_second = tie(grad_second, early)
    early = first_half.advance(grad_second)
    grad_terms = (grad_terms + times_transpose(grad_second, rings[1].whole)).astype(BF16)
    grad_normed_two, other, across = narrow_reduce(tie(grad_terms, early))
    later_grad, later_normed, hidden_rows = tie(
        (grad_second, normed_two, (hidden_first, hidden_second)), other
    )
    hidden_rows = jnp.concatenate(hidden_rows, axis=1)
    down_terms = outer_sum(hidden_rows, all_out_grad).astype(BF16)
    down_sums = Reduce(ring, down_terms)
    second_half_terms = outer_sum(later_normed, tie(later_grad, down_terms)).astype(BF16)
    second_half = Reduce(ring, second_half_terms)
    early = [down_sums.advance(), second_half.advance()]
    grad_normed_two = tie(grad_normed_two, early)
    unused_norm, second_pull = jax.vjp(lambda value: row_normalize(value, mlp_gain), middle)
    grad_middle = out_grad.astype(F32) + second_pull(grad_normed_two)[0]

    branch_rows = grad_middle.astype(BF16)
    early = second_half.advance(branch_rows)
    late = down_sums.advance(branch_rows)
    across = tie(swap(branch_rows, 2), early)
    grad_branch, across = narrow_gather(branch_rows, across)
    grad_branch = tie(grad_branch, late)
    early = [second_half.advance(grad_branch), down_sums.advance(grad_branch)]
    grad_mixed = times_transpose(grad_branch, out_weight).astype(BF16)
    grad_pack = pack(value_heads, order, grad_mixed)
    later_hidden = tie(hidden_rows, grad_pack)
    arrived_grad = tie(exchange(grad_pack), early)

    def narrow_rows(share):
        return narrow_exchange(share.astype(BF16).reshape(NARROW, shard, -1))

    grad_pieces = attend_back(table, arrived, arrived_grad, group_heads, head_size)
    later_branch = tie(grad_branch, grad_pieces)
    out_terms = outer_sum(mixed, later_branch).astype(BF16)
    early = [second_half.advance(grad_pieces), down_sums.advance(grad_pieces)]
    first_rows = narrow_rows(tie(first_half.result(), arrived_grad))
    output = (middle + narrow_reduce(dot(later_hidden, down))[0]).astype(BF16)
    grad_pieces = tie(exchange_back(grad_pieces), early, first_rows, output, out_terms)
    projection_grad, norm_sums = unfinish(
        sizes, order, raw, grad_pieces, cosines, sines, norm_gains
    )
    first_terms = outer_sum(normed, projection_grad).astype(BF16)
    out_terms = out_terms.reshape(wide_count, shard, folds, -1).transpose(0, 2, 1, 3)
    norm_terms = jnp.sum(norm_sums.reshape(2, 8, head_size), axis=1)
    norm_terms = norm_terms.reshape(2, wide_count, NARROW, few).transpose(1, 2, 0, 3)
    norm_terms = norm_terms.reshape(wide_count, NARROW, 2 * few).astype(BF16)
    norm_terms = jnp.pad(
        norm_terms, ((0, 0), (0, extra - NARROW), (0, projection_width - 2 * few))
    )
    first_sums = Reduce(
        ring,
        first_terms,
        out_terms.reshape(-1, projection_width),
        norm_terms.reshape(-1, projection_width),
    )
    first_sums.advance()
    grad_normed, other, across = narrow_reduce(
        times_transpose(tie(projection_grad, first_terms), projection)
    )
    second = first_sums.advance(other)
    second_rows = narrow_rows(tie(second_half.result(), second))
    first_sums.advance()
    w_gate_grad, w_up_grad = merge_columns(block, first_rows, second_rows)
    first_sums.advance(second_rows, across)
    unused_first, first_pull = jax.vjp(lambda value: row_normalize(value, attention_gain), inputs)
    tokens_grad = (grad_middle + first_pull(grad_normed)[0]).astype(BF16)

    def all_columns(pieces):
        return pieces.astype(F32).transpose(1, 0, 2).reshape(shard, -1)

    share = first_sums.result().astype(BF16)
    out_share = share[NARROW * shard : (NARROW + folds) * shard].reshape(folds, shard, -1)
    out_share = out_share.transpose(1, 0, 2).reshape(shard, -1)
    w_out_grad = lax.ppermute(out_share, DEVICES, moves_back).astype(F32)
    norm_rows = share[(NARROW + folds) * shard :][:NARROW, None, :]
    norm_rows = jnp.pad(norm_rows, ((0, 0), (0, 15), (0, 0)))
    projection_rows = narrow_exchange(
        jnp.concatenate([share[: NARROW * shard].reshape(NARROW, shard, -1), norm_rows], axis=1)
    )
    norm_grads = jnp.sum(projection_rows[:, shard, : 2 * few].astype(F32), axis=0)
    projection_rows = projection_rows[:, :shard]
    w_query_grad = all_columns(projection_rows[:, :, :query_width])
    w_key_grad = all_columns(projection_rows[:, :, query_width : query_width + key_width])
    w_value_grad = all_columns(projection_rows[:, :, query_width + key_width :])
    w_down_grad = down_sums.result()

    def row_sums(pairs):
        total = 0.0
        for weight, grad in pairs:
            total = total + jnp.sum(weight.astype(F32) * grad, axis=1)
        return total

    attn_norm_grad = row_sums(
        [(w_query, w_query_grad), (key_weight, w_key_grad), (value_weight, w_value_grad)]
    ) / attn_norm.astype(F32)
    mlp_norm_grad = row_sums([(w_gate, w_gate_grad), (w_up, w_up_grad)]) / mlp_norm.astype(F32)
    return (
        output,
        tokens_grad,
        attn_norm_grad,
        w_query_grad,
        w_key_grad,
        w_value_grad,
        norm_grads[:few],
        norm_grads[few:],
        w_out_grad,
        mlp_norm_grad,
        w_gate_grad,
        w_up_grad,
        w_down_grad,
    )


def solution(mesh):
    rows = P(DEVICES, None)
    vector = P(DEVICES)
    in_specs = (
        (rows, rows, vector, rows, rows, rows, vector, vector, rows, vector, rows, rows, rows)
        + (P(),) * 4
    )
    out_specs = (
        (rows, rows, vector, rows, rows, rows, vector, vector, rows, vector, rows, rows, rows)
    )
    return jax.shard_map(body, mesh=mesh, in_specs=in_specs, out_specs=out_specs, check_vma=False)
```

time: 1090 us -> 984 us (0.903)
  starting transfers between devices: 193 us -> 123 us
  other arithmetic: 149 us -> 106 us
  Pallas kernels: 33.2 us -> 62.2 us
  local copies, waits for them, and re-layouts: 148 us -> 126 us
    ppermute x26 -> x31, waiting for transfers between devices: 24.2 us -> 93.2 us  [swap(): return lax.ppermute(value, 'narrow', [(i, i ^ bit) for i in range(NARROW)])]
    all_to_all x4 -> x0, starting transfers between devices: 34.9 us -> none  [the longest x2 26.4 us: narrow_rows(): lax.all_to_all(pieces, 'narrow', split_axis=0, concat_axis=0, tiled=True)]
    reshape x18 -> x6, local copies, waits for them, and re-layouts: 34 us -> 4.62 us  [the longest x1 4.51 us: body(): out_terms.reshape(wide_count, shard, folds, -1).transpose(0, 2, 1, 3)]
    pallas_call x0 -> x6, Pallas kernels: none -> 29 us  [the longest x4 22.9 us: by_rows(): pl.pallas_call(kernel, grid_spec=pltpu.PrefetchScalarGridSpec(num_scalar_...]
    ppermute x64, waiting for transfers between devices: 304 us -> 276 us  [send(): return lax.ppermute(value, 'wide', self.onward if forward else self.back)]
    ppermute x64, starting transfers between devices: 78.4 us -> 50.8 us  [send(): return lax.ppermute(value, 'wide', self.onward if forward else self.back)]
    reduce_sum x3 -> x1, other arithmetic: 26.1 us -> 0.37 us  [row_normalize(): values * lax.rsqrt(jnp.mean(values * values, axis=-1, keepdims=True) + EP...]
    convert_element_type x14 -> x6, other arithmetic: 30 us -> 7.78 us  [the longest x1 3.46 us: body(): output = (middle + narrow_reduce(dot(later_hidden, down))[0]).astype(BF16)]
  transfers between devices with their start and end apart: 103 -> 101, of which waited for: 41 -> 49; matrix products, arithmetic and copies ran while one was open for 22% -> 29% of each run, Pallas kernels for 3% -> 5%
where the time goes in v2:
time: 984 us; the launch traced here: 967 us
  waiting for transfers between devices  381 us (39%)
  local copies, waits for them, and re-layouts  126 us (13%)
  matrix products  126 us (13%)
  starting transfers between devices  123 us (12%)
  other arithmetic  106 us (11%)
  Pallas kernels  62.2 us (6%)
  between operations  42 us (4%)
    ppermute x64, waiting for transfers between devices, send(): return lax.ppermute(value, 'wide', self.onward if forward else self.back)  276 us
    ppermute x31, waiting for transfers between devices, swap(): return lax.ppermute(value, 'narrow', [(i, i ^ bit) for i in range(NARROW)])  93.2 us
    ppermute x64, starting transfers between devices, send(): return lax.ppermute(value, 'wide', self.onward if forward else self.back)  50.8 us
    ppermute x31, starting transfers between devices, swap(): return lax.ppermute(value, 'narrow', [(i, i ^ bit) for i in range(NARROW)])  47.8 us
    dot_general x7, matrix products, dot(): return jnp.dot(left, right, preferred_element_type=F32)  46.8 us
    dynamic_update_slice x35, local copies, waits for them, and re-layouts, put(): self.whole = lax.dynamic_update_slice(self.whole, value, (start, 0))  43 us
    dot_general x6, matrix products, times_transpose(): lax.dot_general(left_rows, matrix, CONTRACT_COLS, preferred_element_type=...  42.6 us
    dot_general x5, matrix products, outer_sum(): lax.dot_general(left_rows, right_rows, CONTRACT_ROWS, preferred_element_t...  36.9 us
  transfers between devices with their start and end apart: 101, of which 49 were waited for; matrix products, arithmetic and copies ran while one was open for 29% of the time, Pallas kernels for 5%

profile of v2, /device:TPU:9, one launch (start us, length us, event | category | flops | bytes accessed | tf_op | source)
XLA Modules:
  0.0 966.8 jit_solution(17024814601224513334)
XLA Ops:
  36.0 10.9 %collective-permute-done.5 = bf16[64,2048]{1,0:T(8,128)(2,1)S(1)} collective-permute-done((bf16[64,2048]{1,0:T(8,128)(2,1)}, bf16[64,2048]{1,0:T(8,128)(2,1)S(1)}, u32[]{:S(2)}, u32[]{:S(2)}) %collective-permute-start.5) | collective-permute-done | bytes 262176 | tf_op jit(solution)/shard_map/ppermute | solution.py:631
  55.9 10.2 %collective-permute-done = bf16[256,2048]{1,0:T(8,128)(2,1)S(1)} collective-permute-done((bf16[256,2048]{1,0:T(8,128)(2,1)S(1)}, bf16[256,2048]{1,0:T(8,128)(2,1)S(1)}, u32[]{:S(2)}, u32[]{:S(2)}) %collective-permute-start) | collective-permute-done | bytes 1048608 | tf_op jit(solution)/shard_map/ppermute | solution.py:176
  80.5 7.7 collective-permute-done.18
  98.9 10.2 %collective-permute-done.11 = bf16[416,1024]{1,0:T(8,128)(2,1)} collective-permute-done((bf16[416,1024]{1,0:T(8,128)(2,1)}, bf16[416,1024]{1,0:T(8,128)(2,1)}, u32[]{:S(2)}, u32[]{:S(2)}) %collective-permute-start.11) | collective-permute-done | bytes 852000 | tf_op jit(solution)/shard_map/ppermute | solution.py:68
  119.7 9.2 collective-permute-done.12
  132.6 6.1 collective-permute-done.14
  141.4 4.7 slice.432
  148.7 9.5 fusion.48.raw_ref
  158.2 7.0 finish.1
  167.2 4.9 all-to-all-start
  172.1 15.2 %collective-permute-done.23 = bf16[256,2048]{1,0:T(8,128)(2,1)} collective-permute-done((bf16[256,2048]{1,0:T(8,128)(2,1)}, bf16[256,2048]{1,0:T(8,128)(2,1)}, u32[]{:S(2)}, u32[]{:S(2)}) %collective-permute-start.23) | collective-permute-done | bytes 1048608 | tf_op jit(solution)/shard_map/ppermute | solution.py:176
  190.4 3.9 collective-permute-start.24
  203.6 30.5 %collective-permute-done.21 = bf16[256,1536]{1,0:T(8,128)(2,1)} collective-permute-done((bf16[256,1536]{1,0:T(8,128)(2,1)}, bf16[256,1536]{1,0:T(8,128)(2,1)}, u32[]{:S(2)}, u32[]{:S(2)}) %collective-permute-start.21) | collective-permute-done | bytes 786464 | tf_op jit(solution)/shard_map/ppermute | solution.py:68
  237.7 14.3 %attend.1 = bf16[2048,256]{1,0:T(8,128)(2,1)} custom-call(s32[3,16]{1,0:T(4,128)} %pad_add_fusion.table, bf16[2048,512]{1,0:T(8,128)(2,1)} %bitcast.223), custom_call_target="tpu_custom_call" | custom-call | tf_op jit(solution)/shard_map/attend/pallas_call | solution.py:314
  254.7 5.4 all-to-all-start.1
  267.3 31.6 %collective-permute-done.27 = bf16[192,2048]{1,0:T(8,128)(2,1)S(1)} collective-permute-done((bf16[192,2048]{1,0:T(8,128)(2,1)}, bf16[192,2048]{1,0:T(8,128)(2,1)S(1)}, u32[]{:S(2)}, u32[]{:S(2)}) %collective-permute-start.27) | collective-permute-done | bytes 786464 | tf_op jit(solution)/shard_map/ppermute | solution.py:68
  301.2 4.0 unpack.1
  305.3 4.3 convolution_convert_fusion.4
  312.2 3.8 collective-permute-done.29
  319.4 22.6 %collective-permute-done.30 = bf16[256,2048]{1,0:T(8,128)(2,1)} collective-permute-done((bf16[256,2048]{1,0:T(8,128)(2,1)}, bf16[256,2048]{1,0:T(8,128)(2,1)}, u32[]{:S(2)}, u32[]{:S(2)}) %collective-permute-start.30) | collective-permute-done | bytes 1048608 | tf_op jit(solution)/shard_map/ppermute | solution.py:176
  383.5 5.2 collective-permute-done.36
  403.9 5.1 fusion.19
  409.0 6.9 multiply_convert_fusion.3
  415.9 5.6 collective-permute-done.41
  424.3 7.7 fusion.5
  434.1 6.5 collective-permute-done.43
  441.0 8.9 convolution_convert_fusion.2
  454.5 4.1 collective-permute-done.46
  459.3 10.4 %fusion.57 = f32[1024,2048]{1,0:T(8,128)} fusion(bf16[1024,1536]{0,1:T(8,128)(2,1)} %pad_maximum_fusion.3, bf16[2048,1536]{1,0:T(8,128)(2,1)S(1)} %constant_dynamic-update-slice_fusion.18), kind=kOutput, calls=%fused_computation.335 | convolution fusion | flops 6442450944 | bytes 17825792 | tf_op jit(solution)/shard_map/dot_general | solution.py:44
  474.8 5.2 fusion.13
  480.0 6.7 multiply_convert_fusion.1
  488.7 7.2 fusion.8
  496.2 6.7 collective-permute-done.52
  506.3 9.2 add_convert_fusion
  520.7 8.2 collective-permute-start.55
  528.9 4.0 collective-permute-done.55
  538.7 7.1 convolution_convert_fusion.1
  550.2 7.5 convolution_convert_fusion
  563.1 4.6 collective-permute-done.59
  575.4 15.7 %collective-permute-done.62 = bf16[256,1536]{1,0:T(8,128)(2,1)S(1)} collective-permute-done((bf16[256,1536]{1,0:T(8,128)(2,1)S(1)}, bf16[256,1536]{1,0:T(8,128)(2,1)S(1)}, u32[]{:S(2)}, u32[]{:S(2)}) %collective-permute-start.62) | collective-permute-done | bytes 786464 | tf_op jit(solution)/shard_map/ppermute | solution.py:68
  608.8 13.3 %collective-permute-done.65 = bf16[192,2048]{1,0:T(8,128)(2,1)} collective-permute-done((bf16[192,2048]{1,0:T(8,128)(2,1)S(1)}, bf16[192,2048]{1,0:T(8,128)(2,1)}, u32[]{:S(2)}, u32[]{:S(2)}) %collective-permute-start.65) | collective-permute-done | bytes 786464 | tf_op jit(solution)/shard_map/ppermute | solution.py:68
  626.6 4.0 pack.1
  630.6 3.9 all-to-all-start.2
  642.2 9.1 convolution_convert_fusion.3
  655.7 19.5 %collective-permute-done.70 = bf16[256,1536]{1,0:T(8,128)(2,1)S(1)} collective-permute-done((bf16[256,1536]{1,0:T(8,128)(2,1)S(1)}, bf16[256,1536]{1,0:T(8,128)(2,1)S(1)}, u32[]{:S(2)}, u32[]{:S(2)}) %collective-permute-start.70) | collective-permute-done | bytes 786464 | tf_op jit(solution)/shard_map/ppermute | solution.py:68
  675.2 16.7 %collective-permute-done.72 = bf16[192,2048]{1,0:T(8,128)(2,1)S(1)} collective-permute-done((bf16[192,2048]{1,0:T(8,128)(2,1)S(1)}, bf16[192,2048]{1,0:T(8,128)(2,1)S(1)}, u32[]{:S(2)}, u32[]{:S(2)}) %collective-permute-start.72) | collective-permute-done | bytes 786464 | tf_op jit(solution)/shard_map/ppermute | solution.py:68
  693.9 18.9 %attend_back.1 = bf16[2048,512]{1,0:T(8,128)(2,1)} custom-call(s32[3,16]{1,0:T(4,128)} %pad_add_fusion.table, bf16[2048,512]{1,0:T(8,128)(2,1)} %bitcast.224, bf16[2048,256]{1,0:T(8,128)(2,1)} %bitcast.234), custom_call_target="tpu_custom_call" | custom-call | tf_op jit(solution)/shard_map/attend_back/pallas_call | solution.py:327
  714.7 4.9 all-to-all-start.3
  726.1 3.8 convolution_convert_fusion.7
  744.2 13.6 %collective-permute-done.68 = bf16[256,2048]{1,0:T(8,128)(2,1)} collective-permute-done((bf16[256,2048]{1,0:T(8,128)(2,1)}, bf16[256,2048]{1,0:T(8,128)(2,1)}, u32[]{:S(2)}, u32[]{:S(2)}) %collective-permute-start.68) | collective-permute-done | bytes 1048608 | tf_op jit(solution)/shard_map/ppermute | solution.py:176
  761.3 21.7 %collective-permute-done.74 = bf16[256,1536]{1,0:T(8,128)(2,1)} collective-permute-done((bf16[256,1536]{1,0:T(8,128)(2,1)}, bf16[256,1536]{1,0:T(8,128)(2,1)}, u32[]{:S(2)}, u32[]{:S(2)}) %collective-permute-start.74) | collective-permute-done | bytes 786464 | tf_op jit(solution)/shard_map/ppermute | solution.py:68
  783.0 16.8 %collective-permute-done.76 = bf16[192,2048]{1,0:T(8,128)(2,1)} collective-permute-done((bf16[192,2048]{1,0:T(8,128)(2,1)}, bf16[192,2048]{1,0:T(8,128)(2,1)}, u32[]{:S(2)}, u32[]{:S(2)}) %collective-permute-start.76) | collective-permute-done | bytes 786464 | tf_op jit(solution)/shard_map/ppermute | solution.py:68
  799.9 7.8 unfinish.1
  807.7 9.7 %convolution_convert_fusion.6 = bf16[2048,1024]{1,0:T(8,128)(2,1)} fusion(bf16[1024,1024]{1,0:T(8,128)(2,1)} %get-tuple-element.216, f32[2048]{0:T(1024)S(1)} %copy-done.89, f32[1024]{0:T(1024)S(1)} %copy-done.107, bf16[512,2048]{1,0:T(8,128)(2,1)} %collective-permute-done.1, bf16[256,2048]{1,0:T(8,128)(2,1)} %copy-done.26, bf16[256,2048]{1,0:T(8,128)(2,1)S(1)} %copy-done.5), kind=kOutput, calls=%fused_computation.28 | convolution fusion | flops 4315938816 | bytes 10498048 | tf_op jit(solution)/shard_map/dot_general | solution.py:40
  817.4 4.8 convolution_convert_fusion.5
  837.4 4.5 reshape.503
  848.9 3.9 constant_dynamic-slice_fusion.31
  858.5 5.5 collective-permute-done.83
  874.5 10.5 %collective-permute-done.86 = bf16[416,1024]{1,0:T(8,128)(2,1)S(1)} collective-permute-done((bf16[416,1024]{1,0:T(8,128)(2,1)S(1)}, bf16[416,1024]{1,0:T(8,128)(2,1)S(1)}, u32[]{:S(2)}, u32[]{:S(2)}) %collective-permute-start.86) | collective-permute-done | bytes 852000 | tf_op jit(solution)/shard_map/ppermute | solution.py:68
  897.2 7.6 collective-permute-done.90
  919.4 6.7 collective-permute-done.85
  931.2 4.7 fusion.25
  935.9 12.0 %collective-permute-done.92 = bf16[416,1024]{1,0:T(8,128)(2,1)S(1)} collective-permute-done((bf16[416,1024]{1,0:T(8,128)(2,1)S(1)}, bf16[416,1024]{1,0:T(8,128)(2,1)S(1)}, u32[]{:S(2)}, u32[]{:S(2)}) %collective-permute-start.92) | collective-permute-done | bytes 852000 | tf_op jit(solution)/shard_map/ppermute | solution.py:68
  957.1 4.4 collective-permute-done.94
  (641 shorter events, 338.0 us)
Async XLA Ops:
  0.6 47.8 %collective-permute-start.6 = (bf16[192,2048]{1,0:T(8,128)(2,1)}, bf16[192,2048]{1,0:T(8,128)(2,1)}, u32[]{:S(2)}, u32[]{:S(2)}) collective-permute-start(bf16[192,2048]{1,0:T(8,128)(2,1)} %param.40), channel_id=1, source_target_pairs={{0,8},{8,16},{16,24},{24,28},{28,20},{20,12},{12,4},{4,0},{1,9},{9... | collective-permute-start | bytes 2359304 | tf_op jit(solution)/shard_map/ppermute | solution.py:68
  2.0 46.5 %collective-permute-start.7 = (bf16[192,2048]{1,0:T(8,128)(2,1)}, bf16[192,2048]{1,0:T(8,128)(2,1)}, u32[]{:S(2)}, u32[]{:S(2)}) collective-permute-start(bf16[192,2048]{1,0:T(8,128)(2,1)} %param.40), channel_id=1, source_target_pairs={{8,0},{16,8},{24,16},{28,24},{20,28},{12,20},{4,12},{0,4},{9,1},{1... | collective-permute-start | bytes 2359304 | tf_op jit(solution)/shard_map/ppermute | solution.py:68
  9.1 17.8 %collective-permute-start.4 = (bf16[96,1024]{1,0:T(8,128)(2,1)S(1)}, bf16[96,1024]{1,0:T(8,128)(2,1)S(1)}, u32[]{:S(2)}, u32[]{:S(2)}) collective-permute-start(bf16[96,1024]{1,0:T(8,128)(2,1)S(1)} %get-tuple-element.307), channel_id=1, source_target_pairs={{0,3},{1,2},{2,1},{3,0},{4,7},{5,6},{6,5},{7,4},{8,11},{9,10},{10,... | collective-permute-start | bytes 589832 | tf_op jit(solution)/shard_map/ppermute | solution.py:176
  11.5 18.4 %collective-permute-start.3 = (bf16[96,1024]{1,0:T(8,128)(2,1)S(1)}, bf16[96,1024]{1,0:T(8,128)(2,1)S(1)}, u32[]{:S(2)}, u32[]{:S(2)}) collective-permute-start(bf16[96,1024]{1,0:T(8,128)(2,1)S(1)} %get-tuple-element.308), channel_id=1, source_target_pairs={{0,2},{1,3},{2,0},{3,1},{4,6},{5,7},{6,4},{7,5},{8,10},{9,11},{10,... | collective-permute-start | bytes 589832 | tf_op jit(solution)/shard_map/ppermute | solution.py:176
  11.8 19.6 %collective-permute-start.2 = (bf16[96,1024]{1,0:T(8,128)(2,1)S(1)}, bf16[96,1024]{1,0:T(8,128)(2,1)S(1)}, u32[]{:S(2)}, u32[]{:S(2)}) collective-permute-start(bf16[96,1024]{1,0:T(8,128)(2,1)S(1)} %get-tuple-element.309), channel_id=1, source_target_pairs={{0,1},{1,0},{2,3},{3,2},{4,5},{5,4},{6,7},{7,6},{8,9},{9,8},{10,11... | collective-permute-start | bytes 589832 | tf_op jit(solution)/shard_map/ppermute | solution.py:176
  26.9 20.1 %collective-permute-start.5 = (bf16[64,2048]{1,0:T(8,128)(2,1)}, bf16[64,2048]{1,0:T(8,128)(2,1)S(1)}, u32[]{:S(2)}, u32[]{:S(2)}) collective-permute-start(bf16[64,2048]{1,0:T(8,128)(2,1)} %param.36), channel_id=1, source_target_pairs={{0,0},{1,4},{2,8},{3,12},{4,16},{5,20},{6,24},{7,28},{8,1},{9,5},{... | collective-permute-start | bytes 786440 | tf_op jit(solution)/shard_map/ppermute | solution.py:631
  30.0 36.1 %collective-permute-start = (bf16[256,2048]{1,0:T(8,128)(2,1)S(1)}, bf16[256,2048]{1,0:T(8,128)(2,1)S(1)}, u32[]{:S(2)}, u32[]{:S(2)}) collective-permute-start(bf16[256,2048]{1,0:T(8,128)(2,1)S(1)} %copy-done.4), channel_id=1, source_target_pairs={{0,2},{1,3},{2,0},{3,1},{4,6},{5,7},{6,4},{7,5},{8,10},{9,11},{10,... | collective-permute-start | bytes 3145736 | tf_op jit(solution)/shard_map/ppermute | solution.py:176
  48.4 21.2 %collective-permute-start.8 = (bf16[416,1024]{1,0:T(8,128)(2,1)}, bf16[416,1024]{1,0:T(8,128)(2,1)S(1)}, u32[]{:S(2)}, u32[]{:S(2)}) collective-permute-start(bf16[416,1024]{1,0:T(8,128)(2,1)} %get-tuple-element.122), channel_id=1, source_target_pairs={{0,8},{8,16},{16,24},{24,28},{28,20},{20,12},{12,4},{4,0},{1,9},{9... | collective-permute-start | bytes 2555912 | tf_op jit(solution)/shard_map/ppermute | solution.py:68
  48.5 21.2 %collective-permute-start.9 = (bf16[416,1024]{1,0:T(8,128)(2,1)}, bf16[416,1024]{1,0:T(8,128)(2,1)}, u32[]{:S(2)}, u32[]{:S(2)}) collective-permute-start(bf16[416,1024]{1,0:T(8,128)(2,1)} %get-tuple-element.122), channel_id=1, source_target_pairs={{8,0},{16,8},{24,16},{28,24},{20,28},{12,20},{4,12},{0,4},{9,1},{1... | collective-permute-start | bytes 2555912 | tf_op jit(solution)/shard_map/ppermute | solution.py:68
  67.7 49.8 %collective-permute-start.1 = (bf16[512,2048]{1,0:T(8,128)(2,1)}, bf16[512,2048]{1,0:T(8,128)(2,1)}, u32[]{:S(2)}, u32[]{:S(2)}) collective-permute-start(bf16[512,2048]{1,0:T(8,128)(2,1)} %pad_maximum_fusion.5), channel_id=1, source_target_pairs={{0,1},{1,0},{2,3},{3,2},{4,5},{5,4},{6,7},{7,6},{8,9},{9,8},{10,11... | collective-permute-start | bytes 6291464 | tf_op jit(solution)/shard_map/ppermute | solution.py:176
  76.4 19.9 %collective-permute-start.17 = (bf16[64,3072]{1,0:T(8,128)(2,1)S(1)}, bf16[64,3072]{1,0:T(8,128)(2,1)S(1)}, u32[]{:S(2)}, u32[]{:S(2)}) collective-permute-start(bf16[64,3072]{1,0:T(8,128)(2,1)S(1)} %get-tuple-element.294), channel_id=1, source_target_pairs={{0,2},{1,3},{2,0},{3,1},{4,6},{5,7},{6,4},{7,5},{8,10},{9,11},{10,... | collective-permute-start | bytes 1179656 | tf_op jit(solution)/shard_map/ppermute | solution.py:176
  78.3 18.0 %collective-permute-start.16 = (bf16[64,3072]{1,0:T(8,128)(2,1)S(1)}, bf16[64,3072]{1,0:T(8,128)(2,1)S(1)}, u32[]{:S(2)}, u32[]{:S(2)}) collective-permute-start(bf16[64,3072]{1,0:T(8,128)(2,1)S(1)} %get-tuple-element.295), channel_id=1, source_target_pairs={{0,1},{1,0},{2,3},{3,2},{4,5},{5,4},{6,7},{7,6},{8,9},{9,8},{10,11... | collective-permute-start | bytes 1179656 | tf_op jit(solution)/shard_map/ppermute | solution.py:176
  78.5 20.4 %collective-permute-start.10 = (bf16[416,1024]{1,0:T(8,128)(2,1)S(1)}, bf16[416,1024]{1,0:T(8,128)(2,1)}, u32[]{:S(2)}, u32[]{:S(2)}) collective-permute-start(bf16[416,1024]{1,0:T(8,128)(2,1)S(1)} %collective-permute-done.8), channel_id=1, source_target_pairs={{0,8},{8,16},{16,24},{24,28},{28,20},{20,12},{12,4},{4,0},{1,9},{9... | collective-permute-start | bytes 2555912 | tf_op jit(solution)/shard_map/ppermute | solution.py:68
  88.2 20.8 %collective-permute-start.11 = (bf16[416,1024]{1,0:T(8,128)(2,1)}, bf16[416,1024]{1,0:T(8,128)(2,1)}, u32[]{:S(2)}, u32[]{:S(2)}) collective-permute-start(bf16[416,1024]{1,0:T(8,128)(2,1)} %collective-permute-done.9), channel_id=1, source_target_pairs={{8,0},{16,8},{24,16},{28,24},{20,28},{12,20},{4,12},{0,4},{9,1},{1... | collective-permute-start | bytes 2555912 | tf_op jit(solution)/shard_map/ppermute | solution.py:68
  109.0 19.9 %collective-permute-start.12 = (bf16[416,1024]{1,0:T(8,128)(2,1)}, bf16[416,1024]{1,0:T(8,128)(2,1)S(1)}, u32[]{:S(2)}, u32[]{:S(2)}) collective-permute-start(bf16[416,1024]{1,0:T(8,128)(2,1)} %collective-permute-done.10), channel_id=1, source_target_pairs={{0,8},{8,16},{16,24},{24,28},{28,20},{20,12},{12,4},{4,0},{1,9},{9... | collective-permute-start | bytes 2555912 | tf_op jit(solution)/shard_map/ppermute | solution.py:68
  109.2 20.4 %collective-permute-start.13 = (bf16[416,1024]{1,0:T(8,128)(2,1)}, bf16[416,1024]{1,0:T(8,128)(2,1)S(1)}, u32[]{:S(2)}, u32[]{:S(2)}) collective-permute-start(bf16[416,1024]{1,0:T(8,128)(2,1)} %collective-permute-done.11), channel_id=1, source_target_pairs={{8,0},{16,8},{24,16},{28,24},{20,28},{12,20},{4,12},{0,4},{9,1},{1... | collective-permute-start | bytes 2555912 | tf_op jit(solution)/shard_map/ppermute | solution.py:68
  146.3 20.0 %collective-permute-start.19 = (bf16[192,2048]{1,0:T(8,128)(2,1)}, bf16[192,2048]{1,0:T(8,128)(2,1)S(1)}, u32[]{:S(2)}, u32[]{:S(2)}) collective-permute-start(bf16[192,2048]{1,0:T(8,128)(2,1)} %collective-permute-done.6), channel_id=1, source_target_pairs={{0,8},{8,16},{16,24},{24,28},{28,20},{20,12},{12,4},{4,0},{1,9},{9... | collective-permute-start | bytes 2359304 | tf_op jit(solution)/shard_map/ppermute | solution.py:68
  147.9 18.4 %collective-permute-start.20 = (bf16[192,2048]{1,0:T(8,128)(2,1)}, bf16[192,2048]{1,0:T(8,128)(2,1)}, u32[]{:S(2)}, u32[]{:S(2)}) collective-permute-start(bf16[192,2048]{1,0:T(8,128)(2,1)} %collective-permute-done.7), channel_id=1, source_target_pairs={{8,0},{16,8},{24,16},{28,24},{20,28},{12,20},{4,12},{0,4},{9,1},{1... | collective-permute-start | bytes 2359304 | tf_op jit(solution)/shard_map/ppermute | solution.py:68
  165.2 22.0 %collective-permute-start.23 = (bf16[256,2048]{1,0:T(8,128)(2,1)}, bf16[256,2048]{1,0:T(8,128)(2,1)}, u32[]{:S(2)}, u32[]{:S(2)}) collective-permute-start(bf16[256,2048]{1,0:T(8,128)(2,1)} %param.29), channel_id=1, source_target_pairs={{0,2},{1,3},{2,0},{3,1},{4,6},{5,7},{6,4},{7,5},{8,10},{9,11},{10,... | collective-permute-start | bytes 3145736 | tf_op jit(solution)/shard_map/ppermute | solution.py:176
  167.2 66.9 %all-to-all-start = ((bf16[8,256,512]{2,1,0:T(8,128)(2,1)}), bf16[8,256,512]{2,1,0:T(8,128)(2,1)S(1)}, u32[]{:S(2)}, u32[]{:S(2)}) async-start(bf16[8,256,512]{2,1,0:T(8,128)(2,1)} %bitcast.226), calls=%async_computation | async-start | bytes 4194304 | tf_op jit(solution)/shard_map/all_to_all | solution.py:688
  197.8 36.3 %collective-permute-start.21 = (bf16[256,1536]{1,0:T(8,128)(2,1)}, bf16[256,1536]{1,0:T(8,128)(2,1)}, u32[]{:S(2)}, u32[]{:S(2)}) collective-permute-start(bf16[256,1536]{1,0:T(8,128)(2,1)} %get-tuple-element.152), channel_id=1, source_target_pairs={{0,8},{8,16},{16,24},{24,28},{28,20},{20,12},{12,4},{4,0},{1,9},{9... | collective-permute-start | bytes 2359304 | tf_op jit(solution)/shard_map/ppermute | solution.py:68
  199.2 34.9 %collective-permute-start.22 = (bf16[256,1536]{1,0:T(8,128)(2,1)}, bf16[256,1536]{1,0:T(8,128)(2,1)}, u32[]{:S(2)}, u32[]{:S(2)}) collective-permute-start(bf16[256,1536]{1,0:T(8,128)(2,1)} %get-tuple-element.152), channel_id=1, source_target_pairs={{8,0},{16,8},{24,16},{28,24},{20,28},{12,20},{4,12},{0,4},{9,1},{1... | collective-permute-start | bytes 2359304 | tf_op jit(solution)/shard_map/ppermute | solution.py:68
  234.1 18.6 %collective-permute-start.25 = (bf16[256,1536]{1,0:T(8,128)(2,1)}, bf16[256,1536]{1,0:T(8,128)(2,1)}, u32[]{:S(2)}, u32[]{:S(2)}) collective-permute-start(bf16[256,1536]{1,0:T(8,128)(2,1)} %collective-permute-done.21), channel_id=1, source_target_pairs={{0,8},{8,16},{16,24},{24,28},{28,20},{20,12},{12,4},{4,0},{1,9},{9... | collective-permute-start | bytes 2359304 | tf_op jit(solution)/shard_map/ppermute | solution.py:68
  236.4 18.3 %collective-permute-start.26 = (bf16[256,1536]{1,0:T(8,128)(2,1)}, bf16[256,1536]{1,0:T(8,128)(2,1)}, u32[]{:S(2)}, u32[]{:S(2)}) collective-permute-start(bf16[256,1536]{1,0:T(8,128)(2,1)} %collective-permute-done.22), channel_id=1, source_target_pairs={{8,0},{16,8},{24,16},{28,24},{20,28},{12,20},{4,12},{0,4},{9,1},{1... | collective-permute-start | bytes 2359304 | tf_op jit(solution)/shard_map/ppermute | solution.py:68
  254.7 45.6 %all-to-all-start.1 = ((bf16[8,256,256]{2,1,0:T(8,128)(2,1)}), bf16[8,256,256]{2,1,0:T(8,128)(2,1)S(1)}, u32[]{:S(2)}, u32[]{:S(2)}) async-start(bf16[8,256,256]{2,1,0:T(8,128)(2,1)} %bitcast.239), calls=%async_computation.1 | async-start | bytes 2097152 | tf_op jit(solution)/shard_map/all_to_all | solution.py:693
  260.0 38.9 %collective-permute-start.27 = (bf16[192,2048]{1,0:T(8,128)(2,1)}, bf16[192,2048]{1,0:T(8,128)(2,1)S(1)}, u32[]{:S(2)}, u32[]{:S(2)}) collective-permute-start(bf16[192,2048]{1,0:T(8,128)(2,1)} %copy-done.68), channel_id=1, source_target_pairs={{0,8},{8,16},{16,24},{24,28},{28,20},{20,12},{12,4},{4,0},{1,9},{9... | collective-permute-start | bytes 2359304 | tf_op jit(solution)/shard_map/ppermute | solution.py:68
  261.2 39.0 %collective-permute-start.28 = (bf16[192,2048]{1,0:T(8,128)(2,1)}, bf16[192,2048]{1,0:T(8,128)(2,1)}, u32[]{:S(2)}, u32[]{:S(2)}) collective-permute-start(bf16[192,2048]{1,0:T(8,128)(2,1)} %collective-permute-done.20), channel_id=1, source_target_pairs={{8,0},{16,8},{24,16},{28,24},{20,28},{12,20},{4,12},{0,4},{9,1},{1... | collective-permute-start | bytes 2359304 | tf_op jit(solution)/shard_map/ppermute | solution.py:68
  317.4 24.7 %collective-permute-start.30 = (bf16[256,2048]{1,0:T(8,128)(2,1)}, bf16[256,2048]{1,0:T(8,128)(2,1)}, u32[]{:S(2)}, u32[]{:S(2)}) collective-permute-start(bf16[256,2048]{1,0:T(8,128)(2,1)} %add_convert_fusion.5), channel_id=1, source_target_pairs={{0,2},{1,3},{2,0},{3,1},{4,6},{5,7},{6,4},{7,5},{8,10},{9,11},{10,... | collective-permute-start | bytes 3145736 | tf_op jit(solution)/shard_map/ppermute | solution.py:176
  317.5 26.6 %collective-permute-start.31 = (bf16[256,1536]{1,0:T(8,128)(2,1)}, bf16[256,1536]{1,0:T(8,128)(2,1)}, u32[]{:S(2)}, u32[]{:S(2)}) collective-permute-start(bf16[256,1536]{1,0:T(8,128)(2,1)} %collective-permute-done.25), channel_id=1, source_target_pairs={{0,8},{8,16},{16,24},{24,28},{28,20},{20,12},{12,4},{4,0},{1,9},{9... | collective-permute-start | bytes 2359304 | tf_op jit(solution)/shard_map/ppermute | solution.py:68
  318.1 26.1 %collective-permute-start.32 = (bf16[256,1536]{1,0:T(8,128)(2,1)}, bf16[256,1536]{1,0:T(8,128)(2,1)}, u32[]{:S(2)}, u32[]{:S(2)}) collective-permute-start(bf16[256,1536]{1,0:T(8,128)(2,1)} %collective-permute-done.26), channel_id=1, source_target_pairs={{8,0},{16,8},{24,16},{28,24},{20,28},{12,20},{4,12},{0,4},{9,1},{1... | collective-permute-start | bytes 2359304 | tf_op jit(solution)/shard_map/ppermute | solution.py:68
  360.3 28.3 %collective-permute-start.33 = (bf16[256,2048]{1,0:T(8,128)(2,1)S(1)}, bf16[256,2048]{1,0:T(8,128)(2,1)S(1)}, u32[]{:S(2)}, u32[]{:S(2)}) collective-permute-start(bf16[256,2048]{1,0:T(8,128)(2,1)S(1)} %multiply_convert_fusion.4), channel_id=1, source_target_pairs={{0,2},{1,3},{2,0},{3,1},{4,6},{5,7},{6,4},{7,5},{8,10},{9,11},{10,... | collective-permute-start | bytes 3145736 | tf_op jit(solution)/shard_map/ppermute | solution.py:176
  364.2 24.5 %collective-permute-start.36 = (bf16[256,1536]{1,0:T(8,128)(2,1)}, bf16[256,1536]{1,0:T(8,128)(2,1)S(1)}, u32[]{:S(2)}, u32[]{:S(2)}) collective-permute-start(bf16[256,1536]{1,0:T(8,128)(2,1)} %get-tuple-element.147), channel_id=1, source_target_pairs={{0,8},{8,16},{16,24},{24,28},{28,20},{20,12},{12,4},{4,0},{1,9},{9... | collective-permute-start | bytes 2359304 | tf_op jit(solution)/shard_map/ppermute | solution.py:68
  364.7 23.9 %collective-permute-start.37 = (bf16[256,1536]{1,0:T(8,128)(2,1)}, bf16[256,1536]{1,0:T(8,128)(2,1)}, u32[]{:S(2)}, u32[]{:S(2)}) collective-permute-start(bf16[256,1536]{1,0:T(8,128)(2,1)} %get-tuple-element.147), channel_id=1, source_target_pairs={{8,0},{16,8},{24,16},{28,24},{20,28},{12,20},{4,12},{0,4},{9,1},{1... | collective-permute-start | bytes 2359304 | tf_op jit(solution)/shard_map/ppermute | solution.py:68
  402.4 19.1 %collective-permute-start.41 = (bf16[256,1536]{1,0:T(8,128)(2,1)S(1)}, bf16[256,1536]{1,0:T(8,128)(2,1)S(1)}, u32[]{:S(2)}, u32[]{:S(2)}) collective-permute-start(bf16[256,1536]{1,0:T(8,128)(2,1)S(1)} %collective-permute-done.36), channel_id=1, source_target_pairs={{0,8},{8,16},{16,24},{24,28},{28,20},{20,12},{12,4},{4,0},{1,9},{9... | collective-permute-start | bytes 2359304 | tf_op jit(solution)/shard_map/ppermute | solution.py:68
  403.6 19.0 %collective-permute-start.42 = (bf16[256,1536]{1,0:T(8,128)(2,1)}, bf16[256,1536]{1,0:T(8,128)(2,1)S(1)}, u32[]{:S(2)}, u32[]{:S(2)}) collective-permute-start(bf16[256,1536]{1,0:T(8,128)(2,1)} %collective-permute-done.37), channel_id=1, source_target_pairs={{8,0},{16,8},{24,16},{28,24},{20,28},{12,20},{4,12},{0,4},{9,1},{1... | collective-permute-start | bytes 2359304 | tf_op jit(solution)/shard_map/ppermute | solution.py:68
  422.6 17.9 %collective-permute-start.43 = (bf16[256,1536]{1,0:T(8,128)(2,1)S(1)}, bf16[256,1536]{1,0:T(8,128)(2,1)S(1)}, u32[]{:S(2)}, u32[]{:S(2)}) collective-permute-start(bf16[256,1536]{1,0:T(8,128)(2,1)S(1)} %collective-permute-done.41), channel_id=1, source_target_pairs={{0,8},{8,16},{16,24},{24,28},{28,20},{20,12},{12,4},{4,0},{1,9},{9... | collective-permute-start | bytes 2359304 | tf_op jit(solution)/shard_map/ppermute | solution.py:68
  423.2 17.8 %collective-permute-start.44 = (bf16[256,1536]{1,0:T(8,128)(2,1)S(1)}, bf16[256,1536]{1,0:T(8,128)(2,1)S(1)}, u32[]{:S(2)}, u32[]{:S(2)}) collective-permute-start(bf16[256,1536]{1,0:T(8,128)(2,1)S(1)} %collective-permute-done.42), channel_id=1, source_target_pairs={{8,0},{16,8},{24,16},{28,24},{20,28},{12,20},{4,12},{0,4},{9,1},{1... | collective-permute-start | bytes 2359304 | tf_op jit(solution)/shard_map/ppermute | solution.py:68
  535.3 24.4 %collective-permute-start.56 = (bf16[256,2048]{1,0:T(8,128)(2,1)S(1)}, bf16[256,2048]{1,0:T(8,128)(2,1)S(1)}, u32[]{:S(2)}, u32[]{:S(2)}) collective-permute-start(bf16[256,2048]{1,0:T(8,128)(2,1)S(1)} %add_convert_fusion.4), channel_id=1, source_target_pairs={{0,2},{1,3},{2,0},{3,1},{4,6},{5,7},{6,4},{7,5},{8,10},{9,11},{10,... | collective-permute-start | bytes 3145736 | tf_op jit(solution)/shard_map/ppermute | solution.py:176
  571.7 23.4 %collective-permute-start.61 = (bf16[256,2048]{1,0:T(8,128)(2,1)S(1)}, bf16[256,2048]{1,0:T(8,128)(2,1)S(1)}, u32[]{:S(2)}, u32[]{:S(2)}) collective-permute-start(bf16[256,2048]{1,0:T(8,128)(2,1)S(1)} %fusion.46), channel_id=1, source_target_pairs={{0,2},{1,3},{2,0},{3,1},{4,6},{5,7},{6,4},{7,5},{8,10},{9,11},{10,... | collective-permute-start | bytes 3145736 | tf_op jit(solution)/shard_map/ppermute | solution.py:176
  573.6 17.5 %collective-permute-start.62 = (bf16[256,1536]{1,0:T(8,128)(2,1)S(1)}, bf16[256,1536]{1,0:T(8,128)(2,1)S(1)}, u32[]{:S(2)}, u32[]{:S(2)}) collective-permute-start(bf16[256,1536]{1,0:T(8,128)(2,1)S(1)} %pad_maximum_fusion.16), channel_id=1, source_target_pairs={{0,8},{8,16},{16,24},{24,28},{28,20},{20,12},{12,4},{4,0},{1,9},{9... | collective-permute-start | bytes 2359304 | tf_op jit(solution)/shard_map/ppermute | solution.py:68
  575.0 17.3 %collective-permute-start.63 = (bf16[256,1536]{1,0:T(8,128)(2,1)S(1)}, bf16[256,1536]{1,0:T(8,128)(2,1)S(1)}, u32[]{:S(2)}, u32[]{:S(2)}) collective-permute-start(bf16[256,1536]{1,0:T(8,128)(2,1)S(1)} %pad_maximum_fusion.17), channel_id=1, source_target_pairs={{8,0},{16,8},{24,16},{28,24},{20,28},{12,20},{4,12},{0,4},{9,1},{1... | collective-permute-start | bytes 2359304 | tf_op jit(solution)/shard_map/ppermute | solution.py:68
  602.9 19.3 %collective-permute-start.65 = (bf16[192,2048]{1,0:T(8,128)(2,1)S(1)}, bf16[192,2048]{1,0:T(8,128)(2,1)}, u32[]{:S(2)}, u32[]{:S(2)}) collective-permute-start(bf16[192,2048]{1,0:T(8,128)(2,1)S(1)} %pad_maximum_fusion.18), channel_id=1, source_target_pairs={{0,8},{8,16},{16,24},{24,28},{28,20},{20,12},{12,4},{4,0},{1,9},{9... | collective-permute-start | bytes 2359304 | tf_op jit(solution)/shard_map/ppermute | solution.py:68
  604.3 19.0 %collective-permute-start.66 = (bf16[192,2048]{1,0:T(8,128)(2,1)S(1)}, bf16[192,2048]{1,0:T(8,128)(2,1)}, u32[]{:S(2)}, u32[]{:S(2)}) collective-permute-start(bf16[192,2048]{1,0:T(8,128)(2,1)S(1)} %pad_maximum_fusion.19), channel_id=1, source_target_pairs={{8,0},{16,8},{24,16},{28,24},{20,28},{12,20},{4,12},{0,4},{9,1},{1... | collective-permute-start | bytes 2359304 | tf_op jit(solution)/shard_map/ppermute | solution.py:68
  630.6 62.3 %all-to-all-start.2 = ((bf16[8,256,256]{2,1,0:T(8,128)(2,1)}), bf16[8,256,256]{2,1,0:T(8,128)(2,1)S(1)}, u32[]{:S(2)}, u32[]{:S(2)}) async-start(bf16[8,256,256]{2,1,0:T(8,128)(2,1)} %bitcast.235), calls=%async_computation.2 | async-start | bytes 2097152 | tf_op jit(solution)/shard_map/all_to_all | solution.py:688
  636.8 38.5 %collective-permute-start.70 = (bf16[256,1536]{1,0:T(8,128)(2,1)S(1)}, bf16[256,1536]{1,0:T(8,128)(2,1)S(1)}, u32[]{:S(2)}, u32[]{:S(2)}) collective-permute-start(bf16[256,1536]{1,0:T(8,128)(2,1)S(1)} %get-tuple-element.243), channel_id=1, source_target_pairs={{8,0},{16,8},{24,16},{28,24},{20,28},{12,20},{4,12},{0,4},{9,1},{1... | collective-permute-start | bytes 2359304 | tf_op jit(solution)/shard_map/ppermute | solution.py:68
  636.8 38.4 %collective-permute-start.69 = (bf16[256,1536]{1,0:T(8,128)(2,1)S(1)}, bf16[256,1536]{1,0:T(8,128)(2,1)S(1)}, u32[]{:S(2)}, u32[]{:S(2)}) collective-permute-start(bf16[256,1536]{1,0:T(8,128)(2,1)S(1)} %get-tuple-element.244), channel_id=1, source_target_pairs={{0,8},{8,16},{16,24},{24,28},{28,20},{20,12},{12,4},{4,0},{1,9},{9... | collective-permute-start | bytes 2359304 | tf_op jit(solution)/shard_map/ppermute | solution.py:68
  640.7 51.3 %collective-permute-start.72 = (bf16[192,2048]{1,0:T(8,128)(2,1)S(1)}, bf16[192,2048]{1,0:T(8,128)(2,1)S(1)}, u32[]{:S(2)}, u32[]{:S(2)}) collective-permute-start(bf16[192,2048]{1,0:T(8,128)(2,1)S(1)} %get-tuple-element.241), channel_id=1, source_target_pairs={{8,0},{16,8},{24,16},{28,24},{20,28},{12,20},{4,12},{0,4},{9,1},{1... | collective-permute-start | bytes 2359304 | tf_op jit(solution)/shard_map/ppermute | solution.py:68
  640.8 52.1 %collective-permute-start.71 = (bf16[192,2048]{1,0:T(8,128)(2,1)S(1)}, bf16[192,2048]{1,0:T(8,128)(2,1)}, u32[]{:S(2)}, u32[]{:S(2)}) collective-permute-start(bf16[192,2048]{1,0:T(8,128)(2,1)S(1)} %get-tuple-element.242), channel_id=1, source_target_pairs={{0,8},{8,16},{16,24},{24,28},{28,20},{20,12},{12,4},{4,0},{1,9},{9... | collective-permute-start | bytes 2359304 | tf_op jit(solution)/shard_map/ppermute | solution.py:68
  652.9 76.9 %collective-permute-start.67 = (bf16[512,2048]{1,0:T(8,128)(2,1)}, bf16[512,2048]{1,0:T(8,128)(2,1)}, u32[]{:S(2)}, u32[]{:S(2)}) collective-permute-start(bf16[512,2048]{1,0:T(8,128)(2,1)} %slice.457), channel_id=1, source_target_pairs={{0,1},{1,0},{2,3},{3,2},{4,5},{5,4},{6,7},{7,6},{8,9},{9,8},{10,11... | collective-permute-start | bytes 6291464 | tf_op jit(solution)/shard_map/ppermute | solution.py:176
  714.7 85.2 %all-to-all-start.3 = ((bf16[8,256,512]{2,1,0:T(8,128)(2,1)}), bf16[8,256,512]{2,1,0:T(8,128)(2,1)}, u32[]{:S(2)}, u32[]{:S(2)}) async-start(bf16[8,256,512]{2,1,0:T(8,128)(2,1)} %bitcast.225), calls=%async_computation.3 | async-start | bytes 4194304 | tf_op jit(solution)/shard_map/all_to_all | solution.py:693
  719.8 17.4 %collective-permute-start.79 = (bf16[64,1536]{1,0:T(8,128)(2,1)S(1)}, bf16[64,1536]{1,0:T(8,128)(2,1)S(1)}, u32[]{:S(2)}, u32[]{:S(2)}) collective-permute-start(bf16[64,1536]{1,0:T(8,128)(2,1)S(1)} %get-tuple-element.303), channel_id=1, source_target_pairs={{0,3},{1,2},{2,1},{3,0},{4,7},{5,6},{6,5},{7,4},{8,11},{9,10},{10,... | collective-permute-start | bytes 589832 | tf_op jit(solution)/shard_map/ppermute | solution.py:176
  726.1 56.9 %collective-permute-start.74 = (bf16[256,1536]{1,0:T(8,128)(2,1)}, bf16[256,1536]{1,0:T(8,128)(2,1)}, u32[]{:S(2)}, u32[]{:S(2)}) collective-permute-start(bf16[256,1536]{1,0:T(8,128)(2,1)} %get-tuple-element.239), channel_id=1, source_target_pairs={{8,0},{16,8},{24,16},{28,24},{20,28},{12,20},{4,12},{0,4},{9,1},{1... | collective-permute-start | bytes 2359304 | tf_op jit(solution)/shard_map/ppermute | solution.py:68
  732.8 25.0 %collective-permute-start.68 = (bf16[256,2048]{1,0:T(8,128)(2,1)}, bf16[256,2048]{1,0:T(8,128)(2,1)}, u32[]{:S(2)}, u32[]{:S(2)}) collective-permute-start(bf16[256,2048]{1,0:T(8,128)(2,1)} %add_convert_fusion.3), channel_id=1, source_target_pairs={{0,2},{1,3},{2,0},{3,1},{4,6},{5,7},{6,4},{7,5},{8,10},{9,11},{10,... | collective-permute-start | bytes 3145736 | tf_op jit(solution)/shard_map/ppermute | solution.py:176
  737.3 45.8 %collective-permute-start.73 = (bf16[256,1536]{1,0:T(8,128)(2,1)}, bf16[256,1536]{1,0:T(8,128)(2,1)}, u32[]{:S(2)}, u32[]{:S(2)}) collective-permute-start(bf16[256,1536]{1,0:T(8,128)(2,1)} %get-tuple-element.240), channel_id=1, source_target_pairs={{0,8},{8,16},{16,24},{24,28},{28,20},{20,12},{12,4},{4,0},{1,9},{9... | collective-permute-start | bytes 2359304 | tf_op jit(solution)/shard_map/ppermute | solution.py:68
  738.7 61.2 %collective-permute-start.76 = (bf16[192,2048]{1,0:T(8,128)(2,1)}, bf16[192,2048]{1,0:T(8,128)(2,1)}, u32[]{:S(2)}, u32[]{:S(2)}) collective-permute-start(bf16[192,2048]{1,0:T(8,128)(2,1)} %get-tuple-element.237), channel_id=1, source_target_pairs={{8,0},{16,8},{24,16},{28,24},{20,28},{12,20},{4,12},{0,4},{9,1},{1... | collective-permute-start | bytes 2359304 | tf_op jit(solution)/shard_map/ppermute | solution.py:68
  738.7 61.2 %collective-permute-start.75 = (bf16[192,2048]{1,0:T(8,128)(2,1)}, bf16[192,2048]{1,0:T(8,128)(2,1)}, u32[]{:S(2)}, u32[]{:S(2)}) collective-permute-start(bf16[192,2048]{1,0:T(8,128)(2,1)} %get-tuple-element.238), channel_id=1, source_target_pairs={{0,8},{8,16},{16,24},{24,28},{28,20},{20,12},{12,4},{4,0},{1,9},{9... | collective-permute-start | bytes 2359304 | tf_op jit(solution)/shard_map/ppermute | solution.py:68
  825.7 38.3 %collective-permute-start.80 = (bf16[512,2048]{1,0:T(8,128)(2,1)}, bf16[512,2048]{1,0:T(8,128)(2,1)}, u32[]{:S(2)}, u32[]{:S(2)}) collective-permute-start(bf16[512,2048]{1,0:T(8,128)(2,1)} %slice.466), channel_id=1, source_target_pairs={{0,1},{1,0},{2,3},{3,2},{4,5},{5,4},{6,7},{7,6},{8,9},{9,8},{10,11... | collective-permute-start | bytes 6291464 | tf_op jit(solution)/shard_map/ppermute | solution.py:176
  865.4 19.5 %collective-permute-start.86 = (bf16[416,1024]{1,0:T(8,128)(2,1)S(1)}, bf16[416,1024]{1,0:T(8,128)(2,1)S(1)}, u32[]{:S(2)}, u32[]{:S(2)}) collective-permute-start(bf16[416,1024]{1,0:T(8,128)(2,1)S(1)} %pad_maximum_fusion.11), channel_id=1, source_target_pairs={{8,0},{16,8},{24,16},{28,24},{20,28},{12,20},{4,12},{0,4},{9,1},{1... | collective-permute-start | bytes 2555912 | tf_op jit(solution)/shard_map/ppermute | solution.py:68
  866.0 20.7 %collective-permute-start.84 = (bf16[416,1024]{1,0:T(8,128)(2,1)S(1)}, bf16[416,1024]{1,0:T(8,128)(2,1)}, u32[]{:S(2)}, u32[]{:S(2)}) collective-permute-start(bf16[416,1024]{1,0:T(8,128)(2,1)S(1)} %fusion.32), channel_id=1, source_target_pairs={{0,8},{8,16},{16,24},{24,28},{28,20},{20,12},{12,4},{4,0},{1,9},{9... | collective-permute-start | bytes 2555912 | tf_op jit(solution)/shard_map/ppermute | solution.py:68
  873.0 43.6 %collective-permute-start.81 = (bf16[256,2048]{1,0:T(8,128)(2,1)}, bf16[256,2048]{1,0:T(8,128)(2,1)}, u32[]{:S(2)}, u32[]{:S(2)}) collective-permute-start(bf16[256,2048]{1,0:T(8,128)(2,1)} %add_convert_fusion.1), channel_id=1, source_target_pairs={{0,2},{1,3},{2,0},{3,1},{4,6},{5,7},{6,4},{7,5},{8,10},{9,11},{10,... | collective-permute-start | bytes 3145736 | tf_op jit(solution)/shard_map/ppermute | solution.py:176
  886.2 33.2 %collective-permute-start.87 = (bf16[416,1024]{1,0:T(8,128)(2,1)}, bf16[416,1024]{1,0:T(8,128)(2,1)}, u32[]{:S(2)}, u32[]{:S(2)}) collective-permute-start(bf16[416,1024]{1,0:T(8,128)(2,1)} %add_convert_fusion.9), channel_id=1, source_target_pairs={{8,0},{16,8},{24,16},{28,24},{20,28},{12,20},{4,12},{0,4},{9,1},{1... | collective-permute-start | bytes 2555912 | tf_op jit(solution)/shard_map/ppermute | solution.py:68
  904.8 21.3 %collective-permute-start.85 = (bf16[416,1024]{1,0:T(8,128)(2,1)}, bf16[416,1024]{1,0:T(8,128)(2,1)}, u32[]{:S(2)}, u32[]{:S(2)}) collective-permute-start(bf16[416,1024]{1,0:T(8,128)(2,1)} %add_convert_fusion.10), channel_id=1, source_target_pairs={{0,8},{8,16},{16,24},{24,28},{28,20},{20,12},{12,4},{4,0},{1,9},{9... | collective-permute-start | bytes 2555912 | tf_op jit(solution)/shard_map/ppermute | solution.py:68
  927.7 20.2 %collective-permute-start.92 = (bf16[416,1024]{1,0:T(8,128)(2,1)S(1)}, bf16[416,1024]{1,0:T(8,128)(2,1)S(1)}, u32[]{:S(2)}, u32[]{:S(2)}) collective-permute-start(bf16[416,1024]{1,0:T(8,128)(2,1)S(1)} %add_convert_fusion.7), channel_id=1, source_target_pairs={{8,0},{16,8},{24,16},{28,24},{20,28},{12,20},{4,12},{0,4},{9,1},{1... | collective-permute-start | bytes 2555912 | tf_op jit(solution)/shard_map/ppermute | solution.py:68
  929.6 19.8 %collective-permute-start.91 = (bf16[416,1024]{1,0:T(8,128)(2,1)S(1)}, bf16[416,1024]{1,0:T(8,128)(2,1)S(1)}, u32[]{:S(2)}, u32[]{:S(2)}) collective-permute-start(bf16[416,1024]{1,0:T(8,128)(2,1)S(1)} %add_convert_fusion.8), channel_id=1, source_target_pairs={{0,8},{8,16},{16,24},{24,28},{28,20},{20,12},{12,4},{4,0},{1,9},{9... | collective-permute-start | bytes 2555912 | tf_op jit(solution)/shard_map/ppermute | solution.py:68
  (157 other events, 1825.3 us)

commit v3 on v2

--- a/solution.py
+++ b/solution.py
@@ -86,29 +86,20 @@
 
 
 class Gather:
-    def __init__(self, ring, part, later=False):
-        self.ring, self.rows, self.step, self.later = ring, part.shape[0], 0, later
-        self.ahead, self.behind, self.kept = part, part, []
+    def __init__(self, ring, part):
+        self.ring, self.rows, self.step, self.flight = ring, part.shape[0], 0, []
+        self.ahead, self.behind = part, part
         if ring.count > 8:
             self.whole = lax.all_gather(part, "wide", axis=0, tiled=True)
         else:
-            self.whole = blank((ring.count * self.rows, part.shape[1]), part.dtype)
-            self.put(part, 0, 0)
-
-    def put(self, value, shift, extra):
-        if self.later:
-            self.kept.append((value, shift, extra))
-        else:
-            start = self.ring.device(shift) * self.rows + extra
-            self.whole = lax.dynamic_update_slice(self.whole, value, (start, 0))
-
-    def assemble(self, *after):
-        if self.ring.count <= 8:
-            self.later, kept = False, self.kept
-            values = tie([value for value, shift, extra in kept], after)
-            for value, (unused_value, shift, extra) in zip(values, kept):
-                self.put(value, shift, extra)
-        return self.whole
+            self.whole = self.put(
+                blank((ring.count * self.rows, part.shape[1]), part.dtype), part, 0, 0
+            )
+
+    def put(self, whole, value, shift, extra):
+        return lax.dynamic_update_slice(
+            whole, value, (self.ring.device(shift) * self.rows + extra, 0)
+        )
 
     def advance(self, *after):
         ring, half = self.ring, self.rows // 2
@@ -120,17 +111,18 @@
         if last:
             ahead, behind = ahead[:half], behind[half:]
         self.ahead, self.behind = ring.send(ahead, True), ring.send(behind, False)
-        self.put(self.ahead, -self.step, 0)
-        self.put(self.behind, self.step, half if last else 0)
+        self.whole = self.put(self.whole, self.ahead, -self.step, 0)
+        self.whole = self.put(self.whole, self.behind, self.step, half if last else 0)
         return [self.ahead, self.behind]
 
 
 class Reduce:
-    def __init__(self, ring, *terms):
-        self.ring, self.terms, self.step = ring, terms, 0
-        self.rows = sum(term.shape[0] for term in terms) // ring.count
+    def __init__(self, ring, *terms, shared=None):
+        self.ring, self.terms, self.shared, self.step = ring, terms, shared, 0
         if ring.count > 8:
             parts = [term.reshape(ring.count, -1, term.shape[1]) for term in terms]
+            if shared is not None:
+                parts.append(jnp.broadcast_to(shared[None], (ring.count,) + shared.shape))
             whole = jnp.concatenate(parts, axis=1).reshape(-1, terms[0].shape[1])
             self.total = lax.psum_scatter(whole, "wide", scatter_dimension=0, tiled=True)
 
@@ -140,16 +132,19 @@
             rows = term.shape[0] // self.ring.count
             start = self.ring.device(shift) * rows
             parts.append(lax.dynamic_slice(term, (start, 0), (rows, term.shape[1])))
+        if self.shared is not None:
+            parts.append(self.shared)
         return parts[0] if len(parts) == 1 else jnp.concatenate(parts, axis=0)
 
     def advance(self, *after):
-        ring, half = self.ring, self.rows // 2
+        ring = self.ring
         if ring.count > 8:
             return []
         shift = ring.count // 2 - self.step
         if self.step:
             ahead, behind = tie((self.ahead, self.behind), after)
             mine, other = self.term(shift), self.term(-shift)
+            half = mine.shape[0] // 2
             if self.step == 1:
                 ahead = jnp.concatenate([join(mine[:half], ahead), mine[half:]], axis=0)
                 behind = jnp.concatenate([other[:half], join(other[half:], behind)], axis=0)
@@ -157,6 +152,7 @@
                 ahead, behind = join(mine, ahead), join(other, behind)
         else:
             far = tie(self.term(shift), after)
+            half = far.shape[0] // 2
             ahead, behind = far[:half], far[half:]
         self.step += 1
         self.ahead, self.behind = ring.send(ahead, True), ring.send(behind, False)
@@ -178,17 +174,16 @@
 
 def narrow_gather(value, across=None):
     across = swap(value, 2) if across is None else across
-    chips = jnp.concatenate([value, across], axis=0)
-    return jnp.concatenate([chips, swap(chips, 1)], axis=0), across
+    return jnp.concatenate([value, swap(value, 1), across, swap(across, 1)], axis=0), across
 
 
 def narrow_reduce(terms):
     rows = terms.shape[0] // NARROW
     low = terms.astype(BF16)
-    other = swap(low[2 * rows :], 1)
-    across = swap(join(low[rows : 2 * rows], other[rows:]), 2)
-    total = low[:rows].astype(F32) + other[:rows].astype(F32) + across.astype(F32)
-    return total, other, across
+    parts = [low[i * rows : (i + 1) * rows] for i in range(NARROW)]
+    near, far = swap(parts[1], 1), swap(parts[3], 1)
+    across = swap(join(parts[2], far), 2)
+    return parts[0].astype(F32) + near.astype(F32) + across.astype(F32), (near, far), across
 
 
 def layout(doc_blocks, doc_order, block_home, my_wide, block_count):
@@ -600,14 +595,13 @@
     shard = w_query.shape[0]
     parts = wide_count // (NARROW * value_heads)
 
-    order = me ^ jnp.array([0, 2, 1, 3], dtype=jnp.int32)
-    partner = me ^ jnp.arange(NARROW, dtype=jnp.int32)
+    order = me ^ jnp.arange(NARROW, dtype=jnp.int32)
     sizes = (value_heads, group_heads, head_size)
 
     def narrow_exchange(pieces):
-        pieces = jnp.take(pieces, partner, axis=0)
+        pieces = jnp.take(pieces, order, axis=0)
         moved = [pieces[0]] + [swap(pieces[i], i) for i in range(1, NARROW)]
-        return jnp.take(jnp.stack(moved), partner, axis=0)
+        return jnp.take(jnp.stack(moved), order, axis=0)
 
     def narrow_columns(weight):
         return weight.reshape(shard, NARROW, -1).transpose(1, 0, 2)
@@ -637,13 +631,13 @@
     )
     block = w_down.shape[0]
     first_ring = Gather(ring, first_part)
-    down_ring = Gather(ring, w_down, later=True)
+    down_ring = Gather(ring, w_down)
     begun = first_ring.advance(down_ring.advance())
-    first_ring.advance()
+    first_ring.advance(tokens_across)
     gate_part, up_part = tie((w_gate, w_up), begun)
     gate_up_pieces = split_columns(block, gate_part, up_part)
     gate_up_part = narrow_exchange(gate_up_pieces).reshape(NARROW * shard, -1)
-    first_ring.advance(tokens_across)
+    first_ring.advance()
     first_done = first_ring.advance()
     gathered = first_ring.whole.reshape(wide_count, -1, projection_width)
     projection = gathered[:, : NARROW * shard].reshape(-1, projection_width)
@@ -658,10 +652,7 @@
         [gain_rows[:, 2, :few].reshape(head_size), gain_rows[:, 3, :few].reshape(head_size)]
     )
     norm_gains = jnp.concatenate([norm_gains, jnp.zeros((6, head_size), F32)])
-    rings = [
-        Gather(ring, gate_up_part[:, :hidden], later=True),
-        Gather(ring, gate_up_part[:, hidden:]),
-    ]
+    rings = [Gather(ring, gate_up_part[:, :hidden]), Gather(ring, gate_up_part[:, hidden:])]
 
     inputs = tokens.astype(F32)
     all_inputs = narrow_gather(tokens, tokens_across)[0].astype(F32)
@@ -696,26 +687,25 @@
         return pieces.reshape(NARROW, value_heads, parts, rows, -1)[:, :, 0]
 
     finished = finish(sizes, order, raw, cosines, sines, norm_gains)
-    arrived = exchange(tie(finished, down_ring.advance(first_done, gate_up_part)))
+    arrived = exchange(tie(finished, down_ring.advance(first_done)))
     table = stream_table(
         my_wide // (wide_count // NARROW), owner_start, doc_blocks, doc_tail, block_home, block_count
     )
-    all_out_grad, unused_across = narrow_gather(tie(out_grad, finished))
-    arrived = tie(arrived, rings[0].advance(finished), all_out_grad)
+    arrived = tie(arrived, rings[0].advance(first_done), down_ring.advance(finished))
     attended = tie(attend(table, arrived, group_heads, head_size), rings[0].advance(arrived))
-    mixed = tie(exchange_back(attended), down_ring.advance(attended))
-    early = rings[0].advance(mixed)
-    mixed = unpack(order, mixed)
-
-    reduced, unused_other, across = narrow_reduce(dot(mixed, out_weight))
-    middle = inputs + tie(reduced, early)
-    normed_rows = row_normalize(middle, mlp_gain).astype(BF16)
-    early = [rings[0].advance(normed_rows), rings[1].advance(normed_rows)]
-    across = tie(swap(normed_rows, 2), early)
-    late = down_ring.advance(normed_rows)
-    normed_two, across = narrow_gather(normed_rows, across)
-    normed_two = tie(normed_two, late)
-    gate_up_first, down = rings[0].assemble(middle), down_ring.assemble(middle)
+    mixed = exchange_back(attended)
+    third = rings[0].advance(attended)
+    mixed = unpack(order, tie(mixed, down_ring.advance(attended)))
+
+    reduced, unused_near, across = narrow_reduce(dot(mixed, out_weight))
+    fourth = rings[0].advance(mixed)
+    middle = inputs + tie(reduced, third)
+    begun = rings[1].advance(across)
+    normed_two, across = narrow_gather(row_normalize(middle, mlp_gain).astype(BF16))
+    all_out_grad, unused_across = narrow_gather(tie(out_grad, mixed))
+    normed_two = tie(normed_two, fourth, all_out_grad)
+    second = rings[1].advance(across)
+    down = down_ring.whole
     part = hidden // 2
 
     def half_forward(rows, weights):
@@ -726,87 +716,74 @@
         unused_gated, pull = jax.vjp(gated, gate_sum, up_sum)
         return jnp.concatenate([grad.astype(BF16) for grad in pull(grad_hidden)], axis=1)
 
-    early = rings[1].advance(normed_two)
-    gate_sum, up_sum, hidden_first = half_forward(normed_two, gate_up_first)
-    wait_first = tie(all_out_grad, hidden_first, early)
-    early = rings[1].advance(hidden_first)
+    gate_sum, up_sum, hidden_first = half_forward(normed_two, rings[0].whole)
+    wait_first = tie(all_out_grad, hidden_first, second)
     grad_first = half_back(gate_sum, up_sum, times_transpose(wait_first, down[:part]))
-    grad_first = tie(grad_first, early)
-    early = rings[1].advance(grad_first)
-    first_half_terms = outer_sum(normed_two, grad_first).astype(BF16)
+    third = rings[1].advance(hidden_first)
+    first_half_terms = outer_sum(normed_two, tie(grad_first, third)).astype(BF16)
     first_half = Reduce(ring, first_half_terms)
-    grad_terms = times_transpose(tie(grad_first, first_half_terms, early), gate_up_first)
-    grad_terms = tie(grad_terms, first_half.advance())
-    early = first_half.advance(grad_terms)
-    gate_sum, up_sum, hidden_second = half_forward(tie(normed_two, grad_terms), rings[1].whole)
-    wait_second = tie(all_out_grad, hidden_second, early)
+    wait_second = tie(normed_two, first_half_terms, rings[1].advance(grad_first))
+    gate_sum, up_sum, hidden_second = half_forward(wait_second, rings[1].whole)
+    wait_second = tie(all_out_grad, hidden_second, first_half.advance())
+    grad_second = half_back(gate_sum, up_sum, times_transpose(wait_second, down[part:]))
     early = first_half.advance(hidden_second)
-    grad_second = half_back(gate_sum, up_sum, times_transpose(wait_second, down[part:]))
-    grad_second = tie(grad_second, early)
-    early = first_half.advance(grad_second)
-    grad_terms = (grad_terms + times_transpose(grad_second, rings[1].whole)).astype(BF16)
-    grad_normed_two, other, across = narrow_reduce(tie(grad_terms, early))
+    grad_first = tie(grad_first, grad_second)
+    grad_terms = (
+        times_transpose(grad_first, rings[0].whole) + times_transpose(grad_second, rings[1].whole)
+    ).astype(BF16)
+    grad_terms = tie(grad_terms, early)
+    grad_normed_two, near, across = narrow_reduce(grad_terms)
+    third = first_half.advance(grad_terms)
     later_grad, later_normed, hidden_rows = tie(
-        (grad_second, normed_two, (hidden_first, hidden_second)), other
+        (grad_second, normed_two, (hidden_first, hidden_second)), near
     )
     hidden_rows = jnp.concatenate(hidden_rows, axis=1)
+    second_half_terms = outer_sum(later_normed, later_grad).astype(BF16)
+    second_half = Reduce(ring, second_half_terms)
     down_terms = outer_sum(hidden_rows, all_out_grad).astype(BF16)
-    down_sums = Reduce(ring, down_terms)
-    second_half_terms = outer_sum(later_normed, tie(later_grad, down_terms)).astype(BF16)
-    second_half = Reduce(ring, second_half_terms)
-    early = [down_sums.advance(), second_half.advance()]
-    grad_normed_two = tie(grad_normed_two, early)
+    grad_normed_two = tie(grad_normed_two, third, second_half_terms, down_terms)
     unused_norm, second_pull = jax.vjp(lambda value: row_normalize(value, mlp_gain), middle)
     grad_middle = out_grad.astype(F32) + second_pull(grad_normed_two)[0]
 
-    branch_rows = grad_middle.astype(BF16)
-    early = second_half.advance(branch_rows)
-    late = down_sums.advance(branch_rows)
-    across = tie(swap(branch_rows, 2), early)
-    grad_branch, across = narrow_gather(branch_rows, across)
-    grad_branch = tie(grad_branch, late)
-    early = [second_half.advance(grad_branch), down_sums.advance(grad_branch)]
+    early = [first_half.advance(across), second_half.advance(across)]
+    grad_branch, across = narrow_gather(grad_middle.astype(BF16))
     grad_mixed = times_transpose(grad_branch, out_weight).astype(BF16)
-    grad_pack = pack(value_heads, order, grad_mixed)
-    later_hidden = tie(hidden_rows, grad_pack)
-    arrived_grad = tie(exchange(grad_pack), early)
+    grad_pack = tie(pack(value_heads, order, grad_mixed), early)
+    second = second_half.advance(across)
+    later_branch, later_hidden = tie((grad_branch, hidden_rows), grad_pack)
+    arrived_grad = exchange(grad_pack)
 
     def narrow_rows(share):
         return narrow_exchange(share.astype(BF16).reshape(NARROW, shard, -1))
 
+    last_sums = Reduce(ring, down_terms, outer_sum(mixed, later_branch).astype(BF16))
+    arrived_grad = tie(arrived_grad, second, last_sums.advance())
+    third = second_half.advance(arrived_grad)
     grad_pieces = attend_back(table, arrived, arrived_grad, group_heads, head_size)
-    later_branch = tie(grad_branch, grad_pieces)
-    out_terms = outer_sum(mixed, later_branch).astype(BF16)
-    early = [second_half.advance(grad_pieces), down_sums.advance(grad_pieces)]
+    grad_pieces = tie(grad_pieces, third)
     first_rows = narrow_rows(tie(first_half.result(), arrived_grad))
     output = (middle + narrow_reduce(dot(later_hidden, down))[0]).astype(BF16)
-    grad_pieces = tie(exchange_back(grad_pieces), early, first_rows, output, out_terms)
+    early = [second_half.advance(grad_pieces), last_sums.advance(grad_pieces)]
+    grad_pieces = tie(exchange_back(grad_pieces), early, first_rows, output)
     projection_grad, norm_sums = unfinish(
         sizes, order, raw, grad_pieces, cosines, sines, norm_gains
     )
+    third = last_sums.advance(grad_pieces)
     first_terms = outer_sum(normed, projection_grad).astype(BF16)
-    out_terms = out_terms.reshape(wide_count, shard, folds, -1).transpose(0, 2, 1, 3)
-    norm_terms = jnp.sum(norm_sums.reshape(2, 8, head_size), axis=1)
-    norm_terms = norm_terms.reshape(2, wide_count, NARROW, few).transpose(1, 2, 0, 3)
-    norm_terms = norm_terms.reshape(wide_count, NARROW, 2 * few).astype(BF16)
     norm_terms = jnp.pad(
-        norm_terms, ((0, 0), (0, extra - NARROW), (0, projection_width - 2 * few))
-    )
-    first_sums = Reduce(
-        ring,
-        first_terms,
-        out_terms.reshape(-1, projection_width),
-        norm_terms.reshape(-1, projection_width),
+        norm_sums.astype(BF16), ((0, extra - 16), (0, projection_width - head_size))
+    )
+    first_sums = Reduce(ring, first_terms, shared=norm_terms)
+    grad_normed, near, across = narrow_reduce(
+        times_transpose(tie(projection_grad, first_terms), projection)
     )
     first_sums.advance()
-    grad_normed, other, across = narrow_reduce(
-        times_transpose(tie(projection_grad, first_terms), projection)
-    )
-    second = first_sums.advance(other)
-    second_rows = narrow_rows(tie(second_half.result(), second))
-    first_sums.advance()
+    second_rows = narrow_rows(tie(second_half.result(), first_terms))
+    last_sums.advance(first_terms)
+    first_sums.advance(near)
+    first_sums.advance(across, third)
     w_gate_grad, w_up_grad = merge_columns(block, first_rows, second_rows)
-    first_sums.advance(second_rows, across)
+    first_sums.advance(second_rows)
     unused_first, first_pull = jax.vjp(lambda value: row_normalize(value, attention_gain), inputs)
     tokens_grad = (grad_middle + first_pull(grad_normed)[0]).astype(BF16)
 
@@ -814,20 +791,20 @@
         return pieces.astype(F32).transpose(1, 0, 2).reshape(shard, -1)
 
     share = first_sums.result().astype(BF16)
-    out_share = share[NARROW * shard : (NARROW + folds) * shard].reshape(folds, shard, -1)
-    out_share = out_share.transpose(1, 0, 2).reshape(shard, -1)
-    w_out_grad = lax.ppermute(out_share, DEVICES, moves_back).astype(F32)
-    norm_rows = share[(NARROW + folds) * shard :][:NARROW, None, :]
-    norm_rows = jnp.pad(norm_rows, ((0, 0), (0, 15), (0, 0)))
+    norm_rows = share[NARROW * shard :][:16]
+    norm_rows = jnp.broadcast_to(norm_rows[None], (NARROW,) + norm_rows.shape)
     projection_rows = narrow_exchange(
         jnp.concatenate([share[: NARROW * shard].reshape(NARROW, shard, -1), norm_rows], axis=1)
     )
-    norm_grads = jnp.sum(projection_rows[:, shard, : 2 * few].astype(F32), axis=0)
+    norm_grads = jnp.sum(projection_rows[:, shard:, :head_size].astype(F32), axis=0)
+    norm_grads = jnp.sum(norm_grads.reshape(2, 8, head_size), axis=1)
     projection_rows = projection_rows[:, :shard]
     w_query_grad = all_columns(projection_rows[:, :, :query_width])
     w_key_grad = all_columns(projection_rows[:, :, query_width : query_width + key_width])
     w_value_grad = all_columns(projection_rows[:, :, query_width + key_width :])
-    w_down_grad = down_sums.result()
+    last_share = last_sums.result()
+    w_down_grad = last_share[:block]
+    w_out_grad = lax.ppermute(last_share[block:].astype(BF16), DEVICES, moves_back).astype(F32)
 
     def row_sums(pairs):
         total = 0.0
@@ -839,6 +816,7 @@
         [(w_query, w_query_grad), (key_weight, w_key_grad), (value_weight, w_value_grad)]
     ) / attn_norm.astype(F32)
     mlp_norm_grad = row_sums([(w_gate, w_gate_grad), (w_up, w_up_grad)]) / mlp_norm.astype(F32)
+    mine = lax.dynamic_slice(norm_grads, (0, (my_wide * NARROW + me) * few), (2, few))
     return (
         output,
         tokens_grad,
@@ -846,8 +824,8 @@
         w_query_grad,
         w_key_grad,
         w_value_grad,
-        norm_grads[:few],
-        norm_grads[few:],
+        mine[0],
+        mine[1],
         w_out_grad,
         mlp_norm_grad,
         w_gate_grad,

time: 984 us -> 947 us (0.962)
  waiting for transfers between devices: 381 us -> 352 us
  starting transfers between devices: 123 us -> 137 us
    ppermute x31 -> x39, waiting for transfers between devices: 93.2 us -> 61.6 us  [swap(): return lax.ppermute(value, 'narrow', [(i, i ^ bit) for i in range(NARROW)])]
    unnamed x246 -> x203, local copies, waits for them, and re-layouts: 21.7 us -> 12.9 us
    ppermute x31 -> x39, starting transfers between devices: 47.8 us -> 56 us  [swap(): return lax.ppermute(value, 'narrow', [(i, i ^ bit) for i in range(NARROW)])]
    dynamic_update_slice x35 -> x34, local copies, waits for them, and re-layouts: 43 us -> 41.3 us  [put(): lax.dynamic_update_slice(whole, value, (self.ring.device(shift) * self.ro...]
    convert_element_type x19 -> x20, other arithmetic: 33.8 us -> 33.7 us  [join(): return (left.astype(F32) + right.astype(F32)).astype(BF16)]
  transfers between devices with their start and end apart: 101 -> 109, of which waited for: 49 -> 40; matrix products, arithmetic and copies ran while one was open for 29% -> 27% of each run, Pallas kernels for 5% -> 5%
where the time goes in v3:
time: 947 us; the launch traced here: 937 us
  waiting for transfers between devices  352 us (37%)
  starting transfers between devices  137 us (14%)
  matrix products  129 us (14%)
  local copies, waits for them, and re-layouts  119 us (13%)
  other arithmetic  99.4 us (10%)
  Pallas kernels  62.4 us (7%)
  between operations  37.2 us (4%)
    ppermute x64, waiting for transfers between devices, send(): return lax.ppermute(value, 'wide', self.onward if forward else self.back)  277 us
    ppermute x39, waiting for transfers between devices, swap(): return lax.ppermute(value, 'narrow', [(i, i ^ bit) for i in range(NARROW)])  61.6 us
    ppermute x39, starting transfers between devices, swap(): return lax.ppermute(value, 'narrow', [(i, i ^ bit) for i in range(NARROW)])  56 us
    ppermute x64, starting transfers between devices, send(): return lax.ppermute(value, 'wide', self.onward if forward else self.back)  51.2 us
    dot_general x6, matrix products, times_transpose(): lax.dot_general(left_rows, matrix, CONTRACT_COLS, preferred_element_type=...  50.3 us
    dot_general x7, matrix products, dot(): return jnp.dot(left, right, preferred_element_type=F32)  47.2 us
    dynamic_update_slice x34, local copies, waits for them, and re-layouts, put(): lax.dynamic_update_slice(whole, value, (self.ring.device(shift) * self.ro...  41.3 us
    convert_element_type x20, other arithmetic, join(): return (left.astype(F32) + right.astype(F32)).astype(BF16)  33.7 us
  transfers between devices with their start and end apart: 109, of which 40 were waited for; matrix products, arithmetic and copies ran while one was open for 27% of the time, Pallas kernels for 5%

profile of v3, /device:TPU:9, one launch (start us, length us, event | category | flops | bytes accessed | tf_op | source)
XLA Modules:
  0.0 937.3 jit_solution(13197744367908851352)
XLA Ops:
  30.8 13.7 %collective-permute-done.6 = bf16[64,2048]{1,0:T(8,128)(2,1)} collective-permute-done((bf16[64,2048]{1,0:T(8,128)(2,1)}, bf16[64,2048]{1,0:T(8,128)(2,1)}, u32[]{:S(2)}, u32[]{:S(2)}) %collective-permute-start.6) | collective-permute-done | bytes 262176 | tf_op jit(solution)/shard_map/ppermute | solution.py:625
  55.7 7.4 collective-permute-done.1
  63.4 5.4 collective-permute-done.9
  75.6 14.0 %collective-permute-done.11 = bf16[416,1024]{1,0:T(8,128)(2,1)} collective-permute-done((bf16[416,1024]{1,0:T(8,128)(2,1)S(1)}, bf16[416,1024]{1,0:T(8,128)(2,1)}, u32[]{:S(2)}, u32[]{:S(2)}) %collective-permute-start.11) | collective-permute-done | bytes 852000 | tf_op jit(solution)/shard_map/ppermute | solution.py:68
  101.5 7.4 collective-permute-done.13
  123.3 4.7 slice.421
  130.7 9.7 %fusion.30.raw_ref = f32[1024,1024]{1,0:T(8,128)} fusion(bf16[2048,1024]{1,0:T(8,128)(2,1)} %bitcast.217, f32[2048]{0:T(1024)S(1)} %mul.549, f32[1024]{0:T(1024)S(1)} %add_rsqrt_fusion, bf16[256,2048]{1,0:T(8,128)(2,1)} %collective-permute-done.2, bf16[256,2048]{1,0:T(8,128)(2,1)} %collective-permute-done.1, bf16[256,2048]{1,0:T(8,128)(2,1)} %collective-permute-done, ...), kind=kOutput, calls=%fused_computation.103 | convolution fusion | flops 4318035968 | bytes 12595200 | tf_op jit(solution)/shard_map/dot_general | solution.py:36
  140.3 7.0 finish.1
  147.3 6.3 all-to-all-start
  161.6 4.1 collective-permute-done.21
  165.7 11.0 %collective-permute-done.20 = bf16[64,3072]{1,0:T(8,128)(2,1)} collective-permute-done((bf16[64,3072]{1,0:T(8,128)(2,1)}, bf16[64,3072]{1,0:T(8,128)(2,1)}, u32[]{:S(2)}, u32[]{:S(2)}) %collective-permute-start.20) | collective-permute-done | bytes 393248 | tf_op jit(solution)/shard_map/ppermute | solution.py:172
  188.8 26.5 %collective-permute-done.22 = bf16[256,1536]{1,0:T(8,128)(2,1)} collective-permute-done((bf16[256,1536]{1,0:T(8,128)(2,1)}, bf16[256,1536]{1,0:T(8,128)(2,1)}, u32[]{:S(2)}, u32[]{:S(2)}) %collective-permute-start.22) | collective-permute-done | bytes 786464 | tf_op jit(solution)/shard_map/ppermute | solution.py:68
  215.3 16.8 %collective-permute-done.24 = bf16[192,2048]{1,0:T(8,128)(2,1)} collective-permute-done((bf16[192,2048]{1,0:T(8,128)(2,1)}, bf16[192,2048]{1,0:T(8,128)(2,1)}, u32[]{:S(2)}, u32[]{:S(2)}) %collective-permute-start.24) | collective-permute-done | bytes 786464 | tf_op jit(solution)/shard_map/ppermute | solution.py:68
  236.5 14.3 %attend.1 = bf16[2048,256]{1,0:T(8,128)(2,1)} custom-call(s32[3,16]{1,0:T(4,128)} %pad_add_fusion.table, bf16[2048,512]{1,0:T(8,128)(2,1)} %bitcast.207), custom_call_target="tpu_custom_call" | custom-call | tf_op jit(solution)/shard_map/attend/pallas_call | solution.py:309
  252.4 6.0 all-to-all-start.1
  290.3 4.0 unpack.1
  294.3 3.6 convolution_convert_fusion.4
  321.4 9.0 collective-permute-done.33
  333.8 4.5 collective-permute-done.32
  341.7 19.1 %collective-permute-done.36 = bf16[256,2048]{1,0:T(8,128)(2,1)S(1)} collective-permute-done((bf16[256,2048]{1,0:T(8,128)(2,1)S(1)}, bf16[256,2048]{1,0:T(8,128)(2,1)S(1)}, u32[]{:S(2)}, u32[]{:S(2)}) %collective-permute-start.36) | collective-permute-done | bytes 1048608 | tf_op jit(solution)/shard_map/ppermute | solution.py:172
  363.9 17.4 %collective-permute-done.43 = bf16[256,1536]{1,0:T(8,128)(2,1)S(1)} collective-permute-done((bf16[256,1536]{1,0:T(8,128)(2,1)S(1)}, bf16[256,1536]{1,0:T(8,128)(2,1)S(1)}, u32[]{:S(2)}, u32[]{:S(2)}) %collective-permute-start.43) | collective-permute-done | bytes 786464 | tf_op jit(solution)/shard_map/ppermute | solution.py:68
  387.1 14.4 %collective-permute-done.45 = bf16[256,1536]{1,0:T(8,128)(2,1)S(1)} collective-permute-done((bf16[256,1536]{1,0:T(8,128)(2,1)S(1)}, bf16[256,1536]{1,0:T(8,128)(2,1)S(1)}, u32[]{:S(2)}, u32[]{:S(2)}) %collective-permute-start.45) | collective-permute-done | bytes 786464 | tf_op jit(solution)/shard_map/ppermute | solution.py:68
  404.5 5.1 fusion.19
  409.6 6.8 multiply_convert_fusion.3
  418.1 9.3 fusion.5
  427.7 7.3 collective-permute-done.47
  438.6 7.3 convolution_convert_fusion.2
  450.8 5.2 fusion.13
  455.9 6.9 multiply_convert_fusion.1
  462.9 9.3 fusion.8
  472.2 8.9 fusion.47
  486.2 9.6 %add_convert_fusion = bf16[1024,2048]{1,0:T(8,128)(2,1)S(1)} fusion(f32[1024,2048]{1,0:T(8,128)} %fusion.47, bf16[1024,1536]{0,1:T(8,128)(2,1)S(1)} %copy-done.26, bf16[2048,1536]{1,0:T(8,128)(2,1)S(1)} %constant_dynamic-update-slice_fusion.18), kind=kOutput, calls=%fused_computation.16 | convolution fusion | flops 6446645248 | bytes 22020096 | tf_op jit(solution)/shard_map/dot_general | solution.py:44
  495.8 4.7 collective-permute-done.53
  502.9 4.3 collective-permute-start.55
  512.4 3.6 add_convert_fusion.16
  522.5 7.1 convolution_convert_fusion
  529.6 7.5 convolution_convert_fusion.1
  556.4 11.0 %collective-permute-done.64 = bf16[256,1536]{1,0:T(8,128)(2,1)S(1)} collective-permute-done((bf16[256,1536]{1,0:T(8,128)(2,1)S(1)}, bf16[256,1536]{1,0:T(8,128)(2,1)S(1)}, u32[]{:S(2)}, u32[]{:S(2)}) %collective-permute-start.64) | collective-permute-done | bytes 786464 | tf_op jit(solution)/shard_map/ppermute | solution.py:68
  570.4 4.0 collective-permute-start.62
  576.8 10.6 %collective-permute-done.65 = bf16[128,1536]{1,0:T(8,128)(2,1)S(1)} collective-permute-done((bf16[128,1536]{1,0:T(8,128)(2,1)S(1)}, bf16[128,1536]{1,0:T(8,128)(2,1)S(1)}, u32[]{:S(2)}, u32[]{:S(2)}) %collective-permute-start.65) | collective-permute-done | bytes 393248 | tf_op jit(solution)/shard_map/ppermute | solution.py:68
  592.9 6.0 convolution_convert_fusion.8.rows_ref
  598.9 4.0 pack.1
  602.9 3.7 pad_maximum_fusion.2
  606.6 5.6 all-to-all-start.2
  612.2 10.0 %convolution_convert_fusion.3 = bf16[1024,2048]{1,0:T(8,128)(2,1)S(1)} fusion(bf16[1024,1536]{0,1:T(8,128)(2,1)} %copy-done.70, bf16[1536,2048]{1,0:T(8,128)(2,1)} %constant_dynamic-update-slice_fusion.9), kind=kOutput, calls=%fused_computation.25 | convolution fusion | flops 6444548096 | bytes 13631488 | tf_op jit(solution)/shard_map/dot_general | solution.py:36
  627.8 3.7 collective-permute-start.68
  631.5 14.9 %collective-permute-done.73 = bf16[128,2048]{1,0:T(8,128)(2,1)} collective-permute-done((bf16[128,2048]{1,0:T(8,128)(2,1)S(1)}, bf16[128,2048]{1,0:T(8,128)(2,1)}, u32[]{:S(2)}, u32[]{:S(2)}) %collective-permute-start.73) | collective-permute-done | bytes 524320 | tf_op jit(solution)/shard_map/ppermute | solution.py:68
  656.0 4.0 collective-permute-start.82
  663.6 18.9 %attend_back.1 = bf16[2048,512]{1,0:T(8,128)(2,1)} custom-call(s32[3,16]{1,0:T(4,128)} %pad_add_fusion.table, bf16[2048,512]{1,0:T(8,128)(2,1)} %bitcast.208, bf16[2048,256]{1,0:T(8,128)(2,1)} %bitcast.83.grad_ref), custom_call_target="tpu_custom_call" | custom-call | tf_op jit(solution)/shard_map/attend_back/pallas_call | solution.py:322
  683.8 4.3 all-to-all-start.3
  703.4 4.5 collective-permute-done.69
  707.9 3.7 add_convert_fusion.6
  711.6 40.0 %collective-permute-done.77 = bf16[256,1536]{1,0:T(8,128)(2,1)S(1)} collective-permute-done((bf16[256,1536]{1,0:T(8,128)(2,1)S(1)}, bf16[256,1536]{1,0:T(8,128)(2,1)S(1)}, u32[]{:S(2)}, u32[]{:S(2)}) %collective-permute-start.77) | collective-permute-done | bytes 786464 | tf_op jit(solution)/shard_map/ppermute | solution.py:68
  753.9 20.2 %collective-permute-done.79 = bf16[256,2048]{1,0:T(8,128)(2,1)} collective-permute-done((bf16[256,2048]{1,0:T(8,128)(2,1)S(1)}, bf16[256,2048]{1,0:T(8,128)(2,1)}, u32[]{:S(2)}, u32[]{:S(2)}) %collective-permute-start.79) | collective-permute-done | bytes 1048608 | tf_op jit(solution)/shard_map/ppermute | solution.py:68
  774.1 8.0 unfinish.1
  782.1 7.5 convolution_convert_fusion.6
  797.4 7.1 convolution_convert_fusion.5
  819.8 4.5 collective-permute-done.95
  852.9 7.0 collective-permute-done.88
  863.4 31.8 %collective-permute-done.93 = bf16[288,1024]{1,0:T(8,128)(2,1)S(1)} collective-permute-done((bf16[288,1024]{1,0:T(8,128)(2,1)S(1)}, bf16[288,1024]{1,0:T(8,128)(2,1)S(1)}, u32[]{:S(2)}, u32[]{:S(2)}) %collective-permute-start.93) | collective-permute-done | bytes 589856 | tf_op jit(solution)/shard_map/ppermute | solution.py:68
  898.6 5.0 collective-permute-start.104
  913.8 9.9 %collective-permute-start.101 = (bf16[80,1024]{1,0:T(8,128)(2,1)S(1)}, bf16[80,1024]{1,0:T(8,128)(2,1)S(1)}, u32[]{:S(2)}, u32[]{:S(2)}) collective-permute-start(bf16[80,1024]{1,0:T(8,128)(2,1)S(1)} %get-tuple-element.280), channel_id=1, source_target_pairs={{0,3},{1,2},{2,1},{3,0},{4,7},{5,6},{6,5},{7,4},{8,11},{9,10},{10,... | collective-permute-start | bytes 491528 | tf_op jit(solution)/shard_map/ppermute | solution.py:172
  923.7 3.4 collective-permute-start.100
  927.1 5.0 fusion.25
  (612 shorter events, 312.8 us)
Async XLA Ops:
  8.6 19.6 %collective-permute-start.3 = (bf16[96,1024]{1,0:T(8,128)(2,1)S(1)}, bf16[96,1024]{1,0:T(8,128)(2,1)S(1)}, u32[]{:S(2)}, u32[]{:S(2)}) collective-permute-start(bf16[96,1024]{1,0:T(8,128)(2,1)S(1)} %get-tuple-element.276), channel_id=1, source_target_pairs={{0,1},{1,0},{2,3},{3,2},{4,5},{5,4},{6,7},{7,6},{8,9},{9,8},{10,11... | collective-permute-start | bytes 589832 | tf_op jit(solution)/shard_map/ppermute | solution.py:172
  8.8 38.1 %collective-permute-start.7 = (bf16[192,2048]{1,0:T(8,128)(2,1)S(1)}, bf16[192,2048]{1,0:T(8,128)(2,1)}, u32[]{:S(2)}, u32[]{:S(2)}) collective-permute-start(bf16[192,2048]{1,0:T(8,128)(2,1)S(1)} %copy-done.71), channel_id=1, source_target_pairs={{0,8},{8,16},{16,24},{24,28},{28,20},{20,12},{12,4},{4,0},{1,9},{9... | collective-permute-start | bytes 2359304 | tf_op jit(solution)/shard_map/ppermute | solution.py:68
  10.1 36.8 %collective-permute-start.8 = (bf16[192,2048]{1,0:T(8,128)(2,1)S(1)}, bf16[192,2048]{1,0:T(8,128)(2,1)}, u32[]{:S(2)}, u32[]{:S(2)}) collective-permute-start(bf16[192,2048]{1,0:T(8,128)(2,1)S(1)} %copy-done.71), channel_id=1, source_target_pairs={{8,0},{16,8},{24,16},{28,24},{20,28},{12,20},{4,12},{0,4},{9,1},{1... | collective-permute-start | bytes 2359304 | tf_op jit(solution)/shard_map/ppermute | solution.py:68
  23.8 20.7 %collective-permute-start.6 = (bf16[64,2048]{1,0:T(8,128)(2,1)}, bf16[64,2048]{1,0:T(8,128)(2,1)}, u32[]{:S(2)}, u32[]{:S(2)}) collective-permute-start(bf16[64,2048]{1,0:T(8,128)(2,1)} %param.35), channel_id=1, source_target_pairs={{0,0},{1,4},{2,8},{3,12},{4,16},{5,20},{6,24},{7,28},{8,1},{9,5},{... | collective-permute-start | bytes 786440 | tf_op jit(solution)/shard_map/ppermute | solution.py:625
  26.9 36.2 %collective-permute-start.1 = (bf16[256,2048]{1,0:T(8,128)(2,1)S(1)}, bf16[256,2048]{1,0:T(8,128)(2,1)}, u32[]{:S(2)}, u32[]{:S(2)}) collective-permute-start(bf16[256,2048]{1,0:T(8,128)(2,1)S(1)} %copy-done), channel_id=1, source_target_pairs={{0,2},{1,3},{2,0},{3,1},{4,6},{5,7},{6,4},{7,5},{8,10},{9,11},{10,... | collective-permute-start | bytes 3145736 | tf_op jit(solution)/shard_map/ppermute | solution.py:172
  46.9 21.9 %collective-permute-start.9 = (bf16[416,1024]{1,0:T(8,128)(2,1)}, bf16[416,1024]{1,0:T(8,128)(2,1)S(1)}, u32[]{:S(2)}, u32[]{:S(2)}) collective-permute-start(bf16[416,1024]{1,0:T(8,128)(2,1)} %get-tuple-element.103), channel_id=1, source_target_pairs={{0,8},{8,16},{16,24},{24,28},{28,20},{20,12},{12,4},{4,0},{1,9},{9... | collective-permute-start | bytes 2555912 | tf_op jit(solution)/shard_map/ppermute | solution.py:68
  46.9 21.9 %collective-permute-start.10 = (bf16[416,1024]{1,0:T(8,128)(2,1)}, bf16[416,1024]{1,0:T(8,128)(2,1)S(1)}, u32[]{:S(2)}, u32[]{:S(2)}) collective-permute-start(bf16[416,1024]{1,0:T(8,128)(2,1)} %get-tuple-element.103), channel_id=1, source_target_pairs={{8,0},{16,8},{24,16},{28,24},{20,28},{12,20},{4,12},{0,4},{9,1},{1... | collective-permute-start | bytes 2555912 | tf_op jit(solution)/shard_map/ppermute | solution.py:68
  49.3 49.8 %collective-permute-start = (bf16[256,2048]{1,0:T(8,128)(2,1)S(1)}, bf16[256,2048]{1,0:T(8,128)(2,1)}, u32[]{:S(2)}, u32[]{:S(2)}) collective-permute-start(bf16[256,2048]{1,0:T(8,128)(2,1)S(1)} %copy-done), channel_id=1, source_target_pairs={{0,1},{1,0},{2,3},{3,2},{4,5},{5,4},{6,7},{7,6},{8,9},{9,8},{10,11... | collective-permute-start | bytes 3145736 | tf_op jit(solution)/shard_map/ppermute | solution.py:172
  63.1 36.0 %collective-permute-start.2 = (bf16[256,2048]{1,0:T(8,128)(2,1)}, bf16[256,2048]{1,0:T(8,128)(2,1)}, u32[]{:S(2)}, u32[]{:S(2)}) collective-permute-start(bf16[256,2048]{1,0:T(8,128)(2,1)} %collective-permute-done.1), channel_id=1, source_target_pairs={{0,1},{1,0},{2,3},{3,2},{4,5},{5,4},{6,7},{7,6},{8,9},{9,8},{10,11... | collective-permute-start | bytes 3145736 | tf_op jit(solution)/shard_map/ppermute | solution.py:172
  69.5 20.1 %collective-permute-start.11 = (bf16[416,1024]{1,0:T(8,128)(2,1)S(1)}, bf16[416,1024]{1,0:T(8,128)(2,1)}, u32[]{:S(2)}, u32[]{:S(2)}) collective-permute-start(bf16[416,1024]{1,0:T(8,128)(2,1)S(1)} %collective-permute-done.9), channel_id=1, source_target_pairs={{0,8},{8,16},{16,24},{24,28},{28,20},{20,12},{12,4},{4,0},{1,9},{9... | collective-permute-start | bytes 2555912 | tf_op jit(solution)/shard_map/ppermute | solution.py:68
  70.2 20.7 %collective-permute-start.12 = (bf16[416,1024]{1,0:T(8,128)(2,1)S(1)}, bf16[416,1024]{1,0:T(8,128)(2,1)}, u32[]{:S(2)}, u32[]{:S(2)}) collective-permute-start(bf16[416,1024]{1,0:T(8,128)(2,1)S(1)} %collective-permute-done.10), channel_id=1, source_target_pairs={{8,0},{16,8},{24,16},{28,24},{20,28},{12,20},{4,12},{0,4},{9,1},{1... | collective-permute-start | bytes 2555912 | tf_op jit(solution)/shard_map/ppermute | solution.py:68
  90.9 20.8 %collective-permute-start.14 = (bf16[416,1024]{1,0:T(8,128)(2,1)}, bf16[416,1024]{1,0:T(8,128)(2,1)S(1)}, u32[]{:S(2)}, u32[]{:S(2)}) collective-permute-start(bf16[416,1024]{1,0:T(8,128)(2,1)} %collective-permute-done.12), channel_id=1, source_target_pairs={{8,0},{16,8},{24,16},{28,24},{20,28},{12,20},{4,12},{0,4},{9,1},{1... | collective-permute-start | bytes 2555912 | tf_op jit(solution)/shard_map/ppermute | solution.py:68
  147.3 84.8 %all-to-all-start = ((bf16[8,256,512]{2,1,0:T(8,128)(2,1)}), bf16[8,256,512]{2,1,0:T(8,128)(2,1)S(1)}, u32[]{:S(2)}, u32[]{:S(2)}) async-start(bf16[8,256,512]{2,1,0:T(8,128)(2,1)} %bitcast.209), calls=%async_computation | async-start | bytes 4194304 | tf_op jit(solution)/shard_map/all_to_all | solution.py:679
  185.9 29.4 %collective-permute-start.22 = (bf16[256,1536]{1,0:T(8,128)(2,1)}, bf16[256,1536]{1,0:T(8,128)(2,1)}, u32[]{:S(2)}, u32[]{:S(2)}) collective-permute-start(bf16[256,1536]{1,0:T(8,128)(2,1)} %get-tuple-element.113), channel_id=1, source_target_pairs={{0,8},{8,16},{16,24},{24,28},{28,20},{20,12},{12,4},{4,0},{1,9},{9... | collective-permute-start | bytes 2359304 | tf_op jit(solution)/shard_map/ppermute | solution.py:68
  187.0 28.3 %collective-permute-start.23 = (bf16[256,1536]{1,0:T(8,128)(2,1)}, bf16[256,1536]{1,0:T(8,128)(2,1)}, u32[]{:S(2)}, u32[]{:S(2)}) collective-permute-start(bf16[256,1536]{1,0:T(8,128)(2,1)} %get-tuple-element.113), channel_id=1, source_target_pairs={{8,0},{16,8},{24,16},{28,24},{20,28},{12,20},{4,12},{0,4},{9,1},{1... | collective-permute-start | bytes 2359304 | tf_op jit(solution)/shard_map/ppermute | solution.py:68
  187.4 44.8 %collective-permute-start.24 = (bf16[192,2048]{1,0:T(8,128)(2,1)}, bf16[192,2048]{1,0:T(8,128)(2,1)}, u32[]{:S(2)}, u32[]{:S(2)}) collective-permute-start(bf16[192,2048]{1,0:T(8,128)(2,1)} %collective-permute-done.17), channel_id=1, source_target_pairs={{0,8},{8,16},{16,24},{24,28},{28,20},{20,12},{12,4},{4,0},{1,9},{9... | collective-permute-start | bytes 2359304 | tf_op jit(solution)/shard_map/ppermute | solution.py:68
  188.5 43.7 %collective-permute-start.25 = (bf16[192,2048]{1,0:T(8,128)(2,1)}, bf16[192,2048]{1,0:T(8,128)(2,1)}, u32[]{:S(2)}, u32[]{:S(2)}) collective-permute-start(bf16[192,2048]{1,0:T(8,128)(2,1)} %collective-permute-done.18), channel_id=1, source_target_pairs={{8,0},{16,8},{24,16},{28,24},{20,28},{12,20},{4,12},{0,4},{9,1},{1... | collective-permute-start | bytes 2359304 | tf_op jit(solution)/shard_map/ppermute | solution.py:68
  252.4 37.8 %all-to-all-start.1 = ((bf16[8,256,256]{2,1,0:T(8,128)(2,1)}), bf16[8,256,256]{2,1,0:T(8,128)(2,1)}, u32[]{:S(2)}, u32[]{:S(2)}) async-start(bf16[8,256,256]{2,1,0:T(8,128)(2,1)} %bitcast.219), calls=%async_computation.1 | async-start | bytes 2097152 | tf_op jit(solution)/shard_map/all_to_all | solution.py:684
  311.1 21.1 %collective-permute-start.34 = (bf16[256,1536]{1,0:T(8,128)(2,1)}, bf16[256,1536]{1,0:T(8,128)(2,1)S(1)}, u32[]{:S(2)}, u32[]{:S(2)}) collective-permute-start(bf16[256,1536]{1,0:T(8,128)(2,1)} %collective-permute-done.27), channel_id=1, source_target_pairs={{8,0},{16,8},{24,16},{28,24},{20,28},{12,20},{4,12},{0,4},{9,1},{1... | collective-permute-start | bytes 2359304 | tf_op jit(solution)/shard_map/ppermute | solution.py:68
  312.5 19.8 %collective-permute-start.30 = (bf16[256,2048]{1,0:T(8,128)(2,1)S(1)}, bf16[256,2048]{1,0:T(8,128)(2,1)S(1)}, u32[]{:S(2)}, u32[]{:S(2)}) collective-permute-start(bf16[256,2048]{1,0:T(8,128)(2,1)S(1)} %get-tuple-element.243), channel_id=1, source_target_pairs={{0,1},{1,0},{2,3},{3,2},{4,5},{5,4},{6,7},{7,6},{8,9},{9,8},{10,11... | collective-permute-start | bytes 3145736 | tf_op jit(solution)/shard_map/ppermute | solution.py:172
  313.5 24.8 %collective-permute-start.32 = (bf16[256,2048]{1,0:T(8,128)(2,1)S(1)}, bf16[256,2048]{1,0:T(8,128)(2,1)S(1)}, u32[]{:S(2)}, u32[]{:S(2)}) collective-permute-start(bf16[256,2048]{1,0:T(8,128)(2,1)S(1)} %add_convert_fusion.9), channel_id=1, source_target_pairs={{0,2},{1,3},{2,0},{3,1},{4,6},{5,7},{6,4},{7,5},{8,10},{9,11},{10,... | collective-permute-start | bytes 3145736 | tf_op jit(solution)/shard_map/ppermute | solution.py:172
  331.3 29.5 %collective-permute-start.36 = (bf16[256,2048]{1,0:T(8,128)(2,1)S(1)}, bf16[256,2048]{1,0:T(8,128)(2,1)S(1)}, u32[]{:S(2)}, u32[]{:S(2)}) collective-permute-start(bf16[256,2048]{1,0:T(8,128)(2,1)S(1)} %copy-done.5), channel_id=1, source_target_pairs={{0,2},{1,3},{2,0},{3,1},{4,6},{5,7},{6,4},{7,5},{8,10},{9,11},{10,... | collective-permute-start | bytes 3145736 | tf_op jit(solution)/shard_map/ppermute | solution.py:172
  331.3 32.5 %collective-permute-start.35 = (bf16[256,2048]{1,0:T(8,128)(2,1)S(1)}, bf16[256,2048]{1,0:T(8,128)(2,1)S(1)}, u32[]{:S(2)}, u32[]{:S(2)}) collective-permute-start(bf16[256,2048]{1,0:T(8,128)(2,1)S(1)} %copy-done.5), channel_id=1, source_target_pairs={{0,1},{1,0},{2,3},{3,2},{4,5},{5,4},{6,7},{7,6},{8,9},{9,8},{10,11... | collective-permute-start | bytes 3145736 | tf_op jit(solution)/shard_map/ppermute | solution.py:172
  332.3 29.8 %collective-permute-start.42 = (bf16[128,1536]{1,0:T(8,128)(2,1)S(1)}, bf16[128,1536]{1,0:T(8,128)(2,1)S(1)}, u32[]{:S(2)}, u32[]{:S(2)}) collective-permute-start(bf16[128,1536]{1,0:T(8,128)(2,1)S(1)} %slice.321), channel_id=1, source_target_pairs={{8,0},{16,8},{24,16},{28,24},{20,28},{12,20},{4,12},{0,4},{9,1},{1... | collective-permute-start | bytes 1179656 | tf_op jit(solution)/shard_map/ppermute | solution.py:68
  332.3 29.8 %collective-permute-start.41 = (bf16[128,1536]{1,0:T(8,128)(2,1)S(1)}, bf16[128,1536]{1,0:T(8,128)(2,1)S(1)}, u32[]{:S(2)}, u32[]{:S(2)}) collective-permute-start(bf16[128,1536]{1,0:T(8,128)(2,1)S(1)} %slice.320), channel_id=1, source_target_pairs={{0,8},{8,16},{16,24},{24,28},{28,20},{20,12},{12,4},{4,0},{1,9},{9... | collective-permute-start | bytes 1179656 | tf_op jit(solution)/shard_map/ppermute | solution.py:68
  339.6 43.7 %collective-permute-start.39 = (bf16[256,2048]{1,0:T(8,128)(2,1)S(1)}, bf16[256,2048]{1,0:T(8,128)(2,1)S(1)}, u32[]{:S(2)}, u32[]{:S(2)}) collective-permute-start(bf16[256,2048]{1,0:T(8,128)(2,1)S(1)} %multiply_convert_fusion.4), channel_id=1, source_target_pairs={{0,2},{1,3},{2,0},{3,1},{4,6},{5,7},{6,4},{7,5},{8,10},{9,11},{10,... | collective-permute-start | bytes 3145736 | tf_op jit(solution)/shard_map/ppermute | solution.py:172
  360.8 26.0 %collective-permute-start.37 = (bf16[256,2048]{1,0:T(8,128)(2,1)S(1)}, bf16[256,2048]{1,0:T(8,128)(2,1)S(1)}, u32[]{:S(2)}, u32[]{:S(2)}) collective-permute-start(bf16[256,2048]{1,0:T(8,128)(2,1)S(1)} %collective-permute-done.36), channel_id=1, source_target_pairs={{0,1},{1,0},{2,3},{3,2},{4,5},{5,4},{6,7},{7,6},{8,9},{9,8},{10,11... | collective-permute-start | bytes 3145736 | tf_op jit(solution)/shard_map/ppermute | solution.py:172
  383.3 20.5 %collective-permute-start.38 = (bf16[256,2048]{1,0:T(8,128)(2,1)S(1)}, bf16[256,2048]{1,0:T(8,128)(2,1)S(1)}, u32[]{:S(2)}, u32[]{:S(2)}) collective-permute-start(bf16[256,2048]{1,0:T(8,128)(2,1)S(1)} %multiply_convert_fusion.4), channel_id=1, source_target_pairs={{0,1},{1,0},{2,3},{3,2},{4,5},{5,4},{6,7},{7,6},{8,9},{9,8},{10,11... | collective-permute-start | bytes 3145736 | tf_op jit(solution)/shard_map/ppermute | solution.py:172
  384.3 19.5 %collective-permute-start.46 = (bf16[256,1536]{1,0:T(8,128)(2,1)S(1)}, bf16[256,1536]{1,0:T(8,128)(2,1)S(1)}, u32[]{:S(2)}, u32[]{:S(2)}) collective-permute-start(bf16[256,1536]{1,0:T(8,128)(2,1)S(1)} %collective-permute-done.44), channel_id=1, source_target_pairs={{8,0},{16,8},{24,16},{28,24},{20,28},{12,20},{4,12},{0,4},{9,1},{1... | collective-permute-start | bytes 2359304 | tf_op jit(solution)/shard_map/ppermute | solution.py:68
  516.0 24.3 %collective-permute-start.59 = (bf16[256,1536]{1,0:T(8,128)(2,1)}, bf16[256,1536]{1,0:T(8,128)(2,1)}, u32[]{:S(2)}, u32[]{:S(2)}) collective-permute-start(bf16[256,1536]{1,0:T(8,128)(2,1)} %get-tuple-element.215), channel_id=1, source_target_pairs={{8,0},{16,8},{24,16},{28,24},{20,28},{12,20},{4,12},{0,4},{9,1},{1... | collective-permute-start | bytes 2359304 | tf_op jit(solution)/shard_map/ppermute | solution.py:68
  516.6 23.7 %collective-permute-start.58 = (bf16[256,1536]{1,0:T(8,128)(2,1)}, bf16[256,1536]{1,0:T(8,128)(2,1)}, u32[]{:S(2)}, u32[]{:S(2)}) collective-permute-start(bf16[256,1536]{1,0:T(8,128)(2,1)} %get-tuple-element.216), channel_id=1, source_target_pairs={{0,8},{8,16},{16,24},{24,28},{28,20},{20,12},{12,4},{4,0},{1,9},{9... | collective-permute-start | bytes 2359304 | tf_op jit(solution)/shard_map/ppermute | solution.py:68
  519.1 23.8 %collective-permute-start.57 = (bf16[256,2048]{1,0:T(8,128)(2,1)S(1)}, bf16[256,2048]{1,0:T(8,128)(2,1)S(1)}, u32[]{:S(2)}, u32[]{:S(2)}) collective-permute-start(bf16[256,2048]{1,0:T(8,128)(2,1)S(1)} %add_convert_fusion.8), channel_id=1, source_target_pairs={{0,2},{1,3},{2,0},{3,1},{4,6},{5,7},{6,4},{7,5},{8,10},{9,11},{10,... | collective-permute-start | bytes 3145736 | tf_op jit(solution)/shard_map/ppermute | solution.py:172
  547.5 22.9 %collective-permute-start.61 = (bf16[256,2048]{1,0:T(8,128)(2,1)S(1)}, bf16[256,2048]{1,0:T(8,128)(2,1)S(1)}, u32[]{:S(2)}, u32[]{:S(2)}) collective-permute-start(bf16[256,2048]{1,0:T(8,128)(2,1)S(1)} %fusion.48), channel_id=1, source_target_pairs={{0,2},{1,3},{2,0},{3,1},{4,6},{5,7},{6,4},{7,5},{8,10},{9,11},{10,... | collective-permute-start | bytes 3145736 | tf_op jit(solution)/shard_map/ppermute | solution.py:172
  552.7 78.8 %collective-permute-start.72 = (bf16[128,2048]{1,0:T(8,128)(2,1)}, bf16[128,2048]{1,0:T(8,128)(2,1)}, u32[]{:S(2)}, u32[]{:S(2)}) collective-permute-start(bf16[128,2048]{1,0:T(8,128)(2,1)} %get-tuple-element.204), channel_id=1, source_target_pairs={{0,8},{8,16},{16,24},{24,28},{28,20},{20,12},{12,4},{4,0},{1,9},{9... | collective-permute-start | bytes 1572872 | tf_op jit(solution)/shard_map/ppermute | solution.py:68
  553.6 37.3 %collective-permute-start.60 = (bf16[256,2048]{1,0:T(8,128)(2,1)S(1)}, bf16[256,2048]{1,0:T(8,128)(2,1)S(1)}, u32[]{:S(2)}, u32[]{:S(2)}) collective-permute-start(bf16[256,2048]{1,0:T(8,128)(2,1)S(1)} %fusion.48), channel_id=1, source_target_pairs={{0,1},{1,0},{2,3},{3,2},{4,5},{5,4},{6,7},{7,6},{8,9},{9,8},{10,11... | collective-permute-start | bytes 3145736 | tf_op jit(solution)/shard_map/ppermute | solution.py:172
  568.0 19.4 %collective-permute-start.65 = (bf16[128,1536]{1,0:T(8,128)(2,1)S(1)}, bf16[128,1536]{1,0:T(8,128)(2,1)S(1)}, u32[]{:S(2)}, u32[]{:S(2)}) collective-permute-start(bf16[128,1536]{1,0:T(8,128)(2,1)S(1)} %get-tuple-element.272), channel_id=1, source_target_pairs={{0,8},{8,16},{16,24},{24,28},{28,20},{20,12},{12,4},{4,0},{1,9},{9... | collective-permute-start | bytes 1179656 | tf_op jit(solution)/shard_map/ppermute | solution.py:68
  570.4 20.5 %collective-permute-start.62 = (bf16[256,2048]{1,0:T(8,128)(2,1)S(1)}, bf16[256,2048]{1,0:T(8,128)(2,1)S(1)}, u32[]{:S(2)}, u32[]{:S(2)}) collective-permute-start(bf16[256,2048]{1,0:T(8,128)(2,1)S(1)} %collective-permute-done.61), channel_id=1, source_target_pairs={{0,1},{1,0},{2,3},{3,2},{4,5},{5,4},{6,7},{7,6},{8,9},{9,8},{10,11... | collective-permute-start | bytes 3145736 | tf_op jit(solution)/shard_map/ppermute | solution.py:172
  588.5 43.0 %collective-permute-start.70 = (bf16[256,1536]{1,0:T(8,128)(2,1)}, bf16[256,1536]{1,0:T(8,128)(2,1)}, u32[]{:S(2)}, u32[]{:S(2)}) collective-permute-start(bf16[256,1536]{1,0:T(8,128)(2,1)} %pad_maximum_fusion.12), channel_id=1, source_target_pairs={{0,8},{8,16},{16,24},{24,28},{28,20},{20,12},{12,4},{4,0},{1,9},{9... | collective-permute-start | bytes 2359304 | tf_op jit(solution)/shard_map/ppermute | solution.py:68
  590.3 41.2 %collective-permute-start.71 = (bf16[256,1536]{1,0:T(8,128)(2,1)}, bf16[256,1536]{1,0:T(8,128)(2,1)}, u32[]{:S(2)}, u32[]{:S(2)}) collective-permute-start(bf16[256,1536]{1,0:T(8,128)(2,1)} %pad_maximum_fusion.13), channel_id=1, source_target_pairs={{8,0},{16,8},{24,16},{28,24},{20,28},{12,20},{4,12},{0,4},{9,1},{1... | collective-permute-start | bytes 2359304 | tf_op jit(solution)/shard_map/ppermute | solution.py:68
  606.6 39.8 %all-to-all-start.2 = ((bf16[8,256,256]{2,1,0:T(8,128)(2,1)}), bf16[8,256,256]{2,1,0:T(8,128)(2,1)}, u32[]{:S(2)}, u32[]{:S(2)}) async-start(bf16[8,256,256]{2,1,0:T(8,128)(2,1)} %bitcast.216), calls=%async_computation.2 | async-start | bytes 2097152 | tf_op jit(solution)/shard_map/all_to_all | solution.py:679
  626.3 20.1 %collective-permute-start.73 = (bf16[128,2048]{1,0:T(8,128)(2,1)S(1)}, bf16[128,2048]{1,0:T(8,128)(2,1)}, u32[]{:S(2)}, u32[]{:S(2)}) collective-permute-start(bf16[128,2048]{1,0:T(8,128)(2,1)S(1)} %pad_maximum_fusion.21), channel_id=1, source_target_pairs={{8,0},{16,8},{24,16},{28,24},{20,28},{12,20},{4,12},{0,4},{9,1},{1... | collective-permute-start | bytes 1572872 | tf_op jit(solution)/shard_map/ppermute | solution.py:68
  627.8 32.8 %collective-permute-start.68 = (bf16[256,2048]{1,0:T(8,128)(2,1)}, bf16[256,2048]{1,0:T(8,128)(2,1)}, u32[]{:S(2)}, u32[]{:S(2)}) collective-permute-start(bf16[256,2048]{1,0:T(8,128)(2,1)} %get-tuple-element.240), channel_id=1, source_target_pairs={{0,1},{1,0},{2,3},{3,2},{4,5},{5,4},{6,7},{7,6},{8,9},{9,8},{10,11... | collective-permute-start | bytes 3145736 | tf_op jit(solution)/shard_map/ppermute | solution.py:172
  652.4 30.1 %collective-permute-start.75 = (bf16[256,1536]{1,0:T(8,128)(2,1)}, bf16[256,1536]{1,0:T(8,128)(2,1)}, u32[]{:S(2)}, u32[]{:S(2)}) collective-permute-start(bf16[256,1536]{1,0:T(8,128)(2,1)} %get-tuple-element.207), channel_id=1, source_target_pairs={{8,0},{16,8},{24,16},{28,24},{20,28},{12,20},{4,12},{0,4},{9,1},{1... | collective-permute-start | bytes 2359304 | tf_op jit(solution)/shard_map/ppermute | solution.py:68
  652.4 30.6 %collective-permute-start.74 = (bf16[256,1536]{1,0:T(8,128)(2,1)}, bf16[256,1536]{1,0:T(8,128)(2,1)}, u32[]{:S(2)}, u32[]{:S(2)}) collective-permute-start(bf16[256,1536]{1,0:T(8,128)(2,1)} %get-tuple-element.208), channel_id=1, source_target_pairs={{0,8},{8,16},{16,24},{24,28},{28,20},{20,12},{12,4},{4,0},{1,9},{9... | collective-permute-start | bytes 2359304 | tf_op jit(solution)/shard_map/ppermute | solution.py:68
  656.0 32.1 %collective-permute-start.82 = (bf16[64,1536]{1,0:T(8,128)(2,1)}, bf16[64,1536]{1,0:T(8,128)(2,1)}, u32[]{:S(2)}, u32[]{:S(2)}) collective-permute-start(bf16[64,1536]{1,0:T(8,128)(2,1)} %get-tuple-element.268), channel_id=1, source_target_pairs={{0,3},{1,2},{2,1},{3,0},{4,7},{5,6},{6,5},{7,4},{8,11},{9,10},{10,... | collective-permute-start | bytes 589832 | tf_op jit(solution)/shard_map/ppermute | solution.py:172
  660.0 28.1 %collective-permute-start.81 = (bf16[64,1536]{1,0:T(8,128)(2,1)}, bf16[64,1536]{1,0:T(8,128)(2,1)}, u32[]{:S(2)}, u32[]{:S(2)}) collective-permute-start(bf16[64,1536]{1,0:T(8,128)(2,1)} %get-tuple-element.269), channel_id=1, source_target_pairs={{0,2},{1,3},{2,0},{3,1},{4,6},{5,7},{6,4},{7,5},{8,10},{9,11},{10,... | collective-permute-start | bytes 589832 | tf_op jit(solution)/shard_map/ppermute | solution.py:172
  660.7 27.5 %collective-permute-start.80 = (bf16[64,1536]{1,0:T(8,128)(2,1)}, bf16[64,1536]{1,0:T(8,128)(2,1)}, u32[]{:S(2)}, u32[]{:S(2)}) collective-permute-start(bf16[64,1536]{1,0:T(8,128)(2,1)} %get-tuple-element.270), channel_id=1, source_target_pairs={{0,1},{1,0},{2,3},{3,2},{4,5},{5,4},{6,7},{7,6},{8,9},{9,8},{10,11... | collective-permute-start | bytes 589832 | tf_op jit(solution)/shard_map/ppermute | solution.py:172
  682.5 19.5 %collective-permute-start.67 = (bf16[256,2048]{1,0:T(8,128)(2,1)}, bf16[256,2048]{1,0:T(8,128)(2,1)}, u32[]{:S(2)}, u32[]{:S(2)}) collective-permute-start(bf16[256,2048]{1,0:T(8,128)(2,1)} %get-tuple-element.239), channel_id=1, source_target_pairs={{0,1},{1,0},{2,3},{3,2},{4,5},{5,4},{6,7},{7,6},{8,9},{9,8},{10,11... | collective-permute-start | bytes 3145736 | tf_op jit(solution)/shard_map/ppermute | solution.py:172
  683.0 25.0 %collective-permute-start.69 = (bf16[256,2048]{1,0:T(8,128)(2,1)}, bf16[256,2048]{1,0:T(8,128)(2,1)}, u32[]{:S(2)}, u32[]{:S(2)}) collective-permute-start(bf16[256,2048]{1,0:T(8,128)(2,1)} %add_convert_fusion.7), channel_id=1, source_target_pairs={{0,2},{1,3},{2,0},{3,1},{4,6},{5,7},{6,4},{7,5},{8,10},{9,11},{10,... | collective-permute-start | bytes 3145736 | tf_op jit(solution)/shard_map/ppermute | solution.py:172
  683.8 90.3 %all-to-all-start.3 = ((bf16[8,256,512]{2,1,0:T(8,128)(2,1)}), bf16[8,256,512]{2,1,0:T(8,128)(2,1)}, u32[]{:S(2)}, u32[]{:S(2)}) async-start(bf16[8,256,512]{2,1,0:T(8,128)(2,1)} %bitcast.210), calls=%async_computation.3 | async-start | bytes 4194304 | tf_op jit(solution)/shard_map/all_to_all | solution.py:684
  697.5 54.1 %collective-permute-start.77 = (bf16[256,1536]{1,0:T(8,128)(2,1)S(1)}, bf16[256,1536]{1,0:T(8,128)(2,1)S(1)}, u32[]{:S(2)}, u32[]{:S(2)}) collective-permute-start(bf16[256,1536]{1,0:T(8,128)(2,1)S(1)} %get-tuple-element.205), channel_id=1, source_target_pairs={{8,0},{16,8},{24,16},{28,24},{20,28},{12,20},{4,12},{0,4},{9,1},{1... | collective-permute-start | bytes 2359304 | tf_op jit(solution)/shard_map/ppermute | solution.py:68
  697.6 54.0 %collective-permute-start.76 = (bf16[256,1536]{1,0:T(8,128)(2,1)S(1)}, bf16[256,1536]{1,0:T(8,128)(2,1)S(1)}, u32[]{:S(2)}, u32[]{:S(2)}) collective-permute-start(bf16[256,1536]{1,0:T(8,128)(2,1)S(1)} %get-tuple-element.206), channel_id=1, source_target_pairs={{0,8},{8,16},{16,24},{24,28},{28,20},{20,12},{12,4},{4,0},{1,9},{9... | collective-permute-start | bytes 2359304 | tf_op jit(solution)/shard_map/ppermute | solution.py:68
  700.3 73.7 %collective-permute-start.79 = (bf16[256,2048]{1,0:T(8,128)(2,1)S(1)}, bf16[256,2048]{1,0:T(8,128)(2,1)}, u32[]{:S(2)}, u32[]{:S(2)}) collective-permute-start(bf16[256,2048]{1,0:T(8,128)(2,1)S(1)} %pad_maximum_fusion.6), channel_id=1, source_target_pairs={{8,0},{16,8},{24,16},{28,24},{20,28},{12,20},{4,12},{0,4},{9,1},{1... | collective-permute-start | bytes 3145736 | tf_op jit(solution)/shard_map/ppermute | solution.py:68
  701.9 72.2 %collective-permute-start.78 = (bf16[256,2048]{1,0:T(8,128)(2,1)S(1)}, bf16[256,2048]{1,0:T(8,128)(2,1)}, u32[]{:S(2)}, u32[]{:S(2)}) collective-permute-start(bf16[256,2048]{1,0:T(8,128)(2,1)S(1)} %fusion.34), channel_id=1, source_target_pairs={{0,8},{8,16},{16,24},{24,28},{28,20},{20,12},{12,4},{4,0},{1,9},{9... | collective-permute-start | bytes 3145736 | tf_op jit(solution)/shard_map/ppermute | solution.py:68
  808.9 26.9 %collective-permute-start.91 = (bf16[256,2048]{1,0:T(8,128)(2,1)}, bf16[256,2048]{1,0:T(8,128)(2,1)}, u32[]{:S(2)}, u32[]{:S(2)}) collective-permute-start(bf16[256,2048]{1,0:T(8,128)(2,1)} %add_convert_fusion.3), channel_id=1, source_target_pairs={{8,0},{16,8},{24,16},{28,24},{20,28},{12,20},{4,12},{0,4},{9,1},{1... | collective-permute-start | bytes 3145736 | tf_op jit(solution)/shard_map/ppermute | solution.py:68
  811.5 24.5 %collective-permute-start.90 = (bf16[256,2048]{1,0:T(8,128)(2,1)}, bf16[256,2048]{1,0:T(8,128)(2,1)}, u32[]{:S(2)}, u32[]{:S(2)}) collective-permute-start(bf16[256,2048]{1,0:T(8,128)(2,1)} %add_convert_fusion.4), channel_id=1, source_target_pairs={{0,8},{8,16},{16,24},{24,28},{28,20},{20,12},{12,4},{4,0},{1,9},{9... | collective-permute-start | bytes 3145736 | tf_op jit(solution)/shard_map/ppermute | solution.py:68
  814.8 21.2 %collective-permute-start.84 = (bf16[256,2048]{1,0:T(8,128)(2,1)}, bf16[256,2048]{1,0:T(8,128)(2,1)}, u32[]{:S(2)}, u32[]{:S(2)}) collective-permute-start(bf16[256,2048]{1,0:T(8,128)(2,1)} %get-tuple-element.238), channel_id=1, source_target_pairs={{0,1},{1,0},{2,3},{3,2},{4,5},{5,4},{6,7},{7,6},{8,9},{9,8},{10,11... | collective-permute-start | bytes 3145736 | tf_op jit(solution)/shard_map/ppermute | solution.py:172
  838.0 22.2 %collective-permute-start.85 = (bf16[256,2048]{1,0:T(8,128)(2,1)S(1)}, bf16[256,2048]{1,0:T(8,128)(2,1)S(1)}, u32[]{:S(2)}, u32[]{:S(2)}) collective-permute-start(bf16[256,2048]{1,0:T(8,128)(2,1)S(1)} %add_convert_fusion.5), channel_id=1, source_target_pairs={{0,2},{1,3},{2,0},{3,1},{4,6},{5,7},{6,4},{7,5},{8,10},{9,11},{10,... | collective-permute-start | bytes 3145736 | tf_op jit(solution)/shard_map/ppermute | solution.py:172
  849.6 47.7 %collective-permute-start.103 = (bf16[256,2048]{1,0:T(8,128)(2,1)S(1)}, bf16[256,2048]{1,0:T(8,128)(2,1)S(1)}, u32[]{:S(2)}, u32[]{:S(2)}) collective-permute-start(bf16[256,2048]{1,0:T(8,128)(2,1)S(1)} %add_convert_fusion.1), channel_id=1, source_target_pairs={{8,0},{16,8},{24,16},{28,24},{20,28},{12,20},{4,12},{0,4},{9,1},{1... | collective-permute-start | bytes 3145736 | tf_op jit(solution)/shard_map/ppermute | solution.py:68
  851.6 45.7 %collective-permute-start.102 = (bf16[256,2048]{1,0:T(8,128)(2,1)S(1)}, bf16[256,2048]{1,0:T(8,128)(2,1)S(1)}, u32[]{:S(2)}, u32[]{:S(2)}) collective-permute-start(bf16[256,2048]{1,0:T(8,128)(2,1)S(1)} %add_convert_fusion.2), channel_id=1, source_target_pairs={{0,8},{8,16},{16,24},{24,28},{28,20},{20,12},{12,4},{4,0},{1,9},{9... | collective-permute-start | bytes 3145736 | tf_op jit(solution)/shard_map/ppermute | solution.py:68
  860.8 34.4 %collective-permute-start.93 = (bf16[288,1024]{1,0:T(8,128)(2,1)S(1)}, bf16[288,1024]{1,0:T(8,128)(2,1)S(1)}, u32[]{:S(2)}, u32[]{:S(2)}) collective-permute-start(bf16[288,1024]{1,0:T(8,128)(2,1)S(1)} %get-tuple-element.290), channel_id=1, source_target_pairs={{8,0},{16,8},{24,16},{28,24},{20,28},{12,20},{4,12},{0,4},{9,1},{1... | collective-permute-start | bytes 1769480 | tf_op jit(solution)/shard_map/ppermute | solution.py:68
  862.1 33.1 %collective-permute-start.92 = (bf16[288,1024]{1,0:T(8,128)(2,1)S(1)}, bf16[288,1024]{1,0:T(8,128)(2,1)S(1)}, u32[]{:S(2)}, u32[]{:S(2)}) collective-permute-start(bf16[288,1024]{1,0:T(8,128)(2,1)S(1)} %get-tuple-element.291), channel_id=1, source_target_pairs={{0,8},{8,16},{16,24},{24,28},{28,20},{20,12},{12,4},{4,0},{1,9},{9... | collective-permute-start | bytes 1769480 | tf_op jit(solution)/shard_map/ppermute | solution.py:68
  898.6 34.8 %collective-permute-start.104 = (bf16[64,2048]{1,0:T(8,128)(2,1)}, bf16[64,2048]{1,0:T(8,128)(2,1)S(1)}, u32[]{:S(2)}, u32[]{:S(2)}) collective-permute-start(bf16[64,2048]{1,0:T(8,128)(2,1)} %slice.527), channel_id=1, source_target_pairs={{0,0},{4,1},{8,2},{12,3},{16,4},{20,5},{24,6},{28,7},{1,8},{5,9},{... | collective-permute-start | bytes 786440 | tf_op jit(solution)/shard_map/ppermute | solution.py:807
  913.8 20.4 %collective-permute-start.101 = (bf16[80,1024]{1,0:T(8,128)(2,1)S(1)}, bf16[80,1024]{1,0:T(8,128)(2,1)S(1)}, u32[]{:S(2)}, u32[]{:S(2)}) collective-permute-start(bf16[80,1024]{1,0:T(8,128)(2,1)S(1)} %get-tuple-element.280), channel_id=1, source_target_pairs={{0,3},{1,2},{2,1},{3,0},{4,7},{5,6},{6,5},{7,4},{8,11},{9,10},{10,... | collective-permute-start | bytes 491528 | tf_op jit(solution)/shard_map/ppermute | solution.py:172
  (144 other events, 2196.2 us)

commit v4 on v3

--- a/solution.py
+++ b/solution.py
@@ -726,7 +726,8 @@
     gate_sum, up_sum, hidden_second = half_forward(wait_second, rings[1].whole)
     wait_second = tie(all_out_grad, hidden_second, first_half.advance())
     grad_second = half_back(gate_sum, up_sum, times_transpose(wait_second, down[part:]))
-    early = first_half.advance(hidden_second)
+    grad_second = tie(grad_second, first_half.advance(hidden_second))
+    early = first_half.advance(grad_second)
     grad_first = tie(grad_first, grad_second)
     grad_terms = (
         times_transpose(grad_first, rings[0].whole) + times_transpose(grad_second, rings[1].whole)
@@ -745,11 +746,11 @@
     unused_norm, second_pull = jax.vjp(lambda value: row_normalize(value, mlp_gain), middle)
     grad_middle = out_grad.astype(F32) + second_pull(grad_normed_two)[0]
 
-    early = [first_half.advance(across), second_half.advance(across)]
+    early = second_half.advance(across)
     grad_branch, across = narrow_gather(grad_middle.astype(BF16))
     grad_mixed = times_transpose(grad_branch, out_weight).astype(BF16)
-    grad_pack = tie(pack(value_heads, order, grad_mixed), early)
-    second = second_half.advance(across)
+    grad_pack = tie(pack(value_heads, order, grad_mixed), early, second_half.advance(across))
+    third = second_half.advance(grad_pack)
     later_branch, later_hidden = tie((grad_branch, hidden_rows), grad_pack)
     arrived_grad = exchange(grad_pack)
 
@@ -757,33 +758,33 @@
         return narrow_exchange(share.astype(BF16).reshape(NARROW, shard, -1))
 
     last_sums = Reduce(ring, down_terms, outer_sum(mixed, later_branch).astype(BF16))
-    arrived_grad = tie(arrived_grad, second, last_sums.advance())
-    third = second_half.advance(arrived_grad)
+    arrived_grad = tie(arrived_grad, third, last_sums.advance())
+    fourth = second_half.advance(arrived_grad)
+    last_sums.advance(arrived_grad)
     grad_pieces = attend_back(table, arrived, arrived_grad, group_heads, head_size)
-    grad_pieces = tie(grad_pieces, third)
+    grad_pieces = tie(grad_pieces, fourth)
     first_rows = narrow_rows(tie(first_half.result(), arrived_grad))
     output = (middle + narrow_reduce(dot(later_hidden, down))[0]).astype(BF16)
-    early = [second_half.advance(grad_pieces), last_sums.advance(grad_pieces)]
+    second_rows = narrow_rows(tie(second_half.result(), grad_pieces))
+    early = [last_sums.advance(grad_pieces), second_rows]
     grad_pieces = tie(exchange_back(grad_pieces), early, first_rows, output)
     projection_grad, norm_sums = unfinish(
         sizes, order, raw, grad_pieces, cosines, sines, norm_gains
     )
-    third = last_sums.advance(grad_pieces)
     first_terms = outer_sum(normed, projection_grad).astype(BF16)
     norm_terms = jnp.pad(
         norm_sums.astype(BF16), ((0, extra - 16), (0, projection_width - head_size))
     )
     first_sums = Reduce(ring, first_terms, shared=norm_terms)
+    begun = first_sums.advance()
     grad_normed, near, across = narrow_reduce(
         times_transpose(tie(projection_grad, first_terms), projection)
     )
+    fourth = last_sums.advance(begun)
+    first_sums.advance(near)
+    first_sums.advance(across, fourth)
+    w_gate_grad, w_up_grad = merge_columns(block, first_rows, second_rows)
     first_sums.advance()
-    second_rows = narrow_rows(tie(second_half.result(), first_terms))
-    last_sums.advance(first_terms)
-    first_sums.advance(near)
-    first_sums.advance(across, third)
-    w_gate_grad, w_up_grad = merge_columns(block, first_rows, second_rows)
-    first_sums.advance(second_rows)
     unused_first, first_pull = jax.vjp(lambda value: row_normalize(value, attention_gain), inputs)
     tokens_grad = (grad_middle + first_pull(grad_normed)[0]).astype(BF16)
 

time: 947 us -> 961 us (1.015)
  starting transfers between devices: 137 us -> 149 us
  waiting for transfers between devices: 352 us -> 364 us
    ppermute x64, waiting for transfers between devices: 277 us -> 294 us  [send(): return lax.ppermute(value, 'wide', self.onward if forward else self.back)]
    convert_element_type x20 -> x21, other arithmetic: 33.7 us -> 25.8 us  [join(): return (left.astype(F32) + right.astype(F32)).astype(BF16)]
  transfers between devices with their start and end apart: 109 -> 109, of which waited for: 40 -> 44; matrix products, arithmetic and copies ran while one was open for 27% -> 26% of each run, Pallas kernels for 5% -> 3%
where the time goes in v4:
time: 961 us; the launch traced here: 951 us
  waiting for transfers between devices  364 us (38%)
  starting transfers between devices  149 us (16%)
  matrix products  129 us (13%)
  local copies, waits for them, and re-layouts  115 us (12%)
  other arithmetic  94.1 us (10%)
  Pallas kernels  62.2 us (6%)
  between operations  37.8 us (4%)
    ppermute x64, waiting for transfers between devices, send(): return lax.ppermute(value, 'wide', self.onward if forward else self.back)  294 us
    ppermute x39, starting transfers between devices, swap(): return lax.ppermute(value, 'narrow', [(i, i ^ bit) for i in range(NARROW)])  63.1 us
    ppermute x39, waiting for transfers between devices, swap(): return lax.ppermute(value, 'narrow', [(i, i ^ bit) for i in range(NARROW)])  56.4 us
    ppermute x64, starting transfers between devices, send(): return lax.ppermute(value, 'wide', self.onward if forward else self.back)  52.9 us
    dot_general x6, matrix products, times_transpose(): lax.dot_general(left_rows, matrix, CONTRACT_COLS, preferred_element_type=...  48.8 us
    dot_general x7, matrix products, dot(): return jnp.dot(left, right, preferred_element_type=F32)  47 us
    dynamic_update_slice x34, local copies, waits for them, and re-layouts, put(): lax.dynamic_update_slice(whole, value, (self.ring.device(shift) * self.ro...  41.2 us
    dot_general x5, matrix products, outer_sum(): lax.dot_general(left_rows, right_rows, CONTRACT_ROWS, preferred_element_t...  33.2 us
  transfers between devices with their start and end apart: 109, of which 44 were waited for; matrix products, arithmetic and copies ran while one was open for 26% of the time, Pallas kernels for 3%

profile of v4, /device:TPU:9, one launch (start us, length us, event | category | flops | bytes accessed | tf_op | source)
XLA Modules:
  0.0 951.3 jit_solution(13297027223066929854)
XLA Ops:
  31.0 13.7 %collective-permute-done.6 = bf16[64,2048]{1,0:T(8,128)(2,1)} collective-permute-done((bf16[64,2048]{1,0:T(8,128)(2,1)}, bf16[64,2048]{1,0:T(8,128)(2,1)}, u32[]{:S(2)}, u32[]{:S(2)}) %collective-permute-start.6) | collective-permute-done | bytes 262176 | tf_op jit(solution)/shard_map/ppermute | solution.py:625
  55.8 7.5 collective-permute-done.1
  63.6 5.1 collective-permute-done.9
  75.4 13.9 %collective-permute-done.11 = bf16[416,1024]{1,0:T(8,128)(2,1)} collective-permute-done((bf16[416,1024]{1,0:T(8,128)(2,1)S(1)}, bf16[416,1024]{1,0:T(8,128)(2,1)}, u32[]{:S(2)}, u32[]{:S(2)}) %collective-permute-start.11) | collective-permute-done | bytes 852000 | tf_op jit(solution)/shard_map/ppermute | solution.py:68
  101.3 7.4 collective-permute-done.13
  123.0 4.7 slice.421
  130.7 9.8 %fusion.30.raw_ref = f32[1024,1024]{1,0:T(8,128)} fusion(bf16[2048,1024]{1,0:T(8,128)(2,1)} %bitcast.218, f32[2048]{0:T(1024)S(1)} %mul.549, f32[1024]{0:T(1024)S(1)} %add_rsqrt_fusion, bf16[256,2048]{1,0:T(8,128)(2,1)} %collective-permute-done.2, bf16[256,2048]{1,0:T(8,128)(2,1)} %collective-permute-done.1, bf16[256,2048]{1,0:T(8,128)(2,1)} %collective-permute-done, ...), kind=kOutput, calls=%fused_computation.103 | convolution fusion | flops 4318035968 | bytes 12595200 | tf_op jit(solution)/shard_map/dot_general | solution.py:36
  140.5 7.0 finish.1
  147.5 6.1 all-to-all-start
  161.7 3.9 collective-permute-done.21
  165.6 11.0 %collective-permute-done.20 = bf16[64,3072]{1,0:T(8,128)(2,1)} collective-permute-done((bf16[64,3072]{1,0:T(8,128)(2,1)}, bf16[64,3072]{1,0:T(8,128)(2,1)}, u32[]{:S(2)}, u32[]{:S(2)}) %collective-permute-start.20) | collective-permute-done | bytes 393248 | tf_op jit(solution)/shard_map/ppermute | solution.py:172
  188.7 26.5 %collective-permute-done.22 = bf16[256,1536]{1,0:T(8,128)(2,1)} collective-permute-done((bf16[256,1536]{1,0:T(8,128)(2,1)}, bf16[256,1536]{1,0:T(8,128)(2,1)}, u32[]{:S(2)}, u32[]{:S(2)}) %collective-permute-start.22) | collective-permute-done | bytes 786464 | tf_op jit(solution)/shard_map/ppermute | solution.py:68
  215.2 16.8 %collective-permute-done.24 = bf16[192,2048]{1,0:T(8,128)(2,1)} collective-permute-done((bf16[192,2048]{1,0:T(8,128)(2,1)}, bf16[192,2048]{1,0:T(8,128)(2,1)}, u32[]{:S(2)}, u32[]{:S(2)}) %collective-permute-start.24) | collective-permute-done | bytes 786464 | tf_op jit(solution)/shard_map/ppermute | solution.py:68
  236.4 14.3 %attend.1 = bf16[2048,256]{1,0:T(8,128)(2,1)} custom-call(s32[3,16]{1,0:T(4,128)} %pad_add_fusion.table, bf16[2048,512]{1,0:T(8,128)(2,1)} %bitcast.208), custom_call_target="tpu_custom_call" | custom-call | tf_op jit(solution)/shard_map/attend/pallas_call | solution.py:309
  252.3 6.0 all-to-all-start.1
  290.2 4.0 unpack.1
  321.4 8.9 collective-permute-done.33
  333.8 4.5 collective-permute-done.32
  341.6 19.1 %collective-permute-done.36 = bf16[256,2048]{1,0:T(8,128)(2,1)S(1)} collective-permute-done((bf16[256,2048]{1,0:T(8,128)(2,1)S(1)}, bf16[256,2048]{1,0:T(8,128)(2,1)S(1)}, u32[]{:S(2)}, u32[]{:S(2)}) %collective-permute-start.36) | collective-permute-done | bytes 1048608 | tf_op jit(solution)/shard_map/ppermute | solution.py:172
  363.9 17.3 %collective-permute-done.43 = bf16[256,1536]{1,0:T(8,128)(2,1)S(1)} collective-permute-done((bf16[256,1536]{1,0:T(8,128)(2,1)S(1)}, bf16[256,1536]{1,0:T(8,128)(2,1)S(1)}, u32[]{:S(2)}, u32[]{:S(2)}) %collective-permute-start.43) | collective-permute-done | bytes 786464 | tf_op jit(solution)/shard_map/ppermute | solution.py:68
  387.1 14.4 %collective-permute-done.45 = bf16[256,1536]{1,0:T(8,128)(2,1)S(1)} collective-permute-done((bf16[256,1536]{1,0:T(8,128)(2,1)S(1)}, bf16[256,1536]{1,0:T(8,128)(2,1)S(1)}, u32[]{:S(2)}, u32[]{:S(2)}) %collective-permute-start.45) | collective-permute-done | bytes 786464 | tf_op jit(solution)/shard_map/ppermute | solution.py:68
  404.6 3.6 fusion.19
  408.1 5.4 multiply_convert_fusion.3
  415.3 9.3 fusion.5
  425.0 7.3 collective-permute-done.47
  435.7 7.5 convolution_convert_fusion.2
  448.0 5.4 fusion.13
  453.4 8.0 multiply_convert_fusion.1
  464.4 9.4 fusion.8
  474.1 3.6 collective-permute-done.53
  480.0 9.0 fusion.59
  490.9 10.2 %add_convert_fusion = bf16[1024,2048]{1,0:T(8,128)(2,1)S(1)} fusion(f32[1024,2048]{1,0:T(8,128)} %fusion.59, bf16[1024,1536]{0,1:T(8,128)(2,1)} %copy-done.25, bf16[2048,1536]{1,0:T(8,128)(2,1)S(1)} %constant_dynamic-update-slice_fusion.18), kind=kOutput, calls=%fused_computation.16 | convolution fusion | flops 6446645248 | bytes 22020096 | tf_op jit(solution)/shard_map/dot_general | solution.py:44
  509.2 6.0 collective-permute-start.57
  529.8 7.1 convolution_convert_fusion
  536.9 7.5 convolution_convert_fusion.1
  544.9 3.6 convert_add_fusion.2
  555.8 7.6 collective-permute-start.62
  563.4 6.3 collective-permute-done.63
  569.7 7.3 collective-permute-start.64
  584.3 6.1 convolution_convert_fusion.8.rows_ref
  590.3 4.0 pack.1
  598.7 3.7 pad_maximum_fusion.2
  602.4 11.3 %convolution_convert_fusion.3 = bf16[1024,2048]{1,0:T(8,128)(2,1)} fusion(bf16[1024,1536]{0,1:T(8,128)(2,1)S(1)} %copy-done.60, bf16[1536,2048]{1,0:T(8,128)(2,1)} %constant_dynamic-update-slice_fusion.9), kind=kOutput, calls=%fused_computation.25 | convolution fusion | flops 6444548096 | bytes 13631488 | tf_op jit(solution)/shard_map/dot_general | solution.py:36
  613.7 5.1 all-to-all-start.2
  625.9 3.7 convolution_convert_fusion.7
  632.6 38.0 %collective-permute-done.75 = bf16[128,2048]{1,0:T(8,128)(2,1)S(1)} collective-permute-done((bf16[128,2048]{1,0:T(8,128)(2,1)S(1)}, bf16[128,2048]{1,0:T(8,128)(2,1)S(1)}, u32[]{:S(2)}, u32[]{:S(2)}) %collective-permute-start.75) | collective-permute-done | bytes 524320 | tf_op jit(solution)/shard_map/ppermute | solution.py:68
  671.5 18.9 %attend_back.1 = bf16[2048,512]{1,0:T(8,128)(2,1)} custom-call(s32[3,16]{1,0:T(4,128)} %pad_add_fusion.table, bf16[2048,512]{1,0:T(8,128)(2,1)} %bitcast.209, bf16[2048,256]{1,0:T(8,128)(2,1)} %bitcast.83.grad_ref), custom_call_target="tpu_custom_call" | custom-call | tf_op jit(solution)/shard_map/attend_back/pallas_call | solution.py:322
  712.3 9.3 collective-permute-done.77
  721.8 5.4 all-to-all-start.3
  738.1 6.0 collective-permute-done.79
  744.8 6.5 collective-permute-start.82
  759.3 3.7 add_convert_fusion.6
  768.8 42.7 %collective-permute-done.81 = bf16[256,2048]{1,0:T(8,128)(2,1)} collective-permute-done((bf16[256,2048]{1,0:T(8,128)(2,1)}, bf16[256,2048]{1,0:T(8,128)(2,1)}, u32[]{:S(2)}, u32[]{:S(2)}) %collective-permute-start.81) | collective-permute-done | bytes 1048608 | tf_op jit(solution)/shard_map/ppermute | solution.py:68
  811.5 7.8 unfinish.1
  819.3 7.4 convolution_convert_fusion.6
  830.5 4.8 convolution_convert_fusion.5
  851.3 14.4 %collective-permute-done.96 = bf16[256,2048]{1,0:T(8,128)(2,1)S(1)} collective-permute-done((bf16[256,2048]{1,0:T(8,128)(2,1)S(1)}, bf16[256,2048]{1,0:T(8,128)(2,1)S(1)}, u32[]{:S(2)}, u32[]{:S(2)}) %collective-permute-start.96) | collective-permute-done | bytes 1048608 | tf_op jit(solution)/shard_map/ppermute | solution.py:68
  868.7 12.5 %collective-permute-done.93 = bf16[288,1024]{1,0:T(8,128)(2,1)S(1)} collective-permute-done((bf16[288,1024]{1,0:T(8,128)(2,1)S(1)}, bf16[288,1024]{1,0:T(8,128)(2,1)S(1)}, u32[]{:S(2)}, u32[]{:S(2)}) %collective-permute-start.93) | collective-permute-done | bytes 589856 | tf_op jit(solution)/shard_map/ppermute | solution.py:68
  887.7 5.9 collective-permute-done.97
  898.5 7.3 collective-permute-start.104
  913.4 9.2 collective-permute-done.98
  922.7 9.0 collective-permute-done.100
  937.0 4.9 collective-permute-start.102
  941.9 4.8 fusion.25
  (596 shorter events, 314.9 us)
Async XLA Ops:
  8.3 18.7 %collective-permute-start.4 = (bf16[96,1024]{1,0:T(8,128)(2,1)S(1)}, bf16[96,1024]{1,0:T(8,128)(2,1)S(1)}, u32[]{:S(2)}, u32[]{:S(2)}) collective-permute-start(bf16[96,1024]{1,0:T(8,128)(2,1)S(1)} %get-tuple-element.273), channel_id=1, source_target_pairs={{0,2},{1,3},{2,0},{3,1},{4,6},{5,7},{6,4},{7,5},{8,10},{9,11},{10,... | collective-permute-start | bytes 589832 | tf_op jit(solution)/shard_map/ppermute | solution.py:172
  8.6 19.8 %collective-permute-start.3 = (bf16[96,1024]{1,0:T(8,128)(2,1)S(1)}, bf16[96,1024]{1,0:T(8,128)(2,1)S(1)}, u32[]{:S(2)}, u32[]{:S(2)}) collective-permute-start(bf16[96,1024]{1,0:T(8,128)(2,1)S(1)} %get-tuple-element.274), channel_id=1, source_target_pairs={{0,1},{1,0},{2,3},{3,2},{4,5},{5,4},{6,7},{7,6},{8,9},{9,8},{10,11... | collective-permute-start | bytes 589832 | tf_op jit(solution)/shard_map/ppermute | solution.py:172
  8.8 38.3 %collective-permute-start.7 = (bf16[192,2048]{1,0:T(8,128)(2,1)S(1)}, bf16[192,2048]{1,0:T(8,128)(2,1)}, u32[]{:S(2)}, u32[]{:S(2)}) collective-permute-start(bf16[192,2048]{1,0:T(8,128)(2,1)S(1)} %copy-done.61), channel_id=1, source_target_pairs={{0,8},{8,16},{16,24},{24,28},{28,20},{20,12},{12,4},{4,0},{1,9},{9... | collective-permute-start | bytes 2359304 | tf_op jit(solution)/shard_map/ppermute | solution.py:68
  10.1 37.0 %collective-permute-start.8 = (bf16[192,2048]{1,0:T(8,128)(2,1)S(1)}, bf16[192,2048]{1,0:T(8,128)(2,1)}, u32[]{:S(2)}, u32[]{:S(2)}) collective-permute-start(bf16[192,2048]{1,0:T(8,128)(2,1)S(1)} %copy-done.61), channel_id=1, source_target_pairs={{8,0},{16,8},{24,16},{28,24},{20,28},{12,20},{4,12},{0,4},{9,1},{1... | collective-permute-start | bytes 2359304 | tf_op jit(solution)/shard_map/ppermute | solution.py:68
  24.0 20.7 %collective-permute-start.6 = (bf16[64,2048]{1,0:T(8,128)(2,1)}, bf16[64,2048]{1,0:T(8,128)(2,1)}, u32[]{:S(2)}, u32[]{:S(2)}) collective-permute-start(bf16[64,2048]{1,0:T(8,128)(2,1)} %param.35), channel_id=1, source_target_pairs={{0,0},{1,4},{2,8},{3,12},{4,16},{5,20},{6,24},{7,28},{8,1},{9,5},{... | collective-permute-start | bytes 786440 | tf_op jit(solution)/shard_map/ppermute | solution.py:625
  27.0 36.2 %collective-permute-start.1 = (bf16[256,2048]{1,0:T(8,128)(2,1)S(1)}, bf16[256,2048]{1,0:T(8,128)(2,1)}, u32[]{:S(2)}, u32[]{:S(2)}) collective-permute-start(bf16[256,2048]{1,0:T(8,128)(2,1)S(1)} %copy-done), channel_id=1, source_target_pairs={{0,2},{1,3},{2,0},{3,1},{4,6},{5,7},{6,4},{7,5},{8,10},{9,11},{10,... | collective-permute-start | bytes 3145736 | tf_op jit(solution)/shard_map/ppermute | solution.py:172
  47.1 21.5 %collective-permute-start.9 = (bf16[416,1024]{1,0:T(8,128)(2,1)}, bf16[416,1024]{1,0:T(8,128)(2,1)S(1)}, u32[]{:S(2)}, u32[]{:S(2)}) collective-permute-start(bf16[416,1024]{1,0:T(8,128)(2,1)} %get-tuple-element.102), channel_id=1, source_target_pairs={{0,8},{8,16},{16,24},{24,28},{28,20},{20,12},{12,4},{4,0},{1,9},{9... | collective-permute-start | bytes 2555912 | tf_op jit(solution)/shard_map/ppermute | solution.py:68
  47.2 21.5 %collective-permute-start.10 = (bf16[416,1024]{1,0:T(8,128)(2,1)}, bf16[416,1024]{1,0:T(8,128)(2,1)S(1)}, u32[]{:S(2)}, u32[]{:S(2)}) collective-permute-start(bf16[416,1024]{1,0:T(8,128)(2,1)} %get-tuple-element.102), channel_id=1, source_target_pairs={{8,0},{16,8},{24,16},{28,24},{20,28},{12,20},{4,12},{0,4},{9,1},{1... | collective-permute-start | bytes 2555912 | tf_op jit(solution)/shard_map/ppermute | solution.py:68
  49.2 49.7 %collective-permute-start = (bf16[256,2048]{1,0:T(8,128)(2,1)S(1)}, bf16[256,2048]{1,0:T(8,128)(2,1)}, u32[]{:S(2)}, u32[]{:S(2)}) collective-permute-start(bf16[256,2048]{1,0:T(8,128)(2,1)S(1)} %copy-done), channel_id=1, source_target_pairs={{0,1},{1,0},{2,3},{3,2},{4,5},{5,4},{6,7},{7,6},{8,9},{9,8},{10,11... | collective-permute-start | bytes 3145736 | tf_op jit(solution)/shard_map/ppermute | solution.py:172
  63.3 35.6 %collective-permute-start.2 = (bf16[256,2048]{1,0:T(8,128)(2,1)}, bf16[256,2048]{1,0:T(8,128)(2,1)}, u32[]{:S(2)}, u32[]{:S(2)}) collective-permute-start(bf16[256,2048]{1,0:T(8,128)(2,1)} %collective-permute-done.1), channel_id=1, source_target_pairs={{0,1},{1,0},{2,3},{3,2},{4,5},{5,4},{6,7},{7,6},{8,9},{9,8},{10,11... | collective-permute-start | bytes 3145736 | tf_op jit(solution)/shard_map/ppermute | solution.py:172
  69.3 20.0 %collective-permute-start.11 = (bf16[416,1024]{1,0:T(8,128)(2,1)S(1)}, bf16[416,1024]{1,0:T(8,128)(2,1)}, u32[]{:S(2)}, u32[]{:S(2)}) collective-permute-start(bf16[416,1024]{1,0:T(8,128)(2,1)S(1)} %collective-permute-done.9), channel_id=1, source_target_pairs={{0,8},{8,16},{16,24},{24,28},{28,20},{20,12},{12,4},{4,0},{1,9},{9... | collective-permute-start | bytes 2555912 | tf_op jit(solution)/shard_map/ppermute | solution.py:68
  70.1 20.6 %collective-permute-start.12 = (bf16[416,1024]{1,0:T(8,128)(2,1)S(1)}, bf16[416,1024]{1,0:T(8,128)(2,1)}, u32[]{:S(2)}, u32[]{:S(2)}) collective-permute-start(bf16[416,1024]{1,0:T(8,128)(2,1)S(1)} %collective-permute-done.10), channel_id=1, source_target_pairs={{8,0},{16,8},{24,16},{28,24},{20,28},{12,20},{4,12},{0,4},{9,1},{1... | collective-permute-start | bytes 2555912 | tf_op jit(solution)/shard_map/ppermute | solution.py:68
  89.4 19.3 %collective-permute-start.13 = (bf16[416,1024]{1,0:T(8,128)(2,1)}, bf16[416,1024]{1,0:T(8,128)(2,1)S(1)}, u32[]{:S(2)}, u32[]{:S(2)}) collective-permute-start(bf16[416,1024]{1,0:T(8,128)(2,1)} %collective-permute-done.11), channel_id=1, source_target_pairs={{0,8},{8,16},{16,24},{24,28},{28,20},{20,12},{12,4},{4,0},{1,9},{9... | collective-permute-start | bytes 2555912 | tf_op jit(solution)/shard_map/ppermute | solution.py:68
  90.6 20.7 %collective-permute-start.14 = (bf16[416,1024]{1,0:T(8,128)(2,1)}, bf16[416,1024]{1,0:T(8,128)(2,1)S(1)}, u32[]{:S(2)}, u32[]{:S(2)}) collective-permute-start(bf16[416,1024]{1,0:T(8,128)(2,1)} %collective-permute-done.12), channel_id=1, source_target_pairs={{8,0},{16,8},{24,16},{28,24},{20,28},{12,20},{4,12},{0,4},{9,1},{1... | collective-permute-start | bytes 2555912 | tf_op jit(solution)/shard_map/ppermute | solution.py:68
  127.9 19.6 %collective-permute-start.17 = (bf16[192,2048]{1,0:T(8,128)(2,1)}, bf16[192,2048]{1,0:T(8,128)(2,1)}, u32[]{:S(2)}, u32[]{:S(2)}) collective-permute-start(bf16[192,2048]{1,0:T(8,128)(2,1)} %collective-permute-done.7), channel_id=1, source_target_pairs={{0,8},{8,16},{16,24},{24,28},{28,20},{20,12},{12,4},{4,0},{1,9},{9... | collective-permute-start | bytes 2359304 | tf_op jit(solution)/shard_map/ppermute | solution.py:68
  128.5 19.0 %collective-permute-start.18 = (bf16[192,2048]{1,0:T(8,128)(2,1)}, bf16[192,2048]{1,0:T(8,128)(2,1)}, u32[]{:S(2)}, u32[]{:S(2)}) collective-permute-start(bf16[192,2048]{1,0:T(8,128)(2,1)} %collective-permute-done.8), channel_id=1, source_target_pairs={{8,0},{16,8},{24,16},{28,24},{20,28},{12,20},{4,12},{0,4},{9,1},{1... | collective-permute-start | bytes 2359304 | tf_op jit(solution)/shard_map/ppermute | solution.py:68
  147.5 84.6 %all-to-all-start = ((bf16[8,256,512]{2,1,0:T(8,128)(2,1)}), bf16[8,256,512]{2,1,0:T(8,128)(2,1)S(1)}, u32[]{:S(2)}, u32[]{:S(2)}) async-start(bf16[8,256,512]{2,1,0:T(8,128)(2,1)} %bitcast.211), calls=%async_computation | async-start | bytes 4194304 | tf_op jit(solution)/shard_map/all_to_all | solution.py:679
  157.8 18.8 %collective-permute-start.20 = (bf16[64,3072]{1,0:T(8,128)(2,1)}, bf16[64,3072]{1,0:T(8,128)(2,1)}, u32[]{:S(2)}, u32[]{:S(2)}) collective-permute-start(bf16[64,3072]{1,0:T(8,128)(2,1)} %get-tuple-element.257), channel_id=1, source_target_pairs={{0,2},{1,3},{2,0},{3,1},{4,6},{5,7},{6,4},{7,5},{8,10},{9,11},{10,... | collective-permute-start | bytes 1179656 | tf_op jit(solution)/shard_map/ppermute | solution.py:172
  185.8 29.5 %collective-permute-start.22 = (bf16[256,1536]{1,0:T(8,128)(2,1)}, bf16[256,1536]{1,0:T(8,128)(2,1)}, u32[]{:S(2)}, u32[]{:S(2)}) collective-permute-start(bf16[256,1536]{1,0:T(8,128)(2,1)} %get-tuple-element.112), channel_id=1, source_target_pairs={{0,8},{8,16},{16,24},{24,28},{28,20},{20,12},{12,4},{4,0},{1,9},{9... | collective-permute-start | bytes 2359304 | tf_op jit(solution)/shard_map/ppermute | solution.py:68
  187.0 28.3 %collective-permute-start.23 = (bf16[256,1536]{1,0:T(8,128)(2,1)}, bf16[256,1536]{1,0:T(8,128)(2,1)}, u32[]{:S(2)}, u32[]{:S(2)}) collective-permute-start(bf16[256,1536]{1,0:T(8,128)(2,1)} %get-tuple-element.112), channel_id=1, source_target_pairs={{8,0},{16,8},{24,16},{28,24},{20,28},{12,20},{4,12},{0,4},{9,1},{1... | collective-permute-start | bytes 2359304 | tf_op jit(solution)/shard_map/ppermute | solution.py:68
  187.2 44.9 %collective-permute-start.24 = (bf16[192,2048]{1,0:T(8,128)(2,1)}, bf16[192,2048]{1,0:T(8,128)(2,1)}, u32[]{:S(2)}, u32[]{:S(2)}) collective-permute-start(bf16[192,2048]{1,0:T(8,128)(2,1)} %collective-permute-done.17), channel_id=1, source_target_pairs={{0,8},{8,16},{16,24},{24,28},{28,20},{20,12},{12,4},{4,0},{1,9},{9... | collective-permute-start | bytes 2359304 | tf_op jit(solution)/shard_map/ppermute | solution.py:68
  188.4 43.6 %collective-permute-start.25 = (bf16[192,2048]{1,0:T(8,128)(2,1)}, bf16[192,2048]{1,0:T(8,128)(2,1)}, u32[]{:S(2)}, u32[]{:S(2)}) collective-permute-start(bf16[192,2048]{1,0:T(8,128)(2,1)} %collective-permute-done.18), channel_id=1, source_target_pairs={{8,0},{16,8},{24,16},{28,24},{20,28},{12,20},{4,12},{0,4},{9,1},{1... | collective-permute-start | bytes 2359304 | tf_op jit(solution)/shard_map/ppermute | solution.py:68
  232.1 18.7 %collective-permute-start.26 = (bf16[256,1536]{1,0:T(8,128)(2,1)}, bf16[256,1536]{1,0:T(8,128)(2,1)}, u32[]{:S(2)}, u32[]{:S(2)}) collective-permute-start(bf16[256,1536]{1,0:T(8,128)(2,1)} %collective-permute-done.22), channel_id=1, source_target_pairs={{0,8},{8,16},{16,24},{24,28},{28,20},{20,12},{12,4},{4,0},{1,9},{9... | collective-permute-start | bytes 2359304 | tf_op jit(solution)/shard_map/ppermute | solution.py:68
  252.3 37.9 %all-to-all-start.1 = ((bf16[8,256,256]{2,1,0:T(8,128)(2,1)}), bf16[8,256,256]{2,1,0:T(8,128)(2,1)}, u32[]{:S(2)}, u32[]{:S(2)}) async-start(bf16[8,256,256]{2,1,0:T(8,128)(2,1)} %bitcast.220), calls=%async_computation.1 | async-start | bytes 2097152 | tf_op jit(solution)/shard_map/all_to_all | solution.py:684
  311.0 19.3 %collective-permute-start.33 = (bf16[256,1536]{1,0:T(8,128)(2,1)}, bf16[256,1536]{1,0:T(8,128)(2,1)S(1)}, u32[]{:S(2)}, u32[]{:S(2)}) collective-permute-start(bf16[256,1536]{1,0:T(8,128)(2,1)} %collective-permute-done.26), channel_id=1, source_target_pairs={{0,8},{8,16},{16,24},{24,28},{28,20},{20,12},{12,4},{4,0},{1,9},{9... | collective-permute-start | bytes 2359304 | tf_op jit(solution)/shard_map/ppermute | solution.py:68
  311.0 21.2 %collective-permute-start.34 = (bf16[256,1536]{1,0:T(8,128)(2,1)}, bf16[256,1536]{1,0:T(8,128)(2,1)S(1)}, u32[]{:S(2)}, u32[]{:S(2)}) collective-permute-start(bf16[256,1536]{1,0:T(8,128)(2,1)} %collective-permute-done.27), channel_id=1, source_target_pairs={{8,0},{16,8},{24,16},{28,24},{20,28},{12,20},{4,12},{0,4},{9,1},{1... | collective-permute-start | bytes 2359304 | tf_op jit(solution)/shard_map/ppermute | solution.py:68
  312.5 19.8 %collective-permute-start.30 = (bf16[256,2048]{1,0:T(8,128)(2,1)S(1)}, bf16[256,2048]{1,0:T(8,128)(2,1)S(1)}, u32[]{:S(2)}, u32[]{:S(2)}) collective-permute-start(bf16[256,2048]{1,0:T(8,128)(2,1)S(1)} %get-tuple-element.241), channel_id=1, source_target_pairs={{0,1},{1,0},{2,3},{3,2},{4,5},{5,4},{6,7},{7,6},{8,9},{9,8},{10,11... | collective-permute-start | bytes 3145736 | tf_op jit(solution)/shard_map/ppermute | solution.py:172
  313.5 24.8 %collective-permute-start.32 = (bf16[256,2048]{1,0:T(8,128)(2,1)S(1)}, bf16[256,2048]{1,0:T(8,128)(2,1)S(1)}, u32[]{:S(2)}, u32[]{:S(2)}) collective-permute-start(bf16[256,2048]{1,0:T(8,128)(2,1)S(1)} %add_convert_fusion.9), channel_id=1, source_target_pairs={{0,2},{1,3},{2,0},{3,1},{4,6},{5,7},{6,4},{7,5},{8,10},{9,11},{10,... | collective-permute-start | bytes 3145736 | tf_op jit(solution)/shard_map/ppermute | solution.py:172
  331.3 29.4 %collective-permute-start.36 = (bf16[256,2048]{1,0:T(8,128)(2,1)S(1)}, bf16[256,2048]{1,0:T(8,128)(2,1)S(1)}, u32[]{:S(2)}, u32[]{:S(2)}) collective-permute-start(bf16[256,2048]{1,0:T(8,128)(2,1)S(1)} %copy-done.5), channel_id=1, source_target_pairs={{0,2},{1,3},{2,0},{3,1},{4,6},{5,7},{6,4},{7,5},{8,10},{9,11},{10,... | collective-permute-start | bytes 3145736 | tf_op jit(solution)/shard_map/ppermute | solution.py:172
  331.3 32.5 %collective-permute-start.35 = (bf16[256,2048]{1,0:T(8,128)(2,1)S(1)}, bf16[256,2048]{1,0:T(8,128)(2,1)S(1)}, u32[]{:S(2)}, u32[]{:S(2)}) collective-permute-start(bf16[256,2048]{1,0:T(8,128)(2,1)S(1)} %copy-done.5), channel_id=1, source_target_pairs={{0,1},{1,0},{2,3},{3,2},{4,5},{5,4},{6,7},{7,6},{8,9},{9,8},{10,11... | collective-permute-start | bytes 3145736 | tf_op jit(solution)/shard_map/ppermute | solution.py:172
  332.3 29.8 %collective-permute-start.42 = (bf16[128,1536]{1,0:T(8,128)(2,1)S(1)}, bf16[128,1536]{1,0:T(8,128)(2,1)S(1)}, u32[]{:S(2)}, u32[]{:S(2)}) collective-permute-start(bf16[128,1536]{1,0:T(8,128)(2,1)S(1)} %slice.321), channel_id=1, source_target_pairs={{8,0},{16,8},{24,16},{28,24},{20,28},{12,20},{4,12},{0,4},{9,1},{1... | collective-permute-start | bytes 1179656 | tf_op jit(solution)/shard_map/ppermute | solution.py:68
  332.3 29.8 %collective-permute-start.41 = (bf16[128,1536]{1,0:T(8,128)(2,1)S(1)}, bf16[128,1536]{1,0:T(8,128)(2,1)S(1)}, u32[]{:S(2)}, u32[]{:S(2)}) collective-permute-start(bf16[128,1536]{1,0:T(8,128)(2,1)S(1)} %slice.320), channel_id=1, source_target_pairs={{0,8},{8,16},{16,24},{24,28},{28,20},{20,12},{12,4},{4,0},{1,9},{9... | collective-permute-start | bytes 1179656 | tf_op jit(solution)/shard_map/ppermute | solution.py:68
  339.5 43.7 %collective-permute-start.39 = (bf16[256,2048]{1,0:T(8,128)(2,1)S(1)}, bf16[256,2048]{1,0:T(8,128)(2,1)S(1)}, u32[]{:S(2)}, u32[]{:S(2)}) collective-permute-start(bf16[256,2048]{1,0:T(8,128)(2,1)S(1)} %multiply_convert_fusion.4), channel_id=1, source_target_pairs={{0,2},{1,3},{2,0},{3,1},{4,6},{5,7},{6,4},{7,5},{8,10},{9,11},{10,... | collective-permute-start | bytes 3145736 | tf_op jit(solution)/shard_map/ppermute | solution.py:172
  360.7 26.1 %collective-permute-start.37 = (bf16[256,2048]{1,0:T(8,128)(2,1)S(1)}, bf16[256,2048]{1,0:T(8,128)(2,1)S(1)}, u32[]{:S(2)}, u32[]{:S(2)}) collective-permute-start(bf16[256,2048]{1,0:T(8,128)(2,1)S(1)} %collective-permute-done.36), channel_id=1, source_target_pairs={{0,1},{1,0},{2,3},{3,2},{4,5},{5,4},{6,7},{7,6},{8,9},{9,8},{10,11... | collective-permute-start | bytes 3145736 | tf_op jit(solution)/shard_map/ppermute | solution.py:172
  362.1 19.1 %collective-permute-start.43 = (bf16[256,1536]{1,0:T(8,128)(2,1)S(1)}, bf16[256,1536]{1,0:T(8,128)(2,1)S(1)}, u32[]{:S(2)}, u32[]{:S(2)}) collective-permute-start(bf16[256,1536]{1,0:T(8,128)(2,1)S(1)} %copy-done.58), channel_id=1, source_target_pairs={{0,8},{8,16},{16,24},{24,28},{28,20},{20,12},{12,4},{4,0},{1,9},{9... | collective-permute-start | bytes 2359304 | tf_op jit(solution)/shard_map/ppermute | solution.py:68
  362.1 19.1 %collective-permute-start.44 = (bf16[256,1536]{1,0:T(8,128)(2,1)S(1)}, bf16[256,1536]{1,0:T(8,128)(2,1)S(1)}, u32[]{:S(2)}, u32[]{:S(2)}) collective-permute-start(bf16[256,1536]{1,0:T(8,128)(2,1)S(1)} %copy-done.58), channel_id=1, source_target_pairs={{8,0},{16,8},{24,16},{28,24},{20,28},{12,20},{4,12},{0,4},{9,1},{1... | collective-permute-start | bytes 2359304 | tf_op jit(solution)/shard_map/ppermute | solution.py:68
  383.3 20.5 %collective-permute-start.38 = (bf16[256,2048]{1,0:T(8,128)(2,1)S(1)}, bf16[256,2048]{1,0:T(8,128)(2,1)S(1)}, u32[]{:S(2)}, u32[]{:S(2)}) collective-permute-start(bf16[256,2048]{1,0:T(8,128)(2,1)S(1)} %multiply_convert_fusion.4), channel_id=1, source_target_pairs={{0,1},{1,0},{2,3},{3,2},{4,5},{5,4},{6,7},{7,6},{8,9},{9,8},{10,11... | collective-permute-start | bytes 3145736 | tf_op jit(solution)/shard_map/ppermute | solution.py:172
  384.2 19.5 %collective-permute-start.46 = (bf16[256,1536]{1,0:T(8,128)(2,1)S(1)}, bf16[256,1536]{1,0:T(8,128)(2,1)S(1)}, u32[]{:S(2)}, u32[]{:S(2)}) collective-permute-start(bf16[256,1536]{1,0:T(8,128)(2,1)S(1)} %collective-permute-done.44), channel_id=1, source_target_pairs={{8,0},{16,8},{24,16},{28,24},{20,28},{12,20},{4,12},{0,4},{9,1},{1... | collective-permute-start | bytes 2359304 | tf_op jit(solution)/shard_map/ppermute | solution.py:68
  413.6 18.7 %collective-permute-start.47 = (bf16[256,1536]{1,0:T(8,128)(2,1)S(1)}, bf16[256,1536]{1,0:T(8,128)(2,1)S(1)}, u32[]{:S(2)}, u32[]{:S(2)}) collective-permute-start(bf16[256,1536]{1,0:T(8,128)(2,1)S(1)} %collective-permute-done.45), channel_id=1, source_target_pairs={{0,8},{8,16},{16,24},{24,28},{28,20},{20,12},{12,4},{4,0},{1,9},{9... | collective-permute-start | bytes 2359304 | tf_op jit(solution)/shard_map/ppermute | solution.py:68
  555.8 26.5 %collective-permute-start.62 = (bf16[256,2048]{1,0:T(8,128)(2,1)S(1)}, bf16[256,2048]{1,0:T(8,128)(2,1)S(1)}, u32[]{:S(2)}, u32[]{:S(2)}) collective-permute-start(bf16[256,2048]{1,0:T(8,128)(2,1)S(1)} %fusion.47), channel_id=1, source_target_pairs={{0,1},{1,0},{2,3},{3,2},{4,5},{5,4},{6,7},{7,6},{8,9},{9,8},{10,11... | collective-permute-start | bytes 3145736 | tf_op jit(solution)/shard_map/ppermute | solution.py:172
  578.1 19.4 %collective-permute-start.67 = (bf16[256,1536]{1,0:T(8,128)(2,1)}, bf16[256,1536]{1,0:T(8,128)(2,1)}, u32[]{:S(2)}, u32[]{:S(2)}) collective-permute-start(bf16[256,1536]{1,0:T(8,128)(2,1)} %pad_maximum_fusion.12), channel_id=1, source_target_pairs={{0,8},{8,16},{16,24},{24,28},{28,20},{20,12},{12,4},{4,0},{1,9},{9... | collective-permute-start | bytes 2359304 | tf_op jit(solution)/shard_map/ppermute | solution.py:68
  579.6 19.1 %collective-permute-start.68 = (bf16[256,1536]{1,0:T(8,128)(2,1)}, bf16[256,1536]{1,0:T(8,128)(2,1)}, u32[]{:S(2)}, u32[]{:S(2)}) collective-permute-start(bf16[256,1536]{1,0:T(8,128)(2,1)} %pad_maximum_fusion.13), channel_id=1, source_target_pairs={{8,0},{16,8},{24,16},{28,24},{20,28},{12,20},{4,12},{0,4},{9,1},{1... | collective-permute-start | bytes 2359304 | tf_op jit(solution)/shard_map/ppermute | solution.py:68
  581.6 51.0 %collective-permute-start.74 = (bf16[128,2048]{1,0:T(8,128)(2,1)}, bf16[128,2048]{1,0:T(8,128)(2,1)}, u32[]{:S(2)}, u32[]{:S(2)}) collective-permute-start(bf16[128,2048]{1,0:T(8,128)(2,1)} %get-tuple-element.202), channel_id=1, source_target_pairs={{0,8},{8,16},{16,24},{24,28},{28,20},{20,12},{12,4},{4,0},{1,9},{9... | collective-permute-start | bytes 1572872 | tf_op jit(solution)/shard_map/ppermute | solution.py:68
  613.7 57.7 %all-to-all-start.2 = ((bf16[8,256,256]{2,1,0:T(8,128)(2,1)}), bf16[8,256,256]{2,1,0:T(8,128)(2,1)}, u32[]{:S(2)}, u32[]{:S(2)}) async-start(bf16[8,256,256]{2,1,0:T(8,128)(2,1)} %bitcast.217), calls=%async_computation.2 | async-start | bytes 2097152 | tf_op jit(solution)/shard_map/all_to_all | solution.py:679
  621.2 49.5 %collective-permute-start.73 = (bf16[256,1536]{1,0:T(8,128)(2,1)S(1)}, bf16[256,1536]{1,0:T(8,128)(2,1)}, u32[]{:S(2)}, u32[]{:S(2)}) collective-permute-start(bf16[256,1536]{1,0:T(8,128)(2,1)S(1)} %get-tuple-element.205), channel_id=1, source_target_pairs={{8,0},{16,8},{24,16},{28,24},{20,28},{12,20},{4,12},{0,4},{9,1},{1... | collective-permute-start | bytes 2359304 | tf_op jit(solution)/shard_map/ppermute | solution.py:68
  621.4 50.0 %collective-permute-start.72 = (bf16[256,1536]{1,0:T(8,128)(2,1)S(1)}, bf16[256,1536]{1,0:T(8,128)(2,1)}, u32[]{:S(2)}, u32[]{:S(2)}) collective-permute-start(bf16[256,1536]{1,0:T(8,128)(2,1)S(1)} %get-tuple-element.206), channel_id=1, source_target_pairs={{0,8},{8,16},{16,24},{24,28},{28,20},{20,12},{12,4},{4,0},{1,9},{9... | collective-permute-start | bytes 2359304 | tf_op jit(solution)/shard_map/ppermute | solution.py:68
  631.2 39.5 %collective-permute-start.75 = (bf16[128,2048]{1,0:T(8,128)(2,1)S(1)}, bf16[128,2048]{1,0:T(8,128)(2,1)S(1)}, u32[]{:S(2)}, u32[]{:S(2)}) collective-permute-start(bf16[128,2048]{1,0:T(8,128)(2,1)S(1)} %pad_maximum_fusion.21), channel_id=1, source_target_pairs={{8,0},{16,8},{24,16},{28,24},{20,28},{12,20},{4,12},{0,4},{9,1},{1... | collective-permute-start | bytes 1572872 | tf_op jit(solution)/shard_map/ppermute | solution.py:68
  702.6 19.0 %collective-permute-start.77 = (bf16[256,1536]{1,0:T(8,128)(2,1)}, bf16[256,1536]{1,0:T(8,128)(2,1)}, u32[]{:S(2)}, u32[]{:S(2)}) collective-permute-start(bf16[256,1536]{1,0:T(8,128)(2,1)} %get-tuple-element.203), channel_id=1, source_target_pairs={{8,0},{16,8},{24,16},{28,24},{20,28},{12,20},{4,12},{0,4},{9,1},{1... | collective-permute-start | bytes 2359304 | tf_op jit(solution)/shard_map/ppermute | solution.py:68
  702.6 19.2 %collective-permute-start.76 = (bf16[256,1536]{1,0:T(8,128)(2,1)}, bf16[256,1536]{1,0:T(8,128)(2,1)}, u32[]{:S(2)}, u32[]{:S(2)}) collective-permute-start(bf16[256,1536]{1,0:T(8,128)(2,1)} %get-tuple-element.204), channel_id=1, source_target_pairs={{0,8},{8,16},{16,24},{24,28},{28,20},{20,12},{12,4},{4,0},{1,9},{9... | collective-permute-start | bytes 2359304 | tf_op jit(solution)/shard_map/ppermute | solution.py:68
  706.5 50.0 %collective-permute-start.69 = (bf16[256,2048]{1,0:T(8,128)(2,1)}, bf16[256,2048]{1,0:T(8,128)(2,1)}, u32[]{:S(2)}, u32[]{:S(2)}) collective-permute-start(bf16[256,2048]{1,0:T(8,128)(2,1)} %get-tuple-element.237), channel_id=1, source_target_pairs={{0,1},{1,0},{2,3},{3,2},{4,5},{5,4},{6,7},{7,6},{8,9},{9,8},{10,11... | collective-permute-start | bytes 3145736 | tf_op jit(solution)/shard_map/ppermute | solution.py:172
  707.8 48.7 %collective-permute-start.71 = (bf16[256,2048]{1,0:T(8,128)(2,1)}, bf16[256,2048]{1,0:T(8,128)(2,1)}, u32[]{:S(2)}, u32[]{:S(2)}) collective-permute-start(bf16[256,2048]{1,0:T(8,128)(2,1)} %add_convert_fusion.7), channel_id=1, source_target_pairs={{0,2},{1,3},{2,0},{3,1},{4,6},{5,7},{6,4},{7,5},{8,10},{9,11},{10,... | collective-permute-start | bytes 3145736 | tf_op jit(solution)/shard_map/ppermute | solution.py:172
  708.7 35.4 %collective-permute-start.79 = (bf16[256,2048]{1,0:T(8,128)(2,1)}, bf16[256,2048]{1,0:T(8,128)(2,1)}, u32[]{:S(2)}, u32[]{:S(2)}) collective-permute-start(bf16[256,2048]{1,0:T(8,128)(2,1)} %pad_maximum_fusion.6), channel_id=1, source_target_pairs={{8,0},{16,8},{24,16},{28,24},{20,28},{12,20},{4,12},{0,4},{9,1},{1... | collective-permute-start | bytes 3145736 | tf_op jit(solution)/shard_map/ppermute | solution.py:68
  721.6 23.2 %collective-permute-start.78 = (bf16[256,2048]{1,0:T(8,128)(2,1)}, bf16[256,2048]{1,0:T(8,128)(2,1)}, u32[]{:S(2)}, u32[]{:S(2)}) collective-permute-start(bf16[256,2048]{1,0:T(8,128)(2,1)} %fusion.34), channel_id=1, source_target_pairs={{0,8},{8,16},{16,24},{24,28},{28,20},{20,12},{12,4},{4,0},{1,9},{9... | collective-permute-start | bytes 3145736 | tf_op jit(solution)/shard_map/ppermute | solution.py:68
  721.8 89.7 %all-to-all-start.3 = ((bf16[8,256,512]{2,1,0:T(8,128)(2,1)}), bf16[8,256,512]{2,1,0:T(8,128)(2,1)}, u32[]{:S(2)}, u32[]{:S(2)}) async-start(bf16[8,256,512]{2,1,0:T(8,128)(2,1)} %bitcast.210), calls=%async_computation.3 | async-start | bytes 4194304 | tf_op jit(solution)/shard_map/all_to_all | solution.py:684
  735.3 27.7 %collective-permute-start.84 = (bf16[64,1536]{1,0:T(8,128)(2,1)S(1)}, bf16[64,1536]{1,0:T(8,128)(2,1)S(1)}, u32[]{:S(2)}, u32[]{:S(2)}) collective-permute-start(bf16[64,1536]{1,0:T(8,128)(2,1)S(1)} %get-tuple-element.266), channel_id=1, source_target_pairs={{0,3},{1,2},{2,1},{3,0},{4,7},{5,6},{6,5},{7,4},{8,11},{9,10},{10,... | collective-permute-start | bytes 589832 | tf_op jit(solution)/shard_map/ppermute | solution.py:172
  744.0 18.9 %collective-permute-start.83 = (bf16[64,1536]{1,0:T(8,128)(2,1)S(1)}, bf16[64,1536]{1,0:T(8,128)(2,1)S(1)}, u32[]{:S(2)}, u32[]{:S(2)}) collective-permute-start(bf16[64,1536]{1,0:T(8,128)(2,1)S(1)} %get-tuple-element.267), channel_id=1, source_target_pairs={{0,2},{1,3},{2,0},{3,1},{4,6},{5,7},{6,4},{7,5},{8,10},{9,11},{10,... | collective-permute-start | bytes 589832 | tf_op jit(solution)/shard_map/ppermute | solution.py:172
  756.5 55.0 %collective-permute-start.81 = (bf16[256,2048]{1,0:T(8,128)(2,1)}, bf16[256,2048]{1,0:T(8,128)(2,1)}, u32[]{:S(2)}, u32[]{:S(2)}) collective-permute-start(bf16[256,2048]{1,0:T(8,128)(2,1)} %add_convert_fusion.4), channel_id=1, source_target_pairs={{8,0},{16,8},{24,16},{28,24},{20,28},{12,20},{4,12},{0,4},{9,1},{1... | collective-permute-start | bytes 3145736 | tf_op jit(solution)/shard_map/ppermute | solution.py:68
  756.5 55.0 %collective-permute-start.80 = (bf16[256,2048]{1,0:T(8,128)(2,1)}, bf16[256,2048]{1,0:T(8,128)(2,1)}, u32[]{:S(2)}, u32[]{:S(2)}) collective-permute-start(bf16[256,2048]{1,0:T(8,128)(2,1)} %add_convert_fusion.5), channel_id=1, source_target_pairs={{0,8},{8,16},{16,24},{24,28},{28,20},{20,12},{12,4},{4,0},{1,9},{9... | collective-permute-start | bytes 3145736 | tf_op jit(solution)/shard_map/ppermute | solution.py:68
  844.2 21.5 %collective-permute-start.96 = (bf16[256,2048]{1,0:T(8,128)(2,1)S(1)}, bf16[256,2048]{1,0:T(8,128)(2,1)S(1)}, u32[]{:S(2)}, u32[]{:S(2)}) collective-permute-start(bf16[256,2048]{1,0:T(8,128)(2,1)S(1)} %add_convert_fusion.1), channel_id=1, source_target_pairs={{8,0},{16,8},{24,16},{28,24},{20,28},{12,20},{4,12},{0,4},{9,1},{1... | collective-permute-start | bytes 3145736 | tf_op jit(solution)/shard_map/ppermute | solution.py:68
  846.9 21.8 %collective-permute-start.95 = (bf16[256,2048]{1,0:T(8,128)(2,1)S(1)}, bf16[256,2048]{1,0:T(8,128)(2,1)S(1)}, u32[]{:S(2)}, u32[]{:S(2)}) collective-permute-start(bf16[256,2048]{1,0:T(8,128)(2,1)S(1)} %add_convert_fusion.2), channel_id=1, source_target_pairs={{0,8},{8,16},{16,24},{24,28},{28,20},{20,12},{12,4},{4,0},{1,9},{9... | collective-permute-start | bytes 3145736 | tf_op jit(solution)/shard_map/ppermute | solution.py:68
  847.8 33.4 %collective-permute-start.90 = (bf16[256,2048]{1,0:T(8,128)(2,1)S(1)}, bf16[256,2048]{1,0:T(8,128)(2,1)}, u32[]{:S(2)}, u32[]{:S(2)}) collective-permute-start(bf16[256,2048]{1,0:T(8,128)(2,1)S(1)} %add_convert_fusion.3), channel_id=1, source_target_pairs={{0,2},{1,3},{2,0},{3,1},{4,6},{5,7},{6,4},{7,5},{8,10},{9,11},{10,... | collective-permute-start | bytes 3145736 | tf_op jit(solution)/shard_map/ppermute | solution.py:172
  849.3 31.9 %collective-permute-start.93 = (bf16[288,1024]{1,0:T(8,128)(2,1)S(1)}, bf16[288,1024]{1,0:T(8,128)(2,1)S(1)}, u32[]{:S(2)}, u32[]{:S(2)}) collective-permute-start(bf16[288,1024]{1,0:T(8,128)(2,1)S(1)} %pad_maximum_fusion.18), channel_id=1, source_target_pairs={{0,8},{8,16},{16,24},{24,28},{28,20},{20,12},{12,4},{4,0},{1,9},{9... | collective-permute-start | bytes 1769480 | tf_op jit(solution)/shard_map/ppermute | solution.py:68
  849.8 31.4 %collective-permute-start.94 = (bf16[288,1024]{1,0:T(8,128)(2,1)S(1)}, bf16[288,1024]{1,0:T(8,128)(2,1)S(1)}, u32[]{:S(2)}, u32[]{:S(2)}) collective-permute-start(bf16[288,1024]{1,0:T(8,128)(2,1)S(1)} %pad_maximum_fusion.19), channel_id=1, source_target_pairs={{8,0},{16,8},{24,16},{28,24},{20,28},{12,20},{4,12},{0,4},{9,1},{1... | collective-permute-start | bytes 1769480 | tf_op jit(solution)/shard_map/ppermute | solution.py:68
  906.8 24.8 %collective-permute-start.100 = (bf16[288,1024]{1,0:T(8,128)(2,1)S(1)}, bf16[288,1024]{1,0:T(8,128)(2,1)S(1)}, u32[]{:S(2)}, u32[]{:S(2)}) collective-permute-start(bf16[288,1024]{1,0:T(8,128)(2,1)S(1)} %add_convert_fusion.19), channel_id=1, source_target_pairs={{8,0},{16,8},{24,16},{28,24},{20,28},{12,20},{4,12},{0,4},{9,1},{1... | collective-permute-start | bytes 1769480 | tf_op jit(solution)/shard_map/ppermute | solution.py:68
  (136 other events, 2015.7 us)

commit v5 on v3

--- a/solution.py
+++ b/solution.py
@@ -768,19 +768,19 @@
     projection_grad, norm_sums = unfinish(
         sizes, order, raw, grad_pieces, cosines, sines, norm_gains
     )
-    third = last_sums.advance(grad_pieces)
     first_terms = outer_sum(normed, projection_grad).astype(BF16)
     norm_terms = jnp.pad(
         norm_sums.astype(BF16), ((0, extra - 16), (0, projection_width - head_size))
     )
     first_sums = Reduce(ring, first_terms, shared=norm_terms)
+    begun = first_sums.advance()
     grad_normed, near, across = narrow_reduce(
         times_transpose(tie(projection_grad, first_terms), projection)
     )
-    first_sums.advance()
-    second_rows = narrow_rows(tie(second_half.result(), first_terms))
-    last_sums.advance(first_terms)
-    first_sums.advance(near)
+    second_rows = narrow_rows(tie(second_half.result(), begun))
+    third = last_sums.advance(begun)
+    begun = first_sums.advance(near)
+    last_sums.advance(begun)
     first_sums.advance(across, third)
     w_gate_grad, w_up_grad = merge_columns(block, first_rows, second_rows)
     first_sums.advance(second_rows)

time: 947 us -> 953 us (level)
  transfers between devices with their start and end apart: 109 -> 109, of which waited for: 40 -> 39; matrix products, arithmetic and copies ran while one was open for 27% -> 28% of each run, Pallas kernels for 5% -> 5%
where the time goes in v5:
time: 953 us; the launch traced here: 943 us
  waiting for transfers between devices  355 us (37%)
  starting transfers between devices  135 us (14%)
  matrix products  127 us (13%)
  local copies, waits for them, and re-layouts  121 us (13%)
  other arithmetic  106 us (11%)
  Pallas kernels  62.4 us (7%)
  between operations  36.9 us (4%)
    ppermute x64, waiting for transfers between devices, send(): return lax.ppermute(value, 'wide', self.onward if forward else self.back)  281 us
    ppermute x39, waiting for transfers between devices, swap(): return lax.ppermute(value, 'narrow', [(i, i ^ bit) for i in range(NARROW)])  60.6 us
    ppermute x39, starting transfers between devices, swap(): return lax.ppermute(value, 'narrow', [(i, i ^ bit) for i in range(NARROW)])  54.4 us
    ppermute x64, starting transfers between devices, send(): return lax.ppermute(value, 'wide', self.onward if forward else self.back)  49.9 us
    dot_general x6, matrix products, times_transpose(): lax.dot_general(left_rows, matrix, CONTRACT_COLS, preferred_element_type=...  47.9 us
    dot_general x7, matrix products, dot(): return jnp.dot(left, right, preferred_element_type=F32)  47.3 us
    dynamic_update_slice x34, local copies, waits for them, and re-layouts, put(): lax.dynamic_update_slice(whole, value, (self.ring.device(shift) * self.ro...  41.4 us
    convert_element_type x20, other arithmetic, join(): return (left.astype(F32) + right.astype(F32)).astype(BF16)  36.8 us
  transfers between devices with their start and end apart: 109, of which 39 were waited for; matrix products, arithmetic and copies ran while one was open for 28% of the time, Pallas kernels for 5%

profile of v5, /device:TPU:9, one launch (start us, length us, event | category | flops | bytes accessed | tf_op | source)
XLA Modules:
  0.0 943.1 jit_solution(15586515006061439112)
XLA Ops:
  30.8 13.7 %collective-permute-done.6 = bf16[64,2048]{1,0:T(8,128)(2,1)} collective-permute-done((bf16[64,2048]{1,0:T(8,128)(2,1)}, bf16[64,2048]{1,0:T(8,128)(2,1)}, u32[]{:S(2)}, u32[]{:S(2)}) %collective-permute-start.6) | collective-permute-done | bytes 262176 | tf_op jit(solution)/shard_map/ppermute | solution.py:625
  55.6 7.5 collective-permute-done.1
  63.4 5.4 collective-permute-done.9
  75.6 14.0 %collective-permute-done.11 = bf16[416,1024]{1,0:T(8,128)(2,1)} collective-permute-done((bf16[416,1024]{1,0:T(8,128)(2,1)S(1)}, bf16[416,1024]{1,0:T(8,128)(2,1)}, u32[]{:S(2)}, u32[]{:S(2)}) %collective-permute-start.11) | collective-permute-done | bytes 852000 | tf_op jit(solution)/shard_map/ppermute | solution.py:68
  101.5 7.4 collective-permute-done.13
  123.3 4.7 slice.421
  130.6 9.7 %fusion.30.raw_ref = f32[1024,1024]{1,0:T(8,128)} fusion(bf16[2048,1024]{1,0:T(8,128)(2,1)} %bitcast.217, f32[2048]{0:T(1024)S(1)} %mul.549, f32[1024]{0:T(1024)S(1)} %add_rsqrt_fusion, bf16[256,2048]{1,0:T(8,128)(2,1)} %collective-permute-done.2, bf16[256,2048]{1,0:T(8,128)(2,1)} %collective-permute-done.1, bf16[256,2048]{1,0:T(8,128)(2,1)} %collective-permute-done, ...), kind=kOutput, calls=%fused_computation.103 | convolution fusion | flops 4318035968 | bytes 12595200 | tf_op jit(solution)/shard_map/dot_general | solution.py:36
  140.3 7.0 finish.1
  147.4 6.3 all-to-all-start
  161.6 4.1 collective-permute-done.21
  165.7 10.9 %collective-permute-done.20 = bf16[64,3072]{1,0:T(8,128)(2,1)} collective-permute-done((bf16[64,3072]{1,0:T(8,128)(2,1)}, bf16[64,3072]{1,0:T(8,128)(2,1)}, u32[]{:S(2)}, u32[]{:S(2)}) %collective-permute-start.20) | collective-permute-done | bytes 393248 | tf_op jit(solution)/shard_map/ppermute | solution.py:172
  188.8 26.5 %collective-permute-done.22 = bf16[256,1536]{1,0:T(8,128)(2,1)} collective-permute-done((bf16[256,1536]{1,0:T(8,128)(2,1)}, bf16[256,1536]{1,0:T(8,128)(2,1)}, u32[]{:S(2)}, u32[]{:S(2)}) %collective-permute-start.22) | collective-permute-done | bytes 786464 | tf_op jit(solution)/shard_map/ppermute | solution.py:68
  215.3 16.8 %collective-permute-done.24 = bf16[192,2048]{1,0:T(8,128)(2,1)} collective-permute-done((bf16[192,2048]{1,0:T(8,128)(2,1)}, bf16[192,2048]{1,0:T(8,128)(2,1)}, u32[]{:S(2)}, u32[]{:S(2)}) %collective-permute-start.24) | collective-permute-done | bytes 786464 | tf_op jit(solution)/shard_map/ppermute | solution.py:68
  236.5 14.3 %attend.1 = bf16[2048,256]{1,0:T(8,128)(2,1)} custom-call(s32[3,16]{1,0:T(4,128)} %pad_add_fusion.table, bf16[2048,512]{1,0:T(8,128)(2,1)} %bitcast.207), custom_call_target="tpu_custom_call" | custom-call | tf_op jit(solution)/shard_map/attend/pallas_call | solution.py:309
  252.5 5.9 all-to-all-start.1
  290.3 4.0 unpack.1
  294.3 3.6 convolution_convert_fusion.4
  321.4 8.9 collective-permute-done.33
  333.8 4.5 collective-permute-done.32
  341.7 19.1 %collective-permute-done.36 = bf16[256,2048]{1,0:T(8,128)(2,1)S(1)} collective-permute-done((bf16[256,2048]{1,0:T(8,128)(2,1)S(1)}, bf16[256,2048]{1,0:T(8,128)(2,1)S(1)}, u32[]{:S(2)}, u32[]{:S(2)}) %collective-permute-start.36) | collective-permute-done | bytes 1048608 | tf_op jit(solution)/shard_map/ppermute | solution.py:172
  363.9 17.4 %collective-permute-done.43 = bf16[256,1536]{1,0:T(8,128)(2,1)S(1)} collective-permute-done((bf16[256,1536]{1,0:T(8,128)(2,1)S(1)}, bf16[256,1536]{1,0:T(8,128)(2,1)S(1)}, u32[]{:S(2)}, u32[]{:S(2)}) %collective-permute-start.43) | collective-permute-done | bytes 786464 | tf_op jit(solution)/shard_map/ppermute | solution.py:68
  387.1 14.4 %collective-permute-done.45 = bf16[256,1536]{1,0:T(8,128)(2,1)S(1)} collective-permute-done((bf16[256,1536]{1,0:T(8,128)(2,1)S(1)}, bf16[256,1536]{1,0:T(8,128)(2,1)S(1)}, u32[]{:S(2)}, u32[]{:S(2)}) %collective-permute-start.45) | collective-permute-done | bytes 786464 | tf_op jit(solution)/shard_map/ppermute | solution.py:68
  404.5 5.1 fusion.19
  409.7 6.8 multiply_convert_fusion.3
  418.1 9.3 fusion.5
  427.8 7.3 collective-permute-done.47
  438.7 7.3 convolution_convert_fusion.2
  450.8 5.2 fusion.13
  455.9 7.0 multiply_convert_fusion.1
  462.9 9.3 fusion.8
  472.2 8.9 fusion.47
  486.3 9.6 %add_convert_fusion = bf16[1024,2048]{1,0:T(8,128)(2,1)S(1)} fusion(f32[1024,2048]{1,0:T(8,128)} %fusion.47, bf16[1024,1536]{0,1:T(8,128)(2,1)S(1)} %copy-done.26, bf16[2048,1536]{1,0:T(8,128)(2,1)S(1)} %constant_dynamic-update-slice_fusion.18), kind=kOutput, calls=%fused_computation.16 | convolution fusion | flops 6446645248 | bytes 22020096 | tf_op jit(solution)/shard_map/dot_general | solution.py:44
  495.9 4.7 collective-permute-done.53
  502.7 4.4 collective-permute-start.55
  512.2 3.6 add_convert_fusion.16
  522.3 7.1 convolution_convert_fusion
  529.4 7.5 convolution_convert_fusion.1
  556.4 10.8 %collective-permute-done.64 = bf16[256,1536]{1,0:T(8,128)(2,1)S(1)} collective-permute-done((bf16[256,1536]{1,0:T(8,128)(2,1)S(1)}, bf16[256,1536]{1,0:T(8,128)(2,1)S(1)}, u32[]{:S(2)}, u32[]{:S(2)}) %collective-permute-start.64) | collective-permute-done | bytes 786464 | tf_op jit(solution)/shard_map/ppermute | solution.py:68
  570.2 4.0 collective-permute-start.62
  576.6 10.7 %collective-permute-done.65 = bf16[128,1536]{1,0:T(8,128)(2,1)S(1)} collective-permute-done((bf16[128,1536]{1,0:T(8,128)(2,1)S(1)}, bf16[128,1536]{1,0:T(8,128)(2,1)S(1)}, u32[]{:S(2)}, u32[]{:S(2)}) %collective-permute-start.65) | collective-permute-done | bytes 393248 | tf_op jit(solution)/shard_map/ppermute | solution.py:68
  592.8 6.0 convolution_convert_fusion.8.rows_ref
  598.8 4.0 pack.1
  602.8 3.7 pad_maximum_fusion.2
  606.5 5.5 all-to-all-start.2
  612.0 10.0 %convolution_convert_fusion.3 = bf16[1024,2048]{1,0:T(8,128)(2,1)S(1)} fusion(bf16[1024,1536]{0,1:T(8,128)(2,1)} %copy-done.66, bf16[1536,2048]{1,0:T(8,128)(2,1)} %constant_dynamic-update-slice_fusion.9), kind=kOutput, calls=%fused_computation.25 | convolution fusion | flops 6444548096 | bytes 13631488 | tf_op jit(solution)/shard_map/dot_general | solution.py:36
  627.7 3.7 collective-permute-start.68
  631.4 14.9 %collective-permute-done.73 = bf16[128,2048]{1,0:T(8,128)(2,1)} collective-permute-done((bf16[128,2048]{1,0:T(8,128)(2,1)S(1)}, bf16[128,2048]{1,0:T(8,128)(2,1)}, u32[]{:S(2)}, u32[]{:S(2)}) %collective-permute-start.73) | collective-permute-done | bytes 524320 | tf_op jit(solution)/shard_map/ppermute | solution.py:68
  655.9 4.0 collective-permute-start.82
  663.5 18.9 %attend_back.1 = bf16[2048,512]{1,0:T(8,128)(2,1)} custom-call(s32[3,16]{1,0:T(4,128)} %pad_add_fusion.table, bf16[2048,512]{1,0:T(8,128)(2,1)} %bitcast.208, bf16[2048,256]{1,0:T(8,128)(2,1)} %bitcast.83.grad_ref), custom_call_target="tpu_custom_call" | custom-call | tf_op jit(solution)/shard_map/attend_back/pallas_call | solution.py:322
  683.7 4.3 all-to-all-start.3
  703.2 4.6 collective-permute-done.69
  707.8 3.7 add_convert_fusion.6
  711.5 40.0 %collective-permute-done.77 = bf16[256,1536]{1,0:T(8,128)(2,1)S(1)} collective-permute-done((bf16[256,1536]{1,0:T(8,128)(2,1)S(1)}, bf16[256,1536]{1,0:T(8,128)(2,1)S(1)}, u32[]{:S(2)}, u32[]{:S(2)}) %collective-permute-start.77) | collective-permute-done | bytes 786464 | tf_op jit(solution)/shard_map/ppermute | solution.py:68
  753.8 20.2 %collective-permute-done.79 = bf16[256,2048]{1,0:T(8,128)(2,1)} collective-permute-done((bf16[256,2048]{1,0:T(8,128)(2,1)S(1)}, bf16[256,2048]{1,0:T(8,128)(2,1)}, u32[]{:S(2)}, u32[]{:S(2)}) %collective-permute-start.79) | collective-permute-done | bytes 1048608 | tf_op jit(solution)/shard_map/ppermute | solution.py:68
  774.0 8.0 unfinish.1
  782.0 7.5 convolution_convert_fusion.6
  794.9 4.8 convolution_convert_fusion.5
  822.7 3.6 collective-permute-done.95
  851.2 12.6 %collective-permute-done.88 = bf16[288,1024]{1,0:T(8,128)(2,1)} collective-permute-done((bf16[288,1024]{1,0:T(8,128)(2,1)}, bf16[288,1024]{1,0:T(8,128)(2,1)}, u32[]{:S(2)}, u32[]{:S(2)}) %collective-permute-start.88) | collective-permute-done | bytes 589856 | tf_op jit(solution)/shard_map/ppermute | solution.py:68
  875.3 26.7 %collective-permute-done.93 = bf16[288,1024]{1,0:T(8,128)(2,1)S(1)} collective-permute-done((bf16[288,1024]{1,0:T(8,128)(2,1)S(1)}, bf16[288,1024]{1,0:T(8,128)(2,1)S(1)}, u32[]{:S(2)}, u32[]{:S(2)}) %collective-permute-start.93) | collective-permute-done | bytes 589856 | tf_op jit(solution)/shard_map/ppermute | solution.py:68
  906.7 5.6 collective-permute-start.104
  912.3 3.6 collective-permute-done.97
  921.1 9.8 %collective-permute-start.101 = (bf16[80,1024]{1,0:T(8,128)(2,1)S(1)}, bf16[80,1024]{1,0:T(8,128)(2,1)S(1)}, u32[]{:S(2)}, u32[]{:S(2)}) collective-permute-start(bf16[80,1024]{1,0:T(8,128)(2,1)S(1)} %get-tuple-element.280), channel_id=1, source_target_pairs={{0,3},{1,2},{2,1},{3,0},{4,7},{5,6},{6,5},{7,4},{8,11},{9,10},{10,... | collective-permute-start | bytes 491528 | tf_op jit(solution)/shard_map/ppermute | solution.py:172
  932.9 5.0 fusion.25
  (604 shorter events, 320.9 us)
Async XLA Ops:
  8.6 19.6 %collective-permute-start.3 = (bf16[96,1024]{1,0:T(8,128)(2,1)S(1)}, bf16[96,1024]{1,0:T(8,128)(2,1)S(1)}, u32[]{:S(2)}, u32[]{:S(2)}) collective-permute-start(bf16[96,1024]{1,0:T(8,128)(2,1)S(1)} %get-tuple-element.276), channel_id=1, source_target_pairs={{0,1},{1,0},{2,3},{3,2},{4,5},{5,4},{6,7},{7,6},{8,9},{9,8},{10,11... | collective-permute-start | bytes 589832 | tf_op jit(solution)/shard_map/ppermute | solution.py:172
  8.8 38.1 %collective-permute-start.7 = (bf16[192,2048]{1,0:T(8,128)(2,1)S(1)}, bf16[192,2048]{1,0:T(8,128)(2,1)}, u32[]{:S(2)}, u32[]{:S(2)}) collective-permute-start(bf16[192,2048]{1,0:T(8,128)(2,1)S(1)} %copy-done.67), channel_id=1, source_target_pairs={{0,8},{8,16},{16,24},{24,28},{28,20},{20,12},{12,4},{4,0},{1,9},{9... | collective-permute-start | bytes 2359304 | tf_op jit(solution)/shard_map/ppermute | solution.py:68
  10.1 36.8 %collective-permute-start.8 = (bf16[192,2048]{1,0:T(8,128)(2,1)S(1)}, bf16[192,2048]{1,0:T(8,128)(2,1)}, u32[]{:S(2)}, u32[]{:S(2)}) collective-permute-start(bf16[192,2048]{1,0:T(8,128)(2,1)S(1)} %copy-done.67), channel_id=1, source_target_pairs={{8,0},{16,8},{24,16},{28,24},{20,28},{12,20},{4,12},{0,4},{9,1},{1... | collective-permute-start | bytes 2359304 | tf_op jit(solution)/shard_map/ppermute | solution.py:68
  23.8 20.7 %collective-permute-start.6 = (bf16[64,2048]{1,0:T(8,128)(2,1)}, bf16[64,2048]{1,0:T(8,128)(2,1)}, u32[]{:S(2)}, u32[]{:S(2)}) collective-permute-start(bf16[64,2048]{1,0:T(8,128)(2,1)} %param.35), channel_id=1, source_target_pairs={{0,0},{1,4},{2,8},{3,12},{4,16},{5,20},{6,24},{7,28},{8,1},{9,5},{... | collective-permute-start | bytes 786440 | tf_op jit(solution)/shard_map/ppermute | solution.py:625
  26.9 36.2 %collective-permute-start.1 = (bf16[256,2048]{1,0:T(8,128)(2,1)S(1)}, bf16[256,2048]{1,0:T(8,128)(2,1)}, u32[]{:S(2)}, u32[]{:S(2)}) collective-permute-start(bf16[256,2048]{1,0:T(8,128)(2,1)S(1)} %copy-done), channel_id=1, source_target_pairs={{0,2},{1,3},{2,0},{3,1},{4,6},{5,7},{6,4},{7,5},{8,10},{9,11},{10,... | collective-permute-start | bytes 3145736 | tf_op jit(solution)/shard_map/ppermute | solution.py:172
  46.9 21.9 %collective-permute-start.9 = (bf16[416,1024]{1,0:T(8,128)(2,1)}, bf16[416,1024]{1,0:T(8,128)(2,1)S(1)}, u32[]{:S(2)}, u32[]{:S(2)}) collective-permute-start(bf16[416,1024]{1,0:T(8,128)(2,1)} %get-tuple-element.103), channel_id=1, source_target_pairs={{0,8},{8,16},{16,24},{24,28},{28,20},{20,12},{12,4},{4,0},{1,9},{9... | collective-permute-start | bytes 2555912 | tf_op jit(solution)/shard_map/ppermute | solution.py:68
  46.9 21.9 %collective-permute-start.10 = (bf16[416,1024]{1,0:T(8,128)(2,1)}, bf16[416,1024]{1,0:T(8,128)(2,1)S(1)}, u32[]{:S(2)}, u32[]{:S(2)}) collective-permute-start(bf16[416,1024]{1,0:T(8,128)(2,1)} %get-tuple-element.103), channel_id=1, source_target_pairs={{8,0},{16,8},{24,16},{28,24},{20,28},{12,20},{4,12},{0,4},{9,1},{1... | collective-permute-start | bytes 2555912 | tf_op jit(solution)/shard_map/ppermute | solution.py:68
  49.3 49.8 %collective-permute-start = (bf16[256,2048]{1,0:T(8,128)(2,1)S(1)}, bf16[256,2048]{1,0:T(8,128)(2,1)}, u32[]{:S(2)}, u32[]{:S(2)}) collective-permute-start(bf16[256,2048]{1,0:T(8,128)(2,1)S(1)} %copy-done), channel_id=1, source_target_pairs={{0,1},{1,0},{2,3},{3,2},{4,5},{5,4},{6,7},{7,6},{8,9},{9,8},{10,11... | collective-permute-start | bytes 3145736 | tf_op jit(solution)/shard_map/ppermute | solution.py:172
  63.1 36.0 %collective-permute-start.2 = (bf16[256,2048]{1,0:T(8,128)(2,1)}, bf16[256,2048]{1,0:T(8,128)(2,1)}, u32[]{:S(2)}, u32[]{:S(2)}) collective-permute-start(bf16[256,2048]{1,0:T(8,128)(2,1)} %collective-permute-done.1), channel_id=1, source_target_pairs={{0,1},{1,0},{2,3},{3,2},{4,5},{5,4},{6,7},{7,6},{8,9},{9,8},{10,11... | collective-permute-start | bytes 3145736 | tf_op jit(solution)/shard_map/ppermute | solution.py:172
  69.5 20.1 %collective-permute-start.11 = (bf16[416,1024]{1,0:T(8,128)(2,1)S(1)}, bf16[416,1024]{1,0:T(8,128)(2,1)}, u32[]{:S(2)}, u32[]{:S(2)}) collective-permute-start(bf16[416,1024]{1,0:T(8,128)(2,1)S(1)} %collective-permute-done.9), channel_id=1, source_target_pairs={{0,8},{8,16},{16,24},{24,28},{28,20},{20,12},{12,4},{4,0},{1,9},{9... | collective-permute-start | bytes 2555912 | tf_op jit(solution)/shard_map/ppermute | solution.py:68
  70.2 20.7 %collective-permute-start.12 = (bf16[416,1024]{1,0:T(8,128)(2,1)S(1)}, bf16[416,1024]{1,0:T(8,128)(2,1)}, u32[]{:S(2)}, u32[]{:S(2)}) collective-permute-start(bf16[416,1024]{1,0:T(8,128)(2,1)S(1)} %collective-permute-done.10), channel_id=1, source_target_pairs={{8,0},{16,8},{24,16},{28,24},{20,28},{12,20},{4,12},{0,4},{9,1},{1... | collective-permute-start | bytes 2555912 | tf_op jit(solution)/shard_map/ppermute | solution.py:68
  90.9 20.8 %collective-permute-start.14 = (bf16[416,1024]{1,0:T(8,128)(2,1)}, bf16[416,1024]{1,0:T(8,128)(2,1)S(1)}, u32[]{:S(2)}, u32[]{:S(2)}) collective-permute-start(bf16[416,1024]{1,0:T(8,128)(2,1)} %collective-permute-done.12), channel_id=1, source_target_pairs={{8,0},{16,8},{24,16},{28,24},{20,28},{12,20},{4,12},{0,4},{9,1},{1... | collective-permute-start | bytes 2555912 | tf_op jit(solution)/shard_map/ppermute | solution.py:68
  147.4 84.8 %all-to-all-start = ((bf16[8,256,512]{2,1,0:T(8,128)(2,1)}), bf16[8,256,512]{2,1,0:T(8,128)(2,1)S(1)}, u32[]{:S(2)}, u32[]{:S(2)}) async-start(bf16[8,256,512]{2,1,0:T(8,128)(2,1)} %bitcast.209), calls=%async_computation | async-start | bytes 4194304 | tf_op jit(solution)/shard_map/all_to_all | solution.py:679
  185.9 29.4 %collective-permute-start.22 = (bf16[256,1536]{1,0:T(8,128)(2,1)}, bf16[256,1536]{1,0:T(8,128)(2,1)}, u32[]{:S(2)}, u32[]{:S(2)}) collective-permute-start(bf16[256,1536]{1,0:T(8,128)(2,1)} %get-tuple-element.113), channel_id=1, source_target_pairs={{0,8},{8,16},{16,24},{24,28},{28,20},{20,12},{12,4},{4,0},{1,9},{9... | collective-permute-start | bytes 2359304 | tf_op jit(solution)/shard_map/ppermute | solution.py:68
  187.0 28.3 %collective-permute-start.23 = (bf16[256,1536]{1,0:T(8,128)(2,1)}, bf16[256,1536]{1,0:T(8,128)(2,1)}, u32[]{:S(2)}, u32[]{:S(2)}) collective-permute-start(bf16[256,1536]{1,0:T(8,128)(2,1)} %get-tuple-element.113), channel_id=1, source_target_pairs={{8,0},{16,8},{24,16},{28,24},{20,28},{12,20},{4,12},{0,4},{9,1},{1... | collective-permute-start | bytes 2359304 | tf_op jit(solution)/shard_map/ppermute | solution.py:68
  187.4 44.8 %collective-permute-start.24 = (bf16[192,2048]{1,0:T(8,128)(2,1)}, bf16[192,2048]{1,0:T(8,128)(2,1)}, u32[]{:S(2)}, u32[]{:S(2)}) collective-permute-start(bf16[192,2048]{1,0:T(8,128)(2,1)} %collective-permute-done.17), channel_id=1, source_target_pairs={{0,8},{8,16},{16,24},{24,28},{28,20},{20,12},{12,4},{4,0},{1,9},{9... | collective-permute-start | bytes 2359304 | tf_op jit(solution)/shard_map/ppermute | solution.py:68
  188.5 43.7 %collective-permute-start.25 = (bf16[192,2048]{1,0:T(8,128)(2,1)}, bf16[192,2048]{1,0:T(8,128)(2,1)}, u32[]{:S(2)}, u32[]{:S(2)}) collective-permute-start(bf16[192,2048]{1,0:T(8,128)(2,1)} %collective-permute-done.18), channel_id=1, source_target_pairs={{8,0},{16,8},{24,16},{28,24},{20,28},{12,20},{4,12},{0,4},{9,1},{1... | collective-permute-start | bytes 2359304 | tf_op jit(solution)/shard_map/ppermute | solution.py:68
  252.5 37.8 %all-to-all-start.1 = ((bf16[8,256,256]{2,1,0:T(8,128)(2,1)}), bf16[8,256,256]{2,1,0:T(8,128)(2,1)}, u32[]{:S(2)}, u32[]{:S(2)}) async-start(bf16[8,256,256]{2,1,0:T(8,128)(2,1)} %bitcast.219), calls=%async_computation.1 | async-start | bytes 2097152 | tf_op jit(solution)/shard_map/all_to_all | solution.py:684
  311.1 21.1 %collective-permute-start.34 = (bf16[256,1536]{1,0:T(8,128)(2,1)}, bf16[256,1536]{1,0:T(8,128)(2,1)S(1)}, u32[]{:S(2)}, u32[]{:S(2)}) collective-permute-start(bf16[256,1536]{1,0:T(8,128)(2,1)} %collective-permute-done.27), channel_id=1, source_target_pairs={{8,0},{16,8},{24,16},{28,24},{20,28},{12,20},{4,12},{0,4},{9,1},{1... | collective-permute-start | bytes 2359304 | tf_op jit(solution)/shard_map/ppermute | solution.py:68
  312.5 19.8 %collective-permute-start.30 = (bf16[256,2048]{1,0:T(8,128)(2,1)S(1)}, bf16[256,2048]{1,0:T(8,128)(2,1)S(1)}, u32[]{:S(2)}, u32[]{:S(2)}) collective-permute-start(bf16[256,2048]{1,0:T(8,128)(2,1)S(1)} %get-tuple-element.243), channel_id=1, source_target_pairs={{0,1},{1,0},{2,3},{3,2},{4,5},{5,4},{6,7},{7,6},{8,9},{9,8},{10,11... | collective-permute-start | bytes 3145736 | tf_op jit(solution)/shard_map/ppermute | solution.py:172
  313.5 24.8 %collective-permute-start.32 = (bf16[256,2048]{1,0:T(8,128)(2,1)S(1)}, bf16[256,2048]{1,0:T(8,128)(2,1)S(1)}, u32[]{:S(2)}, u32[]{:S(2)}) collective-permute-start(bf16[256,2048]{1,0:T(8,128)(2,1)S(1)} %add_convert_fusion.9), channel_id=1, source_target_pairs={{0,2},{1,3},{2,0},{3,1},{4,6},{5,7},{6,4},{7,5},{8,10},{9,11},{10,... | collective-permute-start | bytes 3145736 | tf_op jit(solution)/shard_map/ppermute | solution.py:172
  331.3 29.5 %collective-permute-start.36 = (bf16[256,2048]{1,0:T(8,128)(2,1)S(1)}, bf16[256,2048]{1,0:T(8,128)(2,1)S(1)}, u32[]{:S(2)}, u32[]{:S(2)}) collective-permute-start(bf16[256,2048]{1,0:T(8,128)(2,1)S(1)} %copy-done.5), channel_id=1, source_target_pairs={{0,2},{1,3},{2,0},{3,1},{4,6},{5,7},{6,4},{7,5},{8,10},{9,11},{10,... | collective-permute-start | bytes 3145736 | tf_op jit(solution)/shard_map/ppermute | solution.py:172
  331.3 32.5 %collective-permute-start.35 = (bf16[256,2048]{1,0:T(8,128)(2,1)S(1)}, bf16[256,2048]{1,0:T(8,128)(2,1)S(1)}, u32[]{:S(2)}, u32[]{:S(2)}) collective-permute-start(bf16[256,2048]{1,0:T(8,128)(2,1)S(1)} %copy-done.5), channel_id=1, source_target_pairs={{0,1},{1,0},{2,3},{3,2},{4,5},{5,4},{6,7},{7,6},{8,9},{9,8},{10,11... | collective-permute-start | bytes 3145736 | tf_op jit(solution)/shard_map/ppermute | solution.py:172
  332.3 29.8 %collective-permute-start.42 = (bf16[128,1536]{1,0:T(8,128)(2,1)S(1)}, bf16[128,1536]{1,0:T(8,128)(2,1)S(1)}, u32[]{:S(2)}, u32[]{:S(2)}) collective-permute-start(bf16[128,1536]{1,0:T(8,128)(2,1)S(1)} %slice.321), channel_id=1, source_target_pairs={{8,0},{16,8},{24,16},{28,24},{20,28},{12,20},{4,12},{0,4},{9,1},{1... | collective-permute-start | bytes 1179656 | tf_op jit(solution)/shard_map/ppermute | solution.py:68
  332.3 29.8 %collective-permute-start.41 = (bf16[128,1536]{1,0:T(8,128)(2,1)S(1)}, bf16[128,1536]{1,0:T(8,128)(2,1)S(1)}, u32[]{:S(2)}, u32[]{:S(2)}) collective-permute-start(bf16[128,1536]{1,0:T(8,128)(2,1)S(1)} %slice.320), channel_id=1, source_target_pairs={{0,8},{8,16},{16,24},{24,28},{28,20},{20,12},{12,4},{4,0},{1,9},{9... | collective-permute-start | bytes 1179656 | tf_op jit(solution)/shard_map/ppermute | solution.py:68
  339.6 43.7 %collective-permute-start.39 = (bf16[256,2048]{1,0:T(8,128)(2,1)S(1)}, bf16[256,2048]{1,0:T(8,128)(2,1)S(1)}, u32[]{:S(2)}, u32[]{:S(2)}) collective-permute-start(bf16[256,2048]{1,0:T(8,128)(2,1)S(1)} %multiply_convert_fusion.4), channel_id=1, source_target_pairs={{0,2},{1,3},{2,0},{3,1},{4,6},{5,7},{6,4},{7,5},{8,10},{9,11},{10,... | collective-permute-start | bytes 3145736 | tf_op jit(solution)/shard_map/ppermute | solution.py:172
  360.8 26.0 %collective-permute-start.37 = (bf16[256,2048]{1,0:T(8,128)(2,1)S(1)}, bf16[256,2048]{1,0:T(8,128)(2,1)S(1)}, u32[]{:S(2)}, u32[]{:S(2)}) collective-permute-start(bf16[256,2048]{1,0:T(8,128)(2,1)S(1)} %collective-permute-done.36), channel_id=1, source_target_pairs={{0,1},{1,0},{2,3},{3,2},{4,5},{5,4},{6,7},{7,6},{8,9},{9,8},{10,11... | collective-permute-start | bytes 3145736 | tf_op jit(solution)/shard_map/ppermute | solution.py:172
  383.3 20.5 %collective-permute-start.38 = (bf16[256,2048]{1,0:T(8,128)(2,1)S(1)}, bf16[256,2048]{1,0:T(8,128)(2,1)S(1)}, u32[]{:S(2)}, u32[]{:S(2)}) collective-permute-start(bf16[256,2048]{1,0:T(8,128)(2,1)S(1)} %multiply_convert_fusion.4), channel_id=1, source_target_pairs={{0,1},{1,0},{2,3},{3,2},{4,5},{5,4},{6,7},{7,6},{8,9},{9,8},{10,11... | collective-permute-start | bytes 3145736 | tf_op jit(solution)/shard_map/ppermute | solution.py:172
  384.3 19.5 %collective-permute-start.46 = (bf16[256,1536]{1,0:T(8,128)(2,1)S(1)}, bf16[256,1536]{1,0:T(8,128)(2,1)S(1)}, u32[]{:S(2)}, u32[]{:S(2)}) collective-permute-start(bf16[256,1536]{1,0:T(8,128)(2,1)S(1)} %collective-permute-done.44), channel_id=1, source_target_pairs={{8,0},{16,8},{24,16},{28,24},{20,28},{12,20},{4,12},{0,4},{9,1},{1... | collective-permute-start | bytes 2359304 | tf_op jit(solution)/shard_map/ppermute | solution.py:68
  515.8 24.3 %collective-permute-start.59 = (bf16[256,1536]{1,0:T(8,128)(2,1)}, bf16[256,1536]{1,0:T(8,128)(2,1)}, u32[]{:S(2)}, u32[]{:S(2)}) collective-permute-start(bf16[256,1536]{1,0:T(8,128)(2,1)} %get-tuple-element.215), channel_id=1, source_target_pairs={{8,0},{16,8},{24,16},{28,24},{20,28},{12,20},{4,12},{0,4},{9,1},{1... | collective-permute-start | bytes 2359304 | tf_op jit(solution)/shard_map/ppermute | solution.py:68
  516.5 23.6 %collective-permute-start.58 = (bf16[256,1536]{1,0:T(8,128)(2,1)}, bf16[256,1536]{1,0:T(8,128)(2,1)}, u32[]{:S(2)}, u32[]{:S(2)}) collective-permute-start(bf16[256,1536]{1,0:T(8,128)(2,1)} %get-tuple-element.216), channel_id=1, source_target_pairs={{0,8},{8,16},{16,24},{24,28},{28,20},{20,12},{12,4},{4,0},{1,9},{9... | collective-permute-start | bytes 2359304 | tf_op jit(solution)/shard_map/ppermute | solution.py:68
  518.9 23.8 %collective-permute-start.57 = (bf16[256,2048]{1,0:T(8,128)(2,1)S(1)}, bf16[256,2048]{1,0:T(8,128)(2,1)S(1)}, u32[]{:S(2)}, u32[]{:S(2)}) collective-permute-start(bf16[256,2048]{1,0:T(8,128)(2,1)S(1)} %add_convert_fusion.8), channel_id=1, source_target_pairs={{0,2},{1,3},{2,0},{3,1},{4,6},{5,7},{6,4},{7,5},{8,10},{9,11},{10,... | collective-permute-start | bytes 3145736 | tf_op jit(solution)/shard_map/ppermute | solution.py:172
  547.3 22.9 %collective-permute-start.61 = (bf16[256,2048]{1,0:T(8,128)(2,1)S(1)}, bf16[256,2048]{1,0:T(8,128)(2,1)S(1)}, u32[]{:S(2)}, u32[]{:S(2)}) collective-permute-start(bf16[256,2048]{1,0:T(8,128)(2,1)S(1)} %fusion.48), channel_id=1, source_target_pairs={{0,2},{1,3},{2,0},{3,1},{4,6},{5,7},{6,4},{7,5},{8,10},{9,11},{10,... | collective-permute-start | bytes 3145736 | tf_op jit(solution)/shard_map/ppermute | solution.py:172
  552.5 78.9 %collective-permute-start.72 = (bf16[128,2048]{1,0:T(8,128)(2,1)}, bf16[128,2048]{1,0:T(8,128)(2,1)}, u32[]{:S(2)}, u32[]{:S(2)}) collective-permute-start(bf16[128,2048]{1,0:T(8,128)(2,1)} %get-tuple-element.204), channel_id=1, source_target_pairs={{0,8},{8,16},{16,24},{24,28},{28,20},{20,12},{12,4},{4,0},{1,9},{9... | collective-permute-start | bytes 1572872 | tf_op jit(solution)/shard_map/ppermute | solution.py:68
  553.6 37.3 %collective-permute-start.60 = (bf16[256,2048]{1,0:T(8,128)(2,1)S(1)}, bf16[256,2048]{1,0:T(8,128)(2,1)S(1)}, u32[]{:S(2)}, u32[]{:S(2)}) collective-permute-start(bf16[256,2048]{1,0:T(8,128)(2,1)S(1)} %fusion.48), channel_id=1, source_target_pairs={{0,1},{1,0},{2,3},{3,2},{4,5},{5,4},{6,7},{7,6},{8,9},{9,8},{10,11... | collective-permute-start | bytes 3145736 | tf_op jit(solution)/shard_map/ppermute | solution.py:172
  570.2 20.6 %collective-permute-start.62 = (bf16[256,2048]{1,0:T(8,128)(2,1)S(1)}, bf16[256,2048]{1,0:T(8,128)(2,1)S(1)}, u32[]{:S(2)}, u32[]{:S(2)}) collective-permute-start(bf16[256,2048]{1,0:T(8,128)(2,1)S(1)} %collective-permute-done.61), channel_id=1, source_target_pairs={{0,1},{1,0},{2,3},{3,2},{4,5},{5,4},{6,7},{7,6},{8,9},{9,8},{10,11... | collective-permute-start | bytes 3145736 | tf_op jit(solution)/shard_map/ppermute | solution.py:172
  588.4 43.0 %collective-permute-start.70 = (bf16[256,1536]{1,0:T(8,128)(2,1)}, bf16[256,1536]{1,0:T(8,128)(2,1)}, u32[]{:S(2)}, u32[]{:S(2)}) collective-permute-start(bf16[256,1536]{1,0:T(8,128)(2,1)} %pad_maximum_fusion.12), channel_id=1, source_target_pairs={{0,8},{8,16},{16,24},{24,28},{28,20},{20,12},{12,4},{4,0},{1,9},{9... | collective-permute-start | bytes 2359304 | tf_op jit(solution)/shard_map/ppermute | solution.py:68
  590.1 41.3 %collective-permute-start.71 = (bf16[256,1536]{1,0:T(8,128)(2,1)}, bf16[256,1536]{1,0:T(8,128)(2,1)}, u32[]{:S(2)}, u32[]{:S(2)}) collective-permute-start(bf16[256,1536]{1,0:T(8,128)(2,1)} %pad_maximum_fusion.13), channel_id=1, source_target_pairs={{8,0},{16,8},{24,16},{28,24},{20,28},{12,20},{4,12},{0,4},{9,1},{1... | collective-permute-start | bytes 2359304 | tf_op jit(solution)/shard_map/ppermute | solution.py:68
  606.5 39.8 %all-to-all-start.2 = ((bf16[8,256,256]{2,1,0:T(8,128)(2,1)}), bf16[8,256,256]{2,1,0:T(8,128)(2,1)}, u32[]{:S(2)}, u32[]{:S(2)}) async-start(bf16[8,256,256]{2,1,0:T(8,128)(2,1)} %bitcast.216), calls=%async_computation.2 | async-start | bytes 2097152 | tf_op jit(solution)/shard_map/all_to_all | solution.py:679
  626.1 20.1 %collective-permute-start.73 = (bf16[128,2048]{1,0:T(8,128)(2,1)S(1)}, bf16[128,2048]{1,0:T(8,128)(2,1)}, u32[]{:S(2)}, u32[]{:S(2)}) collective-permute-start(bf16[128,2048]{1,0:T(8,128)(2,1)S(1)} %pad_maximum_fusion.21), channel_id=1, source_target_pairs={{8,0},{16,8},{24,16},{28,24},{20,28},{12,20},{4,12},{0,4},{9,1},{1... | collective-permute-start | bytes 1572872 | tf_op jit(solution)/shard_map/ppermute | solution.py:68
  627.7 32.8 %collective-permute-start.68 = (bf16[256,2048]{1,0:T(8,128)(2,1)}, bf16[256,2048]{1,0:T(8,128)(2,1)}, u32[]{:S(2)}, u32[]{:S(2)}) collective-permute-start(bf16[256,2048]{1,0:T(8,128)(2,1)} %get-tuple-element.240), channel_id=1, source_target_pairs={{0,1},{1,0},{2,3},{3,2},{4,5},{5,4},{6,7},{7,6},{8,9},{9,8},{10,11... | collective-permute-start | bytes 3145736 | tf_op jit(solution)/shard_map/ppermute | solution.py:172
  652.3 30.1 %collective-permute-start.75 = (bf16[256,1536]{1,0:T(8,128)(2,1)}, bf16[256,1536]{1,0:T(8,128)(2,1)}, u32[]{:S(2)}, u32[]{:S(2)}) collective-permute-start(bf16[256,1536]{1,0:T(8,128)(2,1)} %get-tuple-element.207), channel_id=1, source_target_pairs={{8,0},{16,8},{24,16},{28,24},{20,28},{12,20},{4,12},{0,4},{9,1},{1... | collective-permute-start | bytes 2359304 | tf_op jit(solution)/shard_map/ppermute | solution.py:68
  652.3 30.6 %collective-permute-start.74 = (bf16[256,1536]{1,0:T(8,128)(2,1)}, bf16[256,1536]{1,0:T(8,128)(2,1)}, u32[]{:S(2)}, u32[]{:S(2)}) collective-permute-start(bf16[256,1536]{1,0:T(8,128)(2,1)} %get-tuple-element.208), channel_id=1, source_target_pairs={{0,8},{8,16},{16,24},{24,28},{28,20},{20,12},{12,4},{4,0},{1,9},{9... | collective-permute-start | bytes 2359304 | tf_op jit(solution)/shard_map/ppermute | solution.py:68
  655.9 32.1 %collective-permute-start.82 = (bf16[64,1536]{1,0:T(8,128)(2,1)}, bf16[64,1536]{1,0:T(8,128)(2,1)}, u32[]{:S(2)}, u32[]{:S(2)}) collective-permute-start(bf16[64,1536]{1,0:T(8,128)(2,1)} %get-tuple-element.268), channel_id=1, source_target_pairs={{0,3},{1,2},{2,1},{3,0},{4,7},{5,6},{6,5},{7,4},{8,11},{9,10},{10,... | collective-permute-start | bytes 589832 | tf_op jit(solution)/shard_map/ppermute | solution.py:172
  659.9 28.1 %collective-permute-start.81 = (bf16[64,1536]{1,0:T(8,128)(2,1)}, bf16[64,1536]{1,0:T(8,128)(2,1)}, u32[]{:S(2)}, u32[]{:S(2)}) collective-permute-start(bf16[64,1536]{1,0:T(8,128)(2,1)} %get-tuple-element.269), channel_id=1, source_target_pairs={{0,2},{1,3},{2,0},{3,1},{4,6},{5,7},{6,4},{7,5},{8,10},{9,11},{10,... | collective-permute-start | bytes 589832 | tf_op jit(solution)/shard_map/ppermute | solution.py:172
  660.5 27.5 %collective-permute-start.80 = (bf16[64,1536]{1,0:T(8,128)(2,1)}, bf16[64,1536]{1,0:T(8,128)(2,1)}, u32[]{:S(2)}, u32[]{:S(2)}) collective-permute-start(bf16[64,1536]{1,0:T(8,128)(2,1)} %get-tuple-element.270), channel_id=1, source_target_pairs={{0,1},{1,0},{2,3},{3,2},{4,5},{5,4},{6,7},{7,6},{8,9},{9,8},{10,11... | collective-permute-start | bytes 589832 | tf_op jit(solution)/shard_map/ppermute | solution.py:172
  682.8 25.0 %collective-permute-start.69 = (bf16[256,2048]{1,0:T(8,128)(2,1)}, bf16[256,2048]{1,0:T(8,128)(2,1)}, u32[]{:S(2)}, u32[]{:S(2)}) collective-permute-start(bf16[256,2048]{1,0:T(8,128)(2,1)} %add_convert_fusion.7), channel_id=1, source_target_pairs={{0,2},{1,3},{2,0},{3,1},{4,6},{5,7},{6,4},{7,5},{8,10},{9,11},{10,... | collective-permute-start | bytes 3145736 | tf_op jit(solution)/shard_map/ppermute | solution.py:172
  683.7 90.3 %all-to-all-start.3 = ((bf16[8,256,512]{2,1,0:T(8,128)(2,1)}), bf16[8,256,512]{2,1,0:T(8,128)(2,1)}, u32[]{:S(2)}, u32[]{:S(2)}) async-start(bf16[8,256,512]{2,1,0:T(8,128)(2,1)} %bitcast.210), calls=%async_computation.3 | async-start | bytes 4194304 | tf_op jit(solution)/shard_map/all_to_all | solution.py:684
  697.4 54.1 %collective-permute-start.77 = (bf16[256,1536]{1,0:T(8,128)(2,1)S(1)}, bf16[256,1536]{1,0:T(8,128)(2,1)S(1)}, u32[]{:S(2)}, u32[]{:S(2)}) collective-permute-start(bf16[256,1536]{1,0:T(8,128)(2,1)S(1)} %get-tuple-element.205), channel_id=1, source_target_pairs={{8,0},{16,8},{24,16},{28,24},{20,28},{12,20},{4,12},{0,4},{9,1},{1... | collective-permute-start | bytes 2359304 | tf_op jit(solution)/shard_map/ppermute | solution.py:68
  697.5 54.0 %collective-permute-start.76 = (bf16[256,1536]{1,0:T(8,128)(2,1)S(1)}, bf16[256,1536]{1,0:T(8,128)(2,1)S(1)}, u32[]{:S(2)}, u32[]{:S(2)}) collective-permute-start(bf16[256,1536]{1,0:T(8,128)(2,1)S(1)} %get-tuple-element.206), channel_id=1, source_target_pairs={{0,8},{8,16},{16,24},{24,28},{28,20},{20,12},{12,4},{4,0},{1,9},{9... | collective-permute-start | bytes 2359304 | tf_op jit(solution)/shard_map/ppermute | solution.py:68
  700.2 73.8 %collective-permute-start.79 = (bf16[256,2048]{1,0:T(8,128)(2,1)S(1)}, bf16[256,2048]{1,0:T(8,128)(2,1)}, u32[]{:S(2)}, u32[]{:S(2)}) collective-permute-start(bf16[256,2048]{1,0:T(8,128)(2,1)S(1)} %pad_maximum_fusion.6), channel_id=1, source_target_pairs={{8,0},{16,8},{24,16},{28,24},{20,28},{12,20},{4,12},{0,4},{9,1},{1... | collective-permute-start | bytes 3145736 | tf_op jit(solution)/shard_map/ppermute | solution.py:68
  701.8 72.2 %collective-permute-start.78 = (bf16[256,2048]{1,0:T(8,128)(2,1)S(1)}, bf16[256,2048]{1,0:T(8,128)(2,1)}, u32[]{:S(2)}, u32[]{:S(2)}) collective-permute-start(bf16[256,2048]{1,0:T(8,128)(2,1)S(1)} %fusion.34), channel_id=1, source_target_pairs={{0,8},{8,16},{16,24},{24,28},{28,20},{20,12},{12,4},{4,0},{1,9},{9... | collective-permute-start | bytes 3145736 | tf_op jit(solution)/shard_map/ppermute | solution.py:68
  803.9 30.5 %collective-permute-start.83 = (bf16[256,2048]{1,0:T(8,128)(2,1)}, bf16[256,2048]{1,0:T(8,128)(2,1)}, u32[]{:S(2)}, u32[]{:S(2)}) collective-permute-start(bf16[256,2048]{1,0:T(8,128)(2,1)} %get-tuple-element.237), channel_id=1, source_target_pairs={{0,1},{1,0},{2,3},{3,2},{4,5},{5,4},{6,7},{7,6},{8,9},{9,8},{10,11... | collective-permute-start | bytes 3145736 | tf_op jit(solution)/shard_map/ppermute | solution.py:172
  805.2 24.9 %collective-permute-start.84 = (bf16[256,2048]{1,0:T(8,128)(2,1)}, bf16[256,2048]{1,0:T(8,128)(2,1)}, u32[]{:S(2)}, u32[]{:S(2)}) collective-permute-start(bf16[256,2048]{1,0:T(8,128)(2,1)} %get-tuple-element.238), channel_id=1, source_target_pairs={{0,1},{1,0},{2,3},{3,2},{4,5},{5,4},{6,7},{7,6},{8,9},{9,8},{10,11... | collective-permute-start | bytes 3145736 | tf_op jit(solution)/shard_map/ppermute | solution.py:172
  822.7 25.3 %collective-permute-start.91 = (bf16[256,2048]{1,0:T(8,128)(2,1)}, bf16[256,2048]{1,0:T(8,128)(2,1)}, u32[]{:S(2)}, u32[]{:S(2)}) collective-permute-start(bf16[256,2048]{1,0:T(8,128)(2,1)} %add_convert_fusion.3), channel_id=1, source_target_pairs={{8,0},{16,8},{24,16},{28,24},{20,28},{12,20},{4,12},{0,4},{9,1},{1... | collective-permute-start | bytes 3145736 | tf_op jit(solution)/shard_map/ppermute | solution.py:68
  826.3 24.9 %collective-permute-start.90 = (bf16[256,2048]{1,0:T(8,128)(2,1)}, bf16[256,2048]{1,0:T(8,128)(2,1)}, u32[]{:S(2)}, u32[]{:S(2)}) collective-permute-start(bf16[256,2048]{1,0:T(8,128)(2,1)} %add_convert_fusion.4), channel_id=1, source_target_pairs={{0,8},{8,16},{16,24},{24,28},{28,20},{20,12},{12,4},{4,0},{1,9},{9... | collective-permute-start | bytes 3145736 | tf_op jit(solution)/shard_map/ppermute | solution.py:68
  833.2 32.5 %collective-permute-start.85 = (bf16[256,2048]{1,0:T(8,128)(2,1)}, bf16[256,2048]{1,0:T(8,128)(2,1)}, u32[]{:S(2)}, u32[]{:S(2)}) collective-permute-start(bf16[256,2048]{1,0:T(8,128)(2,1)} %add_convert_fusion.5), channel_id=1, source_target_pairs={{0,2},{1,3},{2,0},{3,1},{4,6},{5,7},{6,4},{7,5},{8,10},{9,11},{10,... | collective-permute-start | bytes 3145736 | tf_op jit(solution)/shard_map/ppermute | solution.py:172
  836.4 27.4 %collective-permute-start.88 = (bf16[288,1024]{1,0:T(8,128)(2,1)}, bf16[288,1024]{1,0:T(8,128)(2,1)}, u32[]{:S(2)}, u32[]{:S(2)}) collective-permute-start(bf16[288,1024]{1,0:T(8,128)(2,1)} %pad_maximum_fusion.18), channel_id=1, source_target_pairs={{0,8},{8,16},{16,24},{24,28},{28,20},{20,12},{12,4},{4,0},{1,9},{9... | collective-permute-start | bytes 1769480 | tf_op jit(solution)/shard_map/ppermute | solution.py:68
  838.5 25.3 %collective-permute-start.89 = (bf16[288,1024]{1,0:T(8,128)(2,1)}, bf16[288,1024]{1,0:T(8,128)(2,1)}, u32[]{:S(2)}, u32[]{:S(2)}) collective-permute-start(bf16[288,1024]{1,0:T(8,128)(2,1)} %pad_maximum_fusion.19), channel_id=1, source_target_pairs={{8,0},{16,8},{24,16},{28,24},{20,28},{12,20},{4,12},{0,4},{9,1},{1... | collective-permute-start | bytes 1769480 | tf_op jit(solution)/shard_map/ppermute | solution.py:68
  865.6 38.4 %collective-permute-start.103 = (bf16[256,2048]{1,0:T(8,128)(2,1)S(1)}, bf16[256,2048]{1,0:T(8,128)(2,1)S(1)}, u32[]{:S(2)}, u32[]{:S(2)}) collective-permute-start(bf16[256,2048]{1,0:T(8,128)(2,1)S(1)} %add_convert_fusion.1), channel_id=1, source_target_pairs={{8,0},{16,8},{24,16},{28,24},{20,28},{12,20},{4,12},{0,4},{9,1},{1... | collective-permute-start | bytes 3145736 | tf_op jit(solution)/shard_map/ppermute | solution.py:68
  867.3 34.6 %collective-permute-start.93 = (bf16[288,1024]{1,0:T(8,128)(2,1)S(1)}, bf16[288,1024]{1,0:T(8,128)(2,1)S(1)}, u32[]{:S(2)}, u32[]{:S(2)}) collective-permute-start(bf16[288,1024]{1,0:T(8,128)(2,1)S(1)} %get-tuple-element.290), channel_id=1, source_target_pairs={{8,0},{16,8},{24,16},{28,24},{20,28},{12,20},{4,12},{0,4},{9,1},{1... | collective-permute-start | bytes 1769480 | tf_op jit(solution)/shard_map/ppermute | solution.py:68
  867.4 34.6 %collective-permute-start.92 = (bf16[288,1024]{1,0:T(8,128)(2,1)S(1)}, bf16[288,1024]{1,0:T(8,128)(2,1)S(1)}, u32[]{:S(2)}, u32[]{:S(2)}) collective-permute-start(bf16[288,1024]{1,0:T(8,128)(2,1)S(1)} %get-tuple-element.291), channel_id=1, source_target_pairs={{0,8},{8,16},{16,24},{24,28},{28,20},{20,12},{12,4},{4,0},{1,9},{9... | collective-permute-start | bytes 1769480 | tf_op jit(solution)/shard_map/ppermute | solution.py:68
  870.6 33.4 %collective-permute-start.102 = (bf16[256,2048]{1,0:T(8,128)(2,1)S(1)}, bf16[256,2048]{1,0:T(8,128)(2,1)S(1)}, u32[]{:S(2)}, u32[]{:S(2)}) collective-permute-start(bf16[256,2048]{1,0:T(8,128)(2,1)S(1)} %add_convert_fusion.2), channel_id=1, source_target_pairs={{0,8},{8,16},{16,24},{24,28},{28,20},{20,12},{12,4},{4,0},{1,9},{9... | collective-permute-start | bytes 3145736 | tf_op jit(solution)/shard_map/ppermute | solution.py:68
  906.7 32.4 %collective-permute-start.104 = (bf16[64,2048]{1,0:T(8,128)(2,1)}, bf16[64,2048]{1,0:T(8,128)(2,1)S(1)}, u32[]{:S(2)}, u32[]{:S(2)}) collective-permute-start(bf16[64,2048]{1,0:T(8,128)(2,1)} %slice.527), channel_id=1, source_target_pairs={{0,0},{4,1},{8,2},{12,3},{16,4},{20,5},{24,6},{28,7},{1,8},{5,9},{... | collective-permute-start | bytes 786440 | tf_op jit(solution)/shard_map/ppermute | solution.py:807
  (140 other events, 2115.5 us)
